TPU v7x, 32 devices: a whole 2x2x4 slice. The times are simulated.
32 devices in a mesh: dp: 2 (over core), expert: 4 (over z), tensor: 4 (over y, x).
Axes of the slice: x: 2, y: 2, z: 4, core: 2. Of those that a mesh axis runs over, the one named last changes fastest.
Arguments:
- tokens: bfloat16 [24, 197, 768], P(('dp', 'expert'))
- cotangent: bfloat16 [24, 197, 768], P(('dp', 'expert')), may hold values from -6 to 6
- expert_ids: int32 [24, 197, 2], P(('dp', 'expert')), may hold values from 0 to 3, as said below
- slot_rank: int32 [24, 197, 2], P(('dp', 'expert')), may hold values from -1 to 368, as said below
- qkv_weight: bfloat16 [3, 768, 768], P(None, None, 'tensor'), may hold values from -0.3125 to 0.3125
- out_weight: bfloat16 [768, 768], P('tensor'), may hold values from -0.625 to 0.625
- router_weight: bfloat16 [768, 4], replicated, may hold values from -0.15625 to 0.15625
- expert_in: bfloat16 [4, 768, 3072], P('expert', None, 'tensor'), may hold values from -0.21875 to 0.21875
- expert_out: bfloat16 [4, 3072, 768], P('expert', 'tensor'), may hold values from -0.875 to 0.875
- gain_attention: float32 [768], replicated, may hold values from 0.25 to 1.75
- gain_experts: float32 [768], replicated, may hold values from 0.25 to 1.75
Outputs:
- block_out: bfloat16 [24, 197, 768], P(('dp', 'expert'))
- grad_tokens: float32 [24, 197, 768], P(('dp', 'expert'))
- grad_qkv: float32 [3, 768, 768], P(None, None, 'tensor')
- grad_out: float32 [768, 768], P('tensor')
- grad_router: float32 [768, 4], replicated
- grad_expert_in: float32 [4, 768, 3072], P('expert', None, 'tensor')
- grad_expert_out: float32 [4, 3072, 768], P('expert', 'tensor')
- grad_gain_attention: float32 [768], replicated
- grad_gain_experts: float32 [768], replicated
- balance_loss: float32 [], replicated
Inputs may be any that keep to these rules, and one draw needn't show every extreme that they name: `expert_ids`: the two experts of a token differ. Within each aligned block of 591 tokens, the pairs that name one expert are ranked: first choices of all the block's tokens in token order, then second choices in token order. A pair's slot_rank is its rank if that is below 369, else -1. In every block some expert has its slot 368 filled and a pair dropped.
All inputs are finite; a program needn't handle non-finite values.
Results may differ from a plain program's by a relative error of at most 0.017.
The roundings to bfloat16 on the way count: a program that leaves them out, or rounds other values in their place, can miss the bound.
Values may be sent and summed in bfloat16 or wider, within the bound.
No kernel may reach another device: no remote copies, remote signals or barrier semaphores. Data moves between devices by JAX's collectives and lax.ppermute only.
A program may use at most 192 MiB of HBM per device.

v0:
```python
import functools
import math

import jax
import jax.numpy as jnp
from jax import lax
from jax.experimental import pallas as pl
from jax.experimental.pallas import tpu as pltpu
from jax.sharding import PartitionSpec as P

HD = 64


epsilon = 1e-06


def normalize(values, gain_row):
    center = values - jnp.mean(values, axis=-1, keepdims=True)
    inverse = lax.rsqrt(jnp.mean(center * center, axis=-1, keepdims=True) + epsilon)
    normed = center * inverse
    return (normed, inverse, normed * gain_row)


def normalize_back(upstream, normed, inverse, gain_row):
    scaled = upstream * gain_row
    result = inverse * (
        scaled
        - jnp.mean(scaled, axis=-1, keepdims=True)
        - normed * jnp.mean(scaled * normed, axis=-1, keepdims=True)
    )
    return (result, jnp.sum(upstream * normed, axis=0))


def exact_gelu(values):
    return jax.nn.gelu(values, approximate=False)


def body(
    tokens,
    cotangent,
    expert_ids,
    slot_rank,
    qkv_weight,
    out_weight,
    router_weight,
    expert_in,
    expert_out,
    gain_attention,
    gain_experts,
):
    images, seq_len, model_width = tokens.shape
    token_rows = images * seq_len
    local_width = qkv_weight.shape[2]
    local_heads = local_width // HD
    slice_width = model_width // lax.axis_size("tensor")
    experts = router_weight.shape[1]
    capacity = 5 * token_rows // (2 * experts)
    owners = lax.axis_size("expert")
    per_owner = experts // owners
    slot_total = experts * capacity
    score_scale = HD ** (-0.5)
    inputs = tokens.reshape(token_rows, model_width).astype(jnp.float32)
    normed_one, inverse_one, mixed_one = normalize(inputs, gain_attention)
    entered = mixed_one.astype(jnp.bfloat16)
    project = jnp.einsum(
        "td,cdf->ctf", entered, qkv_weight, preferred_element_type=jnp.float32
    ).astype(jnp.bfloat16)
    projected_heads = project.reshape(3, images, seq_len, local_heads, HD)
    queries, key_rows, value_rows = (projected_heads[0], projected_heads[1], projected_heads[2])
    scores = (
        jnp.einsum("ishe,ithe->ihst", queries, key_rows, preferred_element_type=jnp.float32)
        * score_scale
    )
    log_total = jax.nn.logsumexp(scores, axis=-1, keepdims=True)
    attn_probs = jnp.exp(scores - log_total).astype(jnp.bfloat16)
    attended = jnp.einsum(
        "ihst,ithe->ishe", attn_probs, value_rows, preferred_element_type=jnp.float32
    )
    attended = attended.astype(jnp.bfloat16).reshape(token_rows, local_width)
    attn_part = jnp.dot(attended, out_weight, preferred_element_type=jnp.float32)
    residual = inputs + lax.psum(attn_part, "tensor")
    normed_two, inverse_two, mixed_two = normalize(residual, gain_experts)
    routed = mixed_two.astype(jnp.bfloat16)
    route_prob = jax.nn.softmax(
        jnp.dot(routed, router_weight, preferred_element_type=jnp.float32), axis=-1
    )
    chosen = expert_ids.reshape(token_rows, 2)
    ranked = slot_rank.reshape(token_rows, 2)
    kept_mask = (ranked >= 0).astype(jnp.float32)
    position = jnp.where(ranked >= 0, chosen * capacity + ranked, slot_total).reshape(-1)
    send_rows = (
        jnp.zeros((slot_total, model_width), jnp.bfloat16)
        .at[position]
        .set(jnp.repeat(routed, 2, axis=0), mode="drop")
        .reshape(experts, capacity, model_width)
    )
    fragment = lax.all_to_all(send_rows, "expert", split_axis=0, concat_axis=0, tiled=True)
    grouped = fragment.reshape(owners, per_owner, fragment.shape[1], model_width)
    before = jnp.einsum("sjcd,jdf->sjcf", grouped, expert_in, preferred_element_type=jnp.float32)
    hidden = exact_gelu(before).astype(jnp.bfloat16)
    expert_part = jnp.einsum(
        "sjcf,jfd->sjcd", hidden, expert_out, preferred_element_type=jnp.float32
    )
    produced = lax.psum_scatter(expert_part, "tensor", scatter_dimension=3, tiled=True).astype(
        jnp.bfloat16
    )
    returned = lax.all_to_all(
        produced.reshape(experts, capacity, slice_width),
        "expert",
        split_axis=0,
        concat_axis=0,
        tiled=True,
    )
    returned = lax.all_gather(returned, "tensor", axis=2, tiled=True).reshape(
        slot_total, model_width
    )
    safe_index = jnp.minimum(position, slot_total - 1)
    picked = returned[safe_index].reshape(token_rows, 2, model_width).astype(jnp.float32)
    gate_values = jnp.take_along_axis(route_prob, chosen, axis=1) * kept_mask
    output = residual + jnp.sum(gate_values[:, :, None] * picked, axis=1)
    block_out = output.astype(jnp.bfloat16).reshape(images, seq_len, model_width)
    upstream = cotangent.reshape(token_rows, model_width).astype(jnp.float32)
    gate_grad = jnp.sum(upstream[:, None, :] * picked, axis=-1) * kept_mask
    member = (chosen[:, :, None] == jnp.arange(experts)[None, None, :]).astype(jnp.float32)
    route_grad = jnp.sum(member * gate_grad[:, :, None], axis=1)
    logit_grad = (
        route_prob * (route_grad - jnp.sum(route_grad * route_prob, axis=-1, keepdims=True))
    ).astype(jnp.bfloat16)
    row_grad = (
        (gate_values[:, :, None] * upstream[:, None, :])
        .astype(jnp.bfloat16)
        .reshape(2 * token_rows, model_width)
    )
    grad_send = (
        jnp.zeros((slot_total, model_width), jnp.bfloat16)
        .at[position]
        .set(row_grad, mode="drop")
        .reshape(experts, capacity, model_width)
    )
    grad_arrived = lax.all_to_all(grad_send, "expert", split_axis=0, concat_axis=0, tiled=True)
    grad_arrived = grad_arrived.reshape(owners, per_owner, capacity, model_width)
    hidden_grad = jnp.einsum(
        "sjcd,jfd->sjcf", grad_arrived, expert_out, preferred_element_type=jnp.float32
    )
    grad_expert_out = jnp.einsum(
        "sjcf,sjcd->jfd", hidden, grad_arrived, preferred_element_type=jnp.float32
    )
    pre_grad = jax.vjp(exact_gelu, before)[1](hidden_grad)[0].astype(jnp.bfloat16)
    grad_expert_in = jnp.einsum(
        "sjcd,sjcf->jdf", grouped, pre_grad, preferred_element_type=jnp.float32
    )
    buffer_part = jnp.einsum(
        "sjcf,jdf->sjcd", pre_grad, expert_in, preferred_element_type=jnp.float32
    )
    buffer_share = lax.psum_scatter(buffer_part, "tensor", scatter_dimension=3, tiled=True).astype(
        jnp.bfloat16
    )
    buffer_back = lax.all_to_all(
        buffer_share.reshape(experts, capacity, slice_width),
        "expert",
        split_axis=0,
        concat_axis=0,
        tiled=True,
    )
    buffer_grad = lax.all_gather(buffer_back, "tensor", axis=2, tiled=True).reshape(
        slot_total, model_width
    )
    routed_grad = jnp.sum(
        buffer_grad[safe_index].reshape(token_rows, 2, model_width).astype(jnp.float32)
        * kept_mask[:, :, None],
        axis=1,
    )
    routed_grad = routed_grad + jnp.dot(
        logit_grad, router_weight.T, preferred_element_type=jnp.float32
    )
    grad_router = jnp.einsum("td,te->de", routed, logit_grad, preferred_element_type=jnp.float32)
    from_norm_two, grad_gain_experts = normalize_back(
        routed_grad, normed_two, inverse_two, gain_experts
    )
    residual_grad = upstream + from_norm_two
    attn_grad = residual_grad.astype(jnp.bfloat16)
    grad_out = jnp.einsum("tf,td->fd", attended, attn_grad, preferred_element_type=jnp.float32)
    heads_grad = jnp.dot(attn_grad, out_weight.T, preferred_element_type=jnp.float32).astype(
        jnp.bfloat16
    )
    heads_grad = heads_grad.reshape(images, seq_len, local_heads, HD)
    again = (
        jnp.einsum("ishe,ithe->ihst", queries, key_rows, preferred_element_type=jnp.float32)
        * score_scale
    )
    probs_full = jnp.exp(again - log_total)
    prob_grad = jnp.einsum(
        "ishe,ithe->ihst", heads_grad, value_rows, preferred_element_type=jnp.float32
    )
    value_grad = jnp.einsum(
        "ihst,ishe->ithe",
        probs_full.astype(jnp.bfloat16),
        heads_grad,
        preferred_element_type=jnp.float32,
    )
    score_grad = (
        probs_full * (prob_grad - jnp.sum(prob_grad * probs_full, axis=-1, keepdims=True))
    ).astype(jnp.bfloat16)
    query_grad = (
        jnp.einsum("ihst,ithe->ishe", score_grad, key_rows, preferred_element_type=jnp.float32)
        * score_scale
    )
    key_grad = (
        jnp.einsum("ihst,ishe->ithe", score_grad, queries, preferred_element_type=jnp.float32)
        * score_scale
    )
    project_grad = (
        jnp.stack([query_grad, key_grad, value_grad])
        .astype(jnp.bfloat16)
        .reshape(3, token_rows, local_width)
    )
    grad_qkv = jnp.einsum("td,ctf->cdf", entered, project_grad, preferred_element_type=jnp.float32)
    entered_part = jnp.einsum(
        "ctf,cdf->td", project_grad, qkv_weight, preferred_element_type=jnp.float32
    )
    entered_grad = lax.psum(entered_part.astype(jnp.bfloat16), "tensor").astype(jnp.float32)
    from_norm_one, grad_gain_attention = normalize_back(
        entered_grad, normed_one, inverse_one, gain_attention
    )
    grad_tokens = (residual_grad + from_norm_one).reshape(images, seq_len, model_width)
    counts = jnp.sum(member, axis=(0, 1))
    prob_sum = jnp.sum(route_prob, axis=0)
    grad_qkv, grad_out, grad_router, grad_gain_attention, grad_gain_experts, counts, prob_sum = (
        lax.psum(
            (
                grad_qkv,
                grad_out,
                grad_router,
                grad_gain_attention,
                grad_gain_experts,
                counts,
                prob_sum,
            ),
            ("dp", "expert"),
        )
    )
    grad_expert_in, grad_expert_out = (
        lax.psum(grad_expert_in.astype(jnp.bfloat16), "dp").astype(jnp.float32),
        lax.psum(grad_expert_out.astype(jnp.bfloat16), "dp").astype(jnp.float32),
    )
    token_total = token_rows * lax.axis_size("dp") * lax.axis_size("expert")
    balance_loss = experts * jnp.sum(counts / (2.0 * token_total) * prob_sum / token_total)
    return (
        block_out,
        grad_tokens,
        grad_qkv,
        grad_out,
        grad_router,
        grad_expert_in,
        grad_expert_out,
        grad_gain_attention,
        grad_gain_experts,
        balance_loss,
    )


NN = ((1,), (0,))
NT = ((1,), (1,))
TN = ((0,), (0,))
LANES = 128
SMALL = 8


def round_up(value, step):
    return -(-value // step) * step


def contract(a, b, dims):
    return lax.dot_general(a, b, (dims, ((), ())), preferred_element_type=jnp.float32)


def load_then(kernel, loads, count, *refs):
    pos_ref, *refs = refs
    *refs, sem = refs
    buffers = refs[len(refs) - len(loads) :]
    refs = refs[: len(refs) - len(loads)]
    copies = [
        pltpu.make_async_copy(refs[index], buffer, sem.at[i])
        for i, (index, buffer) in enumerate(zip(loads, buffers))
    ]
    for copy in copies:
        copy.start()
    for copy in copies:
        copy.wait()
    for index, buffer in zip(loads, buffers):
        refs[index] = buffer
    kernel(pos_ref, *refs)


def kernel_call(kernel, name, position, args, outs, scratch=(), flops=0, limit=24, loads=()):
    if loads:
        kernel = functools.partial(load_then, kernel, loads, len(args))
        scratch = [
            *scratch,
            *(pltpu.VMEM(args[i].shape, args[i].dtype) for i in loads),
            pltpu.SemaphoreType.DMA((len(loads),)),
        ]
    places = [pltpu.HBM if i in loads else pltpu.VMEM for i in range(len(args))]
    return pl.pallas_call(
        kernel,
        in_specs=[pl.BlockSpec(memory_space=pltpu.SMEM)]
        + [pl.BlockSpec(memory_space=place) for place in places],
        out_specs=[pl.BlockSpec(memory_space=pltpu.VMEM)] * len(outs),
        out_shape=list(outs),
        scratch_shapes=list(scratch),
        compiler_params=pltpu.CompilerParams(vmem_limit_bytes=limit << 20),
        cost_estimate=pl.CostEstimate(flops=flops, bytes_accessed=0, transcendentals=0),
        name=name,
    )(position, *args)


def like(shape, dtype):
    return jax.ShapeDtypeStruct(shape, dtype)


def live_rows(shape, limit, offset=0):
    return lax.broadcasted_iota(jnp.int32, shape, 0) + offset < limit


def chunk_of(pos_ref, j, size):
    return pl.ds(pl.multiple_of(lax.bitwise_xor(pos_ref[2], j) * size, 16), size)


def head_masks(rows, heads):
    lane = lax.broadcasted_iota(jnp.int32, (rows, heads * HD), 1)
    return [(lane >= h * HD) & (lane < (h + 1) * HD) for h in range(heads)]


def keep_lanes(value, mask):
    return jnp.where(mask, value, jnp.zeros_like(value))


def split_high_low(value):
    high = value.astype(jnp.bfloat16)
    return high, (value - high.astype(jnp.float32)).astype(jnp.bfloat16)


def image_rows(ref, i, scratch_ref):
    seq_len = ref.shape[1]
    scratch_ref[seq_len:, :] = jnp.zeros((scratch_ref.shape[0] - seq_len, ref.shape[2]), jnp.float32)
    scratch_ref[0:seq_len, :] = ref[i].astype(jnp.float32)
    return scratch_ref[...]


def router_matrix(param_ref, experts):
    rows = param_ref[0:SMALL, :]
    rows = jnp.where(live_rows(rows.shape, experts), rows, 0.0).astype(jnp.bfloat16)
    zeros = jnp.zeros((LANES - SMALL, rows.shape[1]), jnp.bfloat16)
    return jnp.concatenate([rows, zeros], axis=0)


def weights_kernel(pos_ref, in_ref, out_ref, mine_ref, first_ref, second_ref):
    half = mine_ref.shape[1]
    quarter = half // 2
    start = pl.multiple_of(pos_ref[0] * half, LANES)
    for s, rows in (
        (0, in_ref[0, :, pl.ds(start, half)].T),
        (1, out_ref[0, pl.ds(start, half), :]),
    ):
        mine_ref[s] = rows
        first_ref[s] = rows[0:quarter]
        second_ref[s] = rows[quarter:]


def chunk_kernel(
    tensors, pos_ref, tok_ref, cot_ref, ids_ref, rank_ref, router_ref, one_ref, two_ref, x_ref, pay_ref,
    param_ref, flat_ref, kept_ref,
):
    images, seq_len, width = tok_ref.shape
    chunk, experts = x_ref.shape[0], router_ref.shape[0]
    start = pl.multiple_of(pos_ref[2] * chunk, 16)
    for source, target in ((tok_ref, x_ref), (cot_ref, pay_ref)):
        flat_ref[images * seq_len :, :] = jnp.zeros(
            (flat_ref.shape[0] - images * seq_len, width), jnp.float32
        )
        for i in range(images):
            flat_ref[pl.ds(i * seq_len, seq_len), :] = source[i].astype(jnp.float32)
        target[:, :width] = flat_ref[pl.ds(start, chunk), :].astype(jnp.bfloat16)
    kept_ref[...] = jnp.zeros_like(kept_ref)
    counts = jnp.zeros((1, LANES), jnp.float32)
    for i in range(images):
        rows, all_rows = [], []
        for e in range(experts):
            named = (ids_ref[i] == e).astype(jnp.float32)
            kept = jnp.where(rank_ref[i] >= 0, named, 0.0)
            rows.append(jnp.sum(kept, axis=0, keepdims=True))
            all_rows.append(jnp.sum(named, axis=0, keepdims=True))
        for group, is_kept in ((rows, True), (all_rows, False)):
            table = jnp.concatenate(group, axis=0)
            table = jnp.concatenate(
                [table, jnp.zeros((LANES - experts, seq_len), jnp.float32)], axis=0
            )
            table = jnp.concatenate(
                [table, jnp.zeros((LANES, 2 * LANES - seq_len), jnp.float32)], axis=1
            ).T
            if is_kept:
                kept_ref[pl.ds(i * seq_len, 2 * LANES), :] = table
            else:
                counts = counts + jnp.sum(table, axis=0, keepdims=True)
    pay_ref[:, width:] = kept_ref[pl.ds(start, chunk), :].astype(jnp.bfloat16)
    param_ref[...] = jnp.zeros_like(param_ref)
    param_ref[0:experts, :] = router_ref[...].astype(jnp.float32)
    param_ref[experts : experts + 1, :] = one_ref[...].reshape(1, width)
    param_ref[experts + 1 : experts + 2, :] = two_ref[...].reshape(1, width)
    param_ref[SMALL - 1 : SMALL, :LANES] = counts * (1.0 / tensors)


def stack_kernel(pos_ref, *refs):
    count = len(refs) // 3
    for i, target in enumerate(refs[2 * count :]):
        target[0] = refs[2 * i][...]
        target[1] = refs[2 * i + 1][...]


def stack_pairs(position, *pairs):
    return kernel_call(
        stack_kernel,
        "stack",
        position,
        [value for pair in pairs for value in pair],
        [like((2, *pair[0].shape), pair[0].dtype) for pair in pairs],
        limit=4,
    )


def gain_row(param_ref, experts, which):
    return param_ref[experts + which : experts + which + 1, :]


def attention_kernel(
    heads, experts, pos_ref, tok_ref, param_ref, w_ref, wo_ref, qkv_ref, lse_ref, att_ref, *refs,
):
    *parts, flat_ref, image_ref, held_ref = refs
    images, rows, width = qkv_ref.shape[1], qkv_ref.shape[2], heads * HD
    seq_len = tok_ref.shape[1]
    masks = head_masks(rows, heads)
    keys_live = lax.broadcasted_iota(jnp.int32, (rows, rows), 1) < seq_len
    lane = lax.broadcasted_iota(jnp.int32, (rows, LANES), 1)
    flat_ref[images * seq_len :, :] = jnp.zeros(
        (flat_ref.shape[0] - images * seq_len, width), jnp.float32
    )

    @pl.loop(0, images)
    def _(i):
        entered = normalize(image_rows(tok_ref, i, image_ref), gain_row(param_ref, experts, 0))[2]
        entered = entered.astype(jnp.bfloat16)
        q, k, v = (
            contract(entered, w_ref[c * width : (c + 1) * width, :], NT).astype(jnp.bfloat16)
            for c in range(3)
        )
        qkv_ref[0, i], qkv_ref[1, i], qkv_ref[2, i] = q, k, v
        attended = jnp.zeros((rows, width), jnp.float32)
        lse_all = jnp.zeros((rows, LANES), jnp.float32)
        for h in range(heads):
            scores = contract(keep_lanes(q, masks[h]), k, NT) * (HD ** (-0.5))
            scores = jnp.where(keys_live, scores, -1e30)
            top = jnp.max(scores, axis=-1, keepdims=True)
            lse = top + jnp.log(jnp.sum(jnp.exp(scores - top), axis=-1, keepdims=True))
            probs = jnp.exp(scores - lse).astype(jnp.bfloat16)
            attended = attended + contract(probs, keep_lanes(v, masks[h]), NN)
            lse_all = jnp.where(lane == h, lse, lse_all)
        lse_ref[i] = lse_all
        held_ref[i] = attended

    for i in range(images):
        flat_ref[pl.ds(i * seq_len, seq_len), :] = held_ref[i, 0:seq_len, :]
    att_ref[...] = flat_ref[...].astype(jnp.bfloat16)
    for j, part in enumerate(parts):
        rows_j = flat_ref[chunk_of(pos_ref, j, part.shape[0]), :].astype(jnp.bfloat16)
        part[...] = contract(rows_j, wo_ref[...], NN).astype(jnp.bfloat16)


def route_kernel(experts, pos_ref, *refs):
    *got, x_ref, param_ref, res_ref, routed_ref, prob_ref = refs
    residual = x_ref[...].astype(jnp.float32)
    for part in got:
        residual = residual + part[...].astype(jnp.float32)
    res_ref[...] = residual
    routed = normalize(residual, gain_row(param_ref, experts, 1))[2].astype(jnp.bfloat16)
    routed_ref[...] = routed
    prob_ref[...] = route_probs(routed, router_matrix(param_ref, experts), experts)


def route_probs(rows, router, experts):
    logits = contract(rows, router, NT)
    lane = lax.broadcasted_iota(jnp.int32, logits.shape, 1)
    logits = jnp.where(lane < experts, logits, -1e30)
    weight = jnp.exp(logits - jnp.max(logits, axis=-1, keepdims=True))
    return weight / jnp.sum(weight, axis=-1, keepdims=True)


def gelu_parts(x):
    square = jnp.exp(-0.5 * x * x)
    share = 0.5 * (1.0 + lax.erf(x * (0.5**0.5)))
    return x * share, share + x * square * (0.5 / math.pi) ** 0.5


def expert_halves(x, rg, w_in, w_out, hidden_ref, pre_ref):
    before = contract(x, w_in, NT)
    value, slope = gelu_parts(before)
    hidden = value.astype(jnp.bfloat16)
    hidden_ref[...] = hidden
    part = contract(hidden, w_out, NN)
    pre = (contract(rg, w_out, NT) * slope).astype(jnp.bfloat16)
    pre_ref[...] = pre
    return part, contract(pre, w_in, NN)


def first_expert_kernel(experts, owners, pos_ref, *refs):
    blocks = refs[:owners]
    pay_refs, param_ref, w0_ref, xa_ref, yb_ref = refs[owners : 2 * owners], *refs[2 * owners :][:4]
    hidden_ref, pre_ref, x_ref, rg_ref, dy_ref, gate_ref, part_ref, back_ref = refs[2 * owners + 4 :]
    chunk, width = blocks[0].shape
    router = router_matrix(param_ref, experts)
    for k in range(owners):
        here = pl.ds(k * chunk, chunk)
        pay = pay_refs[k]
        rows = blocks[k][...]
        x_ref[here, :] = rows
        prob = route_probs(rows, router, experts)
        mine = lax.broadcasted_iota(jnp.int32, prob.shape, 1) == pos_ref[1]
        kept = pay[:, width:].astype(jnp.float32)
        kept = jnp.sum(jnp.where(mine, kept, 0.0), axis=-1, keepdims=True)
        gate = jnp.sum(jnp.where(mine, prob, 0.0), axis=-1, keepdims=True) * kept
        gate_ref[here, :LANES] = jnp.broadcast_to(gate, (chunk, LANES))
        gate_ref[here, LANES:] = jnp.broadcast_to(kept, (chunk, LANES))
        dy = pay[:, :width]
        dy_ref[here, :] = dy
        rg_ref[here, :] = (gate * dy.astype(jnp.float32)).astype(jnp.bfloat16)
    w_in, w_out = (
        jnp.concatenate([w0_ref[s], xa_ref[s], yb_ref[s]], axis=0) for s in range(2)
    )
    part_ref[...], back_ref[...] = expert_halves(
        x_ref[...], rg_ref[...], w_in, w_out, hidden_ref, pre_ref
    )


def second_expert_kernel(
    owners, pos_ref, x_ref, rg_ref, dy_ref, gate_ref, part_in_ref, back_in_ref, pair_y_ref,
    pair_x_ref, hidden_ref, pre_ref, gated_ref, back_ref, part_ref,
):
    width = x_ref.shape[1]
    chunk = x_ref.shape[0] // owners
    w_in, w_out = (
        jnp.concatenate([ref[r, s] for ref in (pair_y_ref, pair_x_ref) for r in range(2)], axis=0)
        for s in range(2)
    )
    part, back = expert_halves(x_ref[...], rg_ref[...], w_in, w_out, hidden_ref, pre_ref)
    part_ref[...] = part_in_ref[...] + part
    back_ref[:, :width] = back_in_ref[...] + back
    for k in range(owners):
        here = pl.ds(k * chunk, chunk)
        total = part_ref[here, :]
        gated_ref[here, :] = (gate_ref[here, 0:1] * total).astype(jnp.bfloat16)
        inner = jnp.sum(total * dy_ref[here, :].astype(jnp.float32), axis=-1, keepdims=True)
        back_ref[here, width:] = gate_ref[here, LANES:] * inner


def first_expert_pass(position, blocks, payload, params, weights, experts):
    chunk, width = blocks[0].shape
    count, hidden = len(blocks) * chunk, 2 * weights[0].shape[1]
    return kernel_call(
        functools.partial(first_expert_kernel, experts, len(blocks)),
        "experts_first",
        position,
        [*blocks, *payload, params, *weights],
        [
            like((count, hidden), jnp.bfloat16),
            like((count, hidden), jnp.bfloat16),
            like((count, width), jnp.bfloat16),
            like((count, width), jnp.bfloat16),
            like((count, width), jnp.bfloat16),
            like((count, 2 * LANES), jnp.float32),
            like((count, width), jnp.float32),
            like((count, width), jnp.float32),
        ],
        limit=16,
    )


def second_expert_pass(position, first, weights, owners):
    x, rg, dy, gate, part, back = first[2:]
    count, width = x.shape
    hidden = 4 * weights[0].shape[2]
    return kernel_call(
        functools.partial(second_expert_kernel, owners),
        "experts_second",
        position,
        [x, rg, dy, gate, part, back, *weights],
        [
            like((count, hidden), jnp.bfloat16),
            like((count, hidden), jnp.bfloat16),
            like((count, width), jnp.bfloat16),
            like((count, width + LANES), jnp.float32),
        ],
        [pltpu.VMEM((count, width), jnp.float32)],
        limit=16,
    )


def join_kernel(pos_ref, back_ref, other_ref, gated_ref, gated_other_ref, *outs):
    owners = len(outs) // 2
    chunk, width = outs[owners].shape
    for k in range(owners):
        here = pl.ds(k * chunk, chunk)
        total = back_ref[here, :] + other_ref[here, :]
        outs[k][0:chunk, :] = total[:, :width].astype(jnp.bfloat16)
        inner = jnp.concatenate(
            [total[:, width:], jnp.zeros((2 * LANES - chunk, LANES), jnp.float32)], axis=0
        ).T
        high, low = split_high_low(inner[0:SMALL, :])
        outs[k][chunk:, : 2 * LANES] = jnp.concatenate([high, low], axis=0)
        outs[k][chunk:, 2 * LANES :] = jnp.zeros((2 * SMALL, width - 2 * LANES), jnp.bfloat16)
        outs[owners + k][...] = (
            gated_ref[here, :].astype(jnp.float32) + gated_other_ref[here, :].astype(jnp.float32)
        ).astype(jnp.bfloat16)


def expert_grad_kernel(pos_ref, *refs):
    *sources, first_ref, second_ref = refs
    part_rows = first_ref.shape[2]
    for j, out in enumerate((first_ref, second_ref)):
        columns = slice(2 * j * part_rows, 2 * (j + 1) * part_rows)
        for s in range(2):
            left_a, right_a, left_b, right_b = sources[4 * s : 4 * s + 4]
            grad = contract(left_a[:, columns], right_a[...], TN)
            grad = grad + contract(left_b[:, columns], right_b[...], TN)
            grad = grad.astype(jnp.bfloat16)
            out[0, s] = grad[0:part_rows]
            out[1, s] = grad[part_rows:]


def expert_grads(position, a, b, rows_a, rows_b):
    width, total = rows_a[0].shape[1], a[0].shape[1]
    return kernel_call(
        expert_grad_kernel,
        "expert_grads",
        position,
        [a[1], rows_a[0], b[1], rows_b[0], a[0], rows_a[1], b[0], rows_b[1]],
        [like((2, 2, total // 4, width), jnp.bfloat16)] * 2,
        limit=10,
    )


def route_back_kernel(
    experts, token_rows, owners, pos_ref, *refs
):
    backs = refs[:owners]
    prob_ref, res_ref, pay_ref, param_ref = refs[owners : owners + 4]
    grad_ref, up_ref, small_ref = refs[owners + 4 :]
    chunk, width = res_ref.shape
    prob = prob_ref[...]
    lane = lax.broadcasted_iota(jnp.int32, prob.shape, 1)
    route_grad = jnp.zeros_like(prob)
    routed_grad = jnp.zeros((chunk, width), jnp.float32)
    for k, back in enumerate(backs):
        owner = lax.bitwise_xor(pos_ref[1], k)
        inner = back[chunk : chunk + SMALL, : 2 * LANES].astype(jnp.float32)
        inner = inner + back[chunk + SMALL :, : 2 * LANES].astype(jnp.float32)
        inner = jnp.concatenate([inner] * (LANES // SMALL), axis=0).T[0:chunk]
        route_grad = jnp.where(lane == owner, inner, route_grad)
        routed_grad = routed_grad + back[0:chunk, :].astype(jnp.float32)
    mean = jnp.sum(route_grad * prob, axis=-1, keepdims=True)
    logit_grad = (prob * (route_grad - mean)).astype(jnp.bfloat16)
    routed_grad = routed_grad + contract(
        logit_grad, router_matrix(param_ref, experts), NN
    )
    normed, inverse, mixed = normalize(res_ref[...], gain_row(param_ref, experts, 1))
    from_norm, gain_grad = normalize_back(
        routed_grad, normed, inverse, gain_row(param_ref, experts, 1)
    )
    total = pay_ref[:, :width].astype(jnp.float32) + from_norm
    grad_ref[...] = total
    up_ref[...] = total.astype(jnp.bfloat16)
    live = live_rows(prob.shape, token_rows, pos_ref[2] * chunk)
    prob_sum = jnp.sum(jnp.where(live, prob, 0.0), axis=0, keepdims=True)
    grad_router = contract(logit_grad, mixed.astype(jnp.bfloat16), TN)
    small_ref[0:SMALL, :] = grad_router[0:SMALL]
    small_ref[experts : experts + 1, :] = gain_grad[None]
    small_ref[experts + 1 : experts + 2, :] = jnp.zeros((1, width), jnp.float32)
    small_ref[experts + 1 : experts + 2, :LANES] = prob_sum
    small_ref[experts + 2 : experts + 3, :] = param_ref[SMALL - 1 : SMALL, :]


def attention_back_kernel(
    heads, experts, owners, pos_ref, tok_ref, param_ref, w_ref, wo_ref, qkv_ref, lse_ref, att_ref,
    up_ref, small_ref, keep_ref, send_ref, *refs,
):
    *parts, hg_ref, flat_ref, big_ref, image_ref, held_ref, sum_ref, gain_ref = refs
    images, rows, width = qkv_ref.shape[1], qkv_ref.shape[2], heads * HD
    seq_len = tok_ref.shape[1]
    scale = HD ** (-0.5)
    padded, model = up_ref.shape
    chunk = padded // len(parts)
    masks = head_masks(rows, heads)
    keys_live = lax.broadcasted_iota(jnp.int32, (rows, rows), 1) < seq_len
    lane = lax.broadcasted_iota(jnp.int32, (rows, LANES), 1)
    up = up_ref[...]
    hg_ref[0:padded, :] = contract(up, wo_ref[...], NT)
    hg_ref[padded:, :] = jnp.zeros((hg_ref.shape[0] - padded, width), jnp.float32)
    big_ref[3 * width :, :] = contract(att_ref[...], up, TN)
    flat_ref[images * seq_len :, :] = jnp.zeros(
        (flat_ref.shape[0] - images * seq_len, model), jnp.float32
    )
    for i in range(images):
        held_ref[i] = hg_ref[pl.ds(i * seq_len, rows), :]
    big_ref[0 : 3 * width, :] = jnp.zeros((3 * width, model), jnp.float32)

    @pl.loop(0, images)
    def _(i):
        normed, _, mixed = normalize(
            image_rows(tok_ref, i, image_ref), gain_row(param_ref, experts, 0)
        )
        entered = mixed.astype(jnp.bfloat16)
        q, k, v = qkv_ref[0, i], qkv_ref[1, i], qkv_ref[2, i]
        heads_grad = held_ref[i]
        heads_grad = jnp.where(live_rows(heads_grad.shape, seq_len), heads_grad, 0.0)
        heads_grad = heads_grad.astype(jnp.bfloat16)
        dq = jnp.zeros((rows, width), jnp.float32)
        dk, dv = dq, dq
        for h in range(heads):
            q_h, k_h = keep_lanes(q, masks[h]), keep_lanes(k, masks[h])
            up_h = keep_lanes(heads_grad, masks[h])
            scores = contract(q_h, k, NT) * scale
            lse = jnp.sum(jnp.where(lane == h, lse_ref[i], 0.0), axis=-1, keepdims=True)
            probs = jnp.where(keys_live, jnp.exp(scores - lse), 0.0)
            prob_grad = contract(up_h, v, NT)
            total = jnp.sum(prob_grad * probs, axis=-1, keepdims=True)
            score_grad = (probs * (prob_grad - total)).astype(jnp.bfloat16)
            dv = dv + contract(probs.astype(jnp.bfloat16), up_h, TN)
            dq = dq + contract(score_grad, k_h, NN)
            dk = dk + contract(score_grad, q_h, TN)
        grads = [g.astype(jnp.bfloat16) for g in (dq * scale, dk * scale, dv)]
        part = jnp.zeros((rows, model), jnp.float32)
        for c in range(3):
            here = slice(c * width, (c + 1) * width)
            part = part + contract(grads[c], w_ref[here, :], NN)
            big_ref[here, :] += contract(grads[c], entered, TN)
        sum_ref[i] = part
        gain_ref[i] = jnp.broadcast_to(
            jnp.sum(part * normed, axis=0, keepdims=True), gain_ref.shape[1:]
        )

    gain_grad = jnp.zeros((1, model), jnp.float32)
    for i in range(images):
        flat_ref[pl.ds(i * seq_len, seq_len), :] = sum_ref[i, 0:seq_len, :]
        gain_grad = gain_grad + gain_ref[i, 0:1, :]
    high, low = split_high_low(
        jnp.concatenate([small_ref[0 : SMALL - 1, :], gain_grad], axis=0)
    )
    for j, part in enumerate(parts):
        part[0:chunk, :] = flat_ref[chunk_of(pos_ref, j, chunk), :].astype(jnp.bfloat16)
        part[chunk:, :] = jnp.concatenate([high, low], axis=0)
    me, core = pos_ref[1], pos_ref[0]
    piece = keep_ref.shape[1]
    for k in range(owners):
        place = lax.bitwise_xor(me, k) * piece
        mine = pl.ds(pl.multiple_of(core * owners * piece + place, 8), piece)
        other = pl.ds(pl.multiple_of((1 - core) * owners * piece + place, 8), piece)
        keep_ref[k] = big_ref[mine, :]
        send_ref[k] = big_ref[other, :].astype(jnp.bfloat16)


def norm_back_kernel(experts, tensors, pos_ref, *refs):
    got = refs[:tensors]
    x_ref, res_ref, param_ref, own_ref, *parts, grad_ref, out_ref, small_ref = refs[tensors:]
    chunk, width = x_ref.shape
    upstream = jnp.zeros((chunk, width), jnp.float32)
    for j, part in enumerate(got):
        upstream = upstream + part[0:chunk, :].astype(jnp.float32)
        small_ref[lax.bitwise_xor(pos_ref[2], j)] = part[chunk : chunk + SMALL, :].astype(
            jnp.float32
        ) + part[chunk + SMALL :, :].astype(jnp.float32)
    small = small_ref[0]
    for j in range(1, tensors):
        small = small + small_ref[j]
    gain = gain_row(param_ref, experts, 0)
    normed, inverse, _ = normalize(x_ref[...].astype(jnp.float32), gain)
    from_norm = normalize_back(upstream, normed, inverse, gain)[0]
    grad_ref[...] = (res_ref[...] + from_norm).astype(jnp.bfloat16)
    piece = own_ref.shape[0]
    total = own_ref[...]
    for part in parts:
        total = total + part[...].astype(jnp.float32)
    out_ref[0:piece, :] = total.astype(jnp.bfloat16)
    out_ref[piece:, :] = jnp.concatenate(split_high_low(small), axis=0)


def second_step_kernel(pos_ref, near_ref, from_y, from_x, x_ref, y_ref):
    for target, row, other in ((x_ref, 0, from_y), (y_ref, 1, from_x)):
        total = near_ref[row].astype(jnp.float32) + other[1].astype(jnp.float32)
        target[...] = total.astype(jnp.bfloat16)


def weight_sum_kernel(pos_ref, own_ref, from_y, from_x, last_x, last_y, out_ref):
    part_rows = last_x.shape[1]
    for row, other, last in ((0, from_y, last_x), (1, from_x, last_y)):
        total = own_ref[row].astype(jnp.float32) + other[0].astype(jnp.float32)
        total = total + last[...].astype(jnp.float32)
        out_ref[:, row * part_rows : (row + 1) * part_rows, :] = total.astype(jnp.bfloat16)


def add_core_kernel(pos_ref, keep_ref, other_ref, own_ref, *outs):
    total = keep_ref[...] + other_ref[...].astype(jnp.float32)
    own_ref[...] = total[0]
    for k, out in enumerate(outs):
        out[...] = total[k + 1].astype(jnp.bfloat16)


def spread_kernel(owners, experts, token_total, pos_ref, *refs):
    blocks = refs[: 2 * owners]
    qkv_ref, wo_ref, router_ref, one_ref, two_ref, loss_ref, big_ref, parts_ref = refs[2 * owners :]
    piece = blocks[0].shape[0] - 2 * SMALL
    core, me = pos_ref[0], pos_ref[1]
    for c in range(2):
        side = core if c == 0 else 1 - core
        for k in range(owners):
            block = blocks[c * owners + k]
            place = side * owners + lax.bitwise_xor(me, k)
            here = pl.ds(pl.multiple_of(place * piece, 8), piece)
            big_ref[here, :] = block[0:piece, :].astype(jnp.float32)
            parts_ref[place] = block[piece : piece + SMALL, :].astype(jnp.float32) + block[
                piece + SMALL :, :
            ].astype(jnp.float32)
    rows = qkv_ref.shape[0]
    qkv_ref[...] = big_ref[0:rows, :]
    wo_ref[...] = big_ref[rows:, :]
    small = parts_ref[0]
    for p in range(1, 2 * owners):
        small = small + parts_ref[p]
    router_ref[...] = small[0:experts, :]
    one_ref[...] = small[SMALL - 1 : SMALL, :].reshape(small.shape[1])
    two_ref[...] = small[experts : experts + 1, :].reshape(small.shape[1])
    product = small[experts + 1 : experts + 2, :LANES] * small[experts + 2 : experts + 3, :LANES]
    lane = lax.broadcasted_iota(jnp.int32, product.shape, 1)
    product = jnp.where(lane < experts, product, 0.0)
    loss = jnp.sum(product, axis=-1, keepdims=True)
    loss_ref[...] = jnp.broadcast_to(
        loss * (experts / (2.0 * token_total * token_total)), loss_ref.shape
    )


def images_kernel(pos_ref, *refs):
    *chunks, out_ref, flat_ref = refs
    images, seq_len, _ = out_ref.shape
    if len(chunks) == 1:
        flat_ref[...] = chunks[0][...].astype(jnp.float32)
    else:
        for j, part in enumerate(chunks):
            flat_ref[chunk_of(pos_ref, j, part.shape[0]), :] = part[...].astype(jnp.float32)
    for i in range(images):
        out_ref[i] = flat_ref[pl.ds(i * seq_len, seq_len), :].astype(out_ref.dtype)


def weight_out_kernel(pos_ref, mine_ref, other_ref, in_ref, out_ref):
    first_is_mine = pos_ref[0] == 0
    half = mine_ref.shape[1]
    for c in range(2):
        here = slice(c * half, (c + 1) * half)
        take = first_is_mine if c == 0 else jnp.logical_not(first_is_mine)
        grad_in = jnp.where(take, mine_ref[0], other_ref[0]).astype(jnp.float32)
        in_ref[0, :, here] = grad_in.T
        out_ref[0, here, :] = jnp.where(take, mine_ref[1], other_ref[1]).astype(jnp.float32)


def swap_core(value):
    return lax.ppermute(value, "dp", [(0, 1), (1, 0)])


def hop(value, bit):
    size = lax.axis_size("expert")
    return lax.ppermute(value, "expert", [(i, i ^ bit) for i in range(size)])


def cross(value, bit):
    size = lax.axis_size("tensor")
    return lax.ppermute(value, "tensor", [(i, i ^ bit) for i in range(size)])


def after(value, *others):
    return lax.optimization_barrier((value, *others))[0]


def dense_body(
    tokens,
    cotangent,
    expert_ids,
    slot_rank,
    qkv_weight,
    out_weight,
    router_weight,
    expert_in,
    expert_out,
    gain_attention,
    gain_experts,
):
    f32, b16 = jnp.float32, jnp.bfloat16
    images, seq_len, width = tokens.shape
    token_rows = images * seq_len
    local = qkv_weight.shape[2]
    heads = local // HD
    experts = router_weight.shape[1]
    owners = lax.axis_size("expert")
    tensors = lax.axis_size("tensor")
    cores = lax.axis_size("dp")
    chunk = round_up(-(-token_rows // tensors), 16)
    padded = chunk * tensors
    rows = round_up(seq_len, 16)
    flat_rows = padded + 32
    half = expert_in.shape[2] // cores
    quarter = half // 2
    position = jnp.stack(
        [lax.axis_index("dp"), lax.axis_index("expert"), lax.axis_index("tensor")]
    ).astype(jnp.int32)
    weight_rows = qkv_weight.transpose(0, 2, 1).reshape(3 * local, width)

    x_chunk, payload, params = kernel_call(
        functools.partial(chunk_kernel, tensors),
        "chunk",
        position,
        [
            tokens,
            cotangent,
            expert_ids.transpose(0, 2, 1),
            slot_rank.transpose(0, 2, 1),
            router_weight.T,
            gain_attention,
            gain_experts,
        ],
        [
            like((chunk, width), b16),
            like((chunk, width + LANES), b16),
            like((SMALL, width), f32),
        ],
        [
            pltpu.VMEM((flat_rows, width), f32),
            pltpu.VMEM((padded + 2 * LANES, LANES), f32),
        ],
        limit=56,
        loads=tuple(range(7)),
    )
    payload_mine = [payload] + [hop(payload, k) for k in range(1, owners)]
    mine, first, second = kernel_call(
        weights_kernel,
        "weights",
        after(position, payload),
        [expert_in, expert_out],
        [
            like((2, half, width), b16),
            like((2, quarter, width), b16),
            like((2, quarter, width), b16),
        ],
        limit=12,
        loads=(0, 1),
    )
    first_x = cross(first, 1)
    second_y = cross(second, 2)

    qkv, lse, attended, *parts = kernel_call(
        functools.partial(attention_kernel, heads, experts),
        "attention",
        after(position, mine),
        [tokens, params, weight_rows, out_weight],
        [
            like((3, images, rows, local), b16),
            like((images, rows, LANES), f32),
            like((padded, local), b16),
        ]
        + [like((chunk, width), b16)] * tensors,
        [
            pltpu.VMEM((padded, local), f32),
            pltpu.VMEM((rows, width), f32),
            pltpu.VMEM((images, rows, local), f32),
        ],
        limit=20,
        loads=(0, 2, 3),
    )
    arrived = [parts[0]] + [cross(parts[j], j) for j in range(1, tensors)]
    pair_first, pair_second = stack_pairs(position, (first, first_x), (second, second_y))

    residual, routed, prob = kernel_call(
        functools.partial(route_kernel, experts),
        "route",
        after(position, pair_first, payload_mine),
        [*arrived, x_chunk, params],
        [like((chunk, width), f32), like((chunk, width), b16), like((chunk, LANES), f32)],
        limit=8,
    )
    blocks = [routed] + [hop(routed, k) for k in range(1, owners)]
    pair_first, pair_second = after((pair_first, pair_second), routed)
    pair_y = cross(pair_first, 2)
    pair_x = cross(pair_second, 1)
    other_blocks = [swap_core(b) for b in blocks]
    payload_other = [swap_core(p) for p in payload_mine]

    near_weights, far_weights = (mine, first_x, second_y), (pair_y, pair_x)
    first_a = first_expert_pass(position, blocks, payload_mine, params, near_weights, experts)
    first_b = first_expert_pass(
        after(position, first_a[2]), other_blocks, payload_other, params, near_weights, experts
    )
    second_b = second_expert_pass(
        after(position, first_b[2]), first_b, far_weights, owners
    )
    back_other, gated_other = swap_core(second_b[3]), swap_core(second_b[2])
    second_a = second_expert_pass(
        after(position, second_b[0]), first_a, far_weights, owners
    )
    joined = kernel_call(
        join_kernel,
        "join",
        position,
        [second_a[3], back_other, second_a[2], gated_other],
        [like((chunk + 2 * SMALL, width), b16)] * owners + [like((chunk, width), b16)] * owners,
        limit=8,
    )
    backs = [joined[0]] + [hop(joined[k], k) for k in range(1, owners)]

    grad_pos = after(position, joined[:owners])
    far_y, far_x = expert_grads(grad_pos, second_a, second_b, first_a[2:4], first_b[2:4])
    from_y, from_x = cross(far_y, 2), cross(far_x, 1)
    own_grad, near_grad = expert_grads(
        after(grad_pos, far_y, backs[1]), first_a, first_b, first_a[2:4], first_b[2:4]
    )

    residual_grad, attn_grad, small = kernel_call(
        functools.partial(route_back_kernel, experts, token_rows, owners),
        "route_back",
        after(position, own_grad),
        [*backs, prob, residual, payload, params],
        [like((chunk, width), f32), like((chunk, width), b16), like((SMALL, width), f32)],
        flops=40_000_000_000,
        limit=8,
    )
    gated_back = [joined[owners]]
    for k in range(1, owners):
        gated_back.append(hop(after(joined[owners + k], attn_grad), k))
    attn_grad = lax.all_gather(attn_grad, "tensor", axis=0, tiled=True)
    piece = 4 * local // (2 * owners)
    keep, send, *parts = kernel_call(
        functools.partial(attention_back_kernel, heads, experts, owners),
        "attention_back",
        after(position, from_y, from_x, gated_back[1:]),
        [tokens, params, weight_rows, out_weight, qkv, lse, attended, attn_grad, small],
        [
            like((owners, piece, width), f32),
            like((owners, piece, width), b16),
        ]
        + [like((chunk + 2 * SMALL, width), b16)] * tensors,
        [
            pltpu.VMEM((flat_rows, local), f32),
            pltpu.VMEM((flat_rows, width), f32),
            pltpu.VMEM((4 * local, width), f32),
            pltpu.VMEM((rows, width), f32),
            pltpu.VMEM((images, rows, local), f32),
            pltpu.VMEM((images, rows, width), f32),
            pltpu.VMEM((images, SMALL, width), f32),
        ],
        limit=20,
        flops=6_000_000_000,
    )
    own_piece, *pieces = kernel_call(
        add_core_kernel,
        "add_core",
        position,
        [keep, swap_core(send)],
        [like((piece, width), f32)] + [like((piece, width), b16)] * (owners - 1),
        limit=8,
    )
    reduced = [hop(p, k + 1) for k, p in enumerate(pieces)]
    got = [parts[0]] + [cross(parts[j], j) for j in range(1, tensors)]
    up_x, up_y = kernel_call(
        second_step_kernel,
        "second_step",
        after(position, got[1:], own_piece),
        [near_grad, from_y, from_x],
        [like((2, quarter, width), b16)] * 2,
        limit=8,
    )
    last_x, last_y = cross(up_x, 1), cross(up_y, 2)

    grad_chunk, summed = kernel_call(
        functools.partial(norm_back_kernel, experts, tensors),
        "norm_back",
        position,
        [*got, x_chunk, residual_grad, params, own_piece, *reduced],
        [like((chunk, width), b16), like((piece + 2 * SMALL, width), b16)],
        [pltpu.VMEM((tensors, SMALL, width), f32)],
        flops=40_000_000_000,
        limit=8,
    )
    around = [summed] + [hop(summed, k) for k in range(1, owners)]
    grad_rows = lax.all_gather(grad_chunk, "tensor", axis=0, tiled=True)
    combined = residual
    for part in gated_back:
        combined = combined + part.astype(f32)
    combined = combined.astype(b16)
    combined = after(combined, grad_rows)
    block_parts = [combined] + [cross(combined, j) for j in range(1, tensors)]

    grad_tokens = kernel_call(
        images_kernel,
        "grad_tokens",
        after(position, around, last_x, last_y),
        [grad_rows],
        [like(tokens.shape, f32)],
        [pltpu.VMEM((padded, width), f32)],
        limit=8,
    )[0]
    grad_half = kernel_call(
        weight_sum_kernel,
        "weight_sum",
        after(position, grad_tokens),
        [own_grad, from_y, from_x, last_x, last_y],
        [like((2, half, width), b16)],
        limit=8,
    )[0]
    grad_expert_in, grad_expert_out = kernel_call(
        weight_out_kernel,
        "weight_out",
        position,
        [grad_half, swap_core(grad_half)],
        [like((1, width, 2 * half), f32), like((1, 2 * half, width), f32)],
        limit=10,
    )
    token_total = token_rows * cores * owners
    grad_qkv, grad_out, grad_router, gain_one, gain_two, loss = kernel_call(
        functools.partial(spread_kernel, owners, experts, token_total),
        "spread",
        position,
        around + [swap_core(a) for a in around],
        [
            like((3 * local, width), f32),
            like((local, width), f32),
            like((experts, width), f32),
            like((width,), f32),
            like((width,), f32),
            like((1, LANES), f32),
        ],
        [
            pltpu.VMEM((4 * local, width), f32),
            pltpu.VMEM((2 * owners, SMALL, width), f32),
        ],
        limit=8,
    )
    block_out = kernel_call(
        images_kernel,
        "block_out",
        after(position, grad_tokens, grad_expert_in, grad_qkv),
        block_parts,
        [like(tokens.shape, b16)],
        [pltpu.VMEM((padded, width), f32)],
        limit=8,
    )[0]
    return (
        block_out,
        grad_tokens,
        grad_qkv.reshape(3, local, width).transpose(0, 2, 1),
        grad_out,
        grad_router.T,
        grad_expert_in,
        grad_expert_out,
        gain_one,
        gain_two,
        loss[0, 0],
    )


def solution(mesh):
    placed = (
        P(("dp", "expert"), None, None),
        P(("dp", "expert"), None, None),
        P(("dp", "expert"), None, None),
        P(("dp", "expert"), None, None),
        P(None, None, "tensor"),
        P("tensor", None),
        P(),
        P("expert", None, "tensor"),
        P("expert", "tensor", None),
        P(),
        P(),
    )
    shape = mesh.shape
    dense = shape["dp"] == 2 and shape["expert"] == 4 and shape["tensor"] == 4
    return jax.shard_map(
        dense_body if dense else body,
        mesh=mesh,
        in_specs=placed,
        out_specs=(
            P(("dp", "expert"), None, None),
            P(("dp", "expert"), None, None),
            P(None, None, "tensor"),
            P("tensor", None),
            P(),
            P("expert", None, "tensor"),
            P("expert", "tensor", None),
            P(),
            P(),
            P(),
        ),
        check_vma=False,
    )
```

profile of v0, /device:TPU:0, one launch (start us, length us, event | category | flops | bytes accessed | tf_op | source)
XLA Modules:
  0.0 209.1 jit_solution(4627353726481942282)
XLA Ops:
  1.2 3.8 %chunk.1 = (bf16[160,768]{1,0:T(8,128)(2,1)}, bf16[160,896]{1,0:T(8,128)(2,1)}, f32[8,768]{1,0:T(8,128)}) custom-call(s32[3]{0:T(128)} %pad_add_fusion.refs_0_.pos_ref, bf16[3,197,768]{2,1,0:T(8,128)(2,1)} %tok_ref.1, bf16[3,197,768]{2,1,0:T(8,128)(2,1)} %refs_2_.2, s32[3,2,197]{2,1,0:T(2,128)} %bitcast.17, s32[3,2,197]{2,1,0:T(2,128)} %bitcast.18, ...), custom_call_target="tpu_custom_call" | custom-call | tf_op jit(solution)/shard_map/chunk/pallas_call | solution.py:304
  7.7 3.0 %collective-permute-start = (bf16[2,192,768]{2,1,0:T(8,128)(2,1)S(1)}, bf16[2,192,768]{2,1,0:T(8,128)(2,1)S(1)}, u32[]{:S(2)}, u32[]{:S(2)}) collective-permute-start(bf16[2,192,768]{2,1,0:T(8,128)(2,1)S(1)} %get-tuple-element.111.refs_0_), channel_id=1, source_target_pairs={{0,1},{1,0},{2,3},{3,2},{4,5},{5,4},{6,7},{7,6},{8,9},{9,8},{10,11... | collective-permute-start | bytes 1769480 | tf_op jit(solution)/shard_map/ppermute | solution.py:882
  12.2 3.6 %collective-permute-start.4 = (bf16[160,896]{1,0:T(8,128)(2,1)}, bf16[160,896]{1,0:T(8,128)(2,1)S(1)}, u32[]{:S(2)}, u32[]{:S(2)}) collective-permute-start(bf16[160,896]{1,0:T(8,128)(2,1)} %get-tuple-element.109.refs_4_.refs_6_), channel_id=1, source_target_pairs={{0,12},{4,8},{8,4},{12,0},{1,13},{5,9},{9,5},{13,1},{2,14},{6,10},... | collective-permute-start | bytes 860168 | tf_op jit(solution)/shard_map/ppermute | solution.py:877
  16.6 5.3 %attention.1 = (bf16[3,3,208,192]{3,2,1,0:T(8,128)(2,1)S(1)}, f32[3,208,128]{2,1,0:T(8,128)S(1)}, bf16[640,192]{1,0:T(8,128)(2,1)S(1)}, bf16[160,768]{1,0:T(8,12...) custom-call(s32[3]{0:T(128)S(1)} %copy-done.8, ...), custom_call_target="tpu_custom_call" | custom-call | tf_op jit(solution)/shard_map/attention/pallas_call | solution.py:304
  22.0 2.1 %collective-permute-done.4.refs_7_ = bf16[160,896]{1,0:T(8,128)(2,1)S(1)} collective-permute-done((bf16[160,896]{1,0:T(8,128)(2,1)}, bf16[160,896]{1,0:T(8,128)(2,1)S(1)}, u32[]{:S(2)}, u32[]{:S(2)}) %collective-permute-start.4) | collective-permute-done | bytes 286752 | tf_op jit(solution)/shard_map/ppermute | solution.py:877
  24.6 2.3 %collective-permute-start.6 = (bf16[160,768]{1,0:T(8,128)(2,1)S(1)}, bf16[160,768]{1,0:T(8,128)(2,1)S(1)}, u32[]{:S(2)}, u32[]{:S(2)}) collective-permute-start(bf16[160,768]{1,0:T(8,128)(2,1)S(1)} %get-tuple-element.120), channel_id=1, source_target_pairs={{0,2},{1,3},{2,0},{3,1},{4,6},{5,7},{6,4},{7,5},{8,10},{9,11},{10,... | collective-permute-start | bytes 737288 | tf_op jit(solution)/shard_map/ppermute | solution.py:882
  29.1 10.8 %collective-permute-done.3.refs_6_ = bf16[160,896]{1,0:T(8,128)(2,1)S(1)} collective-permute-done((bf16[160,896]{1,0:T(8,128)(2,1)}, bf16[160,896]{1,0:T(8,128)(2,1)S(1)}, u32[]{:S(2)}, u32[]{:S(2)}) %collective-permute-start.3) | collective-permute-done | bytes 286752 | tf_op jit(solution)/shard_map/ppermute | solution.py:877
  44.6 2.5 %collective-permute-start.10 = (bf16[160,768]{1,0:T(8,128)(2,1)S(1)}, bf16[160,768]{1,0:T(8,128)(2,1)S(1)}, u32[]{:S(2)}, u32[]{:S(2)}) collective-permute-start(bf16[160,768]{1,0:T(8,128)(2,1)S(1)} %get-tuple-element.123.refs_0_), channel_id=1, source_target_pairs={{0,12},{4,8},{8,4},{12,0},{1,13},{5,9},{9,5},{13,1},{2,14},{6,10},... | collective-permute-start | bytes 737288 | tf_op jit(solution)/shard_map/ppermute | solution.py:877
  47.1 6.9 %collective-permute-start.9 = (bf16[160,768]{1,0:T(8,128)(2,1)S(1)}, bf16[160,768]{1,0:T(8,128)(2,1)S(1)}, u32[]{:S(2)}, u32[]{:S(2)}) collective-permute-start(bf16[160,768]{1,0:T(8,128)(2,1)S(1)} %get-tuple-element.123.refs_0_), channel_id=1, source_target_pairs={{0,8},{4,12},{8,0},{12,4},{1,9},{5,13},{9,1},{13,5},{2,10},{6,14},... | collective-permute-start | bytes 737288 | tf_op jit(solution)/shard_map/ppermute | solution.py:877
  54.4 16.0 %collective-permute-done.9.refs_2_ = bf16[160,768]{1,0:T(8,128)(2,1)S(1)} collective-permute-done((bf16[160,768]{1,0:T(8,128)(2,1)S(1)}, bf16[160,768]{1,0:T(8,128)(2,1)S(1)}, u32[]{:S(2)}, u32[]{:S(2)}) %collective-permute-start.9) | collective-permute-done | bytes 245792 | tf_op jit(solution)/shard_map/ppermute | solution.py:877
  71.0 4.4 %experts_first.2 = (bf16[640,768]{1,0:T(8,128)(2,1)S(1)}, bf16[640,768]{1,0:T(8,128)(2,1)S(1)}, bf16[640,768]{1,0:T(8,128)(2,1)S(1)}, bf16[640,768]{1,0:T(8,128)...) custom-call(s32[3]{0:T(128)S(1)} %copy-done.8, ...), custom_call_target="tpu_custom_call" | custom-call | tf_op jit(solution)/shard_map/experts_first/pallas_call | solution.py:304
  75.4 4.4 %experts_first.3 = (bf16[640,768]{1,0:T(8,128)(2,1)S(1)}, bf16[640,768]{1,0:T(8,128)(2,1)S(1)}, bf16[640,768]{1,0:T(8,128)(2,1)S(1)}, bf16[640,768]{1,0:T(8,128)...) custom-call(s32[3]{0:T(128)S(1)} %copy-done.8, ...), custom_call_target="tpu_custom_call" | custom-call | tf_op jit(solution)/shard_map/experts_first/pallas_call | solution.py:304
  79.9 4.3 %experts_second.2 = (bf16[640,768]{1,0:T(8,128)(2,1)S(1)}, bf16[640,768]{1,0:T(8,128)(2,1)S(1)}, bf16[640,768]{1,0:T(8,128)(2,1)S(1)}, f32[640,896]{1,0:T(8,128)S(1)}) custom-call(s32[3]{0:T(128)S(1)} %copy-done.8, bf16[640,768]{1,0:T(8,128)(2,1)S(1)} %get-tuple-element.126.x_ref.refs_3_, bf16[640,768]{1,0:T(8,128)(2,1)S(1)} %get-tuple-element.128.rg_ref.refs_7_, ...), custom_call_target="tpu_custom_call" | custom-call | tf_op jit(solution)/shard_map/experts_second/pallas_call | solution.py:304
  84.8 4.3 %experts_second.3 = (bf16[640,768]{1,0:T(8,128)(2,1)S(1)}, bf16[640,768]{1,0:T(8,128)(2,1)S(1)}, bf16[640,768]{1,0:T(8,128)(2,1)S(1)}, f32[640,896]{1,0:T(8,128)S(1)}) custom-call(s32[3]{0:T(128)S(1)} %copy-done.8, bf16[640,768]{1,0:T(8,128)(2,1)S(1)} %get-tuple-element.124.x_ref.refs_1_, bf16[640,768]{1,0:T(8,128)(2,1)S(1)} %get-tuple-element.138.rg_ref.refs_5_, ...), custom_call_target="tpu_custom_call" | custom-call | tf_op jit(solution)/shard_map/experts_second/pallas_call | solution.py:304
  91.5 2.8 %collective-permute-start.26 = (bf16[176,768]{1,0:T(8,128)(2,1)S(1)}, bf16[176,768]{1,0:T(8,128)(2,1)S(1)}, u32[]{:S(2)}, u32[]{:S(2)}) collective-permute-start(bf16[176,768]{1,0:T(8,128)(2,1)S(1)} %get-tuple-element.149), channel_id=1, source_target_pairs={{0,8},{4,12},{8,0},{12,4},{1,9},{5,13},{9,1},{13,5},{2,10},{6,14},... | collective-permute-start | bytes 811016 | tf_op jit(solution)/shard_map/ppermute | solution.py:877
  95.9 4.4 %expert_grads.2 = (bf16[2,2,192,768]{3,2,1,0:T(8,128)(2,1)S(1)}, bf16[2,2,192,768]{3,2,1,0:T(8,128)(2,1)S(1)}) custom-call(s32[3]{0:T(128)S(1)} %copy-done.8, bf16[640,768]{1,0:T(8,128)(2,1)S(1)} %get-tuple-element.152.refs_0_, bf16[640,768]{1,0:T(8,128)(2,1)S(1)} %get-tuple-element.124.x_ref.refs_1_, bf16[640,768]{1,0:T(8,128)(2,1)S(1)} %get-tuple-element.153.refs_2_, ...), custom_call_target="tpu_custom_call" | custom-call | tf_op jit(solution)/shard_map/expert_grads/pallas_call | solution.py:304
  105.2 4.4 %expert_grads.3 = (bf16[2,2,192,768]{3,2,1,0:T(8,128)(2,1)S(1)}, bf16[2,2,192,768]{3,2,1,0:T(8,128)(2,1)S(1)}) custom-call(s32[3]{0:T(128)S(1)} %copy-done.8, bf16[640,768]{1,0:T(8,128)(2,1)S(1)} %get-tuple-element.159.refs_0_, bf16[640,768]{1,0:T(8,128)(2,1)S(1)} %get-tuple-element.124.x_ref.refs_1_, bf16[640,768]{1,0:T(8,128)(2,1)S(1)} %get-tuple-element.160.refs_2_, ...), custom_call_target="tpu_custom_call" | custom-call | tf_op jit(solution)/shard_map/expert_grads/pallas_call | solution.py:304
  109.6 3.8 %collective-permute-done.26.refs_2_ = bf16[176,768]{1,0:T(8,128)(2,1)S(1)} collective-permute-done((bf16[176,768]{1,0:T(8,128)(2,1)S(1)}, bf16[176,768]{1,0:T(8,128)(2,1)S(1)}, u32[]{:S(2)}, u32[]{:S(2)}) %collective-permute-start.26) | collective-permute-done | bytes 270368 | tf_op jit(solution)/shard_map/ppermute | solution.py:877
  114.7 5.6 %collective-permute-start.28 = (bf16[160,768]{1,0:T(8,128)(2,1)S(1)}, bf16[160,768]{1,0:T(8,128)(2,1)S(1)}, u32[]{:S(2)}, u32[]{:S(2)}) collective-permute-start(bf16[160,768]{1,0:T(8,128)(2,1)S(1)} %get-tuple-element.168), channel_id=1, source_target_pairs={{0,4},{4,0},{8,12},{12,8},{1,5},{5,1},{9,13},{13,9},{2,6},{6,2},{1... | collective-permute-start | bytes 737288 | tf_op jit(solution)/shard_map/ppermute | solution.py:877
  122.8 14.5 %all_gather.6.up_ref = bf16[640,768]{1,0:T(8,128)(2,1)S(1)} all-gather(bf16[160,768]{1,0:T(8,128)(2,1)S(1)} %get-tuple-element.167), channel_id=1, replica_groups=mesh['dp'=2,'expert'=4,'tensor'=4] {'tensor'}, dimensions={0}, use_global_device_ids=true | all-gather | bytes 1228800 | tf_op jit(solution)/shard_map/all_gather | solution.py:1042
  137.3 3.4 %collective-permute-done.29 = bf16[160,768]{1,0:T(8,128)(2,1)S(1)} collective-permute-done((bf16[160,768]{1,0:T(8,128)(2,1)S(1)}, bf16[160,768]{1,0:T(8,128)(2,1)S(1)}, u32[]{:S(2)}, u32[]{:S(2)}) %collective-permute-start.29) | collective-permute-done | bytes 245792 | tf_op jit(solution)/shard_map/ppermute | solution.py:877
  140.7 7.3 %attention_back.1 = (f32[4,96,768]{2,1,0:T(8,128)S(1)}, bf16[4,96,768]{2,1,0:T(8,128)(2,1)S(1)}, bf16[176,768]{1,0:T(8,128)(2,1)S(1)}, bf16[176,768]{1,0:T(8,128...) custom-call(s32[3]{0:T(128)S(1)} %copy-done.8, bf16[3,197,768]{2,1,0:T(8,128)(2,1)S(1)} %copy-done, ...), custom_call_target="tpu_custom_call" | custom-call | flops 6000000000 | tf_op jit(solution)/shard_map/attention_back/pallas_call | solution.py:304
  152.3 3.9 %collective-permute-start.35 = (bf16[96,768]{1,0:T(8,128)(2,1)S(1)}, bf16[96,768]{1,0:T(8,128)(2,1)S(1)}, u32[]{:S(2)}, u32[]{:S(2)}) collective-permute-start(bf16[96,768]{1,0:T(8,128)(2,1)S(1)} %get-tuple-element.186), channel_id=1, source_target_pairs={{0,4},{4,0},{8,12},{12,8},{1,5},{5,1},{9,13},{13,9},{2,6},{6,2},{1... | collective-permute-start | bytes 442376 | tf_op jit(solution)/shard_map/ppermute | solution.py:877
  157.4 2.2 %collective-permute-start.37 = (bf16[96,768]{1,0:T(8,128)(2,1)S(1)}, bf16[96,768]{1,0:T(8,128)(2,1)S(1)}, u32[]{:S(2)}, u32[]{:S(2)}) collective-permute-start(bf16[96,768]{1,0:T(8,128)(2,1)S(1)} %get-tuple-element.188), channel_id=1, source_target_pairs={{0,12},{4,8},{8,4},{12,0},{1,13},{5,9},{9,5},{13,1},{2,14},{6,10},... | collective-permute-start | bytes 442376 | tf_op jit(solution)/shard_map/ppermute | solution.py:877
  159.6 3.2 %collective-permute-done.32.refs_2_ = bf16[176,768]{1,0:T(8,128)(2,1)S(1)} collective-permute-done((bf16[176,768]{1,0:T(8,128)(2,1)S(1)}, bf16[176,768]{1,0:T(8,128)(2,1)S(1)}, u32[]{:S(2)}, u32[]{:S(2)}) %collective-permute-start.32) | collective-permute-done | bytes 270368 | tf_op jit(solution)/shard_map/ppermute | solution.py:882
  167.3 2.3 %collective-permute-done.36.refs_9_ = bf16[96,768]{1,0:T(8,128)(2,1)S(1)} collective-permute-done((bf16[96,768]{1,0:T(8,128)(2,1)S(1)}, bf16[96,768]{1,0:T(8,128)(2,1)S(1)}, u32[]{:S(2)}, u32[]{:S(2)}) %collective-permute-start.36) | collective-permute-done | bytes 147488 | tf_op jit(solution)/shard_map/ppermute | solution.py:877
  170.8 2.1 collective-permute-start.40
  172.8 2.3 %collective-permute-start.39 = (bf16[112,768]{1,0:T(8,128)(2,1)S(1)}, bf16[112,768]{1,0:T(8,128)(2,1)S(1)}, u32[]{:S(2)}, u32[]{:S(2)}) collective-permute-start(bf16[112,768]{1,0:T(8,128)(2,1)S(1)} %get-tuple-element.189.refs_0_), channel_id=1, source_target_pairs={{0,8},{4,12},{8,0},{12,4},{1,9},{5,13},{9,1},{13,5},{2,10},{6,14},... | collective-permute-start | bytes 516104 | tf_op jit(solution)/shard_map/ppermute | solution.py:877
  175.2 13.6 %all_gather.7.refs_0_ = bf16[640,768]{1,0:T(8,128)(2,1)S(1)} all-gather(bf16[160,768]{1,0:T(8,128)(2,1)S(1)} %get-tuple-element.195), channel_id=1, replica_groups=mesh['dp'=2,'expert'=4,'tensor'=4] {'tensor'}, dimensions={0}, use_global_device_ids=true | all-gather | bytes 1228800 | tf_op jit(solution)/shard_map/all_gather | solution.py:1097
  198.5 2.2 %spread.1 = (f32[576,768]{1,0:T(8,128)}, f32[192,768]{1,0:T(8,128)}, f32[4,768]{1,0:T(4,128)}, f32[768]{0:T(1024)}, f32[768]{0:T(1024)}, /*index=5*/f32[1,128]{1,0:T(1,128)}) custom-call(s32[3]{0:T(128)S(1)} %copy-done.8, bf16[112,768]{1,0:T(8,128)(2,1)S(1)} %get-tuple-element.189.refs_0_, bf16[112,768]{1,0:T(8,128)(2,1)S(1)} %collective-permute-done.38.refs_1_, ...), custom_call_target="tpu_custom_call" | custom-call | tf_op jit(solution)/shard_map/spread/pallas_call | solution.py:304
  200.7 3.1 %weight_out.1 = (f32[1,768,768]{2,1,0:T(8,128)}, f32[1,768,768]{2,1,0:T(8,128)}) custom-call(s32[3]{0:T(128)S(1)} %copy-done.8, bf16[2,384,768]{2,1,0:T(8,128)(2,1)S(1)} %weight_sum.1.mine_ref, bf16[2,384,768]{2,1,0:T(8,128)(2,1)S(1)} %collective-permute-done.43.other_ref), custom_call_target="tpu_custom_call" | custom-call | tf_op jit(solution)/shard_map/weight_out/pallas_call | solution.py:304
  203.8 3.5 %collective-permute-done.49.refs_2_ = bf16[160,768]{1,0:T(8,128)(2,1)S(1)} collective-permute-done((bf16[160,768]{1,0:T(8,128)(2,1)S(1)}, bf16[160,768]{1,0:T(8,128)(2,1)S(1)}, u32[]{:S(2)}, u32[]{:S(2)}) %collective-permute-start.49) | collective-permute-done | bytes 245792 | tf_op jit(solution)/shard_map/ppermute | solution.py:882
  (114 shorter events, 49.7 us)
Async XLA Ops:
  7.7 16.9 %collective-permute-start = (bf16[2,192,768]{2,1,0:T(8,128)(2,1)S(1)}, bf16[2,192,768]{2,1,0:T(8,128)(2,1)S(1)}, u32[]{:S(2)}, u32[]{:S(2)}) collective-permute-start(bf16[2,192,768]{2,1,0:T(8,128)(2,1)S(1)} %get-tuple-element.111.refs_0_), channel_id=1, source_target_pairs={{0,1},{1,0},{2,3},{3,2},{4,5},{5,4},{6,7},{7,6},{8,9},{9,8},{10,11... | collective-permute-start | bytes 1769480 | tf_op jit(solution)/shard_map/ppermute | solution.py:882
  10.7 16.2 %collective-permute-start.1 = (bf16[2,192,768]{2,1,0:T(8,128)(2,1)S(1)}, bf16[2,192,768]{2,1,0:T(8,128)(2,1)S(1)}, u32[]{:S(2)}, u32[]{:S(2)}) collective-permute-start(bf16[2,192,768]{2,1,0:T(8,128)(2,1)S(1)} %get-tuple-element.112.refs_2_), channel_id=1, source_target_pairs={{0,2},{1,3},{2,0},{3,1},{4,6},{5,7},{6,4},{7,5},{8,10},{9,11},{10,... | collective-permute-start | bytes 1769480 | tf_op jit(solution)/shard_map/ppermute | solution.py:882
  12.2 11.9 %collective-permute-start.4 = (bf16[160,896]{1,0:T(8,128)(2,1)}, bf16[160,896]{1,0:T(8,128)(2,1)S(1)}, u32[]{:S(2)}, u32[]{:S(2)}) collective-permute-start(bf16[160,896]{1,0:T(8,128)(2,1)} %get-tuple-element.109.refs_4_.refs_6_), channel_id=1, source_target_pairs={{0,12},{4,8},{8,4},{12,0},{1,13},{5,9},{9,5},{13,1},{2,14},{6,10},... | collective-permute-start | bytes 860168 | tf_op jit(solution)/shard_map/ppermute | solution.py:877
  15.8 24.1 %collective-permute-start.3 = (bf16[160,896]{1,0:T(8,128)(2,1)}, bf16[160,896]{1,0:T(8,128)(2,1)S(1)}, u32[]{:S(2)}, u32[]{:S(2)}) collective-permute-start(bf16[160,896]{1,0:T(8,128)(2,1)} %get-tuple-element.109.refs_4_.refs_6_), channel_id=1, source_target_pairs={{0,8},{4,12},{8,0},{12,4},{1,9},{5,13},{9,1},{13,5},{2,10},{6,14},... | collective-permute-start | bytes 860168 | tf_op jit(solution)/shard_map/ppermute | solution.py:877
  15.8 24.1 %collective-permute-start.2 = (bf16[160,896]{1,0:T(8,128)(2,1)}, bf16[160,896]{1,0:T(8,128)(2,1)S(1)}, u32[]{:S(2)}, u32[]{:S(2)}) collective-permute-start(bf16[160,896]{1,0:T(8,128)(2,1)} %get-tuple-element.109.refs_4_.refs_6_), channel_id=1, source_target_pairs={{0,4},{4,0},{8,12},{12,8},{1,5},{5,1},{9,13},{13,9},{2,6},{6,2},{1... | collective-permute-start | bytes 860168 | tf_op jit(solution)/shard_map/ppermute | solution.py:877
  24.1 15.8 %collective-permute-start.5 = (bf16[160,768]{1,0:T(8,128)(2,1)S(1)}, bf16[160,768]{1,0:T(8,128)(2,1)S(1)}, u32[]{:S(2)}, u32[]{:S(2)}) collective-permute-start(bf16[160,768]{1,0:T(8,128)(2,1)S(1)} %get-tuple-element.119), channel_id=1, source_target_pairs={{0,1},{1,0},{2,3},{3,2},{4,5},{5,4},{6,7},{7,6},{8,9},{9,8},{10,11... | collective-permute-start | bytes 737288 | tf_op jit(solution)/shard_map/ppermute | solution.py:882
  24.6 15.3 %collective-permute-start.6 = (bf16[160,768]{1,0:T(8,128)(2,1)S(1)}, bf16[160,768]{1,0:T(8,128)(2,1)S(1)}, u32[]{:S(2)}, u32[]{:S(2)}) collective-permute-start(bf16[160,768]{1,0:T(8,128)(2,1)S(1)} %get-tuple-element.120), channel_id=1, source_target_pairs={{0,2},{1,3},{2,0},{3,1},{4,6},{5,7},{6,4},{7,5},{8,10},{9,11},{10,... | collective-permute-start | bytes 737288 | tf_op jit(solution)/shard_map/ppermute | solution.py:882
  26.9 13.0 %collective-permute-start.7 = (bf16[160,768]{1,0:T(8,128)(2,1)S(1)}, bf16[160,768]{1,0:T(8,128)(2,1)S(1)}, u32[]{:S(2)}, u32[]{:S(2)}) collective-permute-start(bf16[160,768]{1,0:T(8,128)(2,1)S(1)} %get-tuple-element.121), channel_id=1, source_target_pairs={{0,3},{1,2},{2,1},{3,0},{4,7},{5,6},{6,5},{7,4},{8,11},{9,10},{10,... | collective-permute-start | bytes 737288 | tf_op jit(solution)/shard_map/ppermute | solution.py:882
  41.1 38.7 %collective-permute-start.19 = (bf16[2,2,192,768]{3,2,1,0:T(8,128)(2,1)S(1)}, bf16[2,2,192,768]{3,2,1,0:T(8,128)(2,1)S(1)}, u32[]{:S(2)}, u32[]{:S(2)}) collective-permute-start(bf16[2,2,192,768]{3,2,1,0:T(8,128)(2,1)S(1)} %get-tuple-element.134), channel_id=1, source_target_pairs={{0,2},{1,3},{2,0},{3,1},{4,6},{5,7},{6,4},{7,5},{8,10},{9,11},{10,... | collective-permute-start | bytes 3538952 | tf_op jit(solution)/shard_map/ppermute | solution.py:882
  41.7 38.2 %collective-permute-start.20 = (bf16[2,2,192,768]{3,2,1,0:T(8,128)(2,1)S(1)}, bf16[2,2,192,768]{3,2,1,0:T(8,128)(2,1)S(1)}, u32[]{:S(2)}, u32[]{:S(2)}) collective-permute-start(bf16[2,2,192,768]{3,2,1,0:T(8,128)(2,1)S(1)} %get-tuple-element.135), channel_id=1, source_target_pairs={{0,1},{1,0},{2,3},{3,2},{4,5},{5,4},{6,7},{7,6},{8,9},{9,8},{10,11... | collective-permute-start | bytes 3538952 | tf_op jit(solution)/shard_map/ppermute | solution.py:882
  47.1 23.4 %collective-permute-start.9 = (bf16[160,768]{1,0:T(8,128)(2,1)S(1)}, bf16[160,768]{1,0:T(8,128)(2,1)S(1)}, u32[]{:S(2)}, u32[]{:S(2)}) collective-permute-start(bf16[160,768]{1,0:T(8,128)(2,1)S(1)} %get-tuple-element.123.refs_0_), channel_id=1, source_target_pairs={{0,8},{4,12},{8,0},{12,4},{1,9},{5,13},{9,1},{13,5},{2,10},{6,14},... | collective-permute-start | bytes 737288 | tf_op jit(solution)/shard_map/ppermute | solution.py:877
  53.9 16.5 %collective-permute-start.8 = (bf16[160,768]{1,0:T(8,128)(2,1)S(1)}, bf16[160,768]{1,0:T(8,128)(2,1)S(1)}, u32[]{:S(2)}, u32[]{:S(2)}) collective-permute-start(bf16[160,768]{1,0:T(8,128)(2,1)S(1)} %get-tuple-element.123.refs_0_), channel_id=1, source_target_pairs={{0,4},{4,0},{8,12},{12,8},{1,5},{5,1},{9,13},{13,9},{2,6},{6,2},{1... | collective-permute-start | bytes 737288 | tf_op jit(solution)/shard_map/ppermute | solution.py:877
  54.4 21.0 %collective-permute-start.14 = (bf16[160,768]{1,0:T(8,128)(2,1)S(1)}, bf16[160,768]{1,0:T(8,128)(2,1)S(1)}, u32[]{:S(2)}, u32[]{:S(2)}) collective-permute-start(bf16[160,768]{1,0:T(8,128)(2,1)S(1)} %collective-permute-done.10.refs_3_), channel_id=1, source_target_pairs={{0,16},{16,0},{1,17},{17,1},{2,18},{18,2},{3,19},{19,3},{4,20},{20... | collective-permute-start | bytes 737288 | tf_op jit(solution)/shard_map/ppermute | solution.py:872
  91.4 13.8 %collective-permute-start.25 = (bf16[176,768]{1,0:T(8,128)(2,1)S(1)}, bf16[176,768]{1,0:T(8,128)(2,1)S(1)}, u32[]{:S(2)}, u32[]{:S(2)}) collective-permute-start(bf16[176,768]{1,0:T(8,128)(2,1)S(1)} %get-tuple-element.148), channel_id=1, source_target_pairs={{0,4},{4,0},{8,12},{12,8},{1,5},{5,1},{9,13},{13,9},{2,6},{6,2},{1... | collective-permute-start | bytes 811016 | tf_op jit(solution)/shard_map/ppermute | solution.py:877
  91.5 21.9 %collective-permute-start.26 = (bf16[176,768]{1,0:T(8,128)(2,1)S(1)}, bf16[176,768]{1,0:T(8,128)(2,1)S(1)}, u32[]{:S(2)}, u32[]{:S(2)}) collective-permute-start(bf16[176,768]{1,0:T(8,128)(2,1)S(1)} %get-tuple-element.149), channel_id=1, source_target_pairs={{0,8},{4,12},{8,0},{12,4},{1,9},{5,13},{9,1},{13,5},{2,10},{6,14},... | collective-permute-start | bytes 811016 | tf_op jit(solution)/shard_map/ppermute | solution.py:877
  94.3 19.1 %collective-permute-start.27 = (bf16[176,768]{1,0:T(8,128)(2,1)S(1)}, bf16[176,768]{1,0:T(8,128)(2,1)S(1)}, u32[]{:S(2)}, u32[]{:S(2)}) collective-permute-start(bf16[176,768]{1,0:T(8,128)(2,1)S(1)} %get-tuple-element.150), channel_id=1, source_target_pairs={{0,12},{4,8},{8,4},{12,0},{1,13},{5,9},{9,5},{13,1},{2,14},{6,10},... | collective-permute-start | bytes 811016 | tf_op jit(solution)/shard_map/ppermute | solution.py:877
  100.3 40.4 %collective-permute-start.24 = (bf16[2,2,192,768]{3,2,1,0:T(8,128)(2,1)S(1)}, bf16[2,2,192,768]{3,2,1,0:T(8,128)(2,1)S(1)}, u32[]{:S(2)}, u32[]{:S(2)}) collective-permute-start(bf16[2,2,192,768]{3,2,1,0:T(8,128)(2,1)S(1)} %get-tuple-element.156), channel_id=1, source_target_pairs={{0,1},{1,0},{2,3},{3,2},{4,5},{5,4},{6,7},{7,6},{8,9},{9,8},{10,11... | collective-permute-start | bytes 3538952 | tf_op jit(solution)/shard_map/ppermute | solution.py:882
  101.6 39.1 %collective-permute-start.23 = (bf16[2,2,192,768]{3,2,1,0:T(8,128)(2,1)S(1)}, bf16[2,2,192,768]{3,2,1,0:T(8,128)(2,1)S(1)}, u32[]{:S(2)}, u32[]{:S(2)}) collective-permute-start(bf16[2,2,192,768]{3,2,1,0:T(8,128)(2,1)S(1)} %get-tuple-element.155), channel_id=1, source_target_pairs={{0,2},{1,3},{2,0},{3,1},{4,6},{5,7},{6,4},{7,5},{8,10},{9,11},{10,... | collective-permute-start | bytes 3538952 | tf_op jit(solution)/shard_map/ppermute | solution.py:882
  114.7 22.6 %collective-permute-start.28 = (bf16[160,768]{1,0:T(8,128)(2,1)S(1)}, bf16[160,768]{1,0:T(8,128)(2,1)S(1)}, u32[]{:S(2)}, u32[]{:S(2)}) collective-permute-start(bf16[160,768]{1,0:T(8,128)(2,1)S(1)} %get-tuple-element.168), channel_id=1, source_target_pairs={{0,4},{4,0},{8,12},{12,8},{1,5},{5,1},{9,13},{13,9},{2,6},{6,2},{1... | collective-permute-start | bytes 737288 | tf_op jit(solution)/shard_map/ppermute | solution.py:877
  120.3 20.3 %collective-permute-start.29 = (bf16[160,768]{1,0:T(8,128)(2,1)S(1)}, bf16[160,768]{1,0:T(8,128)(2,1)S(1)}, u32[]{:S(2)}, u32[]{:S(2)}) collective-permute-start(bf16[160,768]{1,0:T(8,128)(2,1)S(1)} %get-tuple-element.170), channel_id=1, source_target_pairs={{0,8},{4,12},{8,0},{12,4},{1,9},{5,13},{9,1},{13,5},{2,10},{6,14},... | collective-permute-start | bytes 737288 | tf_op jit(solution)/shard_map/ppermute | solution.py:877
  121.2 19.5 %collective-permute-start.30 = (bf16[160,768]{1,0:T(8,128)(2,1)S(1)}, bf16[160,768]{1,0:T(8,128)(2,1)S(1)}, u32[]{:S(2)}, u32[]{:S(2)}) collective-permute-start(bf16[160,768]{1,0:T(8,128)(2,1)S(1)} %get-tuple-element.172), channel_id=1, source_target_pairs={{0,12},{4,8},{8,4},{12,0},{1,13},{5,9},{9,5},{13,1},{2,14},{6,10},... | collective-permute-start | bytes 737288 | tf_op jit(solution)/shard_map/ppermute | solution.py:877
  149.4 13.4 %collective-permute-start.32 = (bf16[176,768]{1,0:T(8,128)(2,1)S(1)}, bf16[176,768]{1,0:T(8,128)(2,1)S(1)}, u32[]{:S(2)}, u32[]{:S(2)}) collective-permute-start(bf16[176,768]{1,0:T(8,128)(2,1)S(1)} %get-tuple-element.180), channel_id=1, source_target_pairs={{0,2},{1,3},{2,0},{3,1},{4,6},{5,7},{6,4},{7,5},{8,10},{9,11},{10,... | collective-permute-start | bytes 811016 | tf_op jit(solution)/shard_map/ppermute | solution.py:882
  150.9 13.2 %collective-permute-start.33 = (bf16[176,768]{1,0:T(8,128)(2,1)S(1)}, bf16[176,768]{1,0:T(8,128)(2,1)S(1)}, u32[]{:S(2)}, u32[]{:S(2)}) collective-permute-start(bf16[176,768]{1,0:T(8,128)(2,1)S(1)} %get-tuple-element.181), channel_id=1, source_target_pairs={{0,3},{1,2},{2,1},{3,0},{4,7},{5,6},{6,5},{7,4},{8,11},{9,10},{10,... | collective-permute-start | bytes 811016 | tf_op jit(solution)/shard_map/ppermute | solution.py:882
  152.3 15.1 %collective-permute-start.35 = (bf16[96,768]{1,0:T(8,128)(2,1)S(1)}, bf16[96,768]{1,0:T(8,128)(2,1)S(1)}, u32[]{:S(2)}, u32[]{:S(2)}) collective-permute-start(bf16[96,768]{1,0:T(8,128)(2,1)S(1)} %get-tuple-element.186), channel_id=1, source_target_pairs={{0,4},{4,0},{8,12},{12,8},{1,5},{5,1},{9,13},{13,9},{2,6},{6,2},{1... | collective-permute-start | bytes 442376 | tf_op jit(solution)/shard_map/ppermute | solution.py:877
  156.2 13.5 %collective-permute-start.36 = (bf16[96,768]{1,0:T(8,128)(2,1)S(1)}, bf16[96,768]{1,0:T(8,128)(2,1)S(1)}, u32[]{:S(2)}, u32[]{:S(2)}) collective-permute-start(bf16[96,768]{1,0:T(8,128)(2,1)S(1)} %get-tuple-element.187), channel_id=1, source_target_pairs={{0,8},{4,12},{8,0},{12,4},{1,9},{5,13},{9,1},{13,5},{2,10},{6,14},... | collective-permute-start | bytes 442376 | tf_op jit(solution)/shard_map/ppermute | solution.py:877
  157.4 12.3 %collective-permute-start.37 = (bf16[96,768]{1,0:T(8,128)(2,1)S(1)}, bf16[96,768]{1,0:T(8,128)(2,1)S(1)}, u32[]{:S(2)}, u32[]{:S(2)}) collective-permute-start(bf16[96,768]{1,0:T(8,128)(2,1)S(1)} %get-tuple-element.188), channel_id=1, source_target_pairs={{0,12},{4,8},{8,4},{12,0},{1,13},{5,9},{9,5},{13,1},{2,14},{6,10},... | collective-permute-start | bytes 442376 | tf_op jit(solution)/shard_map/ppermute | solution.py:877
  165.0 23.9 %collective-permute-start.41 = (bf16[2,192,768]{2,1,0:T(8,128)(2,1)S(1)}, bf16[2,192,768]{2,1,0:T(8,128)(2,1)S(1)}, u32[]{:S(2)}, u32[]{:S(2)}) collective-permute-start(bf16[2,192,768]{2,1,0:T(8,128)(2,1)S(1)} %get-tuple-element.192), channel_id=1, source_target_pairs={{0,1},{1,0},{2,3},{3,2},{4,5},{5,4},{6,7},{7,6},{8,9},{9,8},{10,11... | collective-permute-start | bytes 1769480 | tf_op jit(solution)/shard_map/ppermute | solution.py:882
  165.9 23.0 %collective-permute-start.42 = (bf16[2,192,768]{2,1,0:T(8,128)(2,1)S(1)}, bf16[2,192,768]{2,1,0:T(8,128)(2,1)S(1)}, u32[]{:S(2)}, u32[]{:S(2)}) collective-permute-start(bf16[2,192,768]{2,1,0:T(8,128)(2,1)S(1)} %get-tuple-element.193), channel_id=1, source_target_pairs={{0,2},{1,3},{2,0},{3,1},{4,6},{5,7},{6,4},{7,5},{8,10},{9,11},{10,... | collective-permute-start | bytes 1769480 | tf_op jit(solution)/shard_map/ppermute | solution.py:882
  170.8 18.1 %collective-permute-start.40 = (bf16[112,768]{1,0:T(8,128)(2,1)S(1)}, bf16[112,768]{1,0:T(8,128)(2,1)S(1)}, u32[]{:S(2)}, u32[]{:S(2)}) collective-permute-start(bf16[112,768]{1,0:T(8,128)(2,1)S(1)} %get-tuple-element.189.refs_0_), channel_id=1, source_target_pairs={{0,12},{4,8},{8,4},{12,0},{1,13},{5,9},{9,5},{13,1},{2,14},{6,10},... | collective-permute-start | bytes 516104 | tf_op jit(solution)/shard_map/ppermute | solution.py:877
  172.8 16.0 %collective-permute-start.39 = (bf16[112,768]{1,0:T(8,128)(2,1)S(1)}, bf16[112,768]{1,0:T(8,128)(2,1)S(1)}, u32[]{:S(2)}, u32[]{:S(2)}) collective-permute-start(bf16[112,768]{1,0:T(8,128)(2,1)S(1)} %get-tuple-element.189.refs_0_), channel_id=1, source_target_pairs={{0,8},{4,12},{8,0},{12,4},{1,9},{5,13},{9,1},{13,5},{2,10},{6,14},... | collective-permute-start | bytes 516104 | tf_op jit(solution)/shard_map/ppermute | solution.py:877
  175.1 13.8 %collective-permute-start.38 = (bf16[112,768]{1,0:T(8,128)(2,1)S(1)}, bf16[112,768]{1,0:T(8,128)(2,1)S(1)}, u32[]{:S(2)}, u32[]{:S(2)}) collective-permute-start(bf16[112,768]{1,0:T(8,128)(2,1)S(1)} %get-tuple-element.189.refs_0_), channel_id=1, source_target_pairs={{0,4},{4,0},{8,12},{12,8},{1,5},{5,1},{9,13},{13,9},{2,6},{6,2},{1... | collective-permute-start | bytes 516104 | tf_op jit(solution)/shard_map/ppermute | solution.py:877
  195.0 12.3 %collective-permute-start.49 = (bf16[160,768]{1,0:T(8,128)(2,1)S(1)}, bf16[160,768]{1,0:T(8,128)(2,1)S(1)}, u32[]{:S(2)}, u32[]{:S(2)}) collective-permute-start(bf16[160,768]{1,0:T(8,128)(2,1)S(1)} %add_convert_fusion.refs_0_), channel_id=1, source_target_pairs={{0,2},{1,3},{2,0},{3,1},{4,6},{5,7},{6,4},{7,5},{8,10},{9,11},{10,... | collective-permute-start | bytes 737288 | tf_op jit(solution)/shard_map/ppermute | solution.py:882
  (28 other events, 182.9 us)
where the time goes:
time: 210 us; the launch traced here: 209 us
  starting transfers between devices  63 us (30%)
  Pallas kernels  61.1 us (29%)
  waiting for transfers between devices  53.8 us (26%)
  blocking collectives  28.1 us (13%)
    pallas_call x22, Pallas kernels, kernel_call(): pl.pallas_call(kernel, in_specs=[pl.BlockSpec(memory_space=pltpu.SMEM)] +...  61.1 us
    ppermute x18, waiting for transfers between devices, hop(): return lax.ppermute(value, 'expert', [(i, i ^ bit) for i in range(size)])  41 us
    ppermute x18, starting transfers between devices, hop(): return lax.ppermute(value, 'expert', [(i, i ^ bit) for i in range(size)])  37.7 us
    ppermute x17, starting transfers between devices, cross(): return lax.ppermute(value, 'tensor', [(i, i ^ bit) for i in range(size)])  22.2 us
    all_gather x1, blocking collectives, dense_body(): attn_grad = lax.all_gather(attn_grad, 'tensor', axis=0, tiled=True)  14.5 us
    all_gather x1, blocking collectives, dense_body(): grad_rows = lax.all_gather(grad_chunk, 'tensor', axis=0, tiled=True)  13.6 us
    ppermute x17, waiting for transfers between devices, cross(): return lax.ppermute(value, 'tensor', [(i, i ^ bit) for i in range(size)])  8.3 us
    ppermute x16, waiting for transfers between devices, swap_core(): return lax.ppermute(value, 'dp', [(0, 1), (1, 0)])  4.48 us
  transfers between devices with their start and end apart: 51, of which 18 were waited for; matrix products, arithmetic and copies ran while one was open for 0% of the time, Pallas kernels for 18%

commit v1 on v0

--- a/solution.py
+++ b/solution.py
@@ -323,7 +323,7 @@
 
 
 def chunk_of(pos_ref, j, size):
-    return pl.ds(pl.multiple_of(lax.bitwise_xor(pos_ref[2], j) * size, 16), size)
+    return pl.ds(pl.multiple_of(lax.bitwise_xor(lax.axis_index("tensor"), j) * size, 16), size)
 
 
 def head_masks(rows, heads):
@@ -354,26 +354,19 @@
     return jnp.concatenate([rows, zeros], axis=0)
 
 
-def weights_kernel(pos_ref, in_ref, out_ref, mine_ref, first_ref, second_ref):
+def chunk_kernel(
+    tensors, pos_ref, tok_ref, cot_ref, ids_ref, rank_ref, router_ref, one_ref, two_ref, in_ref, out_ref,
+    x_ref, pay_ref, param_ref, mine_ref, first_ref, second_ref, flat_ref, kept_ref,
+):
     half = mine_ref.shape[1]
-    quarter = half // 2
-    start = pl.multiple_of(pos_ref[0] * half, LANES)
-    for s, rows in (
-        (0, in_ref[0, :, pl.ds(start, half)].T),
-        (1, out_ref[0, pl.ds(start, half), :]),
-    ):
-        mine_ref[s] = rows
-        first_ref[s] = rows[0:quarter]
-        second_ref[s] = rows[quarter:]
-
-
-def chunk_kernel(
-    tensors, pos_ref, tok_ref, cot_ref, ids_ref, rank_ref, router_ref, one_ref, two_ref, x_ref, pay_ref,
-    param_ref, flat_ref, kept_ref,
-):
+    core = pl.multiple_of(lax.axis_index("dp") * half, LANES)
+    for s, part in ((0, in_ref[0, :, pl.ds(core, half)].T), (1, out_ref[0, pl.ds(core, half), :])):
+        mine_ref[s] = part
+        first_ref[s] = part[0 : half // 2]
+        second_ref[s] = part[half // 2 :]
     images, seq_len, width = tok_ref.shape
     chunk, experts = x_ref.shape[0], router_ref.shape[0]
-    start = pl.multiple_of(pos_ref[2] * chunk, 16)
+    start = pl.multiple_of(lax.axis_index("tensor") * chunk, 16)
     for source, target in ((tok_ref, x_ref), (cot_ref, pay_ref)):
         flat_ref[images * seq_len :, :] = jnp.zeros(
             (flat_ref.shape[0] - images * seq_len, width), jnp.float32
@@ -428,6 +421,25 @@
     )
 
 
+def lay_kernel(pos_ref, *refs):
+    *blocks, out_ref = refs
+    chunk = blocks[0].shape[0]
+    for k, block in enumerate(blocks):
+        out_ref[k * chunk : (k + 1) * chunk, :] = block[...]
+
+
+def lay_rows(position, name, blocks):
+    chunk, width = blocks[0].shape
+    return kernel_call(
+        lay_kernel,
+        name,
+        position,
+        blocks,
+        [like((len(blocks) * chunk, width), blocks[0].dtype)],
+        limit=4,
+    )[0]
+
+
 def gain_row(param_ref, experts, which):
     return param_ref[experts + which : experts + which + 1, :]
 
@@ -511,27 +523,19 @@
     return part, contract(pre, w_in, NN)
 
 
-def first_expert_kernel(experts, owners, pos_ref, *refs):
-    blocks = refs[:owners]
-    pay_refs, param_ref, w0_ref, xa_ref, yb_ref = refs[owners : 2 * owners], *refs[2 * owners :][:4]
-    hidden_ref, pre_ref, x_ref, rg_ref, dy_ref, gate_ref, part_ref, back_ref = refs[2 * owners + 4 :]
-    chunk, width = blocks[0].shape
-    router = router_matrix(param_ref, experts)
-    for k in range(owners):
-        here = pl.ds(k * chunk, chunk)
-        pay = pay_refs[k]
-        rows = blocks[k][...]
-        x_ref[here, :] = rows
-        prob = route_probs(rows, router, experts)
-        mine = lax.broadcasted_iota(jnp.int32, prob.shape, 1) == pos_ref[1]
-        kept = pay[:, width:].astype(jnp.float32)
-        kept = jnp.sum(jnp.where(mine, kept, 0.0), axis=-1, keepdims=True)
-        gate = jnp.sum(jnp.where(mine, prob, 0.0), axis=-1, keepdims=True) * kept
-        gate_ref[here, :LANES] = jnp.broadcast_to(gate, (chunk, LANES))
-        gate_ref[here, LANES:] = jnp.broadcast_to(kept, (chunk, LANES))
-        dy = pay[:, :width]
-        dy_ref[here, :] = dy
-        rg_ref[here, :] = (gate * dy.astype(jnp.float32)).astype(jnp.bfloat16)
+def first_expert_kernel(
+    experts, pos_ref, x_ref, pay_ref, param_ref, w0_ref, xa_ref, yb_ref, hidden_ref, pre_ref, rg_ref,
+    gate_ref, part_ref, back_ref,
+):
+    count, width = x_ref.shape
+    prob = route_probs(x_ref[...], router_matrix(param_ref, experts), experts)
+    mine = lax.broadcasted_iota(jnp.int32, prob.shape, 1) == lax.axis_index("expert")
+    kept = pay_ref[:, width:].astype(jnp.float32)
+    kept = jnp.sum(jnp.where(mine, kept, 0.0), axis=-1, keepdims=True)
+    gate = jnp.sum(jnp.where(mine, prob, 0.0), axis=-1, keepdims=True) * kept
+    gate_ref[:, :LANES] = jnp.broadcast_to(gate, (count, LANES))
+    gate_ref[:, LANES:] = jnp.broadcast_to(kept, (count, LANES))
+    rg_ref[...] = (gate * pay_ref[:, :width].astype(jnp.float32)).astype(jnp.bfloat16)
     w_in, w_out = (
         jnp.concatenate([w0_ref[s], xa_ref[s], yb_ref[s]], axis=0) for s in range(2)
     )
@@ -541,65 +545,57 @@
 
 
 def second_expert_kernel(
-    owners, pos_ref, x_ref, rg_ref, dy_ref, gate_ref, part_in_ref, back_in_ref, pair_y_ref,
-    pair_x_ref, hidden_ref, pre_ref, gated_ref, back_ref, part_ref,
+    pos_ref, x_ref, pay_ref, rg_ref, gate_ref, part_in_ref, back_in_ref, pair_y_ref, pair_x_ref,
+    hidden_ref, pre_ref, gated_ref, back_ref,
 ):
     width = x_ref.shape[1]
-    chunk = x_ref.shape[0] // owners
     w_in, w_out = (
         jnp.concatenate([ref[r, s] for ref in (pair_y_ref, pair_x_ref) for r in range(2)], axis=0)
         for s in range(2)
     )
     part, back = expert_halves(x_ref[...], rg_ref[...], w_in, w_out, hidden_ref, pre_ref)
-    part_ref[...] = part_in_ref[...] + part
     back_ref[:, :width] = back_in_ref[...] + back
-    for k in range(owners):
-        here = pl.ds(k * chunk, chunk)
-        total = part_ref[here, :]
-        gated_ref[here, :] = (gate_ref[here, 0:1] * total).astype(jnp.bfloat16)
-        inner = jnp.sum(total * dy_ref[here, :].astype(jnp.float32), axis=-1, keepdims=True)
-        back_ref[here, width:] = gate_ref[here, LANES:] * inner
-
-
-def first_expert_pass(position, blocks, payload, params, weights, experts):
-    chunk, width = blocks[0].shape
-    count, hidden = len(blocks) * chunk, 2 * weights[0].shape[1]
+    part = part_in_ref[...] + part
+    gated_ref[...] = (gate_ref[:, 0:1] * part).astype(jnp.bfloat16)
+    inner = jnp.sum(part * pay_ref[:, :width].astype(jnp.float32), axis=-1, keepdims=True)
+    back_ref[:, width:] = gate_ref[:, LANES:] * inner
+
+
+def first_expert_pass(position, rows, payload, params, weights, experts):
+    count, width = rows.shape
+    hidden = 2 * weights[0].shape[1]
     return kernel_call(
-        functools.partial(first_expert_kernel, experts, len(blocks)),
+        functools.partial(first_expert_kernel, experts),
         "experts_first",
         position,
-        [*blocks, *payload, params, *weights],
+        [rows, payload, params, *weights],
         [
             like((count, hidden), jnp.bfloat16),
             like((count, hidden), jnp.bfloat16),
-            like((count, width), jnp.bfloat16),
-            like((count, width), jnp.bfloat16),
             like((count, width), jnp.bfloat16),
             like((count, 2 * LANES), jnp.float32),
             like((count, width), jnp.float32),
             like((count, width), jnp.float32),
         ],
-        limit=16,
-    )
-
-
-def second_expert_pass(position, first, weights, owners):
-    x, rg, dy, gate, part, back = first[2:]
-    count, width = x.shape
+        limit=18,
+    )
+
+
+def second_expert_pass(position, rows, payload, first, weights):
+    count, width = rows.shape
     hidden = 4 * weights[0].shape[2]
     return kernel_call(
-        functools.partial(second_expert_kernel, owners),
+        second_expert_kernel,
         "experts_second",
         position,
-        [x, rg, dy, gate, part, back, *weights],
+        [rows, payload, *first[2:], *weights],
         [
             like((count, hidden), jnp.bfloat16),
             like((count, hidden), jnp.bfloat16),
             like((count, width), jnp.bfloat16),
             like((count, width + LANES), jnp.float32),
         ],
-        [pltpu.VMEM((count, width), jnp.float32)],
-        limit=16,
+        limit=18,
     )
 
 
@@ -659,7 +655,7 @@
     route_grad = jnp.zeros_like(prob)
     routed_grad = jnp.zeros((chunk, width), jnp.float32)
     for k, back in enumerate(backs):
-        owner = lax.bitwise_xor(pos_ref[1], k)
+        owner = lax.bitwise_xor(lax.axis_index("expert"), k)
         inner = back[chunk : chunk + SMALL, : 2 * LANES].astype(jnp.float32)
         inner = inner + back[chunk + SMALL :, : 2 * LANES].astype(jnp.float32)
         inner = jnp.concatenate([inner] * (LANES // SMALL), axis=0).T[0:chunk]
@@ -677,7 +673,7 @@
     total = pay_ref[:, :width].astype(jnp.float32) + from_norm
     grad_ref[...] = total
     up_ref[...] = total.astype(jnp.bfloat16)
-    live = live_rows(prob.shape, token_rows, pos_ref[2] * chunk)
+    live = live_rows(prob.shape, token_rows, lax.axis_index("tensor") * chunk)
     prob_sum = jnp.sum(jnp.where(live, prob, 0.0), axis=0, keepdims=True)
     grad_router = contract(logit_grad, mixed.astype(jnp.bfloat16), TN)
     small_ref[0:SMALL, :] = grad_router[0:SMALL]
@@ -711,7 +707,7 @@
         held_ref[i] = hg_ref[pl.ds(i * seq_len, rows), :]
     big_ref[0 : 3 * width, :] = jnp.zeros((3 * width, model), jnp.float32)
 
-    @pl.loop(0, images)
+    @pl.loop(0, images, unroll=True)
     def _(i):
         normed, _, mixed = normalize(
             image_rows(tok_ref, i, image_ref), gain_row(param_ref, experts, 0)
@@ -756,7 +752,7 @@
     for j, part in enumerate(parts):
         part[0:chunk, :] = flat_ref[chunk_of(pos_ref, j, chunk), :].astype(jnp.bfloat16)
         part[chunk:, :] = jnp.concatenate([high, low], axis=0)
-    me, core = pos_ref[1], pos_ref[0]
+    me, core = lax.axis_index("expert"), lax.axis_index("dp")
     piece = keep_ref.shape[1]
     for k in range(owners):
         place = lax.bitwise_xor(me, k) * piece
@@ -773,7 +769,7 @@
     upstream = jnp.zeros((chunk, width), jnp.float32)
     for j, part in enumerate(got):
         upstream = upstream + part[0:chunk, :].astype(jnp.float32)
-        small_ref[lax.bitwise_xor(pos_ref[2], j)] = part[chunk : chunk + SMALL, :].astype(
+        small_ref[lax.bitwise_xor(lax.axis_index("tensor"), j)] = part[chunk : chunk + SMALL, :].astype(
             jnp.float32
         ) + part[chunk + SMALL :, :].astype(jnp.float32)
     small = small_ref[0]
@@ -816,7 +812,7 @@
     blocks = refs[: 2 * owners]
     qkv_ref, wo_ref, router_ref, one_ref, two_ref, loss_ref, big_ref, parts_ref = refs[2 * owners :]
     piece = blocks[0].shape[0] - 2 * SMALL
-    core, me = pos_ref[0], pos_ref[1]
+    core, me = lax.axis_index("dp"), lax.axis_index("expert")
     for c in range(2):
         side = core if c == 0 else 1 - core
         for k in range(owners):
@@ -858,7 +854,7 @@
 
 
 def weight_out_kernel(pos_ref, mine_ref, other_ref, in_ref, out_ref):
-    first_is_mine = pos_ref[0] == 0
+    first_is_mine = lax.axis_index("dp") == 0
     half = mine_ref.shape[1]
     for c in range(2):
         here = slice(c * half, (c + 1) * half)
@@ -914,12 +910,10 @@
     flat_rows = padded + 32
     half = expert_in.shape[2] // cores
     quarter = half // 2
-    position = jnp.stack(
-        [lax.axis_index("dp"), lax.axis_index("expert"), lax.axis_index("tensor")]
-    ).astype(jnp.int32)
+    position = jnp.zeros((1,), jnp.int32)
     weight_rows = qkv_weight.transpose(0, 2, 1).reshape(3 * local, width)
 
-    x_chunk, payload, params = kernel_call(
+    x_chunk, payload, params, mine, first, second = kernel_call(
         functools.partial(chunk_kernel, tensors),
         "chunk",
         position,
@@ -931,33 +925,25 @@
             router_weight.T,
             gain_attention,
             gain_experts,
+            expert_in,
+            expert_out,
         ],
         [
             like((chunk, width), b16),
             like((chunk, width + LANES), b16),
             like((SMALL, width), f32),
+            like((2, half, width), b16),
+            like((2, quarter, width), b16),
+            like((2, quarter, width), b16),
         ],
         [
             pltpu.VMEM((flat_rows, width), f32),
             pltpu.VMEM((padded + 2 * LANES, LANES), f32),
         ],
         limit=56,
-        loads=tuple(range(7)),
+        loads=tuple(range(9)),
     )
     payload_mine = [payload] + [hop(payload, k) for k in range(1, owners)]
-    mine, first, second = kernel_call(
-        weights_kernel,
-        "weights",
-        after(position, payload),
-        [expert_in, expert_out],
-        [
-            like((2, half, width), b16),
-            like((2, quarter, width), b16),
-            like((2, quarter, width), b16),
-        ],
-        limit=12,
-        loads=(0, 1),
-    )
     first_x = cross(first, 1)
     second_y = cross(second, 2)
 
@@ -986,7 +972,7 @@
     residual, routed, prob = kernel_call(
         functools.partial(route_kernel, experts),
         "route",
-        after(position, pair_first, payload_mine),
+        after(position, pair_first, payload_mine[::-1]),
         [*arrived, x_chunk, params],
         [like((chunk, width), f32), like((chunk, width), b16), like((chunk, LANES), f32)],
         limit=8,
@@ -995,20 +981,22 @@
     pair_first, pair_second = after((pair_first, pair_second), routed)
     pair_y = cross(pair_first, 2)
     pair_x = cross(pair_second, 1)
-    other_blocks = [swap_core(b) for b in blocks]
-    payload_other = [swap_core(p) for p in payload_mine]
+    payload_mine = lay_rows(after(position, routed), "lay_payload", payload_mine)
+    payload_other = swap_core(payload_mine)
+    rows_mine = lay_rows(position, "lay_rows", blocks)
+    rows_other = swap_core(rows_mine)
 
     near_weights, far_weights = (mine, first_x, second_y), (pair_y, pair_x)
-    first_a = first_expert_pass(position, blocks, payload_mine, params, near_weights, experts)
+    first_a = first_expert_pass(position, rows_mine, payload_mine, params, near_weights, experts)
     first_b = first_expert_pass(
-        after(position, first_a[2]), other_blocks, payload_other, params, near_weights, experts
+        after(position, first_a[2]), rows_other, payload_other, params, near_weights, experts
     )
     second_b = second_expert_pass(
-        after(position, first_b[2]), first_b, far_weights, owners
+        after(position, first_b[2]), rows_other, payload_other, first_b, far_weights
     )
     back_other, gated_other = swap_core(second_b[3]), swap_core(second_b[2])
     second_a = second_expert_pass(
-        after(position, second_b[0]), first_a, far_weights, owners
+        after(position, second_b[0]), rows_mine, payload_mine, first_a, far_weights
     )
     joined = kernel_call(
         join_kernel,
@@ -1021,10 +1009,10 @@
     backs = [joined[0]] + [hop(joined[k], k) for k in range(1, owners)]
 
     grad_pos = after(position, joined[:owners])
-    far_y, far_x = expert_grads(grad_pos, second_a, second_b, first_a[2:4], first_b[2:4])
+    far_y, far_x = expert_grads(grad_pos, second_a, second_b, (rows_mine, first_a[2]), (rows_other, first_b[2]))
     from_y, from_x = cross(far_y, 2), cross(far_x, 1)
     own_grad, near_grad = expert_grads(
-        after(grad_pos, far_y, backs[1]), first_a, first_b, first_a[2:4], first_b[2:4]
+        after(grad_pos, far_y, backs[1]), first_a, first_b, (rows_mine, first_a[2]), (rows_other, first_b[2])
     )
 
     residual_grad, attn_grad, small = kernel_call(

time: 210 us -> 194 us (0.924)
  Pallas kernels: 61.1 us -> 49.3 us
  waiting for transfers between devices: 53.8 us -> 48.3 us
  starting transfers between devices: 63 us -> 66.9 us
    pallas_call x22 -> x23, Pallas kernels: 61.1 us -> 49.3 us  [kernel_call(): pl.pallas_call(kernel, in_specs=[pl.BlockSpec(memory_space=pltpu.SMEM)] +...]
    ppermute x18, starting transfers between devices: 37.7 us -> 45.5 us  [hop(): return lax.ppermute(value, 'expert', [(i, i ^ bit) for i in range(size)])]
    ppermute x18, waiting for transfers between devices: 41 us -> 35.2 us  [hop(): return lax.ppermute(value, 'expert', [(i, i ^ bit) for i in range(size)])]
    ppermute x17, starting transfers between devices: 22.2 us -> 19.5 us  [cross(): return lax.ppermute(value, 'tensor', [(i, i ^ bit) for i in range(size)])]
    ppermute x16 -> x10, waiting for transfers between devices: 4.48 us -> 3.25 us  [swap_core(): return lax.ppermute(value, 'dp', [(0, 1), (1, 0)])]
  transfers between devices with their start and end apart: 51 -> 45, of which waited for: 18 -> 16; matrix products, arithmetic and copies ran while one was open for 0% -> 0% of each run, Pallas kernels for 18% -> 16%
where the time goes in v1:
time: 194 us; the launch traced here: 193 us
  starting transfers between devices  66.9 us (34%)
  Pallas kernels  49.3 us (25%)
  waiting for transfers between devices  48.3 us (25%)
  blocking collectives  26.2 us (14%)
    pallas_call x23, Pallas kernels, kernel_call(): pl.pallas_call(kernel, in_specs=[pl.BlockSpec(memory_space=pltpu.SMEM)] +...  49.3 us
    ppermute x18, starting transfers between devices, hop(): return lax.ppermute(value, 'expert', [(i, i ^ bit) for i in range(size)])  45.5 us
    ppermute x18, waiting for transfers between devices, hop(): return lax.ppermute(value, 'expert', [(i, i ^ bit) for i in range(size)])  35.2 us
    ppermute x17, starting transfers between devices, cross(): return lax.ppermute(value, 'tensor', [(i, i ^ bit) for i in range(size)])  19.5 us
    all_gather x1, blocking collectives, dense_body(): attn_grad = lax.all_gather(attn_grad, 'tensor', axis=0, tiled=True)  13.4 us
    all_gather x1, blocking collectives, dense_body(): grad_rows = lax.all_gather(grad_chunk, 'tensor', axis=0, tiled=True)  12.8 us
    ppermute x17, waiting for transfers between devices, cross(): return lax.ppermute(value, 'tensor', [(i, i ^ bit) for i in range(size)])  9.86 us
  transfers between devices with their start and end apart: 45, of which 16 were waited for; matrix products, arithmetic and copies ran while one was open for 0% of the time, Pallas kernels for 16%

profile of v1, /device:TPU:0, one launch (start us, length us, event | category | flops | bytes accessed | tf_op | source)
XLA Modules:
  0.0 192.6 jit_solution(8462497022724590371)
XLA Ops:
  0.7 4.9 %chunk.1 = (bf16[160,768]{1,0:T(8,128)(2,1)}, bf16[160,896]{1,0:T(8,128)(2,1)}, f32[8,768]{1,0:T(8,128)}, bf16[2,384,768]{2,1,0:T(8,128)(2,1)}, bf16[2,192,768]{...) custom-call(s32[1]{0:T(128)} %constant.0.clone.1.refs_0_.pos_ref, bf16[3,197,768]{2,1,0:T(8,128)(2,1)} %tok_ref.1, ...), custom_call_target="tpu_custom_call" | custom-call | tf_op jit(solution)/shard_map/chunk/pallas_call | solution.py:304
  5.6 3.0 %collective-permute-start = (bf16[2,192,768]{2,1,0:T(8,128)(2,1)}, bf16[2,192,768]{2,1,0:T(8,128)(2,1)S(1)}, u32[]{:S(2)}, u32[]{:S(2)}) collective-permute-start(bf16[2,192,768]{2,1,0:T(8,128)(2,1)} %get-tuple-element.105.refs_0_), channel_id=1, source_target_pairs={{0,1},{1,0},{2,3},{3,2},{4,5},{5,4},{6,7},{7,6},{8,9},{9,8},{10,11... | collective-permute-start | bytes 1769480 | tf_op jit(solution)/shard_map/ppermute | solution.py:878
  11.7 2.6 %collective-permute-start.3 = (bf16[160,896]{1,0:T(8,128)(2,1)}, bf16[160,896]{1,0:T(8,128)(2,1)S(1)}, u32[]{:S(2)}, u32[]{:S(2)}) collective-permute-start(bf16[160,896]{1,0:T(8,128)(2,1)} %get-tuple-element.108.refs_0_.refs_6_), channel_id=1, source_target_pairs={{0,8},{4,12},{8,0},{12,4},{1,9},{5,13},{9,1},{13,5},{2,10},{6,14},... | collective-permute-start | bytes 860168 | tf_op jit(solution)/shard_map/ppermute | solution.py:873
  15.3 4.9 %attention.1 = (bf16[3,3,208,192]{3,2,1,0:T(8,128)(2,1)S(1)}, f32[3,208,128]{2,1,0:T(8,128)S(1)}, bf16[640,192]{1,0:T(8,128)(2,1)S(1)}, bf16[160,768]{1,0:T(8,12...) custom-call(s32[1]{0:T(128)} %constant.0.clone.1.refs_0_.pos_ref, ...), custom_call_target="tpu_custom_call" | custom-call | tf_op jit(solution)/shard_map/attention/pallas_call | solution.py:304
  20.1 3.3 %collective-permute-done.4.refs_1_ = bf16[160,896]{1,0:T(8,128)(2,1)S(1)} collective-permute-done((bf16[160,896]{1,0:T(8,128)(2,1)}, bf16[160,896]{1,0:T(8,128)(2,1)S(1)}, u32[]{:S(2)}, u32[]{:S(2)}) %collective-permute-start.4) | collective-permute-done | bytes 286752 | tf_op jit(solution)/shard_map/ppermute | solution.py:873
  24.3 2.6 %collective-permute-start.7 = (bf16[160,768]{1,0:T(8,128)(2,1)S(1)}, bf16[160,768]{1,0:T(8,128)(2,1)S(1)}, u32[]{:S(2)}, u32[]{:S(2)}) collective-permute-start(bf16[160,768]{1,0:T(8,128)(2,1)S(1)} %get-tuple-element.116), channel_id=1, source_target_pairs={{0,3},{1,2},{2,1},{3,0},{4,7},{5,6},{6,5},{7,4},{8,11},{9,10},{10,... | collective-permute-start | bytes 737288 | tf_op jit(solution)/shard_map/ppermute | solution.py:878
  27.1 7.8 %collective-permute-done.3.refs_2_ = bf16[160,896]{1,0:T(8,128)(2,1)S(1)} collective-permute-done((bf16[160,896]{1,0:T(8,128)(2,1)}, bf16[160,896]{1,0:T(8,128)(2,1)S(1)}, u32[]{:S(2)}, u32[]{:S(2)}) %collective-permute-start.3) | collective-permute-done | bytes 286752 | tf_op jit(solution)/shard_map/ppermute | solution.py:873
  35.6 3.8 %collective-permute-start.10 = (bf16[160,768]{1,0:T(8,128)(2,1)S(1)}, bf16[160,768]{1,0:T(8,128)(2,1)S(1)}, u32[]{:S(2)}, u32[]{:S(2)}) collective-permute-start(bf16[160,768]{1,0:T(8,128)(2,1)S(1)} %get-tuple-element.118.refs_0_), channel_id=1, source_target_pairs={{0,12},{4,8},{8,4},{12,0},{1,13},{5,9},{9,5},{13,1},{2,14},{6,10},... | collective-permute-start | bytes 737288 | tf_op jit(solution)/shard_map/ppermute | solution.py:873
  39.5 11.3 %collective-permute-start.9 = (bf16[160,768]{1,0:T(8,128)(2,1)S(1)}, bf16[160,768]{1,0:T(8,128)(2,1)S(1)}, u32[]{:S(2)}, u32[]{:S(2)}) collective-permute-start(bf16[160,768]{1,0:T(8,128)(2,1)S(1)} %get-tuple-element.118.refs_0_), channel_id=1, source_target_pairs={{0,8},{4,12},{8,0},{12,4},{1,9},{5,13},{9,1},{13,5},{2,10},{6,14},... | collective-permute-start | bytes 737288 | tf_op jit(solution)/shard_map/ppermute | solution.py:873
  51.6 8.7 %collective-permute-done.9.refs_2_ = bf16[160,768]{1,0:T(8,128)(2,1)S(1)} collective-permute-done((bf16[160,768]{1,0:T(8,128)(2,1)S(1)}, bf16[160,768]{1,0:T(8,128)(2,1)S(1)}, u32[]{:S(2)}, u32[]{:S(2)}) %collective-permute-start.9) | collective-permute-done | bytes 245792 | tf_op jit(solution)/shard_map/ppermute | solution.py:873
  60.4 3.8 %experts_first.2 = (bf16[640,768]{1,0:T(8,128)(2,1)S(1)}, bf16[640,768]{1,0:T(8,128)(2,1)S(1)}, bf16[640,768]{1,0:T(8,128)(2,1)S(1)}, f32[640,256]{1,0:T(8,128)S...) custom-call(s32[1]{0:T(128)} %constant.0.clone.1.refs_0_.pos_ref, bf16[640,768]{1,0:T(8,128)(2,1)S(1)} %lay_rows.1.x_ref.refs_1_, ...), custom_call_target="tpu_custom_call" | custom-call | tf_op jit(solution)/shard_map/experts_first/pallas_call | solution.py:304
  64.3 3.8 %experts_first.3 = (bf16[640,768]{1,0:T(8,128)(2,1)S(1)}, bf16[640,768]{1,0:T(8,128)(2,1)S(1)}, bf16[640,768]{1,0:T(8,128)(2,1)S(1)}, f32[640,256]{1,0:T(8,128)S...) custom-call(s32[1]{0:T(128)} %constant.0.clone.1.refs_0_.pos_ref, ...), custom_call_target="tpu_custom_call" | custom-call | tf_op jit(solution)/shard_map/experts_first/pallas_call | solution.py:304
  68.1 3.8 %experts_second.2 = (bf16[640,768]{1,0:T(8,128)(2,1)S(1)}, bf16[640,768]{1,0:T(8,128)(2,1)S(1)}, bf16[640,768]{1,0:T(8,128)(2,1)S(1)}, f32[640,896]{1,0:T(8,128)S(1)}) custom-call(s32[1]{0:T(128)} %constant.0.clone.1.refs_0_.pos_ref, bf16[640,768]{1,0:T(8,128)(2,1)S(1)} %collective-permute-done.11.x_ref.refs_3_, ...), custom_call_target="tpu_custom_call" | custom-call | tf_op jit(solution)/shard_map/experts_second/pallas_call | solution.py:304
  72.5 3.9 %experts_second.3 = (bf16[640,768]{1,0:T(8,128)(2,1)S(1)}, bf16[640,768]{1,0:T(8,128)(2,1)S(1)}, bf16[640,768]{1,0:T(8,128)(2,1)S(1)}, f32[640,896]{1,0:T(8,128)S(1)}) custom-call(s32[1]{0:T(128)} %constant.0.clone.1.refs_0_.pos_ref, bf16[640,768]{1,0:T(8,128)(2,1)S(1)} %lay_rows.1.x_ref.refs_1_, bf16[640,896]{1,0:T(8,128)(2,1)S(1)} %lay_payload.1.pay_ref, ...), custom_call_target="tpu_custom_call" | custom-call | tf_op jit(solution)/shard_map/experts_second/pallas_call | solution.py:304
  79.6 1.9 collective-permute-start.20
  83.0 3.9 %expert_grads.2 = (bf16[2,2,192,768]{3,2,1,0:T(8,128)(2,1)S(1)}, bf16[2,2,192,768]{3,2,1,0:T(8,128)(2,1)S(1)}) custom-call(s32[1]{0:T(128)} %constant.0.clone.1.refs_0_.pos_ref, bf16[640,768]{1,0:T(8,128)(2,1)S(1)} %get-tuple-element.144.refs_0_, bf16[640,768]{1,0:T(8,128)(2,1)S(1)} %lay_rows.1.x_ref.refs_1_, ...), custom_call_target="tpu_custom_call" | custom-call | tf_op jit(solution)/shard_map/expert_grads/pallas_call | solution.py:304
  88.4 4.2 %collective-permute-done.19.refs_1_ = bf16[176,768]{1,0:T(8,128)(2,1)S(1)} collective-permute-done((bf16[176,768]{1,0:T(8,128)(2,1)S(1)}, bf16[176,768]{1,0:T(8,128)(2,1)S(1)}, u32[]{:S(2)}, u32[]{:S(2)}) %collective-permute-start.19) | collective-permute-done | bytes 270368 | tf_op jit(solution)/shard_map/ppermute | solution.py:873
  92.5 3.9 %expert_grads.3 = (bf16[2,2,192,768]{3,2,1,0:T(8,128)(2,1)S(1)}, bf16[2,2,192,768]{3,2,1,0:T(8,128)(2,1)S(1)}) custom-call(s32[1]{0:T(128)} %constant.0.clone.1.refs_0_.pos_ref, bf16[640,768]{1,0:T(8,128)(2,1)S(1)} %get-tuple-element.151.refs_0_, bf16[640,768]{1,0:T(8,128)(2,1)S(1)} %lay_rows.1.x_ref.refs_1_, ...), custom_call_target="tpu_custom_call" | custom-call | tf_op jit(solution)/shard_map/expert_grads/pallas_call | solution.py:304
  96.4 5.1 %collective-permute-done.20.refs_2_ = bf16[176,768]{1,0:T(8,128)(2,1)S(1)} collective-permute-done((bf16[176,768]{1,0:T(8,128)(2,1)S(1)}, bf16[176,768]{1,0:T(8,128)(2,1)S(1)}, u32[]{:S(2)}, u32[]{:S(2)}) %collective-permute-start.20) | collective-permute-done | bytes 270368 | tf_op jit(solution)/shard_map/ppermute | solution.py:873
  102.3 5.3 %collective-permute-start.22 = (bf16[160,768]{1,0:T(8,128)(2,1)S(1)}, bf16[160,768]{1,0:T(8,128)(2,1)S(1)}, u32[]{:S(2)}, u32[]{:S(2)}) collective-permute-start(bf16[160,768]{1,0:T(8,128)(2,1)S(1)} %get-tuple-element.160), channel_id=1, source_target_pairs={{0,4},{4,0},{8,12},{12,8},{1,5},{5,1},{9,13},{13,9},{2,6},{6,2},{1... | collective-permute-start | bytes 737288 | tf_op jit(solution)/shard_map/ppermute | solution.py:873
  110.1 13.4 %all_gather.6.up_ref = bf16[640,768]{1,0:T(8,128)(2,1)S(1)} all-gather(bf16[160,768]{1,0:T(8,128)(2,1)S(1)} %get-tuple-element.159), channel_id=1, replica_groups=mesh['dp'=2,'expert'=4,'tensor'=4] {'tensor'}, dimensions={0}, use_global_device_ids=true | all-gather | bytes 1228800 | tf_op jit(solution)/shard_map/all_gather | solution.py:1030
  123.5 4.5 %collective-permute-done.23 = bf16[160,768]{1,0:T(8,128)(2,1)S(1)} collective-permute-done((bf16[160,768]{1,0:T(8,128)(2,1)S(1)}, bf16[160,768]{1,0:T(8,128)(2,1)S(1)}, u32[]{:S(2)}, u32[]{:S(2)}) %collective-permute-start.23) | collective-permute-done | bytes 245792 | tf_op jit(solution)/shard_map/ppermute | solution.py:873
  127.9 5.8 %attention_back.1 = (f32[4,96,768]{2,1,0:T(8,128)S(1)}, bf16[4,96,768]{2,1,0:T(8,128)(2,1)S(1)}, bf16[176,768]{1,0:T(8,128)(2,1)S(1)}, bf16[176,768]{1,0:T(8,128...) custom-call(s32[1]{0:T(128)} %constant.0.clone.1.refs_0_.pos_ref, ...), custom_call_target="tpu_custom_call" | custom-call | flops 6000000000 | tf_op jit(solution)/shard_map/attention_back/pallas_call | solution.py:304
  134.5 1.8 collective-permute-start.26
  137.6 3.7 %collective-permute-start.29 = (bf16[96,768]{1,0:T(8,128)(2,1)S(1)}, bf16[96,768]{1,0:T(8,128)(2,1)S(1)}, u32[]{:S(2)}, u32[]{:S(2)}) collective-permute-start(bf16[96,768]{1,0:T(8,128)(2,1)S(1)} %get-tuple-element.178), channel_id=1, source_target_pairs={{0,4},{4,0},{8,12},{12,8},{1,5},{5,1},{9,13},{13,9},{2,6},{6,2},{1... | collective-permute-start | bytes 442376 | tf_op jit(solution)/shard_map/ppermute | solution.py:873
  143.2 2.3 %collective-permute-start.31 = (bf16[96,768]{1,0:T(8,128)(2,1)S(1)}, bf16[96,768]{1,0:T(8,128)(2,1)S(1)}, u32[]{:S(2)}, u32[]{:S(2)}) collective-permute-start(bf16[96,768]{1,0:T(8,128)(2,1)S(1)} %get-tuple-element.180), channel_id=1, source_target_pairs={{0,12},{4,8},{8,4},{12,0},{1,13},{5,9},{9,5},{13,1},{2,14},{6,10},... | collective-permute-start | bytes 442376 | tf_op jit(solution)/shard_map/ppermute | solution.py:873
  145.6 2.6 %collective-permute-done.26.refs_2_ = bf16[176,768]{1,0:T(8,128)(2,1)S(1)} collective-permute-done((bf16[176,768]{1,0:T(8,128)(2,1)S(1)}, bf16[176,768]{1,0:T(8,128)(2,1)S(1)}, u32[]{:S(2)}, u32[]{:S(2)}) %collective-permute-start.26) | collective-permute-done | bytes 270368 | tf_op jit(solution)/shard_map/ppermute | solution.py:878
  154.7 2.9 %collective-permute-start.34 = (bf16[112,768]{1,0:T(8,128)(2,1)S(1)}, bf16[112,768]{1,0:T(8,128)(2,1)S(1)}, u32[]{:S(2)}, u32[]{:S(2)}) collective-permute-start(bf16[112,768]{1,0:T(8,128)(2,1)S(1)} %get-tuple-element.181.refs_0_), channel_id=1, source_target_pairs={{0,12},{4,8},{8,4},{12,0},{1,13},{5,9},{9,5},{13,1},{2,14},{6,10},... | collective-permute-start | bytes 516104 | tf_op jit(solution)/shard_map/ppermute | solution.py:873
  157.6 3.2 %collective-permute-start.33 = (bf16[112,768]{1,0:T(8,128)(2,1)S(1)}, bf16[112,768]{1,0:T(8,128)(2,1)S(1)}, u32[]{:S(2)}, u32[]{:S(2)}) collective-permute-start(bf16[112,768]{1,0:T(8,128)(2,1)S(1)} %get-tuple-element.181.refs_0_), channel_id=1, source_target_pairs={{0,8},{4,12},{8,0},{12,4},{1,9},{5,13},{9,1},{13,5},{2,10},{6,14},... | collective-permute-start | bytes 516104 | tf_op jit(solution)/shard_map/ppermute | solution.py:873
  161.3 12.8 %all_gather.7.refs_0_ = bf16[640,768]{1,0:T(8,128)(2,1)S(1)} all-gather(bf16[160,768]{1,0:T(8,128)(2,1)S(1)} %get-tuple-element.187), channel_id=1, replica_groups=mesh['dp'=2,'expert'=4,'tensor'=4] {'tensor'}, dimensions={0}, use_global_device_ids=true | all-gather | bytes 1228800 | tf_op jit(solution)/shard_map/all_gather | solution.py:1085
  184.3 2.6 %weight_out.1 = (f32[1,768,768]{2,1,0:T(8,128)}, f32[1,768,768]{2,1,0:T(8,128)}) custom-call(s32[1]{0:T(128)} %constant.0.clone.1.refs_0_.pos_ref, bf16[2,384,768]{2,1,0:T(8,128)(2,1)S(1)} %weight_sum.1.mine_ref, bf16[2,384,768]{2,1,0:T(8,128)(2,1)S(1)} %collective-permute-done.37.other_ref), custom_call_target="tpu_custom_call" | custom-call | tf_op jit(solution)/shard_map/weight_out/pallas_call | solution.py:304
  187.0 4.3 %collective-permute-done.43.refs_2_ = bf16[160,768]{1,0:T(8,128)(2,1)S(1)} collective-permute-done((bf16[160,768]{1,0:T(8,128)(2,1)S(1)}, bf16[160,768]{1,0:T(8,128)(2,1)S(1)}, u32[]{:S(2)}, u32[]{:S(2)}) %collective-permute-start.43) | collective-permute-done | bytes 245792 | tf_op jit(solution)/shard_map/ppermute | solution.py:878
  (104 shorter events, 39.3 us)
Async XLA Ops:
  5.6 18.4 %collective-permute-start = (bf16[2,192,768]{2,1,0:T(8,128)(2,1)}, bf16[2,192,768]{2,1,0:T(8,128)(2,1)S(1)}, u32[]{:S(2)}, u32[]{:S(2)}) collective-permute-start(bf16[2,192,768]{2,1,0:T(8,128)(2,1)} %get-tuple-element.105.refs_0_), channel_id=1, source_target_pairs={{0,1},{1,0},{2,3},{3,2},{4,5},{5,4},{6,7},{7,6},{8,9},{9,8},{10,11... | collective-permute-start | bytes 1769480 | tf_op jit(solution)/shard_map/ppermute | solution.py:878
  8.6 15.7 %collective-permute-start.1 = (bf16[2,192,768]{2,1,0:T(8,128)(2,1)}, bf16[2,192,768]{2,1,0:T(8,128)(2,1)S(1)}, u32[]{:S(2)}, u32[]{:S(2)}) collective-permute-start(bf16[2,192,768]{2,1,0:T(8,128)(2,1)} %get-tuple-element.106.refs_2_), channel_id=1, source_target_pairs={{0,2},{1,3},{2,0},{3,1},{4,6},{5,7},{6,4},{7,5},{8,10},{9,11},{10,... | collective-permute-start | bytes 1769480 | tf_op jit(solution)/shard_map/ppermute | solution.py:878
  10.1 13.3 %collective-permute-start.4 = (bf16[160,896]{1,0:T(8,128)(2,1)}, bf16[160,896]{1,0:T(8,128)(2,1)S(1)}, u32[]{:S(2)}, u32[]{:S(2)}) collective-permute-start(bf16[160,896]{1,0:T(8,128)(2,1)} %get-tuple-element.108.refs_0_.refs_6_), channel_id=1, source_target_pairs={{0,4},{4,0},{8,12},{12,8},{1,5},{5,1},{9,13},{13,9},{2,6},{6,2},{1... | collective-permute-start | bytes 860168 | tf_op jit(solution)/shard_map/ppermute | solution.py:873
  11.7 23.2 %collective-permute-start.3 = (bf16[160,896]{1,0:T(8,128)(2,1)}, bf16[160,896]{1,0:T(8,128)(2,1)S(1)}, u32[]{:S(2)}, u32[]{:S(2)}) collective-permute-start(bf16[160,896]{1,0:T(8,128)(2,1)} %get-tuple-element.108.refs_0_.refs_6_), channel_id=1, source_target_pairs={{0,8},{4,12},{8,0},{12,4},{1,9},{5,13},{9,1},{13,5},{2,10},{6,14},... | collective-permute-start | bytes 860168 | tf_op jit(solution)/shard_map/ppermute | solution.py:873
  14.3 20.6 %collective-permute-start.2 = (bf16[160,896]{1,0:T(8,128)(2,1)}, bf16[160,896]{1,0:T(8,128)(2,1)S(1)}, u32[]{:S(2)}, u32[]{:S(2)}) collective-permute-start(bf16[160,896]{1,0:T(8,128)(2,1)} %get-tuple-element.108.refs_0_.refs_6_), channel_id=1, source_target_pairs={{0,12},{4,8},{8,4},{12,0},{1,13},{5,9},{9,5},{13,1},{2,14},{6,10},... | collective-permute-start | bytes 860168 | tf_op jit(solution)/shard_map/ppermute | solution.py:873
  23.5 11.4 %collective-permute-start.5 = (bf16[160,768]{1,0:T(8,128)(2,1)S(1)}, bf16[160,768]{1,0:T(8,128)(2,1)S(1)}, u32[]{:S(2)}, u32[]{:S(2)}) collective-permute-start(bf16[160,768]{1,0:T(8,128)(2,1)S(1)} %get-tuple-element.114), channel_id=1, source_target_pairs={{0,1},{1,0},{2,3},{3,2},{4,5},{5,4},{6,7},{7,6},{8,9},{9,8},{10,11... | collective-permute-start | bytes 737288 | tf_op jit(solution)/shard_map/ppermute | solution.py:878
  24.0 11.0 %collective-permute-start.6 = (bf16[160,768]{1,0:T(8,128)(2,1)S(1)}, bf16[160,768]{1,0:T(8,128)(2,1)S(1)}, u32[]{:S(2)}, u32[]{:S(2)}) collective-permute-start(bf16[160,768]{1,0:T(8,128)(2,1)S(1)} %get-tuple-element.115), channel_id=1, source_target_pairs={{0,2},{1,3},{2,0},{3,1},{4,6},{5,7},{6,4},{7,5},{8,10},{9,11},{10,... | collective-permute-start | bytes 737288 | tf_op jit(solution)/shard_map/ppermute | solution.py:878
  35.6 15.8 %collective-permute-start.10 = (bf16[160,768]{1,0:T(8,128)(2,1)S(1)}, bf16[160,768]{1,0:T(8,128)(2,1)S(1)}, u32[]{:S(2)}, u32[]{:S(2)}) collective-permute-start(bf16[160,768]{1,0:T(8,128)(2,1)S(1)} %get-tuple-element.118.refs_0_), channel_id=1, source_target_pairs={{0,12},{4,8},{8,4},{12,0},{1,13},{5,9},{9,5},{13,1},{2,14},{6,10},... | collective-permute-start | bytes 737288 | tf_op jit(solution)/shard_map/ppermute | solution.py:873
  39.5 20.8 %collective-permute-start.9 = (bf16[160,768]{1,0:T(8,128)(2,1)S(1)}, bf16[160,768]{1,0:T(8,128)(2,1)S(1)}, u32[]{:S(2)}, u32[]{:S(2)}) collective-permute-start(bf16[160,768]{1,0:T(8,128)(2,1)S(1)} %get-tuple-element.118.refs_0_), channel_id=1, source_target_pairs={{0,8},{4,12},{8,0},{12,4},{1,9},{5,13},{9,1},{13,5},{2,10},{6,14},... | collective-permute-start | bytes 737288 | tf_op jit(solution)/shard_map/ppermute | solution.py:873
  50.8 17.3 %collective-permute-start.13 = (bf16[2,2,192,768]{3,2,1,0:T(8,128)(2,1)S(1)}, bf16[2,2,192,768]{3,2,1,0:T(8,128)(2,1)S(1)}, u32[]{:S(2)}, u32[]{:S(2)}) collective-permute-start(bf16[2,2,192,768]{3,2,1,0:T(8,128)(2,1)S(1)} %get-tuple-element.128), channel_id=1, source_target_pairs={{0,2},{1,3},{2,0},{3,1},{4,6},{5,7},{6,4},{7,5},{8,10},{9,11},{10,... | collective-permute-start | bytes 3538952 | tf_op jit(solution)/shard_map/ppermute | solution.py:878
  50.8 17.3 %collective-permute-start.14 = (bf16[2,2,192,768]{3,2,1,0:T(8,128)(2,1)S(1)}, bf16[2,2,192,768]{3,2,1,0:T(8,128)(2,1)S(1)}, u32[]{:S(2)}, u32[]{:S(2)}) collective-permute-start(bf16[2,2,192,768]{3,2,1,0:T(8,128)(2,1)S(1)} %get-tuple-element.129), channel_id=1, source_target_pairs={{0,1},{1,0},{2,3},{3,2},{4,5},{5,4},{6,7},{7,6},{8,9},{9,8},{10,11... | collective-permute-start | bytes 3538952 | tf_op jit(solution)/shard_map/ppermute | solution.py:878
  51.5 12.8 %collective-permute-start.12 = (bf16[640,896]{1,0:T(8,128)(2,1)S(1)}, bf16[640,896]{1,0:T(8,128)(2,1)S(1)}, u32[]{:S(2)}, u32[]{:S(2)}) collective-permute-start(bf16[640,896]{1,0:T(8,128)(2,1)S(1)} %lay_payload.1.pay_ref), channel_id=1, source_target_pairs={{0,16},{16,0},{1,17},{17,1},{2,18},{18,2},{3,19},{19,3},{4,20},{20... | collective-permute-start | bytes 3440648 | tf_op jit(solution)/shard_map/ppermute | solution.py:868
  78.5 14.0 %collective-permute-start.19 = (bf16[176,768]{1,0:T(8,128)(2,1)S(1)}, bf16[176,768]{1,0:T(8,128)(2,1)S(1)}, u32[]{:S(2)}, u32[]{:S(2)}) collective-permute-start(bf16[176,768]{1,0:T(8,128)(2,1)S(1)} %get-tuple-element.140), channel_id=1, source_target_pairs={{0,4},{4,0},{8,12},{12,8},{1,5},{5,1},{9,13},{13,9},{2,6},{6,2},{1... | collective-permute-start | bytes 811016 | tf_op jit(solution)/shard_map/ppermute | solution.py:873
  79.6 21.9 %collective-permute-start.20 = (bf16[176,768]{1,0:T(8,128)(2,1)S(1)}, bf16[176,768]{1,0:T(8,128)(2,1)S(1)}, u32[]{:S(2)}, u32[]{:S(2)}) collective-permute-start(bf16[176,768]{1,0:T(8,128)(2,1)S(1)} %get-tuple-element.141), channel_id=1, source_target_pairs={{0,8},{4,12},{8,0},{12,4},{1,9},{5,13},{9,1},{13,5},{2,10},{6,14},... | collective-permute-start | bytes 811016 | tf_op jit(solution)/shard_map/ppermute | solution.py:873
  81.5 20.0 %collective-permute-start.21 = (bf16[176,768]{1,0:T(8,128)(2,1)S(1)}, bf16[176,768]{1,0:T(8,128)(2,1)S(1)}, u32[]{:S(2)}, u32[]{:S(2)}) collective-permute-start(bf16[176,768]{1,0:T(8,128)(2,1)S(1)} %get-tuple-element.142), channel_id=1, source_target_pairs={{0,12},{4,8},{8,4},{12,0},{1,13},{5,9},{9,5},{13,1},{2,14},{6,10},... | collective-permute-start | bytes 811016 | tf_op jit(solution)/shard_map/ppermute | solution.py:873
  86.9 41.1 %collective-permute-start.18 = (bf16[2,2,192,768]{3,2,1,0:T(8,128)(2,1)S(1)}, bf16[2,2,192,768]{3,2,1,0:T(8,128)(2,1)S(1)}, u32[]{:S(2)}, u32[]{:S(2)}) collective-permute-start(bf16[2,2,192,768]{3,2,1,0:T(8,128)(2,1)S(1)} %get-tuple-element.148), channel_id=1, source_target_pairs={{0,1},{1,0},{2,3},{3,2},{4,5},{5,4},{6,7},{7,6},{8,9},{9,8},{10,11... | collective-permute-start | bytes 3538952 | tf_op jit(solution)/shard_map/ppermute | solution.py:878
  87.5 40.5 %collective-permute-start.17 = (bf16[2,2,192,768]{3,2,1,0:T(8,128)(2,1)S(1)}, bf16[2,2,192,768]{3,2,1,0:T(8,128)(2,1)S(1)}, u32[]{:S(2)}, u32[]{:S(2)}) collective-permute-start(bf16[2,2,192,768]{3,2,1,0:T(8,128)(2,1)S(1)} %get-tuple-element.147), channel_id=1, source_target_pairs={{0,2},{1,3},{2,0},{3,1},{4,6},{5,7},{6,4},{7,5},{8,10},{9,11},{10,... | collective-permute-start | bytes 3538952 | tf_op jit(solution)/shard_map/ppermute | solution.py:878
  102.3 21.2 %collective-permute-start.22 = (bf16[160,768]{1,0:T(8,128)(2,1)S(1)}, bf16[160,768]{1,0:T(8,128)(2,1)S(1)}, u32[]{:S(2)}, u32[]{:S(2)}) collective-permute-start(bf16[160,768]{1,0:T(8,128)(2,1)S(1)} %get-tuple-element.160), channel_id=1, source_target_pairs={{0,4},{4,0},{8,12},{12,8},{1,5},{5,1},{9,13},{13,9},{2,6},{6,2},{1... | collective-permute-start | bytes 737288 | tf_op jit(solution)/shard_map/ppermute | solution.py:873
  107.6 20.3 %collective-permute-start.23 = (bf16[160,768]{1,0:T(8,128)(2,1)S(1)}, bf16[160,768]{1,0:T(8,128)(2,1)S(1)}, u32[]{:S(2)}, u32[]{:S(2)}) collective-permute-start(bf16[160,768]{1,0:T(8,128)(2,1)S(1)} %get-tuple-element.162), channel_id=1, source_target_pairs={{0,8},{4,12},{8,0},{12,4},{1,9},{5,13},{9,1},{13,5},{2,10},{6,14},... | collective-permute-start | bytes 737288 | tf_op jit(solution)/shard_map/ppermute | solution.py:873
  108.7 19.3 %collective-permute-start.24 = (bf16[160,768]{1,0:T(8,128)(2,1)S(1)}, bf16[160,768]{1,0:T(8,128)(2,1)S(1)}, u32[]{:S(2)}, u32[]{:S(2)}) collective-permute-start(bf16[160,768]{1,0:T(8,128)(2,1)S(1)} %get-tuple-element.164), channel_id=1, source_target_pairs={{0,12},{4,8},{8,4},{12,0},{1,13},{5,9},{9,5},{13,1},{2,14},{6,10},... | collective-permute-start | bytes 737288 | tf_op jit(solution)/shard_map/ppermute | solution.py:873
  134.5 13.7 %collective-permute-start.26 = (bf16[176,768]{1,0:T(8,128)(2,1)S(1)}, bf16[176,768]{1,0:T(8,128)(2,1)S(1)}, u32[]{:S(2)}, u32[]{:S(2)}) collective-permute-start(bf16[176,768]{1,0:T(8,128)(2,1)S(1)} %get-tuple-element.172), channel_id=1, source_target_pairs={{0,2},{1,3},{2,0},{3,1},{4,6},{5,7},{6,4},{7,5},{8,10},{9,11},{10,... | collective-permute-start | bytes 811016 | tf_op jit(solution)/shard_map/ppermute | solution.py:878
  136.3 13.5 %collective-permute-start.27 = (bf16[176,768]{1,0:T(8,128)(2,1)S(1)}, bf16[176,768]{1,0:T(8,128)(2,1)S(1)}, u32[]{:S(2)}, u32[]{:S(2)}) collective-permute-start(bf16[176,768]{1,0:T(8,128)(2,1)S(1)} %get-tuple-element.173), channel_id=1, source_target_pairs={{0,3},{1,2},{2,1},{3,0},{4,7},{5,6},{6,5},{7,4},{8,11},{9,10},{10,... | collective-permute-start | bytes 811016 | tf_op jit(solution)/shard_map/ppermute | solution.py:878
  137.6 14.9 %collective-permute-start.29 = (bf16[96,768]{1,0:T(8,128)(2,1)S(1)}, bf16[96,768]{1,0:T(8,128)(2,1)S(1)}, u32[]{:S(2)}, u32[]{:S(2)}) collective-permute-start(bf16[96,768]{1,0:T(8,128)(2,1)S(1)} %get-tuple-element.178), channel_id=1, source_target_pairs={{0,4},{4,0},{8,12},{12,8},{1,5},{5,1},{9,13},{13,9},{2,6},{6,2},{1... | collective-permute-start | bytes 442376 | tf_op jit(solution)/shard_map/ppermute | solution.py:873
  141.2 12.9 %collective-permute-start.30 = (bf16[96,768]{1,0:T(8,128)(2,1)S(1)}, bf16[96,768]{1,0:T(8,128)(2,1)S(1)}, u32[]{:S(2)}, u32[]{:S(2)}) collective-permute-start(bf16[96,768]{1,0:T(8,128)(2,1)S(1)} %get-tuple-element.179), channel_id=1, source_target_pairs={{0,8},{4,12},{8,0},{12,4},{1,9},{5,13},{9,1},{13,5},{2,10},{6,14},... | collective-permute-start | bytes 442376 | tf_op jit(solution)/shard_map/ppermute | solution.py:873
  143.2 10.9 %collective-permute-start.31 = (bf16[96,768]{1,0:T(8,128)(2,1)S(1)}, bf16[96,768]{1,0:T(8,128)(2,1)S(1)}, u32[]{:S(2)}, u32[]{:S(2)}) collective-permute-start(bf16[96,768]{1,0:T(8,128)(2,1)S(1)} %get-tuple-element.180), channel_id=1, source_target_pairs={{0,12},{4,8},{8,4},{12,0},{1,13},{5,9},{9,5},{13,1},{2,14},{6,10},... | collective-permute-start | bytes 442376 | tf_op jit(solution)/shard_map/ppermute | solution.py:873
  150.1 24.0 %collective-permute-start.35 = (bf16[2,192,768]{2,1,0:T(8,128)(2,1)S(1)}, bf16[2,192,768]{2,1,0:T(8,128)(2,1)S(1)}, u32[]{:S(2)}, u32[]{:S(2)}) collective-permute-start(bf16[2,192,768]{2,1,0:T(8,128)(2,1)S(1)} %get-tuple-element.184), channel_id=1, source_target_pairs={{0,1},{1,0},{2,3},{3,2},{4,5},{5,4},{6,7},{7,6},{8,9},{9,8},{10,11... | collective-permute-start | bytes 1769480 | tf_op jit(solution)/shard_map/ppermute | solution.py:878
  150.7 23.3 %collective-permute-start.36 = (bf16[2,192,768]{2,1,0:T(8,128)(2,1)S(1)}, bf16[2,192,768]{2,1,0:T(8,128)(2,1)S(1)}, u32[]{:S(2)}, u32[]{:S(2)}) collective-permute-start(bf16[2,192,768]{2,1,0:T(8,128)(2,1)S(1)} %get-tuple-element.185), channel_id=1, source_target_pairs={{0,2},{1,3},{2,0},{3,1},{4,6},{5,7},{6,4},{7,5},{8,10},{9,11},{10,... | collective-permute-start | bytes 1769480 | tf_op jit(solution)/shard_map/ppermute | solution.py:878
  154.7 19.3 %collective-permute-start.34 = (bf16[112,768]{1,0:T(8,128)(2,1)S(1)}, bf16[112,768]{1,0:T(8,128)(2,1)S(1)}, u32[]{:S(2)}, u32[]{:S(2)}) collective-permute-start(bf16[112,768]{1,0:T(8,128)(2,1)S(1)} %get-tuple-element.181.refs_0_), channel_id=1, source_target_pairs={{0,12},{4,8},{8,4},{12,0},{1,13},{5,9},{9,5},{13,1},{2,14},{6,10},... | collective-permute-start | bytes 516104 | tf_op jit(solution)/shard_map/ppermute | solution.py:873
  157.6 16.4 %collective-permute-start.33 = (bf16[112,768]{1,0:T(8,128)(2,1)S(1)}, bf16[112,768]{1,0:T(8,128)(2,1)S(1)}, u32[]{:S(2)}, u32[]{:S(2)}) collective-permute-start(bf16[112,768]{1,0:T(8,128)(2,1)S(1)} %get-tuple-element.181.refs_0_), channel_id=1, source_target_pairs={{0,8},{4,12},{8,0},{12,4},{1,9},{5,13},{9,1},{13,5},{2,10},{6,14},... | collective-permute-start | bytes 516104 | tf_op jit(solution)/shard_map/ppermute | solution.py:873
  160.8 13.3 %collective-permute-start.32 = (bf16[112,768]{1,0:T(8,128)(2,1)S(1)}, bf16[112,768]{1,0:T(8,128)(2,1)S(1)}, u32[]{:S(2)}, u32[]{:S(2)}) collective-permute-start(bf16[112,768]{1,0:T(8,128)(2,1)S(1)} %get-tuple-element.181.refs_0_), channel_id=1, source_target_pairs={{0,4},{4,0},{8,12},{12,8},{1,5},{5,1},{9,13},{13,9},{2,6},{6,2},{1... | collective-permute-start | bytes 516104 | tf_op jit(solution)/shard_map/ppermute | solution.py:873
  179.1 12.3 %collective-permute-start.43 = (bf16[160,768]{1,0:T(8,128)(2,1)S(1)}, bf16[160,768]{1,0:T(8,128)(2,1)S(1)}, u32[]{:S(2)}, u32[]{:S(2)}) collective-permute-start(bf16[160,768]{1,0:T(8,128)(2,1)S(1)} %add_convert_fusion.refs_0_), channel_id=1, source_target_pairs={{0,2},{1,3},{2,0},{3,1},{4,6},{5,7},{6,4},{7,5},{8,10},{9,11},{10,... | collective-permute-start | bytes 737288 | tf_op jit(solution)/shard_map/ppermute | solution.py:878
  179.8 11.6 %collective-permute-start.42 = (bf16[160,768]{1,0:T(8,128)(2,1)S(1)}, bf16[160,768]{1,0:T(8,128)(2,1)S(1)}, u32[]{:S(2)}, u32[]{:S(2)}) collective-permute-start(bf16[160,768]{1,0:T(8,128)(2,1)S(1)} %add_convert_fusion.refs_0_), channel_id=1, source_target_pairs={{0,1},{1,0},{2,3},{3,2},{4,5},{5,4},{6,7},{7,6},{8,9},{9,8},{10,11... | collective-permute-start | bytes 737288 | tf_op jit(solution)/shard_map/ppermute | solution.py:878
  (23 other events, 211.7 us)

commit v2 on v1

--- a/solution.py
+++ b/solution.py
@@ -285,11 +285,14 @@
     ]
     for copy in copies:
         copy.start()
-    for copy in copies:
-        copy.wait()
     for index, buffer in zip(loads, buffers):
         refs[index] = buffer
-    kernel(pos_ref, *refs)
+
+    def arrive(*indices):
+        for index in indices:
+            copies[loads.index(index)].wait()
+
+    kernel(arrive, pos_ref, *refs)
 
 
 def kernel_call(kernel, name, position, args, outs, scratch=(), flops=0, limit=24, loads=()):
@@ -355,25 +358,21 @@
 
 
 def chunk_kernel(
-    tensors, pos_ref, tok_ref, cot_ref, ids_ref, rank_ref, router_ref, one_ref, two_ref, in_ref, out_ref,
+    tensors, arrive, pos_ref, tok_ref, cot_ref, ids_ref, rank_ref, router_ref, one_ref, two_ref, in_ref, out_ref,
     x_ref, pay_ref, param_ref, mine_ref, first_ref, second_ref, flat_ref, kept_ref,
 ):
-    half = mine_ref.shape[1]
-    core = pl.multiple_of(lax.axis_index("dp") * half, LANES)
-    for s, part in ((0, in_ref[0, :, pl.ds(core, half)].T), (1, out_ref[0, pl.ds(core, half), :])):
-        mine_ref[s] = part
-        first_ref[s] = part[0 : half // 2]
-        second_ref[s] = part[half // 2 :]
     images, seq_len, width = tok_ref.shape
     chunk, experts = x_ref.shape[0], router_ref.shape[0]
     start = pl.multiple_of(lax.axis_index("tensor") * chunk, 16)
-    for source, target in ((tok_ref, x_ref), (cot_ref, pay_ref)):
+    for index, source, target in ((0, tok_ref, x_ref), (1, cot_ref, pay_ref)):
+        arrive(index)
         flat_ref[images * seq_len :, :] = jnp.zeros(
             (flat_ref.shape[0] - images * seq_len, width), jnp.float32
         )
         for i in range(images):
             flat_ref[pl.ds(i * seq_len, seq_len), :] = source[i].astype(jnp.float32)
-        target[:, :width] = flat_ref[pl.ds(start, chunk), :].astype(jnp.bfloat16)
+        target[0:chunk, :] = flat_ref[pl.ds(start, chunk), :].astype(jnp.bfloat16)
+    arrive(2, 3, 4, 5, 6)
     kept_ref[...] = jnp.zeros_like(kept_ref)
     counts = jnp.zeros((1, LANES), jnp.float32)
     for i in range(images):
@@ -395,12 +394,23 @@
                 kept_ref[pl.ds(i * seq_len, 2 * LANES), :] = table
             else:
                 counts = counts + jnp.sum(table, axis=0, keepdims=True)
-    pay_ref[:, width:] = kept_ref[pl.ds(start, chunk), :].astype(jnp.bfloat16)
+    kept = jnp.concatenate(
+        [kept_ref[pl.ds(start, chunk), :], jnp.zeros((2 * LANES - chunk, LANES), jnp.float32)], axis=0
+    ).T
+    pay_ref[chunk:, : 2 * LANES] = kept[0 : 2 * SMALL].astype(jnp.bfloat16)
+    pay_ref[chunk:, 2 * LANES :] = jnp.zeros((2 * SMALL, width - 2 * LANES), jnp.bfloat16)
     param_ref[...] = jnp.zeros_like(param_ref)
     param_ref[0:experts, :] = router_ref[...].astype(jnp.float32)
     param_ref[experts : experts + 1, :] = one_ref[...].reshape(1, width)
     param_ref[experts + 1 : experts + 2, :] = two_ref[...].reshape(1, width)
     param_ref[SMALL - 1 : SMALL, :LANES] = counts * (1.0 / tensors)
+    arrive(7, 8)
+    half = mine_ref.shape[1]
+    core = pl.multiple_of(lax.axis_index("dp") * half, LANES)
+    for s, part in ((0, in_ref[0, :, pl.ds(core, half)].T), (1, out_ref[0, pl.ds(core, half), :])):
+        mine_ref[s] = part
+        first_ref[s] = part[0 : half // 2]
+        second_ref[s] = part[half // 2 :]
 
 
 def stack_kernel(pos_ref, *refs):
@@ -426,6 +436,18 @@
     chunk = blocks[0].shape[0]
     for k, block in enumerate(blocks):
         out_ref[k * chunk : (k + 1) * chunk, :] = block[...]
+
+
+def lay_payload_kernel(pos_ref, *refs):
+    *blocks, out_ref = refs
+    chunk = out_ref.shape[0] // len(blocks)
+    width = blocks[0].shape[1]
+    for k, block in enumerate(blocks):
+        here = slice(k * chunk, (k + 1) * chunk)
+        out_ref[here, :width] = block[0:chunk, :]
+        kept = block[chunk:, : 2 * LANES].astype(jnp.float32)
+        kept = jnp.concatenate([kept] * (LANES // kept.shape[0]), axis=0).T[0:chunk]
+        out_ref[here, width:] = kept.astype(jnp.bfloat16)
 
 
 def lay_rows(position, name, blocks):
@@ -445,7 +467,8 @@
 
 
 def attention_kernel(
-    heads, experts, pos_ref, tok_ref, param_ref, w_ref, wo_ref, qkv_ref, lse_ref, att_ref, *refs,
+    heads, experts, arrive, pos_ref, tok_ref, param_ref, w_ref, wo_ref, qkv_ref, lse_ref, att_ref,
+    *refs,
 ):
     *parts, flat_ref, image_ref, held_ref = refs
     images, rows, width = qkv_ref.shape[1], qkv_ref.shape[2], heads * HD
@@ -456,6 +479,7 @@
     flat_ref[images * seq_len :, :] = jnp.zeros(
         (flat_ref.shape[0] - images * seq_len, width), jnp.float32
     )
+    arrive(0, 1, 2)
 
     @pl.loop(0, images)
     def _(i):
@@ -481,6 +505,7 @@
 
     for i in range(images):
         flat_ref[pl.ds(i * seq_len, seq_len), :] = held_ref[i, 0:seq_len, :]
+    arrive(3)
     att_ref[...] = flat_ref[...].astype(jnp.bfloat16)
     for j, part in enumerate(parts):
         rows_j = flat_ref[chunk_of(pos_ref, j, part.shape[0]), :].astype(jnp.bfloat16)
@@ -600,21 +625,35 @@
 
 
 def join_kernel(pos_ref, back_ref, other_ref, gated_ref, gated_other_ref, *outs):
-    owners = len(outs) // 2
-    chunk, width = outs[owners].shape
-    for k in range(owners):
+    *backs, own_ref, pair_ref, far_ref = outs
+    chunk, width = own_ref.shape
+    for k, out in enumerate(backs):
         here = pl.ds(k * chunk, chunk)
         total = back_ref[here, :] + other_ref[here, :]
-        outs[k][0:chunk, :] = total[:, :width].astype(jnp.bfloat16)
+        out[0:chunk, :] = total[:, :width].astype(jnp.bfloat16)
         inner = jnp.concatenate(
             [total[:, width:], jnp.zeros((2 * LANES - chunk, LANES), jnp.float32)], axis=0
         ).T
         high, low = split_high_low(inner[0:SMALL, :])
-        outs[k][chunk:, : 2 * LANES] = jnp.concatenate([high, low], axis=0)
-        outs[k][chunk:, 2 * LANES :] = jnp.zeros((2 * SMALL, width - 2 * LANES), jnp.bfloat16)
-        outs[owners + k][...] = (
-            gated_ref[here, :].astype(jnp.float32) + gated_other_ref[here, :].astype(jnp.float32)
-        ).astype(jnp.bfloat16)
+        both = jnp.where(
+            live_rows(high.shape, SMALL // 2), high.astype(jnp.float32), low.astype(jnp.float32)
+        )
+        out[chunk:, : 2 * LANES] = both.astype(jnp.bfloat16)
+        out[chunk:, 2 * LANES :] = jnp.zeros((SMALL, width - 2 * LANES), jnp.bfloat16)
+        gated = gated_ref[here, :].astype(jnp.float32) + gated_other_ref[here, :].astype(jnp.float32)
+        gated = gated.astype(jnp.bfloat16)
+        if k % 2:
+            pair_ref[k // 2] = gated
+        else:
+            (own_ref, far_ref)[k // 2][...] = gated
+
+
+def pair_sum_kernel(pos_ref, base_ref, own_ref, far_ref, got_ref, sum_ref, send_ref):
+    total = base_ref[...] + own_ref[...].astype(jnp.float32) + got_ref[0].astype(jnp.float32)
+    sum_ref[...] = total
+    send_ref[...] = (far_ref[...].astype(jnp.float32) + got_ref[1].astype(jnp.float32)).astype(
+        jnp.bfloat16
+    )
 
 
 def expert_grad_kernel(pos_ref, *refs):
@@ -631,7 +670,7 @@
             out[1, s] = grad[part_rows:]
 
 
-def expert_grads(position, a, b, rows_a, rows_b):
+def expert_grads(position, a, b, rows_a, rows_b, flops=0):
     width, total = rows_a[0].shape[1], a[0].shape[1]
     return kernel_call(
         expert_grad_kernel,
@@ -639,6 +678,7 @@
         position,
         [a[1], rows_a[0], b[1], rows_b[0], a[0], rows_a[1], b[0], rows_b[1]],
         [like((2, 2, total // 4, width), jnp.bfloat16)] * 2,
+        flops=flops,
         limit=10,
     )
 
@@ -656,9 +696,9 @@
     routed_grad = jnp.zeros((chunk, width), jnp.float32)
     for k, back in enumerate(backs):
         owner = lax.bitwise_xor(lax.axis_index("expert"), k)
-        inner = back[chunk : chunk + SMALL, : 2 * LANES].astype(jnp.float32)
-        inner = inner + back[chunk + SMALL :, : 2 * LANES].astype(jnp.float32)
+        inner = back[chunk:, : 2 * LANES].astype(jnp.float32)
         inner = jnp.concatenate([inner] * (LANES // SMALL), axis=0).T[0:chunk]
+        inner = jnp.sum(inner, axis=-1, keepdims=True) * (2.0 / LANES)
         route_grad = jnp.where(lane == owner, inner, route_grad)
         routed_grad = routed_grad + back[0:chunk, :].astype(jnp.float32)
     mean = jnp.sum(route_grad * prob, axis=-1, keepdims=True)
@@ -670,7 +710,7 @@
     from_norm, gain_grad = normalize_back(
         routed_grad, normed, inverse, gain_row(param_ref, experts, 1)
     )
-    total = pay_ref[:, :width].astype(jnp.float32) + from_norm
+    total = pay_ref[0:chunk, :].astype(jnp.float32) + from_norm
     grad_ref[...] = total
     up_ref[...] = total.astype(jnp.bfloat16)
     live = live_rows(prob.shape, token_rows, lax.axis_index("tensor") * chunk)
@@ -809,14 +849,15 @@
 
 
 def spread_kernel(owners, experts, token_total, pos_ref, *refs):
-    blocks = refs[: 2 * owners]
-    qkv_ref, wo_ref, router_ref, one_ref, two_ref, loss_ref, big_ref, parts_ref = refs[2 * owners :]
-    piece = blocks[0].shape[0] - 2 * SMALL
+    sides = refs[:2]
+    qkv_ref, wo_ref, router_ref, one_ref, two_ref, loss_ref, big_ref, parts_ref = refs[2:]
+    span = sides[0].shape[0] // owners
+    piece = span - 2 * SMALL
     core, me = lax.axis_index("dp"), lax.axis_index("expert")
     for c in range(2):
         side = core if c == 0 else 1 - core
         for k in range(owners):
-            block = blocks[c * owners + k]
+            block = sides[c].at[k * span : (k + 1) * span]
             place = side * owners + lax.bitwise_xor(me, k)
             here = pl.ds(pl.multiple_of(place * piece, 8), piece)
             big_ref[here, :] = block[0:piece, :].astype(jnp.float32)
@@ -930,7 +971,7 @@
         ],
         [
             like((chunk, width), b16),
-            like((chunk, width + LANES), b16),
+            like((chunk + 2 * SMALL, width), b16),
             like((SMALL, width), f32),
             like((2, half, width), b16),
             like((2, quarter, width), b16),
@@ -963,8 +1004,9 @@
             pltpu.VMEM((rows, width), f32),
             pltpu.VMEM((images, rows, local), f32),
         ],
+        flops=40_000_000_000,
         limit=20,
-        loads=(0, 2, 3),
+        loads=(0, 1, 2, 3),
     )
     arrived = [parts[0]] + [cross(parts[j], j) for j in range(1, tensors)]
     pair_first, pair_second = stack_pairs(position, (first, first_x), (second, second_y))
@@ -981,7 +1023,14 @@
     pair_first, pair_second = after((pair_first, pair_second), routed)
     pair_y = cross(pair_first, 2)
     pair_x = cross(pair_second, 1)
-    payload_mine = lay_rows(after(position, routed), "lay_payload", payload_mine)
+    payload_mine = kernel_call(
+        lay_payload_kernel,
+        "lay_payload",
+        after(position, routed),
+        payload_mine,
+        [like((owners * chunk, width + LANES), b16)],
+        limit=6,
+    )[0]
     payload_other = swap_core(payload_mine)
     rows_mine = lay_rows(position, "lay_rows", blocks)
     rows_other = swap_core(rows_mine)
@@ -998,41 +1047,49 @@
     second_a = second_expert_pass(
         after(position, second_b[0]), rows_mine, payload_mine, first_a, far_weights
     )
-    joined = kernel_call(
+    *joined, gated_own, gated_pair, gated_far = kernel_call(
         join_kernel,
         "join",
         position,
         [second_a[3], back_other, second_a[2], gated_other],
-        [like((chunk + 2 * SMALL, width), b16)] * owners + [like((chunk, width), b16)] * owners,
+        [like((chunk + SMALL, width), b16)] * owners
+        + [like((chunk, width), b16), like((2, chunk, width), b16), like((chunk, width), b16)],
         limit=8,
     )
     backs = [joined[0]] + [hop(joined[k], k) for k in range(1, owners)]
 
-    grad_pos = after(position, joined[:owners])
+    grad_pos = after(position, joined)
     far_y, far_x = expert_grads(grad_pos, second_a, second_b, (rows_mine, first_a[2]), (rows_other, first_b[2]))
     from_y, from_x = cross(far_y, 2), cross(far_x, 1)
-    own_grad, near_grad = expert_grads(
-        after(grad_pos, far_y, backs[1]), first_a, first_b, (rows_mine, first_a[2]), (rows_other, first_b[2])
-    )
-
     residual_grad, attn_grad, small = kernel_call(
         functools.partial(route_back_kernel, experts, token_rows, owners),
         "route_back",
-        after(position, own_grad),
+        position,
         [*backs, prob, residual, payload, params],
         [like((chunk, width), f32), like((chunk, width), b16), like((SMALL, width), f32)],
         flops=40_000_000_000,
         limit=8,
     )
-    gated_back = [joined[owners]]
-    for k in range(1, owners):
-        gated_back.append(hop(after(joined[owners + k], attn_grad), k))
+    own_grad, near_grad = expert_grads(
+        after(position, attn_grad), first_a, first_b, (rows_mine, first_a[2]), (rows_other, first_b[2]),
+    )
+    gated_near = hop(after(gated_pair, backs[1]), 1)
+    block_sum, gated_far = kernel_call(
+        pair_sum_kernel,
+        "pair_sum",
+        after(position, own_grad),
+        [residual, gated_own, gated_far, gated_near],
+        [like((chunk, width), f32), like((chunk, width), b16)],
+        limit=4,
+    )
+    attn_grad, gated_far = lax.optimization_barrier((attn_grad, gated_far))
+    gated_last = hop(gated_far, 2)
     attn_grad = lax.all_gather(attn_grad, "tensor", axis=0, tiled=True)
     piece = 4 * local // (2 * owners)
     keep, send, *parts = kernel_call(
         functools.partial(attention_back_kernel, heads, experts, owners),
         "attention_back",
-        after(position, from_y, from_x, gated_back[1:]),
+        after(position, from_y, from_x, gated_last),
         [tokens, params, weight_rows, out_weight, qkv, lse, attended, attn_grad, small],
         [
             like((owners, piece, width), f32),
@@ -1061,6 +1118,7 @@
     )
     reduced = [hop(p, k + 1) for k, p in enumerate(pieces)]
     got = [parts[0]] + [cross(parts[j], j) for j in range(1, tensors)]
+
     up_x, up_y = kernel_call(
         second_step_kernel,
         "second_step",
@@ -1083,17 +1141,14 @@
     )
     around = [summed] + [hop(summed, k) for k in range(1, owners)]
     grad_rows = lax.all_gather(grad_chunk, "tensor", axis=0, tiled=True)
-    combined = residual
-    for part in gated_back:
-        combined = combined + part.astype(f32)
-    combined = combined.astype(b16)
+    combined = (block_sum + gated_last.astype(f32)).astype(b16)
     combined = after(combined, grad_rows)
     block_parts = [combined] + [cross(combined, j) for j in range(1, tensors)]
 
     grad_tokens = kernel_call(
         images_kernel,
         "grad_tokens",
-        after(position, around, last_x, last_y),
+        position,
         [grad_rows],
         [like(tokens.shape, f32)],
         [pltpu.VMEM((padded, width), f32)],
@@ -1102,7 +1157,7 @@
     grad_half = kernel_call(
         weight_sum_kernel,
         "weight_sum",
-        after(position, grad_tokens),
+        after(position, grad_rows, around),
         [own_grad, from_y, from_x, last_x, last_y],
         [like((2, half, width), b16)],
         limit=8,
@@ -1115,12 +1170,13 @@
         [like((1, width, 2 * half), f32), like((1, 2 * half, width), f32)],
         limit=10,
     )
+    around_rows = lay_rows(position, "lay_grads", around)
     token_total = token_rows * cores * owners
     grad_qkv, grad_out, grad_router, gain_one, gain_two, loss = kernel_call(
         functools.partial(spread_kernel, owners, experts, token_total),
         "spread",
         position,
-        around + [swap_core(a) for a in around],
+        [around_rows, swap_core(around_rows)],
         [
             like((3 * local, width), f32),
             like((local, width), f32),

time: 194 us -> 187 us (0.964)
  starting transfers between devices: 66.9 us -> 51.5 us
  waiting for transfers between devices: 48.3 us -> 55.7 us
  blocking collectives: 26.2 us -> 28.5 us
    ppermute x18 -> x17, starting transfers between devices: 45.5 us -> 27.4 us  [hop(): return lax.ppermute(value, 'expert', [(i, i ^ bit) for i in range(size)])]
    ppermute x17, waiting for transfers between devices: 9.86 us -> 24.1 us  [cross(): return lax.ppermute(value, 'tensor', [(i, i ^ bit) for i in range(size)])]
    ppermute x18 -> x17, waiting for transfers between devices: 35.2 us -> 30.2 us  [hop(): return lax.ppermute(value, 'expert', [(i, i ^ bit) for i in range(size)])]
    ppermute x17, starting transfers between devices: 19.5 us -> 22.7 us  [cross(): return lax.ppermute(value, 'tensor', [(i, i ^ bit) for i in range(size)])]
    all_gather x1, blocking collectives: 12.8 us -> 15.7 us  [dense_body(): grad_rows = lax.all_gather(grad_chunk, 'tensor', axis=0, tiled=True)]
    pallas_call x23 -> x25, Pallas kernels: 49.3 us -> 48.8 us  [kernel_call(): pl.pallas_call(kernel, in_specs=[pl.BlockSpec(memory_space=pltpu.SMEM)] +...]
  transfers between devices with their start and end apart: 45 -> 41, of which waited for: 16 -> 16; matrix products, arithmetic and copies ran while one was open for 0% -> 0% of each run, Pallas kernels for 16% -> 17%
where the time goes in v2:
time: 187 us; the launch traced here: 186 us
  waiting for transfers between devices  55.7 us (30%)
  starting transfers between devices  51.5 us (28%)
  Pallas kernels  48.8 us (26%)
  blocking collectives  28.5 us (15%)
    pallas_call x25, Pallas kernels, kernel_call(): pl.pallas_call(kernel, in_specs=[pl.BlockSpec(memory_space=pltpu.SMEM)] +...  48.8 us
    ppermute x17, waiting for transfers between devices, hop(): return lax.ppermute(value, 'expert', [(i, i ^ bit) for i in range(size)])  30.2 us
    ppermute x17, starting transfers between devices, hop(): return lax.ppermute(value, 'expert', [(i, i ^ bit) for i in range(size)])  27.4 us
    ppermute x17, waiting for transfers between devices, cross(): return lax.ppermute(value, 'tensor', [(i, i ^ bit) for i in range(size)])  24.1 us
    ppermute x17, starting transfers between devices, cross(): return lax.ppermute(value, 'tensor', [(i, i ^ bit) for i in range(size)])  22.7 us
    all_gather x1, blocking collectives, dense_body(): grad_rows = lax.all_gather(grad_chunk, 'tensor', axis=0, tiled=True)  15.7 us
    all_gather x1, blocking collectives, dense_body(): attn_grad = lax.all_gather(attn_grad, 'tensor', axis=0, tiled=True)  12.7 us
  transfers between devices with their start and end apart: 41, of which 16 were waited for; matrix products, arithmetic and copies ran while one was open for 0% of the time, Pallas kernels for 17%

profile of v2, /device:TPU:0, one launch (start us, length us, event | category | flops | bytes accessed | tf_op | source)
XLA Modules:
  0.0 186.3 jit_solution(3088585216003323850)
XLA Ops:
  0.7 4.1 %chunk.1 = (bf16[160,768]{1,0:T(8,128)(2,1)}, bf16[176,768]{1,0:T(8,128)(2,1)}, f32[8,768]{1,0:T(8,128)}, bf16[2,384,768]{2,1,0:T(8,128)(2,1)}, bf16[2,192,768]{...) custom-call(s32[1]{0:T(128)} %constant.0.clone.1.refs_0_.pos_ref, bf16[3,197,768]{2,1,0:T(8,128)(2,1)} %tok_ref.1, ...), custom_call_target="tpu_custom_call" | custom-call | tf_op jit(solution)/shard_map/chunk/pallas_call | solution.py:307
  4.8 3.1 %collective-permute-start.4 = (bf16[176,768]{1,0:T(8,128)(2,1)}, bf16[176,768]{1,0:T(8,128)(2,1)S(1)}, u32[]{:S(2)}, u32[]{:S(2)}) collective-permute-start(bf16[176,768]{1,0:T(8,128)(2,1)} %get-tuple-element.108.refs_0_.refs_6_), channel_id=1, source_target_pairs={{0,4},{4,0},{8,12},{12,8},{1,5},{5,1},{9,13},{13,9},{2,6},{6,2},{1... | collective-permute-start | bytes 811016 | tf_op jit(solution)/shard_map/ppermute | solution.py:914
  7.9 2.6 %collective-permute-start.3 = (bf16[176,768]{1,0:T(8,128)(2,1)}, bf16[176,768]{1,0:T(8,128)(2,1)S(1)}, u32[]{:S(2)}, u32[]{:S(2)}) collective-permute-start(bf16[176,768]{1,0:T(8,128)(2,1)} %get-tuple-element.108.refs_0_.refs_6_), channel_id=1, source_target_pairs={{0,8},{4,12},{8,0},{12,4},{1,9},{5,13},{9,1},{13,5},{2,10},{6,14},... | collective-permute-start | bytes 811016 | tf_op jit(solution)/shard_map/ppermute | solution.py:914
  14.5 4.9 %attention.1 = (bf16[3,3,208,192]{3,2,1,0:T(8,128)(2,1)S(1)}, f32[3,208,128]{2,1,0:T(8,128)S(1)}, bf16[640,192]{1,0:T(8,128)(2,1)S(1)}, bf16[160,768]{1,0:T(8,12...) custom-call(s32[1]{0:T(128)} %constant.0.clone.1.refs_0_.pos_ref, ...), custom_call_target="tpu_custom_call" | custom-call | flops 40000000000 | tf_op jit(solution)/shard_map/attention/pallas_call | solution.py:307
  21.3 5.7 %collective-permute-done.refs_1_.xa_ref = bf16[2,192,768]{2,1,0:T(8,128)(2,1)S(1)} collective-permute-done((bf16[2,192,768]{2,1,0:T(8,128)(2,1)}, bf16[2,192,768]{2,1,0:T(8,128)(2,1)S(1)}, u32[]{:S(2)}, u32[]{:S(2)}) %collective-permute-start) | collective-permute-done | bytes 589856 | tf_op jit(solution)/shard_map/ppermute | solution.py:919
  30.3 1.9 %collective-permute-done.5.refs_1_ = bf16[160,768]{1,0:T(8,128)(2,1)S(1)} collective-permute-done((bf16[160,768]{1,0:T(8,128)(2,1)S(1)}, bf16[160,768]{1,0:T(8,128)(2,1)S(1)}, u32[]{:S(2)}, u32[]{:S(2)}) %collective-permute-start.5) | collective-permute-done | bytes 245792 | tf_op jit(solution)/shard_map/ppermute | solution.py:919
  32.2 5.7 %collective-permute-done.6.refs_2_ = bf16[160,768]{1,0:T(8,128)(2,1)S(1)} collective-permute-done((bf16[160,768]{1,0:T(8,128)(2,1)S(1)}, bf16[160,768]{1,0:T(8,128)(2,1)S(1)}, u32[]{:S(2)}, u32[]{:S(2)}) %collective-permute-start.6) | collective-permute-done | bytes 245792 | tf_op jit(solution)/shard_map/ppermute | solution.py:919
  38.5 3.7 %collective-permute-start.10 = (bf16[160,768]{1,0:T(8,128)(2,1)S(1)}, bf16[160,768]{1,0:T(8,128)(2,1)S(1)}, u32[]{:S(2)}, u32[]{:S(2)}) collective-permute-start(bf16[160,768]{1,0:T(8,128)(2,1)S(1)} %get-tuple-element.118.refs_0_), channel_id=1, source_target_pairs={{0,12},{4,8},{8,4},{12,0},{1,13},{5,9},{9,5},{13,1},{2,14},{6,10},... | collective-permute-start | bytes 737288 | tf_op jit(solution)/shard_map/ppermute | solution.py:914
  45.8 3.5 %collective-permute-done.10.refs_3_ = bf16[160,768]{1,0:T(8,128)(2,1)S(1)} collective-permute-done((bf16[160,768]{1,0:T(8,128)(2,1)S(1)}, bf16[160,768]{1,0:T(8,128)(2,1)S(1)}, u32[]{:S(2)}, u32[]{:S(2)}) %collective-permute-start.10) | collective-permute-done | bytes 245792 | tf_op jit(solution)/shard_map/ppermute | solution.py:914
  49.3 9.9 %collective-permute-done.9.refs_2_ = bf16[160,768]{1,0:T(8,128)(2,1)S(1)} collective-permute-done((bf16[160,768]{1,0:T(8,128)(2,1)S(1)}, bf16[160,768]{1,0:T(8,128)(2,1)S(1)}, u32[]{:S(2)}, u32[]{:S(2)}) %collective-permute-start.9) | collective-permute-done | bytes 245792 | tf_op jit(solution)/shard_map/ppermute | solution.py:914
  59.4 3.8 %experts_first.2 = (bf16[640,768]{1,0:T(8,128)(2,1)S(1)}, bf16[640,768]{1,0:T(8,128)(2,1)S(1)}, bf16[640,768]{1,0:T(8,128)(2,1)S(1)}, f32[640,256]{1,0:T(8,128)S...) custom-call(s32[1]{0:T(128)} %constant.0.clone.1.refs_0_.pos_ref, bf16[640,768]{1,0:T(8,128)(2,1)S(1)} %lay_rows.1.x_ref.refs_1_, ...), custom_call_target="tpu_custom_call" | custom-call | tf_op jit(solution)/shard_map/experts_first/pallas_call | solution.py:307
  63.2 3.8 %experts_first.3 = (bf16[640,768]{1,0:T(8,128)(2,1)S(1)}, bf16[640,768]{1,0:T(8,128)(2,1)S(1)}, bf16[640,768]{1,0:T(8,128)(2,1)S(1)}, f32[640,256]{1,0:T(8,128)S...) custom-call(s32[1]{0:T(128)} %constant.0.clone.1.refs_0_.pos_ref, ...), custom_call_target="tpu_custom_call" | custom-call | tf_op jit(solution)/shard_map/experts_first/pallas_call | solution.py:307
  67.5 3.7 %experts_second.2 = (bf16[640,768]{1,0:T(8,128)(2,1)S(1)}, bf16[640,768]{1,0:T(8,128)(2,1)S(1)}, bf16[640,768]{1,0:T(8,128)(2,1)S(1)}, f32[640,896]{1,0:T(8,128)S(1)}) custom-call(s32[1]{0:T(128)} %constant.0.clone.1.refs_0_.pos_ref, bf16[640,768]{1,0:T(8,128)(2,1)S(1)} %collective-permute-done.11.x_ref.refs_3_, ...), custom_call_target="tpu_custom_call" | custom-call | tf_op jit(solution)/shard_map/experts_second/pallas_call | solution.py:307
  71.8 3.9 %experts_second.3 = (bf16[640,768]{1,0:T(8,128)(2,1)S(1)}, bf16[640,768]{1,0:T(8,128)(2,1)S(1)}, bf16[640,768]{1,0:T(8,128)(2,1)S(1)}, f32[640,896]{1,0:T(8,128)S(1)}) custom-call(s32[1]{0:T(128)} %constant.0.clone.1.refs_0_.pos_ref, bf16[640,768]{1,0:T(8,128)(2,1)S(1)} %lay_rows.1.x_ref.refs_1_, bf16[640,896]{1,0:T(8,128)(2,1)S(1)} %lay_payload.1.pay_ref, ...), custom_call_target="tpu_custom_call" | custom-call | tf_op jit(solution)/shard_map/experts_second/pallas_call | solution.py:307
  79.0 2.6 %collective-permute-start.20 = (bf16[168,768]{1,0:T(8,128)(2,1)S(1)}, bf16[168,768]{1,0:T(8,128)(2,1)S(1)}, u32[]{:S(2)}, u32[]{:S(2)}) collective-permute-start(bf16[168,768]{1,0:T(8,128)(2,1)S(1)} %get-tuple-element.141), channel_id=1, source_target_pairs={{0,8},{4,12},{8,0},{12,4},{1,9},{5,13},{9,1},{13,5},{2,10},{6,14},... | collective-permute-start | bytes 774152 | tf_op jit(solution)/shard_map/ppermute | solution.py:914
  82.2 3.9 %expert_grads.2 = (bf16[2,2,192,768]{3,2,1,0:T(8,128)(2,1)S(1)}, bf16[2,2,192,768]{3,2,1,0:T(8,128)(2,1)S(1)}) custom-call(s32[1]{0:T(128)} %constant.0.clone.1.refs_0_.pos_ref, bf16[640,768]{1,0:T(8,128)(2,1)S(1)} %get-tuple-element.144.refs_0_, bf16[640,768]{1,0:T(8,128)(2,1)S(1)} %lay_rows.1.x_ref.refs_1_, ...), custom_call_target="tpu_custom_call" | custom-call | tf_op jit(solution)/shard_map/expert_grads/pallas_call | solution.py:307
  89.0 2.0 %collective-permute-done.19.refs_1_ = bf16[168,768]{1,0:T(8,128)(2,1)S(1)} collective-permute-done((bf16[168,768]{1,0:T(8,128)(2,1)S(1)}, bf16[168,768]{1,0:T(8,128)(2,1)S(1)}, u32[]{:S(2)}, u32[]{:S(2)}) %collective-permute-start.19) | collective-permute-done | bytes 258080 | tf_op jit(solution)/shard_map/ppermute | solution.py:914
  91.0 9.1 %collective-permute-done.20.refs_2_ = bf16[168,768]{1,0:T(8,128)(2,1)S(1)} collective-permute-done((bf16[168,768]{1,0:T(8,128)(2,1)S(1)}, bf16[168,768]{1,0:T(8,128)(2,1)S(1)}, u32[]{:S(2)}, u32[]{:S(2)}) %collective-permute-start.20) | collective-permute-done | bytes 258080 | tf_op jit(solution)/shard_map/ppermute | solution.py:914
  100.9 3.9 %expert_grads.3 = (bf16[2,2,192,768]{3,2,1,0:T(8,128)(2,1)S(1)}, bf16[2,2,192,768]{3,2,1,0:T(8,128)(2,1)S(1)}) custom-call(s32[1]{0:T(128)} %constant.0.clone.1.refs_0_.pos_ref, bf16[640,768]{1,0:T(8,128)(2,1)S(1)} %get-tuple-element.153.refs_0_, bf16[640,768]{1,0:T(8,128)(2,1)S(1)} %lay_rows.1.x_ref.refs_1_, ...), custom_call_target="tpu_custom_call" | custom-call | tf_op jit(solution)/shard_map/expert_grads/pallas_call | solution.py:307
  104.8 4.6 %collective-permute-done.22.got_ref = bf16[2,160,768]{2,1,0:T(8,128)(2,1)S(1)} collective-permute-done((bf16[2,160,768]{2,1,0:T(8,128)(2,1)S(1)}, bf16[2,160,768]{2,1,0:T(8,128)(2,1)S(1)}, u32[]{:S(2)}, u32[]{:S(2)}) %collective-permute-start.22) | collective-permute-done | bytes 491552 | tf_op jit(solution)/shard_map/ppermute | solution.py:914
  111.0 12.7 %all_gather.6.up_ref = bf16[640,768]{1,0:T(8,128)(2,1)S(1)} all-gather(bf16[160,768]{1,0:T(8,128)(2,1)S(1)} %get-tuple-element.169), channel_id=1, replica_groups=mesh['dp'=2,'expert'=4,'tensor'=4] {'tensor'}, dimensions={0}, use_global_device_ids=true | all-gather | bytes 1228800 | tf_op jit(solution)/shard_map/all_gather | solution.py:1087
  123.7 5.8 %attention_back.1 = (f32[4,96,768]{2,1,0:T(8,128)S(1)}, bf16[4,96,768]{2,1,0:T(8,128)(2,1)S(1)}, bf16[176,768]{1,0:T(8,128)(2,1)S(1)}, bf16[176,768]{1,0:T(8,128...) custom-call(s32[1]{0:T(128)} %constant.0.clone.1.refs_0_.pos_ref, ...), custom_call_target="tpu_custom_call" | custom-call | flops 6000000000 | tf_op jit(solution)/shard_map/attention_back/pallas_call | solution.py:307
  129.7 1.8 collective-permute-start.24
  133.4 2.1 %collective-permute-start.28 = (bf16[96,768]{1,0:T(8,128)(2,1)S(1)}, bf16[96,768]{1,0:T(8,128)(2,1)S(1)}, u32[]{:S(2)}, u32[]{:S(2)}) collective-permute-start(bf16[96,768]{1,0:T(8,128)(2,1)S(1)} %get-tuple-element.179), channel_id=1, source_target_pairs={{0,4},{4,0},{8,12},{12,8},{1,5},{5,1},{9,13},{13,9},{2,6},{6,2},{1... | collective-permute-start | bytes 442376 | tf_op jit(solution)/shard_map/ppermute | solution.py:914
  137.1 1.9 %collective-permute-done.24.refs_1_ = bf16[176,768]{1,0:T(8,128)(2,1)S(1)} collective-permute-done((bf16[176,768]{1,0:T(8,128)(2,1)S(1)}, bf16[176,768]{1,0:T(8,128)(2,1)S(1)}, u32[]{:S(2)}, u32[]{:S(2)}) %collective-permute-start.24) | collective-permute-done | bytes 270368 | tf_op jit(solution)/shard_map/ppermute | solution.py:919
  139.0 3.1 %collective-permute-start.30 = (bf16[96,768]{1,0:T(8,128)(2,1)S(1)}, bf16[96,768]{1,0:T(8,128)(2,1)S(1)}, u32[]{:S(2)}, u32[]{:S(2)}) collective-permute-start(bf16[96,768]{1,0:T(8,128)(2,1)S(1)} %get-tuple-element.181), channel_id=1, source_target_pairs={{0,12},{4,8},{8,4},{12,0},{1,13},{5,9},{9,5},{13,1},{2,14},{6,10},... | collective-permute-start | bytes 442376 | tf_op jit(solution)/shard_map/ppermute | solution.py:914
  142.2 3.7 %collective-permute-done.25.refs_2_ = bf16[176,768]{1,0:T(8,128)(2,1)S(1)} collective-permute-done((bf16[176,768]{1,0:T(8,128)(2,1)S(1)}, bf16[176,768]{1,0:T(8,128)(2,1)S(1)}, u32[]{:S(2)}, u32[]{:S(2)}) %collective-permute-start.25) | collective-permute-done | bytes 270368 | tf_op jit(solution)/shard_map/ppermute | solution.py:919
  149.5 1.9 %collective-permute-start.33 = (bf16[112,768]{1,0:T(8,128)(2,1)S(1)}, bf16[112,768]{1,0:T(8,128)(2,1)S(1)}, u32[]{:S(2)}, u32[]{:S(2)}) collective-permute-start(bf16[112,768]{1,0:T(8,128)(2,1)S(1)} %get-tuple-element.183.refs_0_), channel_id=1, source_target_pairs={{0,12},{4,8},{8,4},{12,0},{1,13},{5,9},{9,5},{13,1},{2,14},{6,10},... | collective-permute-start | bytes 516104 | tf_op jit(solution)/shard_map/ppermute | solution.py:914
  151.5 2.2 %collective-permute-start.32 = (bf16[112,768]{1,0:T(8,128)(2,1)S(1)}, bf16[112,768]{1,0:T(8,128)(2,1)S(1)}, u32[]{:S(2)}, u32[]{:S(2)}) collective-permute-start(bf16[112,768]{1,0:T(8,128)(2,1)S(1)} %get-tuple-element.183.refs_0_), channel_id=1, source_target_pairs={{0,8},{4,12},{8,0},{12,4},{1,9},{5,13},{9,1},{13,5},{2,10},{6,14},... | collective-permute-start | bytes 516104 | tf_op jit(solution)/shard_map/ppermute | solution.py:914
  154.0 15.7 %all_gather.7.refs_0_ = bf16[640,768]{1,0:T(8,128)(2,1)S(1)} all-gather(bf16[160,768]{1,0:T(8,128)(2,1)S(1)} %get-tuple-element.182), channel_id=1, replica_groups=mesh['dp'=2,'expert'=4,'tensor'=4] {'tensor'}, dimensions={0}, use_global_device_ids=true | all-gather | bytes 1228800 | tf_op jit(solution)/shard_map/all_gather | solution.py:1143
  177.6 2.6 %weight_out.1 = (f32[1,768,768]{2,1,0:T(8,128)}, f32[1,768,768]{2,1,0:T(8,128)}) custom-call(s32[1]{0:T(128)} %constant.0.clone.1.refs_0_.pos_ref, bf16[2,384,768]{2,1,0:T(8,128)(2,1)S(1)} %weight_sum.1.mine_ref, bf16[2,384,768]{2,1,0:T(8,128)(2,1)S(1)} %collective-permute-done.36.other_ref), custom_call_target="tpu_custom_call" | custom-call | tf_op jit(solution)/shard_map/weight_out/pallas_call | solution.py:307
  180.8 4.3 %collective-permute-done.39.refs_2_ = bf16[160,768]{1,0:T(8,128)(2,1)S(1)} collective-permute-done((bf16[160,768]{1,0:T(8,128)(2,1)S(1)}, bf16[160,768]{1,0:T(8,128)(2,1)S(1)}, u32[]{:S(2)}, u32[]{:S(2)}) %collective-permute-start.39) | collective-permute-done | bytes 245792 | tf_op jit(solution)/shard_map/ppermute | solution.py:919
  (98 shorter events, 40.9 us)
Async XLA Ops:
  4.8 14.8 %collective-permute-start.4 = (bf16[176,768]{1,0:T(8,128)(2,1)}, bf16[176,768]{1,0:T(8,128)(2,1)S(1)}, u32[]{:S(2)}, u32[]{:S(2)}) collective-permute-start(bf16[176,768]{1,0:T(8,128)(2,1)} %get-tuple-element.108.refs_0_.refs_6_), channel_id=1, source_target_pairs={{0,4},{4,0},{8,12},{12,8},{1,5},{5,1},{9,13},{13,9},{2,6},{6,2},{1... | collective-permute-start | bytes 811016 | tf_op jit(solution)/shard_map/ppermute | solution.py:914
  7.9 22.4 %collective-permute-start.3 = (bf16[176,768]{1,0:T(8,128)(2,1)}, bf16[176,768]{1,0:T(8,128)(2,1)S(1)}, u32[]{:S(2)}, u32[]{:S(2)}) collective-permute-start(bf16[176,768]{1,0:T(8,128)(2,1)} %get-tuple-element.108.refs_0_.refs_6_), channel_id=1, source_target_pairs={{0,8},{4,12},{8,0},{12,4},{1,9},{5,13},{9,1},{13,5},{2,10},{6,14},... | collective-permute-start | bytes 811016 | tf_op jit(solution)/shard_map/ppermute | solution.py:914
  10.5 19.8 %collective-permute-start.2 = (bf16[176,768]{1,0:T(8,128)(2,1)}, bf16[176,768]{1,0:T(8,128)(2,1)S(1)}, u32[]{:S(2)}, u32[]{:S(2)}) collective-permute-start(bf16[176,768]{1,0:T(8,128)(2,1)} %get-tuple-element.108.refs_0_.refs_6_), channel_id=1, source_target_pairs={{0,12},{4,8},{8,4},{12,0},{1,13},{5,9},{9,5},{13,1},{2,14},{6,10},... | collective-permute-start | bytes 811016 | tf_op jit(solution)/shard_map/ppermute | solution.py:914
  10.5 16.5 %collective-permute-start = (bf16[2,192,768]{2,1,0:T(8,128)(2,1)}, bf16[2,192,768]{2,1,0:T(8,128)(2,1)S(1)}, u32[]{:S(2)}, u32[]{:S(2)}) collective-permute-start(bf16[2,192,768]{2,1,0:T(8,128)(2,1)} %get-tuple-element.105.refs_0_), channel_id=1, source_target_pairs={{0,1},{1,0},{2,3},{3,2},{4,5},{5,4},{6,7},{7,6},{8,9},{9,8},{10,11... | collective-permute-start | bytes 1769480 | tf_op jit(solution)/shard_map/ppermute | solution.py:919
  12.2 16.5 %collective-permute-start.1 = (bf16[2,192,768]{2,1,0:T(8,128)(2,1)}, bf16[2,192,768]{2,1,0:T(8,128)(2,1)S(1)}, u32[]{:S(2)}, u32[]{:S(2)}) collective-permute-start(bf16[2,192,768]{2,1,0:T(8,128)(2,1)} %get-tuple-element.106.refs_2_), channel_id=1, source_target_pairs={{0,2},{1,3},{2,0},{3,1},{4,6},{5,7},{6,4},{7,5},{8,10},{9,11},{10,... | collective-permute-start | bytes 1769480 | tf_op jit(solution)/shard_map/ppermute | solution.py:919
  19.6 12.6 %collective-permute-start.5 = (bf16[160,768]{1,0:T(8,128)(2,1)S(1)}, bf16[160,768]{1,0:T(8,128)(2,1)S(1)}, u32[]{:S(2)}, u32[]{:S(2)}) collective-permute-start(bf16[160,768]{1,0:T(8,128)(2,1)S(1)} %get-tuple-element.114), channel_id=1, source_target_pairs={{0,1},{1,0},{2,3},{3,2},{4,5},{5,4},{6,7},{7,6},{8,9},{9,8},{10,11... | collective-permute-start | bytes 737288 | tf_op jit(solution)/shard_map/ppermute | solution.py:919
  26.9 10.9 %collective-permute-start.6 = (bf16[160,768]{1,0:T(8,128)(2,1)S(1)}, bf16[160,768]{1,0:T(8,128)(2,1)S(1)}, u32[]{:S(2)}, u32[]{:S(2)}) collective-permute-start(bf16[160,768]{1,0:T(8,128)(2,1)S(1)} %get-tuple-element.115), channel_id=1, source_target_pairs={{0,2},{1,3},{2,0},{3,1},{4,6},{5,7},{6,4},{7,5},{8,10},{9,11},{10,... | collective-permute-start | bytes 737288 | tf_op jit(solution)/shard_map/ppermute | solution.py:919
  38.5 10.8 %collective-permute-start.10 = (bf16[160,768]{1,0:T(8,128)(2,1)S(1)}, bf16[160,768]{1,0:T(8,128)(2,1)S(1)}, u32[]{:S(2)}, u32[]{:S(2)}) collective-permute-start(bf16[160,768]{1,0:T(8,128)(2,1)S(1)} %get-tuple-element.118.refs_0_), channel_id=1, source_target_pairs={{0,12},{4,8},{8,4},{12,0},{1,13},{5,9},{9,5},{13,1},{2,14},{6,10},... | collective-permute-start | bytes 737288 | tf_op jit(solution)/shard_map/ppermute | solution.py:914
  42.3 17.0 %collective-permute-start.9 = (bf16[160,768]{1,0:T(8,128)(2,1)S(1)}, bf16[160,768]{1,0:T(8,128)(2,1)S(1)}, u32[]{:S(2)}, u32[]{:S(2)}) collective-permute-start(bf16[160,768]{1,0:T(8,128)(2,1)S(1)} %get-tuple-element.118.refs_0_), channel_id=1, source_target_pairs={{0,8},{4,12},{8,0},{12,4},{1,9},{5,13},{9,1},{13,5},{2,10},{6,14},... | collective-permute-start | bytes 737288 | tf_op jit(solution)/shard_map/ppermute | solution.py:914
  42.3 17.0 %collective-permute-start.8 = (bf16[160,768]{1,0:T(8,128)(2,1)S(1)}, bf16[160,768]{1,0:T(8,128)(2,1)S(1)}, u32[]{:S(2)}, u32[]{:S(2)}) collective-permute-start(bf16[160,768]{1,0:T(8,128)(2,1)S(1)} %get-tuple-element.118.refs_0_), channel_id=1, source_target_pairs={{0,4},{4,0},{8,12},{12,8},{1,5},{5,1},{9,13},{13,9},{2,6},{6,2},{1... | collective-permute-start | bytes 737288 | tf_op jit(solution)/shard_map/ppermute | solution.py:914
  43.0 24.1 %collective-permute-start.13 = (bf16[2,2,192,768]{3,2,1,0:T(8,128)(2,1)S(1)}, bf16[2,2,192,768]{3,2,1,0:T(8,128)(2,1)S(1)}, u32[]{:S(2)}, u32[]{:S(2)}) collective-permute-start(bf16[2,2,192,768]{3,2,1,0:T(8,128)(2,1)S(1)} %get-tuple-element.128), channel_id=1, source_target_pairs={{0,2},{1,3},{2,0},{3,1},{4,6},{5,7},{6,4},{7,5},{8,10},{9,11},{10,... | collective-permute-start | bytes 3538952 | tf_op jit(solution)/shard_map/ppermute | solution.py:919
  44.2 23.2 %collective-permute-start.14 = (bf16[2,2,192,768]{3,2,1,0:T(8,128)(2,1)S(1)}, bf16[2,2,192,768]{3,2,1,0:T(8,128)(2,1)S(1)}, u32[]{:S(2)}, u32[]{:S(2)}) collective-permute-start(bf16[2,2,192,768]{3,2,1,0:T(8,128)(2,1)S(1)} %get-tuple-element.129), channel_id=1, source_target_pairs={{0,1},{1,0},{2,3},{3,2},{4,5},{5,4},{6,7},{7,6},{8,9},{9,8},{10,11... | collective-permute-start | bytes 3538952 | tf_op jit(solution)/shard_map/ppermute | solution.py:919
  49.3 13.9 %collective-permute-start.12 = (bf16[640,896]{1,0:T(8,128)(2,1)S(1)}, bf16[640,896]{1,0:T(8,128)(2,1)S(1)}, u32[]{:S(2)}, u32[]{:S(2)}) collective-permute-start(bf16[640,896]{1,0:T(8,128)(2,1)S(1)} %lay_payload.1.pay_ref), channel_id=1, source_target_pairs={{0,16},{16,0},{1,17},{17,1},{2,18},{18,2},{3,19},{19,3},{4,20},{20... | collective-permute-start | bytes 3440648 | tf_op jit(solution)/shard_map/ppermute | solution.py:909
  77.8 13.2 %collective-permute-start.19 = (bf16[168,768]{1,0:T(8,128)(2,1)S(1)}, bf16[168,768]{1,0:T(8,128)(2,1)S(1)}, u32[]{:S(2)}, u32[]{:S(2)}) collective-permute-start(bf16[168,768]{1,0:T(8,128)(2,1)S(1)} %get-tuple-element.140), channel_id=1, source_target_pairs={{0,4},{4,0},{8,12},{12,8},{1,5},{5,1},{9,13},{13,9},{2,6},{6,2},{1... | collective-permute-start | bytes 774152 | tf_op jit(solution)/shard_map/ppermute | solution.py:914
  79.0 21.1 %collective-permute-start.20 = (bf16[168,768]{1,0:T(8,128)(2,1)S(1)}, bf16[168,768]{1,0:T(8,128)(2,1)S(1)}, u32[]{:S(2)}, u32[]{:S(2)}) collective-permute-start(bf16[168,768]{1,0:T(8,128)(2,1)S(1)} %get-tuple-element.141), channel_id=1, source_target_pairs={{0,8},{4,12},{8,0},{12,4},{1,9},{5,13},{9,1},{13,5},{2,10},{6,14},... | collective-permute-start | bytes 774152 | tf_op jit(solution)/shard_map/ppermute | solution.py:914
  81.7 18.5 %collective-permute-start.21 = (bf16[168,768]{1,0:T(8,128)(2,1)S(1)}, bf16[168,768]{1,0:T(8,128)(2,1)S(1)}, u32[]{:S(2)}, u32[]{:S(2)}) collective-permute-start(bf16[168,768]{1,0:T(8,128)(2,1)S(1)} %get-tuple-element.142), channel_id=1, source_target_pairs={{0,12},{4,8},{8,4},{12,0},{1,13},{5,9},{9,5},{13,1},{2,14},{6,10},... | collective-permute-start | bytes 774152 | tf_op jit(solution)/shard_map/ppermute | solution.py:914
  86.1 37.6 %collective-permute-start.17 = (bf16[2,2,192,768]{3,2,1,0:T(8,128)(2,1)S(1)}, bf16[2,2,192,768]{3,2,1,0:T(8,128)(2,1)S(1)}, u32[]{:S(2)}, u32[]{:S(2)}) collective-permute-start(bf16[2,2,192,768]{3,2,1,0:T(8,128)(2,1)S(1)} %get-tuple-element.147), channel_id=1, source_target_pairs={{0,2},{1,3},{2,0},{3,1},{4,6},{5,7},{6,4},{7,5},{8,10},{9,11},{10,... | collective-permute-start | bytes 3538952 | tf_op jit(solution)/shard_map/ppermute | solution.py:919
  87.5 36.2 %collective-permute-start.18 = (bf16[2,2,192,768]{3,2,1,0:T(8,128)(2,1)S(1)}, bf16[2,2,192,768]{3,2,1,0:T(8,128)(2,1)S(1)}, u32[]{:S(2)}, u32[]{:S(2)}) collective-permute-start(bf16[2,2,192,768]{3,2,1,0:T(8,128)(2,1)S(1)} %get-tuple-element.148), channel_id=1, source_target_pairs={{0,1},{1,0},{2,3},{3,2},{4,5},{5,4},{6,7},{7,6},{8,9},{9,8},{10,11... | collective-permute-start | bytes 3538952 | tf_op jit(solution)/shard_map/ppermute | solution.py:919
  91.0 18.4 %collective-permute-start.22 = (bf16[2,160,768]{2,1,0:T(8,128)(2,1)S(1)}, bf16[2,160,768]{2,1,0:T(8,128)(2,1)S(1)}, u32[]{:S(2)}, u32[]{:S(2)}) collective-permute-start(bf16[2,160,768]{2,1,0:T(8,128)(2,1)S(1)} %get-tuple-element.162), channel_id=1, source_target_pairs={{0,4},{4,0},{8,12},{12,8},{1,5},{5,1},{9,13},{13,9},{2,6},{6,2},{1... | collective-permute-start | bytes 1474568 | tf_op jit(solution)/shard_map/ppermute | solution.py:914
  109.5 14.2 %collective-permute-start.23 = (bf16[160,768]{1,0:T(8,128)(2,1)S(1)}, bf16[160,768]{1,0:T(8,128)(2,1)S(1)}, u32[]{:S(2)}, u32[]{:S(2)}) collective-permute-start(bf16[160,768]{1,0:T(8,128)(2,1)S(1)} %get-tuple-element.164), channel_id=1, source_target_pairs={{0,8},{4,12},{8,0},{12,4},{1,9},{5,13},{9,1},{13,5},{2,10},{6,14},... | collective-permute-start | bytes 737288 | tf_op jit(solution)/shard_map/ppermute | solution.py:914
  131.5 14.3 %collective-permute-start.25 = (bf16[176,768]{1,0:T(8,128)(2,1)S(1)}, bf16[176,768]{1,0:T(8,128)(2,1)S(1)}, u32[]{:S(2)}, u32[]{:S(2)}) collective-permute-start(bf16[176,768]{1,0:T(8,128)(2,1)S(1)} %get-tuple-element.173), channel_id=1, source_target_pairs={{0,2},{1,3},{2,0},{3,1},{4,6},{5,7},{6,4},{7,5},{8,10},{9,11},{10,... | collective-permute-start | bytes 811016 | tf_op jit(solution)/shard_map/ppermute | solution.py:919
  131.8 14.0 %collective-permute-start.26 = (bf16[176,768]{1,0:T(8,128)(2,1)S(1)}, bf16[176,768]{1,0:T(8,128)(2,1)S(1)}, u32[]{:S(2)}, u32[]{:S(2)}) collective-permute-start(bf16[176,768]{1,0:T(8,128)(2,1)S(1)} %get-tuple-element.174), channel_id=1, source_target_pairs={{0,3},{1,2},{2,1},{3,0},{4,7},{5,6},{6,5},{7,4},{8,11},{9,10},{10,... | collective-permute-start | bytes 811016 | tf_op jit(solution)/shard_map/ppermute | solution.py:919
  133.4 14.8 %collective-permute-start.28 = (bf16[96,768]{1,0:T(8,128)(2,1)S(1)}, bf16[96,768]{1,0:T(8,128)(2,1)S(1)}, u32[]{:S(2)}, u32[]{:S(2)}) collective-permute-start(bf16[96,768]{1,0:T(8,128)(2,1)S(1)} %get-tuple-element.179), channel_id=1, source_target_pairs={{0,4},{4,0},{8,12},{12,8},{1,5},{5,1},{9,13},{13,9},{2,6},{6,2},{1... | collective-permute-start | bytes 442376 | tf_op jit(solution)/shard_map/ppermute | solution.py:914
  135.5 13.4 %collective-permute-start.29 = (bf16[96,768]{1,0:T(8,128)(2,1)S(1)}, bf16[96,768]{1,0:T(8,128)(2,1)S(1)}, u32[]{:S(2)}, u32[]{:S(2)}) collective-permute-start(bf16[96,768]{1,0:T(8,128)(2,1)S(1)} %get-tuple-element.180), channel_id=1, source_target_pairs={{0,8},{4,12},{8,0},{12,4},{1,9},{5,13},{9,1},{13,5},{2,10},{6,14},... | collective-permute-start | bytes 442376 | tf_op jit(solution)/shard_map/ppermute | solution.py:914
  139.0 9.9 %collective-permute-start.30 = (bf16[96,768]{1,0:T(8,128)(2,1)S(1)}, bf16[96,768]{1,0:T(8,128)(2,1)S(1)}, u32[]{:S(2)}, u32[]{:S(2)}) collective-permute-start(bf16[96,768]{1,0:T(8,128)(2,1)S(1)} %get-tuple-element.181), channel_id=1, source_target_pairs={{0,12},{4,8},{8,4},{12,0},{1,13},{5,9},{9,5},{13,1},{2,14},{6,10},... | collective-permute-start | bytes 442376 | tf_op jit(solution)/shard_map/ppermute | solution.py:914
  146.1 23.6 %collective-permute-start.34 = (bf16[2,192,768]{2,1,0:T(8,128)(2,1)S(1)}, bf16[2,192,768]{2,1,0:T(8,128)(2,1)S(1)}, u32[]{:S(2)}, u32[]{:S(2)}) collective-permute-start(bf16[2,192,768]{2,1,0:T(8,128)(2,1)S(1)} %get-tuple-element.187), channel_id=1, source_target_pairs={{0,1},{1,0},{2,3},{3,2},{4,5},{5,4},{6,7},{7,6},{8,9},{9,8},{10,11... | collective-permute-start | bytes 1769480 | tf_op jit(solution)/shard_map/ppermute | solution.py:919
  146.5 23.3 %collective-permute-start.35 = (bf16[2,192,768]{2,1,0:T(8,128)(2,1)S(1)}, bf16[2,192,768]{2,1,0:T(8,128)(2,1)S(1)}, u32[]{:S(2)}, u32[]{:S(2)}) collective-permute-start(bf16[2,192,768]{2,1,0:T(8,128)(2,1)S(1)} %get-tuple-element.188), channel_id=1, source_target_pairs={{0,2},{1,3},{2,0},{3,1},{4,6},{5,7},{6,4},{7,5},{8,10},{9,11},{10,... | collective-permute-start | bytes 1769480 | tf_op jit(solution)/shard_map/ppermute | solution.py:919
  149.5 20.2 %collective-permute-start.33 = (bf16[112,768]{1,0:T(8,128)(2,1)S(1)}, bf16[112,768]{1,0:T(8,128)(2,1)S(1)}, u32[]{:S(2)}, u32[]{:S(2)}) collective-permute-start(bf16[112,768]{1,0:T(8,128)(2,1)S(1)} %get-tuple-element.183.refs_0_), channel_id=1, source_target_pairs={{0,12},{4,8},{8,4},{12,0},{1,13},{5,9},{9,5},{13,1},{2,14},{6,10},... | collective-permute-start | bytes 516104 | tf_op jit(solution)/shard_map/ppermute | solution.py:914
  151.5 18.3 %collective-permute-start.32 = (bf16[112,768]{1,0:T(8,128)(2,1)S(1)}, bf16[112,768]{1,0:T(8,128)(2,1)S(1)}, u32[]{:S(2)}, u32[]{:S(2)}) collective-permute-start(bf16[112,768]{1,0:T(8,128)(2,1)S(1)} %get-tuple-element.183.refs_0_), channel_id=1, source_target_pairs={{0,8},{4,12},{8,0},{12,4},{1,9},{5,13},{9,1},{13,5},{2,10},{6,14},... | collective-permute-start | bytes 516104 | tf_op jit(solution)/shard_map/ppermute | solution.py:914
  153.6 16.1 %collective-permute-start.31 = (bf16[112,768]{1,0:T(8,128)(2,1)S(1)}, bf16[112,768]{1,0:T(8,128)(2,1)S(1)}, u32[]{:S(2)}, u32[]{:S(2)}) collective-permute-start(bf16[112,768]{1,0:T(8,128)(2,1)S(1)} %get-tuple-element.183.refs_0_), channel_id=1, source_target_pairs={{0,4},{4,0},{8,12},{12,8},{1,5},{5,1},{9,13},{13,9},{2,6},{6,2},{1... | collective-permute-start | bytes 516104 | tf_op jit(solution)/shard_map/ppermute | solution.py:914
  172.5 12.6 %collective-permute-start.39 = (bf16[160,768]{1,0:T(8,128)(2,1)S(1)}, bf16[160,768]{1,0:T(8,128)(2,1)S(1)}, u32[]{:S(2)}, u32[]{:S(2)}) collective-permute-start(bf16[160,768]{1,0:T(8,128)(2,1)S(1)} %add_convert_fusion.refs_0_), channel_id=1, source_target_pairs={{0,2},{1,3},{2,0},{3,1},{4,6},{5,7},{6,4},{7,5},{8,10},{9,11},{10,... | collective-permute-start | bytes 737288 | tf_op jit(solution)/shard_map/ppermute | solution.py:919
  173.2 11.8 %collective-permute-start.38 = (bf16[160,768]{1,0:T(8,128)(2,1)S(1)}, bf16[160,768]{1,0:T(8,128)(2,1)S(1)}, u32[]{:S(2)}, u32[]{:S(2)}) collective-permute-start(bf16[160,768]{1,0:T(8,128)(2,1)S(1)} %add_convert_fusion.refs_0_), channel_id=1, source_target_pairs={{0,1},{1,0},{2,3},{3,2},{4,5},{5,4},{6,7},{7,6},{8,9},{9,8},{10,11... | collective-permute-start | bytes 737288 | tf_op jit(solution)/shard_map/ppermute | solution.py:919
  (19 other events, 173.9 us)

commit v3 on v2

--- a/solution.py
+++ b/solution.py
@@ -438,11 +438,11 @@
         out_ref[k * chunk : (k + 1) * chunk, :] = block[...]
 
 
-def lay_payload_kernel(pos_ref, *refs):
-    *blocks, out_ref = refs
-    chunk = out_ref.shape[0] // len(blocks)
-    width = blocks[0].shape[1]
-    for k, block in enumerate(blocks):
+def lay_payload_kernel(pos_ref, near_ref, far_ref, out_ref):
+    chunk = out_ref.shape[0] // 4
+    width = near_ref.shape[2]
+    for k in range(4):
+        block = (near_ref, far_ref)[k % 2].at[k // 2]
         here = slice(k * chunk, (k + 1) * chunk)
         out_ref[here, :width] = block[0:chunk, :]
         kept = block[chunk:, : 2 * LANES].astype(jnp.float32)
@@ -579,11 +579,16 @@
         for s in range(2)
     )
     part, back = expert_halves(x_ref[...], rg_ref[...], w_in, w_out, hidden_ref, pre_ref)
-    back_ref[:, :width] = back_in_ref[...] + back
+    back_ref[:, :width] = (back_in_ref[...] + back).astype(back_ref.dtype)
     part = part_in_ref[...] + part
     gated_ref[...] = (gate_ref[:, 0:1] * part).astype(jnp.bfloat16)
     inner = jnp.sum(part * pay_ref[:, :width].astype(jnp.float32), axis=-1, keepdims=True)
-    back_ref[:, width:] = gate_ref[:, LANES:] * inner
+    inner = gate_ref[:, LANES:] * inner
+    if back_ref.dtype == jnp.bfloat16:
+        high, low = split_high_low(inner)
+        upper = lax.broadcasted_iota(jnp.int32, inner.shape, 1) < LANES // 2
+        inner = jnp.where(upper, high.astype(jnp.float32), low.astype(jnp.float32))
+    back_ref[:, width:] = inner.astype(back_ref.dtype)
 
 
 def first_expert_pass(position, rows, payload, params, weights, experts):
@@ -606,7 +611,7 @@
     )
 
 
-def second_expert_pass(position, rows, payload, first, weights):
+def second_expert_pass(position, rows, payload, first, weights, back_dtype):
     count, width = rows.shape
     hidden = 4 * weights[0].shape[2]
     return kernel_call(
@@ -618,7 +623,7 @@
             like((count, hidden), jnp.bfloat16),
             like((count, hidden), jnp.bfloat16),
             like((count, width), jnp.bfloat16),
-            like((count, width + LANES), jnp.float32),
+            like((count, width + LANES), back_dtype),
         ],
         limit=18,
     )
@@ -629,10 +634,12 @@
     chunk, width = own_ref.shape
     for k, out in enumerate(backs):
         here = pl.ds(k * chunk, chunk)
-        total = back_ref[here, :] + other_ref[here, :]
-        out[0:chunk, :] = total[:, :width].astype(jnp.bfloat16)
+        other = other_ref[here, :].astype(jnp.float32)
+        out[0:chunk, :] = (back_ref[here, :width] + other[:, :width]).astype(jnp.bfloat16)
+        inner = jnp.sum(other[:, width:], axis=-1, keepdims=True) * (2.0 / LANES)
+        inner = back_ref[here, width:] + inner
         inner = jnp.concatenate(
-            [total[:, width:], jnp.zeros((2 * LANES - chunk, LANES), jnp.float32)], axis=0
+            [inner, jnp.zeros((2 * LANES - chunk, LANES), jnp.float32)], axis=0
         ).T
         high, low = split_high_low(inner[0:SMALL, :])
         both = jnp.where(
@@ -984,7 +991,7 @@
         limit=56,
         loads=tuple(range(9)),
     )
-    payload_mine = [payload] + [hop(payload, k) for k in range(1, owners)]
+    payload_two = hop(payload, 2)
     first_x = cross(first, 1)
     second_y = cross(second, 2)
 
@@ -1009,12 +1016,16 @@
         loads=(0, 1, 2, 3),
     )
     arrived = [parts[0]] + [cross(parts[j], j) for j in range(1, tensors)]
-    pair_first, pair_second = stack_pairs(position, (first, first_x), (second, second_y))
+    pair_first, pair_second = stack_pairs(
+        after(position, parts[0]), (first, first_x), (second, second_y)
+    )
+    (payload_near,) = stack_pairs(after(position, pair_first), (payload, payload_two))
+    payload_far = hop(payload_near, 1)
 
     residual, routed, prob = kernel_call(
         functools.partial(route_kernel, experts),
         "route",
-        after(position, pair_first, payload_mine[::-1]),
+        after(position, pair_first, payload_near),
         [*arrived, x_chunk, params],
         [like((chunk, width), f32), like((chunk, width), b16), like((chunk, LANES), f32)],
         limit=8,
@@ -1027,7 +1038,7 @@
         lay_payload_kernel,
         "lay_payload",
         after(position, routed),
-        payload_mine,
+        [payload_near, payload_far],
         [like((owners * chunk, width + LANES), b16)],
         limit=6,
     )[0]
@@ -1041,11 +1052,11 @@
         after(position, first_a[2]), rows_other, payload_other, params, near_weights, experts
     )
     second_b = second_expert_pass(
-        after(position, first_b[2]), rows_other, payload_other, first_b, far_weights
+        after(position, first_b[2]), rows_other, payload_other, first_b, far_weights, b16
     )
     back_other, gated_other = swap_core(second_b[3]), swap_core(second_b[2])
     second_a = second_expert_pass(
-        after(position, second_b[0]), rows_mine, payload_mine, first_a, far_weights
+        after(position, second_b[0]), rows_mine, payload_mine, first_a, far_weights, f32
     )
     *joined, gated_own, gated_pair, gated_far = kernel_call(
         join_kernel,

time: 187 us -> 185 us (0.989)
  starting transfers between devices: 51.5 us -> 47.6 us
    ppermute x17, waiting for transfers between devices: 24.1 us -> 27 us  [cross(): return lax.ppermute(value, 'tensor', [(i, i ^ bit) for i in range(size)])]
    ppermute x17, starting transfers between devices: 22.7 us -> 20.2 us  [cross(): return lax.ppermute(value, 'tensor', [(i, i ^ bit) for i in range(size)])]
    ppermute x17 -> x16, starting transfers between devices: 27.4 us -> 26 us  [hop(): return lax.ppermute(value, 'expert', [(i, i ^ bit) for i in range(size)])]
    pallas_call x25 -> x26, Pallas kernels: 48.8 us -> 49.2 us  [kernel_call(): pl.pallas_call(kernel, in_specs=[pl.BlockSpec(memory_space=pltpu.SMEM)] +...]
    ppermute x17 -> x16, waiting for transfers between devices: 30.2 us -> 30.2 us  [hop(): return lax.ppermute(value, 'expert', [(i, i ^ bit) for i in range(size)])]
  transfers between devices with their start and end apart: 41 -> 40, of which waited for: 16 -> 17; matrix products, arithmetic and copies ran while one was open for 0% -> 0% of each run, Pallas kernels for 17% -> 18%
where the time goes in v3:
time: 185 us
  waiting for transfers between devices  57.3 us (31%)
  Pallas kernels  49.2 us (27%)
  starting transfers between devices  47.6 us (26%)
  blocking collectives  29.2 us (16%)
    pallas_call x26, Pallas kernels, kernel_call(): pl.pallas_call(kernel, in_specs=[pl.BlockSpec(memory_space=pltpu.SMEM)] +...  49.2 us
    ppermute x16, waiting for transfers between devices, hop(): return lax.ppermute(value, 'expert', [(i, i ^ bit) for i in range(size)])  30.2 us
    ppermute x17, waiting for transfers between devices, cross(): return lax.ppermute(value, 'tensor', [(i, i ^ bit) for i in range(size)])  27 us
    ppermute x16, starting transfers between devices, hop(): return lax.ppermute(value, 'expert', [(i, i ^ bit) for i in range(size)])  26 us
    ppermute x17, starting transfers between devices, cross(): return lax.ppermute(value, 'tensor', [(i, i ^ bit) for i in range(size)])  20.2 us
    all_gather x1, blocking collectives, dense_body(): grad_rows = lax.all_gather(grad_chunk, 'tensor', axis=0, tiled=True)  15.5 us
    all_gather x1, blocking collectives, dense_body(): attn_grad = lax.all_gather(attn_grad, 'tensor', axis=0, tiled=True)  13.6 us
  transfers between devices with their start and end apart: 40, of which 17 were waited for; matrix products, arithmetic and copies ran while one was open for 0% of the time, Pallas kernels for 18%

profile of v3, /device:TPU:0, one launch (start us, length us, event | category | flops | bytes accessed | tf_op | source)
XLA Modules:
  0.0 185.0 jit_solution(9146316565488774881)
XLA Ops:
  0.7 4.1 %chunk.1 = (bf16[160,768]{1,0:T(8,128)(2,1)}, bf16[176,768]{1,0:T(8,128)(2,1)}, f32[8,768]{1,0:T(8,128)}, bf16[2,384,768]{2,1,0:T(8,128)(2,1)}, bf16[2,192,768]{...) custom-call(s32[1]{0:T(128)} %constant.0.clone.1.refs_0_.pos_ref, bf16[3,197,768]{2,1,0:T(8,128)(2,1)} %tok_ref.1, ...), custom_call_target="tpu_custom_call" | custom-call | tf_op jit(solution)/shard_map/chunk/pallas_call | solution.py:307
  4.8 4.1 %collective-permute-start.2 = (bf16[176,768]{1,0:T(8,128)(2,1)}, bf16[176,768]{1,0:T(8,128)(2,1)S(1)}, u32[]{:S(2)}, u32[]{:S(2)}) collective-permute-start(bf16[176,768]{1,0:T(8,128)(2,1)} %get-tuple-element.116.refs_0_.refs_6_), channel_id=1, source_target_pairs={{0,8},{4,12},{8,0},{12,4},{1,9},{5,13},{9,1},{13,5},{2,10},{6,14},... | collective-permute-start | bytes 811016 | tf_op jit(solution)/shard_map/ppermute | solution.py:921
  12.7 4.9 %attention.1 = (bf16[3,3,208,192]{3,2,1,0:T(8,128)(2,1)S(1)}, f32[3,208,128]{2,1,0:T(8,128)S(1)}, bf16[640,192]{1,0:T(8,128)(2,1)S(1)}, bf16[160,768]{1,0:T(8,12...) custom-call(s32[1]{0:T(128)} %constant.0.clone.1.refs_0_.pos_ref, ...), custom_call_target="tpu_custom_call" | custom-call | flops 40000000000 | tf_op jit(solution)/shard_map/attention/pallas_call | solution.py:307
  17.6 6.3 %collective-permute-done.refs_1_.xa_ref = bf16[2,192,768]{2,1,0:T(8,128)(2,1)S(1)} collective-permute-done((bf16[2,192,768]{2,1,0:T(8,128)(2,1)}, bf16[2,192,768]{2,1,0:T(8,128)(2,1)S(1)}, u32[]{:S(2)}, u32[]{:S(2)}) %collective-permute-start) | collective-permute-done | bytes 589856 | tf_op jit(solution)/shard_map/ppermute | solution.py:926
  25.3 1.6 collective-permute-start.9
  30.5 5.1 %collective-permute-done.3.refs_1_ = bf16[160,768]{1,0:T(8,128)(2,1)S(1)} collective-permute-done((bf16[160,768]{1,0:T(8,128)(2,1)S(1)}, bf16[160,768]{1,0:T(8,128)(2,1)S(1)}, u32[]{:S(2)}, u32[]{:S(2)}) %collective-permute-start.3) | collective-permute-done | bytes 245792 | tf_op jit(solution)/shard_map/ppermute | solution.py:926
  35.5 2.0 %collective-permute-done.4.refs_2_ = bf16[160,768]{1,0:T(8,128)(2,1)S(1)} collective-permute-done((bf16[160,768]{1,0:T(8,128)(2,1)S(1)}, bf16[160,768]{1,0:T(8,128)(2,1)S(1)}, u32[]{:S(2)}, u32[]{:S(2)}) %collective-permute-start.4) | collective-permute-done | bytes 245792 | tf_op jit(solution)/shard_map/ppermute | solution.py:926
  40.2 1.6 collective-permute-start.7
  41.8 2.5 %collective-permute-start.6 = (bf16[160,768]{1,0:T(8,128)(2,1)S(1)}, bf16[160,768]{1,0:T(8,128)(2,1)S(1)}, u32[]{:S(2)}, u32[]{:S(2)}) collective-permute-start(bf16[160,768]{1,0:T(8,128)(2,1)S(1)} %get-tuple-element.122.refs_0_), channel_id=1, source_target_pairs={{0,4},{4,0},{8,12},{12,8},{1,5},{5,1},{9,13},{13,9},{2,6},{6,2},{1... | collective-permute-start | bytes 737288 | tf_op jit(solution)/shard_map/ppermute | solution.py:921
  46.8 3.8 %collective-permute-done.8.refs_3_ = bf16[160,768]{1,0:T(8,128)(2,1)S(1)} collective-permute-done((bf16[160,768]{1,0:T(8,128)(2,1)S(1)}, bf16[160,768]{1,0:T(8,128)(2,1)S(1)}, u32[]{:S(2)}, u32[]{:S(2)}) %collective-permute-start.8) | collective-permute-done | bytes 245792 | tf_op jit(solution)/shard_map/ppermute | solution.py:921
  50.5 9.7 %collective-permute-done.7.refs_2_ = bf16[160,768]{1,0:T(8,128)(2,1)S(1)} collective-permute-done((bf16[160,768]{1,0:T(8,128)(2,1)S(1)}, bf16[160,768]{1,0:T(8,128)(2,1)S(1)}, u32[]{:S(2)}, u32[]{:S(2)}) %collective-permute-start.7) | collective-permute-done | bytes 245792 | tf_op jit(solution)/shard_map/ppermute | solution.py:921
  60.4 3.8 %experts_first.2 = (bf16[640,768]{1,0:T(8,128)(2,1)S(1)}, bf16[640,768]{1,0:T(8,128)(2,1)S(1)}, bf16[640,768]{1,0:T(8,128)(2,1)S(1)}, f32[640,256]{1,0:T(8,128)S...) custom-call(s32[1]{0:T(128)} %constant.0.clone.1.refs_0_.pos_ref, bf16[640,768]{1,0:T(8,128)(2,1)S(1)} %lay_rows.1.x_ref.refs_1_, ...), custom_call_target="tpu_custom_call" | custom-call | tf_op jit(solution)/shard_map/experts_first/pallas_call | solution.py:307
  64.3 3.8 %experts_first.3 = (bf16[640,768]{1,0:T(8,128)(2,1)S(1)}, bf16[640,768]{1,0:T(8,128)(2,1)S(1)}, bf16[640,768]{1,0:T(8,128)(2,1)S(1)}, f32[640,256]{1,0:T(8,128)S...) custom-call(s32[1]{0:T(128)} %constant.0.clone.1.refs_0_.pos_ref, ...), custom_call_target="tpu_custom_call" | custom-call | tf_op jit(solution)/shard_map/experts_first/pallas_call | solution.py:307
  68.4 3.8 %experts_second.2 = (bf16[640,768]{1,0:T(8,128)(2,1)S(1)}, bf16[640,768]{1,0:T(8,128)(2,1)S(1)}, bf16[640,768]{1,0:T(8,128)(2,1)S(1)}, bf16[640,896]{1,0:T(8,128)(2,1)S(1)}) custom-call(s32[1]{0:T(128)} %constant.0.clone.1.refs_0_.pos_ref, bf16[640,768]{1,0:T(8,128)(2,1)S(1)} %collective-permute-done.10.x_ref.refs_3_, ...), custom_call_target="tpu_custom_call" | custom-call | tf_op jit(solution)/shard_map/experts_second/pallas_call | solution.py:307
  72.7 3.9 %experts_second.3 = (bf16[640,768]{1,0:T(8,128)(2,1)S(1)}, bf16[640,768]{1,0:T(8,128)(2,1)S(1)}, bf16[640,768]{1,0:T(8,128)(2,1)S(1)}, f32[640,896]{1,0:T(8,128)S(1)}) custom-call(s32[1]{0:T(128)} %constant.0.clone.1.refs_0_.pos_ref, bf16[640,768]{1,0:T(8,128)(2,1)S(1)} %lay_rows.1.x_ref.refs_1_, bf16[640,896]{1,0:T(8,128)(2,1)S(1)} %lay_payload.1.pay_ref, ...), custom_call_target="tpu_custom_call" | custom-call | tf_op jit(solution)/shard_map/experts_second/pallas_call | solution.py:307
  79.4 2.6 %collective-permute-start.20 = (bf16[168,768]{1,0:T(8,128)(2,1)S(1)}, bf16[168,768]{1,0:T(8,128)(2,1)S(1)}, u32[]{:S(2)}, u32[]{:S(2)}) collective-permute-start(bf16[168,768]{1,0:T(8,128)(2,1)S(1)} %get-tuple-element.146), channel_id=1, source_target_pairs={{0,12},{4,8},{8,4},{12,0},{1,13},{5,9},{9,5},{13,1},{2,14},{6,10},... | collective-permute-start | bytes 774152 | tf_op jit(solution)/shard_map/ppermute | solution.py:921
  82.0 3.9 %expert_grads.2 = (bf16[2,2,192,768]{3,2,1,0:T(8,128)(2,1)S(1)}, bf16[2,2,192,768]{3,2,1,0:T(8,128)(2,1)S(1)}) custom-call(s32[1]{0:T(128)} %constant.0.clone.1.refs_0_.pos_ref, bf16[640,768]{1,0:T(8,128)(2,1)S(1)} %get-tuple-element.148.refs_0_, bf16[640,768]{1,0:T(8,128)(2,1)S(1)} %lay_rows.1.x_ref.refs_1_, ...), custom_call_target="tpu_custom_call" | custom-call | tf_op jit(solution)/shard_map/expert_grads/pallas_call | solution.py:307
  88.1 2.2 %collective-permute-done.18.refs_1_ = bf16[168,768]{1,0:T(8,128)(2,1)S(1)} collective-permute-done((bf16[168,768]{1,0:T(8,128)(2,1)S(1)}, bf16[168,768]{1,0:T(8,128)(2,1)S(1)}, u32[]{:S(2)}, u32[]{:S(2)}) %collective-permute-start.18) | collective-permute-done | bytes 258080 | tf_op jit(solution)/shard_map/ppermute | solution.py:921
  90.3 8.8 %collective-permute-done.19.refs_2_ = bf16[168,768]{1,0:T(8,128)(2,1)S(1)} collective-permute-done((bf16[168,768]{1,0:T(8,128)(2,1)S(1)}, bf16[168,768]{1,0:T(8,128)(2,1)S(1)}, u32[]{:S(2)}, u32[]{:S(2)}) %collective-permute-start.19) | collective-permute-done | bytes 258080 | tf_op jit(solution)/shard_map/ppermute | solution.py:921
  99.9 3.9 %expert_grads.3 = (bf16[2,2,192,768]{3,2,1,0:T(8,128)(2,1)S(1)}, bf16[2,2,192,768]{3,2,1,0:T(8,128)(2,1)S(1)}) custom-call(s32[1]{0:T(128)} %constant.0.clone.1.refs_0_.pos_ref, bf16[640,768]{1,0:T(8,128)(2,1)S(1)} %get-tuple-element.157.refs_0_, bf16[640,768]{1,0:T(8,128)(2,1)S(1)} %lay_rows.1.x_ref.refs_1_, ...), custom_call_target="tpu_custom_call" | custom-call | tf_op jit(solution)/shard_map/expert_grads/pallas_call | solution.py:307
  103.7 4.9 %collective-permute-done.21.got_ref = bf16[2,160,768]{2,1,0:T(8,128)(2,1)S(1)} collective-permute-done((bf16[2,160,768]{2,1,0:T(8,128)(2,1)S(1)}, bf16[2,160,768]{2,1,0:T(8,128)(2,1)S(1)}, u32[]{:S(2)}, u32[]{:S(2)}) %collective-permute-start.21) | collective-permute-done | bytes 491552 | tf_op jit(solution)/shard_map/ppermute | solution.py:921
  109.1 13.6 %all_gather.6.up_ref = bf16[640,768]{1,0:T(8,128)(2,1)S(1)} all-gather(bf16[160,768]{1,0:T(8,128)(2,1)S(1)} %get-tuple-element.173), channel_id=1, replica_groups=mesh['dp'=2,'expert'=4,'tensor'=4] {'tensor'}, dimensions={0}, use_global_device_ids=true | all-gather | bytes 1228800 | tf_op jit(solution)/shard_map/all_gather | solution.py:1098
  122.7 5.8 %attention_back.1 = (f32[4,96,768]{2,1,0:T(8,128)S(1)}, bf16[4,96,768]{2,1,0:T(8,128)(2,1)S(1)}, bf16[176,768]{1,0:T(8,128)(2,1)S(1)}, bf16[176,768]{1,0:T(8,128...) custom-call(s32[1]{0:T(128)} %constant.0.clone.1.refs_0_.pos_ref, ...), custom_call_target="tpu_custom_call" | custom-call | flops 6000000000 | tf_op jit(solution)/shard_map/attention_back/pallas_call | solution.py:307
  132.3 2.2 %collective-permute-start.27 = (bf16[96,768]{1,0:T(8,128)(2,1)S(1)}, bf16[96,768]{1,0:T(8,128)(2,1)S(1)}, u32[]{:S(2)}, u32[]{:S(2)}) collective-permute-start(bf16[96,768]{1,0:T(8,128)(2,1)S(1)} %get-tuple-element.183), channel_id=1, source_target_pairs={{0,4},{4,0},{8,12},{12,8},{1,5},{5,1},{9,13},{13,9},{2,6},{6,2},{1... | collective-permute-start | bytes 442376 | tf_op jit(solution)/shard_map/ppermute | solution.py:921
  135.9 2.1 %collective-permute-done.23.refs_1_ = bf16[176,768]{1,0:T(8,128)(2,1)S(1)} collective-permute-done((bf16[176,768]{1,0:T(8,128)(2,1)S(1)}, bf16[176,768]{1,0:T(8,128)(2,1)S(1)}, u32[]{:S(2)}, u32[]{:S(2)}) %collective-permute-start.23) | collective-permute-done | bytes 270368 | tf_op jit(solution)/shard_map/ppermute | solution.py:926
  138.0 3.0 %collective-permute-start.29 = (bf16[96,768]{1,0:T(8,128)(2,1)S(1)}, bf16[96,768]{1,0:T(8,128)(2,1)S(1)}, u32[]{:S(2)}, u32[]{:S(2)}) collective-permute-start(bf16[96,768]{1,0:T(8,128)(2,1)S(1)} %get-tuple-element.185), channel_id=1, source_target_pairs={{0,12},{4,8},{8,4},{12,0},{1,13},{5,9},{9,5},{13,1},{2,14},{6,10},... | collective-permute-start | bytes 442376 | tf_op jit(solution)/shard_map/ppermute | solution.py:921
  141.0 3.6 %collective-permute-done.24.refs_2_ = bf16[176,768]{1,0:T(8,128)(2,1)S(1)} collective-permute-done((bf16[176,768]{1,0:T(8,128)(2,1)S(1)}, bf16[176,768]{1,0:T(8,128)(2,1)S(1)}, u32[]{:S(2)}, u32[]{:S(2)}) %collective-permute-start.24) | collective-permute-done | bytes 270368 | tf_op jit(solution)/shard_map/ppermute | solution.py:926
  149.9 2.8 %collective-permute-start.31 = (bf16[112,768]{1,0:T(8,128)(2,1)S(1)}, bf16[112,768]{1,0:T(8,128)(2,1)S(1)}, u32[]{:S(2)}, u32[]{:S(2)}) collective-permute-start(bf16[112,768]{1,0:T(8,128)(2,1)S(1)} %get-tuple-element.187.refs_0_), channel_id=1, source_target_pairs={{0,8},{4,12},{8,0},{12,4},{1,9},{5,13},{9,1},{13,5},{2,10},{6,14},... | collective-permute-start | bytes 516104 | tf_op jit(solution)/shard_map/ppermute | solution.py:921
  152.9 15.5 %all_gather.7.refs_0_ = bf16[640,768]{1,0:T(8,128)(2,1)S(1)} all-gather(bf16[160,768]{1,0:T(8,128)(2,1)S(1)} %get-tuple-element.186), channel_id=1, replica_groups=mesh['dp'=2,'expert'=4,'tensor'=4] {'tensor'}, dimensions={0}, use_global_device_ids=true | all-gather | bytes 1228800 | tf_op jit(solution)/shard_map/all_gather | solution.py:1154
  174.6 1.7 spread.1
  176.3 2.6 %weight_out.1 = (f32[1,768,768]{2,1,0:T(8,128)}, f32[1,768,768]{2,1,0:T(8,128)}) custom-call(s32[1]{0:T(128)} %constant.0.clone.1.refs_0_.pos_ref, bf16[2,384,768]{2,1,0:T(8,128)(2,1)S(1)} %weight_sum.1.mine_ref, bf16[2,384,768]{2,1,0:T(8,128)(2,1)S(1)} %collective-permute-done.35.other_ref), custom_call_target="tpu_custom_call" | custom-call | tf_op jit(solution)/shard_map/weight_out/pallas_call | solution.py:307
  179.5 4.3 %collective-permute-done.38.refs_2_ = bf16[160,768]{1,0:T(8,128)(2,1)S(1)} collective-permute-done((bf16[160,768]{1,0:T(8,128)(2,1)S(1)}, bf16[160,768]{1,0:T(8,128)(2,1)S(1)}, u32[]{:S(2)}, u32[]{:S(2)}) %collective-permute-start.38) | collective-permute-done | bytes 245792 | tf_op jit(solution)/shard_map/ppermute | solution.py:926
  (97 shorter events, 39.6 us)
Async XLA Ops:
  4.8 20.5 %collective-permute-start.2 = (bf16[176,768]{1,0:T(8,128)(2,1)}, bf16[176,768]{1,0:T(8,128)(2,1)S(1)}, u32[]{:S(2)}, u32[]{:S(2)}) collective-permute-start(bf16[176,768]{1,0:T(8,128)(2,1)} %get-tuple-element.116.refs_0_.refs_6_), channel_id=1, source_target_pairs={{0,8},{4,12},{8,0},{12,4},{1,9},{5,13},{9,1},{13,5},{2,10},{6,14},... | collective-permute-start | bytes 811016 | tf_op jit(solution)/shard_map/ppermute | solution.py:921
  8.9 15.0 %collective-permute-start = (bf16[2,192,768]{2,1,0:T(8,128)(2,1)}, bf16[2,192,768]{2,1,0:T(8,128)(2,1)S(1)}, u32[]{:S(2)}, u32[]{:S(2)}) collective-permute-start(bf16[2,192,768]{2,1,0:T(8,128)(2,1)} %get-tuple-element.112.refs_0_), channel_id=1, source_target_pairs={{0,1},{1,0},{2,3},{3,2},{4,5},{5,4},{6,7},{7,6},{8,9},{9,8},{10,11... | collective-permute-start | bytes 1769480 | tf_op jit(solution)/shard_map/ppermute | solution.py:926
  10.4 14.7 %collective-permute-start.1 = (bf16[2,192,768]{2,1,0:T(8,128)(2,1)}, bf16[2,192,768]{2,1,0:T(8,128)(2,1)S(1)}, u32[]{:S(2)}, u32[]{:S(2)}) collective-permute-start(bf16[2,192,768]{2,1,0:T(8,128)(2,1)} %get-tuple-element.113.refs_2_), channel_id=1, source_target_pairs={{0,2},{1,3},{2,0},{3,1},{4,6},{5,7},{6,4},{7,5},{8,10},{9,11},{10,... | collective-permute-start | bytes 1769480 | tf_op jit(solution)/shard_map/ppermute | solution.py:926
  25.3 19.8 %collective-permute-start.9 = (bf16[2,176,768]{2,1,0:T(8,128)(2,1)S(1)}, bf16[2,176,768]{2,1,0:T(8,128)(2,1)S(1)}, u32[]{:S(2)}, u32[]{:S(2)}) collective-permute-start(bf16[2,176,768]{2,1,0:T(8,128)(2,1)S(1)} %stack.3.near_ref), channel_id=1, source_target_pairs={{0,4},{4,0},{8,12},{12,8},{1,5},{5,1},{9,13},{13,9},{2,6},{6,2},{1... | collective-permute-start | bytes 1622024 | tf_op jit(solution)/shard_map/ppermute | solution.py:921
  27.5 10.0 %collective-permute-start.4 = (bf16[160,768]{1,0:T(8,128)(2,1)S(1)}, bf16[160,768]{1,0:T(8,128)(2,1)S(1)}, u32[]{:S(2)}, u32[]{:S(2)}) collective-permute-start(bf16[160,768]{1,0:T(8,128)(2,1)S(1)} %get-tuple-element.119), channel_id=1, source_target_pairs={{0,2},{1,3},{2,0},{3,1},{4,6},{5,7},{6,4},{7,5},{8,10},{9,11},{10,... | collective-permute-start | bytes 737288 | tf_op jit(solution)/shard_map/ppermute | solution.py:926
  29.0 10.1 %collective-permute-start.5 = (bf16[160,768]{1,0:T(8,128)(2,1)S(1)}, bf16[160,768]{1,0:T(8,128)(2,1)S(1)}, u32[]{:S(2)}, u32[]{:S(2)}) collective-permute-start(bf16[160,768]{1,0:T(8,128)(2,1)S(1)} %get-tuple-element.120), channel_id=1, source_target_pairs={{0,3},{1,2},{2,1},{3,0},{4,7},{5,6},{6,5},{7,4},{8,11},{9,10},{10,... | collective-permute-start | bytes 737288 | tf_op jit(solution)/shard_map/ppermute | solution.py:926
  39.8 10.8 %collective-permute-start.8 = (bf16[160,768]{1,0:T(8,128)(2,1)S(1)}, bf16[160,768]{1,0:T(8,128)(2,1)S(1)}, u32[]{:S(2)}, u32[]{:S(2)}) collective-permute-start(bf16[160,768]{1,0:T(8,128)(2,1)S(1)} %get-tuple-element.122.refs_0_), channel_id=1, source_target_pairs={{0,12},{4,8},{8,4},{12,0},{1,13},{5,9},{9,5},{13,1},{2,14},{6,10},... | collective-permute-start | bytes 737288 | tf_op jit(solution)/shard_map/ppermute | solution.py:921
  40.2 20.1 %collective-permute-start.7 = (bf16[160,768]{1,0:T(8,128)(2,1)S(1)}, bf16[160,768]{1,0:T(8,128)(2,1)S(1)}, u32[]{:S(2)}, u32[]{:S(2)}) collective-permute-start(bf16[160,768]{1,0:T(8,128)(2,1)S(1)} %get-tuple-element.122.refs_0_), channel_id=1, source_target_pairs={{0,8},{4,12},{8,0},{12,4},{1,9},{5,13},{9,1},{13,5},{2,10},{6,14},... | collective-permute-start | bytes 737288 | tf_op jit(solution)/shard_map/ppermute | solution.py:921
  41.8 18.5 %collective-permute-start.6 = (bf16[160,768]{1,0:T(8,128)(2,1)S(1)}, bf16[160,768]{1,0:T(8,128)(2,1)S(1)}, u32[]{:S(2)}, u32[]{:S(2)}) collective-permute-start(bf16[160,768]{1,0:T(8,128)(2,1)S(1)} %get-tuple-element.122.refs_0_), channel_id=1, source_target_pairs={{0,4},{4,0},{8,12},{12,8},{1,5},{5,1},{9,13},{13,9},{2,6},{6,2},{1... | collective-permute-start | bytes 737288 | tf_op jit(solution)/shard_map/ppermute | solution.py:921
  44.2 23.9 %collective-permute-start.12 = (bf16[2,2,192,768]{3,2,1,0:T(8,128)(2,1)S(1)}, bf16[2,2,192,768]{3,2,1,0:T(8,128)(2,1)S(1)}, u32[]{:S(2)}, u32[]{:S(2)}) collective-permute-start(bf16[2,2,192,768]{3,2,1,0:T(8,128)(2,1)S(1)} %get-tuple-element.132), channel_id=1, source_target_pairs={{0,2},{1,3},{2,0},{3,1},{4,6},{5,7},{6,4},{7,5},{8,10},{9,11},{10,... | collective-permute-start | bytes 3538952 | tf_op jit(solution)/shard_map/ppermute | solution.py:926
  45.1 23.3 %collective-permute-start.13 = (bf16[2,2,192,768]{3,2,1,0:T(8,128)(2,1)S(1)}, bf16[2,2,192,768]{3,2,1,0:T(8,128)(2,1)S(1)}, u32[]{:S(2)}, u32[]{:S(2)}) collective-permute-start(bf16[2,2,192,768]{3,2,1,0:T(8,128)(2,1)S(1)} %get-tuple-element.133), channel_id=1, source_target_pairs={{0,1},{1,0},{2,3},{3,2},{4,5},{5,4},{6,7},{7,6},{8,9},{9,8},{10,11... | collective-permute-start | bytes 3538952 | tf_op jit(solution)/shard_map/ppermute | solution.py:926
  50.5 13.7 %collective-permute-start.11 = (bf16[640,896]{1,0:T(8,128)(2,1)S(1)}, bf16[640,896]{1,0:T(8,128)(2,1)S(1)}, u32[]{:S(2)}, u32[]{:S(2)}) collective-permute-start(bf16[640,896]{1,0:T(8,128)(2,1)S(1)} %lay_payload.1.pay_ref), channel_id=1, source_target_pairs={{0,16},{16,0},{1,17},{17,1},{2,18},{18,2},{3,19},{19,3},{4,20},{20... | collective-permute-start | bytes 3440648 | tf_op jit(solution)/shard_map/ppermute | solution.py:916
  77.6 12.7 %collective-permute-start.18 = (bf16[168,768]{1,0:T(8,128)(2,1)S(1)}, bf16[168,768]{1,0:T(8,128)(2,1)S(1)}, u32[]{:S(2)}, u32[]{:S(2)}) collective-permute-start(bf16[168,768]{1,0:T(8,128)(2,1)S(1)} %get-tuple-element.144), channel_id=1, source_target_pairs={{0,4},{4,0},{8,12},{12,8},{1,5},{5,1},{9,13},{13,9},{2,6},{6,2},{1... | collective-permute-start | bytes 774152 | tf_op jit(solution)/shard_map/ppermute | solution.py:921
  77.9 21.1 %collective-permute-start.19 = (bf16[168,768]{1,0:T(8,128)(2,1)S(1)}, bf16[168,768]{1,0:T(8,128)(2,1)S(1)}, u32[]{:S(2)}, u32[]{:S(2)}) collective-permute-start(bf16[168,768]{1,0:T(8,128)(2,1)S(1)} %get-tuple-element.145), channel_id=1, source_target_pairs={{0,8},{4,12},{8,0},{12,4},{1,9},{5,13},{9,1},{13,5},{2,10},{6,14},... | collective-permute-start | bytes 774152 | tf_op jit(solution)/shard_map/ppermute | solution.py:921
  79.4 19.6 %collective-permute-start.20 = (bf16[168,768]{1,0:T(8,128)(2,1)S(1)}, bf16[168,768]{1,0:T(8,128)(2,1)S(1)}, u32[]{:S(2)}, u32[]{:S(2)}) collective-permute-start(bf16[168,768]{1,0:T(8,128)(2,1)S(1)} %get-tuple-element.146), channel_id=1, source_target_pairs={{0,12},{4,8},{8,4},{12,0},{1,13},{5,9},{9,5},{13,1},{2,14},{6,10},... | collective-permute-start | bytes 774152 | tf_op jit(solution)/shard_map/ppermute | solution.py:921
  85.9 36.8 %collective-permute-start.16 = (bf16[2,2,192,768]{3,2,1,0:T(8,128)(2,1)S(1)}, bf16[2,2,192,768]{3,2,1,0:T(8,128)(2,1)S(1)}, u32[]{:S(2)}, u32[]{:S(2)}) collective-permute-start(bf16[2,2,192,768]{3,2,1,0:T(8,128)(2,1)S(1)} %get-tuple-element.151), channel_id=1, source_target_pairs={{0,2},{1,3},{2,0},{3,1},{4,6},{5,7},{6,4},{7,5},{8,10},{9,11},{10,... | collective-permute-start | bytes 3538952 | tf_op jit(solution)/shard_map/ppermute | solution.py:926
  87.5 35.2 %collective-permute-start.17 = (bf16[2,2,192,768]{3,2,1,0:T(8,128)(2,1)S(1)}, bf16[2,2,192,768]{3,2,1,0:T(8,128)(2,1)S(1)}, u32[]{:S(2)}, u32[]{:S(2)}) collective-permute-start(bf16[2,2,192,768]{3,2,1,0:T(8,128)(2,1)S(1)} %get-tuple-element.152), channel_id=1, source_target_pairs={{0,1},{1,0},{2,3},{3,2},{4,5},{5,4},{6,7},{7,6},{8,9},{9,8},{10,11... | collective-permute-start | bytes 3538952 | tf_op jit(solution)/shard_map/ppermute | solution.py:926
  90.3 18.3 %collective-permute-start.21 = (bf16[2,160,768]{2,1,0:T(8,128)(2,1)S(1)}, bf16[2,160,768]{2,1,0:T(8,128)(2,1)S(1)}, u32[]{:S(2)}, u32[]{:S(2)}) collective-permute-start(bf16[2,160,768]{2,1,0:T(8,128)(2,1)S(1)} %get-tuple-element.166), channel_id=1, source_target_pairs={{0,4},{4,0},{8,12},{12,8},{1,5},{5,1},{9,13},{13,9},{2,6},{6,2},{1... | collective-permute-start | bytes 1474568 | tf_op jit(solution)/shard_map/ppermute | solution.py:921
  108.8 13.9 %collective-permute-start.22 = (bf16[160,768]{1,0:T(8,128)(2,1)S(1)}, bf16[160,768]{1,0:T(8,128)(2,1)S(1)}, u32[]{:S(2)}, u32[]{:S(2)}) collective-permute-start(bf16[160,768]{1,0:T(8,128)(2,1)S(1)} %get-tuple-element.168), channel_id=1, source_target_pairs={{0,8},{4,12},{8,0},{12,4},{1,9},{5,13},{9,1},{13,5},{2,10},{6,14},... | collective-permute-start | bytes 737288 | tf_op jit(solution)/shard_map/ppermute | solution.py:921
  130.2 14.3 %collective-permute-start.24 = (bf16[176,768]{1,0:T(8,128)(2,1)S(1)}, bf16[176,768]{1,0:T(8,128)(2,1)S(1)}, u32[]{:S(2)}, u32[]{:S(2)}) collective-permute-start(bf16[176,768]{1,0:T(8,128)(2,1)S(1)} %get-tuple-element.177), channel_id=1, source_target_pairs={{0,2},{1,3},{2,0},{3,1},{4,6},{5,7},{6,4},{7,5},{8,10},{9,11},{10,... | collective-permute-start | bytes 811016 | tf_op jit(solution)/shard_map/ppermute | solution.py:926
  130.7 13.8 %collective-permute-start.25 = (bf16[176,768]{1,0:T(8,128)(2,1)S(1)}, bf16[176,768]{1,0:T(8,128)(2,1)S(1)}, u32[]{:S(2)}, u32[]{:S(2)}) collective-permute-start(bf16[176,768]{1,0:T(8,128)(2,1)S(1)} %get-tuple-element.178), channel_id=1, source_target_pairs={{0,3},{1,2},{2,1},{3,0},{4,7},{5,6},{6,5},{7,4},{8,11},{9,10},{10,... | collective-permute-start | bytes 811016 | tf_op jit(solution)/shard_map/ppermute | solution.py:926
  132.3 14.6 %collective-permute-start.27 = (bf16[96,768]{1,0:T(8,128)(2,1)S(1)}, bf16[96,768]{1,0:T(8,128)(2,1)S(1)}, u32[]{:S(2)}, u32[]{:S(2)}) collective-permute-start(bf16[96,768]{1,0:T(8,128)(2,1)S(1)} %get-tuple-element.183), channel_id=1, source_target_pairs={{0,4},{4,0},{8,12},{12,8},{1,5},{5,1},{9,13},{13,9},{2,6},{6,2},{1... | collective-permute-start | bytes 442376 | tf_op jit(solution)/shard_map/ppermute | solution.py:921
  134.6 13.3 %collective-permute-start.28 = (bf16[96,768]{1,0:T(8,128)(2,1)S(1)}, bf16[96,768]{1,0:T(8,128)(2,1)S(1)}, u32[]{:S(2)}, u32[]{:S(2)}) collective-permute-start(bf16[96,768]{1,0:T(8,128)(2,1)S(1)} %get-tuple-element.184), channel_id=1, source_target_pairs={{0,8},{4,12},{8,0},{12,4},{1,9},{5,13},{9,1},{13,5},{2,10},{6,14},... | collective-permute-start | bytes 442376 | tf_op jit(solution)/shard_map/ppermute | solution.py:921
  138.0 9.9 %collective-permute-start.29 = (bf16[96,768]{1,0:T(8,128)(2,1)S(1)}, bf16[96,768]{1,0:T(8,128)(2,1)S(1)}, u32[]{:S(2)}, u32[]{:S(2)}) collective-permute-start(bf16[96,768]{1,0:T(8,128)(2,1)S(1)} %get-tuple-element.185), channel_id=1, source_target_pairs={{0,12},{4,8},{8,4},{12,0},{1,13},{5,9},{9,5},{13,1},{2,14},{6,10},... | collective-permute-start | bytes 442376 | tf_op jit(solution)/shard_map/ppermute | solution.py:921
  144.8 23.6 %collective-permute-start.33 = (bf16[2,192,768]{2,1,0:T(8,128)(2,1)S(1)}, bf16[2,192,768]{2,1,0:T(8,128)(2,1)S(1)}, u32[]{:S(2)}, u32[]{:S(2)}) collective-permute-start(bf16[2,192,768]{2,1,0:T(8,128)(2,1)S(1)} %get-tuple-element.191), channel_id=1, source_target_pairs={{0,1},{1,0},{2,3},{3,2},{4,5},{5,4},{6,7},{7,6},{8,9},{9,8},{10,11... | collective-permute-start | bytes 1769480 | tf_op jit(solution)/shard_map/ppermute | solution.py:926
  145.4 23.0 %collective-permute-start.34 = (bf16[2,192,768]{2,1,0:T(8,128)(2,1)S(1)}, bf16[2,192,768]{2,1,0:T(8,128)(2,1)S(1)}, u32[]{:S(2)}, u32[]{:S(2)}) collective-permute-start(bf16[2,192,768]{2,1,0:T(8,128)(2,1)S(1)} %get-tuple-element.192), channel_id=1, source_target_pairs={{0,2},{1,3},{2,0},{3,1},{4,6},{5,7},{6,4},{7,5},{8,10},{9,11},{10,... | collective-permute-start | bytes 1769480 | tf_op jit(solution)/shard_map/ppermute | solution.py:926
  148.4 20.0 %collective-permute-start.32 = (bf16[112,768]{1,0:T(8,128)(2,1)S(1)}, bf16[112,768]{1,0:T(8,128)(2,1)S(1)}, u32[]{:S(2)}, u32[]{:S(2)}) collective-permute-start(bf16[112,768]{1,0:T(8,128)(2,1)S(1)} %get-tuple-element.187.refs_0_), channel_id=1, source_target_pairs={{0,12},{4,8},{8,4},{12,0},{1,13},{5,9},{9,5},{13,1},{2,14},{6,10},... | collective-permute-start | bytes 516104 | tf_op jit(solution)/shard_map/ppermute | solution.py:921
  149.9 18.6 %collective-permute-start.31 = (bf16[112,768]{1,0:T(8,128)(2,1)S(1)}, bf16[112,768]{1,0:T(8,128)(2,1)S(1)}, u32[]{:S(2)}, u32[]{:S(2)}) collective-permute-start(bf16[112,768]{1,0:T(8,128)(2,1)S(1)} %get-tuple-element.187.refs_0_), channel_id=1, source_target_pairs={{0,8},{4,12},{8,0},{12,4},{1,9},{5,13},{9,1},{13,5},{2,10},{6,14},... | collective-permute-start | bytes 516104 | tf_op jit(solution)/shard_map/ppermute | solution.py:921
  152.7 15.8 %collective-permute-start.30 = (bf16[112,768]{1,0:T(8,128)(2,1)S(1)}, bf16[112,768]{1,0:T(8,128)(2,1)S(1)}, u32[]{:S(2)}, u32[]{:S(2)}) collective-permute-start(bf16[112,768]{1,0:T(8,128)(2,1)S(1)} %get-tuple-element.187.refs_0_), channel_id=1, source_target_pairs={{0,4},{4,0},{8,12},{12,8},{1,5},{5,1},{9,13},{13,9},{2,6},{6,2},{1... | collective-permute-start | bytes 516104 | tf_op jit(solution)/shard_map/ppermute | solution.py:921
  169.6 9.8 %collective-permute-start.39 = (bf16[160,768]{1,0:T(8,128)(2,1)S(1)}, bf16[160,768]{1,0:T(8,128)(2,1)S(1)}, u32[]{:S(2)}, u32[]{:S(2)}) collective-permute-start(bf16[160,768]{1,0:T(8,128)(2,1)S(1)} %add_convert_fusion.refs_0_), channel_id=1, source_target_pairs={{0,3},{1,2},{2,1},{3,0},{4,7},{5,6},{6,5},{7,4},{8,11},{9,10},{10,... | collective-permute-start | bytes 737288 | tf_op jit(solution)/shard_map/ppermute | solution.py:926
  171.2 12.6 %collective-permute-start.38 = (bf16[160,768]{1,0:T(8,128)(2,1)S(1)}, bf16[160,768]{1,0:T(8,128)(2,1)S(1)}, u32[]{:S(2)}, u32[]{:S(2)}) collective-permute-start(bf16[160,768]{1,0:T(8,128)(2,1)S(1)} %add_convert_fusion.refs_0_), channel_id=1, source_target_pairs={{0,2},{1,3},{2,0},{3,1},{4,6},{5,7},{6,4},{7,5},{8,10},{9,11},{10,... | collective-permute-start | bytes 737288 | tf_op jit(solution)/shard_map/ppermute | solution.py:926
  172.0 11.8 %collective-permute-start.37 = (bf16[160,768]{1,0:T(8,128)(2,1)S(1)}, bf16[160,768]{1,0:T(8,128)(2,1)S(1)}, u32[]{:S(2)}, u32[]{:S(2)}) collective-permute-start(bf16[160,768]{1,0:T(8,128)(2,1)S(1)} %add_convert_fusion.refs_0_), channel_id=1, source_target_pairs={{0,1},{1,0},{2,3},{3,2},{4,5},{5,4},{6,7},{7,6},{8,9},{9,8},{10,11... | collective-permute-start | bytes 737288 | tf_op jit(solution)/shard_map/ppermute | solution.py:926
  (18 other events, 153.5 us)

commit v4 on v3

--- a/solution.py
+++ b/solution.py
@@ -326,7 +326,7 @@
 
 
 def chunk_of(pos_ref, j, size):
-    return pl.ds(pl.multiple_of(lax.bitwise_xor(lax.axis_index("tensor"), j) * size, 16), size)
+    return pl.ds(pl.multiple_of(lax.bitwise_xor(lax.axis_index("tensor"), j) * size, 8), size)
 
 
 def head_masks(rows, heads):
@@ -363,7 +363,7 @@
 ):
     images, seq_len, width = tok_ref.shape
     chunk, experts = x_ref.shape[0], router_ref.shape[0]
-    start = pl.multiple_of(lax.axis_index("tensor") * chunk, 16)
+    start = pl.multiple_of(lax.axis_index("tensor") * chunk, 8)
     for index, source, target in ((0, tok_ref, x_ref), (1, cot_ref, pay_ref)):
         arrive(index)
         flat_ref[images * seq_len :, :] = jnp.zeros(
@@ -663,13 +663,14 @@
     )
 
 
-def expert_grad_kernel(pos_ref, *refs):
-    *sources, first_ref, second_ref = refs
-    part_rows = first_ref.shape[2]
-    for j, out in enumerate((first_ref, second_ref)):
-        columns = slice(2 * j * part_rows, 2 * (j + 1) * part_rows)
+def expert_grad_kernel(first, pos_ref, *refs):
+    outs = refs[8:]
+    part_rows = outs[0].shape[2]
+    for j, out in enumerate(outs):
+        start = 2 * (first + j) * part_rows
+        columns = slice(start, start + 2 * part_rows)
         for s in range(2):
-            left_a, right_a, left_b, right_b = sources[4 * s : 4 * s + 4]
+            left_a, right_a, left_b, right_b = refs[4 * s : 4 * s + 4]
             grad = contract(left_a[:, columns], right_a[...], TN)
             grad = grad + contract(left_b[:, columns], right_b[...], TN)
             grad = grad.astype(jnp.bfloat16)
@@ -677,14 +678,14 @@
             out[1, s] = grad[part_rows:]
 
 
-def expert_grads(position, a, b, rows_a, rows_b, flops=0):
+def expert_grads(position, a, b, rows_a, rows_b, first=0, count=2, flops=0):
     width, total = rows_a[0].shape[1], a[0].shape[1]
     return kernel_call(
-        expert_grad_kernel,
+        functools.partial(expert_grad_kernel, first),
         "expert_grads",
         position,
         [a[1], rows_a[0], b[1], rows_b[0], a[0], rows_a[1], b[0], rows_b[1]],
-        [like((2, 2, total // 4, width), jnp.bfloat16)] * 2,
+        [like((2, 2, total // 4, width), jnp.bfloat16)] * count,
         flops=flops,
         limit=10,
     )
@@ -952,7 +953,7 @@
     owners = lax.axis_size("expert")
     tensors = lax.axis_size("tensor")
     cores = lax.axis_size("dp")
-    chunk = round_up(-(-token_rows // tensors), 16)
+    chunk = round_up(-(-token_rows // tensors), 8)
     padded = chunk * tensors
     rows = round_up(seq_len, 16)
     flat_rows = padded + 32
@@ -1070,7 +1071,11 @@
     backs = [joined[0]] + [hop(joined[k], k) for k in range(1, owners)]
 
     grad_pos = after(position, joined)
-    far_y, far_x = expert_grads(grad_pos, second_a, second_b, (rows_mine, first_a[2]), (rows_other, first_b[2]))
+    far_rows = (rows_mine, first_a[2]), (rows_other, first_b[2])
+    (far_y,) = expert_grads(grad_pos, second_a, second_b, *far_rows, first=0, count=1)
+    (far_x,) = expert_grads(
+        after(grad_pos, far_y), second_a, second_b, *far_rows, first=1, count=1, flops=0
+    )
     from_y, from_x = cross(far_y, 2), cross(far_x, 1)
     residual_grad, attn_grad, small = kernel_call(
         functools.partial(route_back_kernel, experts, token_rows, owners),
@@ -1133,11 +1138,12 @@
     up_x, up_y = kernel_call(
         second_step_kernel,
         "second_step",
-        after(position, got[1:], own_piece),
+        after(position, own_piece),
         [near_grad, from_y, from_x],
         [like((2, quarter, width), b16)] * 2,
         limit=8,
     )
+    up_x, up_y = after((up_x, up_y), got[1:])
     last_x, last_y = cross(up_x, 1), cross(up_y, 2)
 
     grad_chunk, summed = kernel_call(

time: 185 us -> 180 us (0.973)
  starting transfers between devices: 47.6 us -> 44.8 us
  waiting for transfers between devices: 57.3 us -> 55.1 us
    ppermute x16, starting transfers between devices: 26 us -> 23.6 us  [hop(): return lax.ppermute(value, 'expert', [(i, i ^ bit) for i in range(size)])]
    ppermute x16, waiting for transfers between devices: 30.2 us -> 28.2 us  [hop(): return lax.ppermute(value, 'expert', [(i, i ^ bit) for i in range(size)])]
    pallas_call x26 -> x27, Pallas kernels: 49.2 us -> 48.6 us  [kernel_call(): pl.pallas_call(kernel, in_specs=[pl.BlockSpec(memory_space=pltpu.SMEM)] +...]
where the time goes in v4:
time: 180 us
  waiting for transfers between devices  55.1 us (31%)
  Pallas kernels  48.6 us (27%)
  starting transfers between devices  44.8 us (25%)
  blocking collectives  29.5 us (16%)
    pallas_call x27, Pallas kernels, kernel_call(): pl.pallas_call(kernel, in_specs=[pl.BlockSpec(memory_space=pltpu.SMEM)] +...  48.6 us
    ppermute x16, waiting for transfers between devices, hop(): return lax.ppermute(value, 'expert', [(i, i ^ bit) for i in range(size)])  28.2 us
    ppermute x17, waiting for transfers between devices, cross(): return lax.ppermute(value, 'tensor', [(i, i ^ bit) for i in range(size)])  26.9 us
    ppermute x16, starting transfers between devices, hop(): return lax.ppermute(value, 'expert', [(i, i ^ bit) for i in range(size)])  23.6 us
    ppermute x17, starting transfers between devices, cross(): return lax.ppermute(value, 'tensor', [(i, i ^ bit) for i in range(size)])  19.8 us
    all_gather x1, blocking collectives, dense_body(): grad_rows = lax.all_gather(grad_chunk, 'tensor', axis=0, tiled=True)  15.5 us
    all_gather x1, blocking collectives, dense_body(): attn_grad = lax.all_gather(attn_grad, 'tensor', axis=0, tiled=True)  13.9 us
  transfers between devices with their start and end apart: 40, of which 17 were waited for; matrix products, arithmetic and copies ran while one was open for 0% of the time, Pallas kernels for 18%

profile of v4, /device:TPU:0, one launch (start us, length us, event | category | flops | bytes accessed | tf_op | source)
XLA Modules:
  0.0 179.9 jit_solution(6592064267880986162)
XLA Ops:
  0.7 4.1 %chunk.1 = (bf16[152,768]{1,0:T(8,128)(2,1)}, bf16[168,768]{1,0:T(8,128)(2,1)}, f32[8,768]{1,0:T(8,128)}, bf16[2,384,768]{2,1,0:T(8,128)(2,1)}, bf16[2,192,768]{...) custom-call(s32[1]{0:T(128)} %constant.0.clone.1.refs_0_.pos_ref, bf16[3,197,768]{2,1,0:T(8,128)(2,1)} %tok_ref.1, ...), custom_call_target="tpu_custom_call" | custom-call | tf_op jit(solution)/shard_map/chunk/pallas_call | solution.py:307
  4.8 4.1 %collective-permute-start.2 = (bf16[168,768]{1,0:T(8,128)(2,1)}, bf16[168,768]{1,0:T(8,128)(2,1)S(1)}, u32[]{:S(2)}, u32[]{:S(2)}) collective-permute-start(bf16[168,768]{1,0:T(8,128)(2,1)} %get-tuple-element.117.refs_0_.refs_6_), channel_id=1, source_target_pairs={{0,8},{4,12},{8,0},{12,4},{1,9},{5,13},{9,1},{13,5},{2,10},{6,14},... | collective-permute-start | bytes 774152 | tf_op jit(solution)/shard_map/ppermute | solution.py:922
  12.7 4.9 %attention.1 = (bf16[3,3,208,192]{3,2,1,0:T(8,128)(2,1)S(1)}, f32[3,208,128]{2,1,0:T(8,128)S(1)}, bf16[608,192]{1,0:T(8,128)(2,1)S(1)}, bf16[152,768]{1,0:T(8,12...) custom-call(s32[1]{0:T(128)} %constant.0.clone.1.refs_0_.pos_ref, ...), custom_call_target="tpu_custom_call" | custom-call | flops 40000000000 | tf_op jit(solution)/shard_map/attention/pallas_call | solution.py:307
  17.6 6.3 %collective-permute-done.refs_1_.xa_ref = bf16[2,192,768]{2,1,0:T(8,128)(2,1)S(1)} collective-permute-done((bf16[2,192,768]{2,1,0:T(8,128)(2,1)}, bf16[2,192,768]{2,1,0:T(8,128)(2,1)S(1)}, u32[]{:S(2)}, u32[]{:S(2)}) %collective-permute-start) | collective-permute-done | bytes 589856 | tf_op jit(solution)/shard_map/ppermute | solution.py:927
  30.5 4.7 %collective-permute-done.3.refs_1_ = bf16[152,768]{1,0:T(8,128)(2,1)S(1)} collective-permute-done((bf16[152,768]{1,0:T(8,128)(2,1)S(1)}, bf16[152,768]{1,0:T(8,128)(2,1)S(1)}, u32[]{:S(2)}, u32[]{:S(2)}) %collective-permute-start.3) | collective-permute-done | bytes 233504 | tf_op jit(solution)/shard_map/ppermute | solution.py:927
  35.1 1.9 %collective-permute-done.4.refs_2_ = bf16[152,768]{1,0:T(8,128)(2,1)S(1)} collective-permute-done((bf16[152,768]{1,0:T(8,128)(2,1)S(1)}, bf16[152,768]{1,0:T(8,128)(2,1)S(1)}, u32[]{:S(2)}, u32[]{:S(2)}) %collective-permute-start.4) | collective-permute-done | bytes 233504 | tf_op jit(solution)/shard_map/ppermute | solution.py:927
  43.7 2.8 %collective-permute-start.6 = (bf16[152,768]{1,0:T(8,128)(2,1)S(1)}, bf16[152,768]{1,0:T(8,128)(2,1)S(1)}, u32[]{:S(2)}, u32[]{:S(2)}) collective-permute-start(bf16[152,768]{1,0:T(8,128)(2,1)S(1)} %get-tuple-element.123.refs_0_), channel_id=1, source_target_pairs={{0,4},{4,0},{8,12},{12,8},{1,5},{5,1},{9,13},{13,9},{2,6},{6,2},{1... | collective-permute-start | bytes 700424 | tf_op jit(solution)/shard_map/ppermute | solution.py:922
  46.7 3.0 %collective-permute-done.8.refs_3_ = bf16[152,768]{1,0:T(8,128)(2,1)S(1)} collective-permute-done((bf16[152,768]{1,0:T(8,128)(2,1)S(1)}, bf16[152,768]{1,0:T(8,128)(2,1)S(1)}, u32[]{:S(2)}, u32[]{:S(2)}) %collective-permute-start.8) | collective-permute-done | bytes 233504 | tf_op jit(solution)/shard_map/ppermute | solution.py:922
  49.8 8.9 %collective-permute-done.7.refs_2_ = bf16[152,768]{1,0:T(8,128)(2,1)S(1)} collective-permute-done((bf16[152,768]{1,0:T(8,128)(2,1)S(1)}, bf16[152,768]{1,0:T(8,128)(2,1)S(1)}, u32[]{:S(2)}, u32[]{:S(2)}) %collective-permute-start.7) | collective-permute-done | bytes 233504 | tf_op jit(solution)/shard_map/ppermute | solution.py:922
  58.8 3.7 %experts_first.2 = (bf16[608,768]{1,0:T(8,128)(2,1)S(1)}, bf16[608,768]{1,0:T(8,128)(2,1)S(1)}, bf16[608,768]{1,0:T(8,128)(2,1)S(1)}, f32[608,256]{1,0:T(8,128)S...) custom-call(s32[1]{0:T(128)} %constant.0.clone.1.refs_0_.pos_ref, bf16[608,768]{1,0:T(8,128)(2,1)S(1)} %lay_rows.1.x_ref.refs_1_, ...), custom_call_target="tpu_custom_call" | custom-call | tf_op jit(solution)/shard_map/experts_first/pallas_call | solution.py:307
  62.5 3.7 %experts_first.3 = (bf16[608,768]{1,0:T(8,128)(2,1)S(1)}, bf16[608,768]{1,0:T(8,128)(2,1)S(1)}, bf16[608,768]{1,0:T(8,128)(2,1)S(1)}, f32[608,256]{1,0:T(8,128)S...) custom-call(s32[1]{0:T(128)} %constant.0.clone.1.refs_0_.pos_ref, ...), custom_call_target="tpu_custom_call" | custom-call | tf_op jit(solution)/shard_map/experts_first/pallas_call | solution.py:307
  66.2 3.6 %experts_second.2 = (bf16[608,768]{1,0:T(8,128)(2,1)S(1)}, bf16[608,768]{1,0:T(8,128)(2,1)S(1)}, bf16[608,768]{1,0:T(8,128)(2,1)S(1)}, bf16[608,896]{1,0:T(8,128)(2,1)S(1)}) custom-call(s32[1]{0:T(128)} %constant.0.clone.1.refs_0_.pos_ref, bf16[608,768]{1,0:T(8,128)(2,1)S(1)} %collective-permute-done.10.x_ref.refs_3_, ...), custom_call_target="tpu_custom_call" | custom-call | tf_op jit(solution)/shard_map/experts_second/pallas_call | solution.py:307
  70.4 3.8 %experts_second.3 = (bf16[608,768]{1,0:T(8,128)(2,1)S(1)}, bf16[608,768]{1,0:T(8,128)(2,1)S(1)}, bf16[608,768]{1,0:T(8,128)(2,1)S(1)}, f32[608,896]{1,0:T(8,128)S(1)}) custom-call(s32[1]{0:T(128)} %constant.0.clone.1.refs_0_.pos_ref, bf16[608,768]{1,0:T(8,128)(2,1)S(1)} %lay_rows.1.x_ref.refs_1_, bf16[608,896]{1,0:T(8,128)(2,1)S(1)} %lay_payload.1.pay_ref, ...), custom_call_target="tpu_custom_call" | custom-call | tf_op jit(solution)/shard_map/experts_second/pallas_call | solution.py:307
  75.2 2.1 %collective-permute-start.19 = (bf16[160,768]{1,0:T(8,128)(2,1)S(1)}, bf16[160,768]{1,0:T(8,128)(2,1)S(1)}, u32[]{:S(2)}, u32[]{:S(2)}) collective-permute-start(bf16[160,768]{1,0:T(8,128)(2,1)S(1)} %get-tuple-element.146), channel_id=1, source_target_pairs={{0,8},{4,12},{8,0},{12,4},{1,9},{5,13},{9,1},{13,5},{2,10},{6,14},... | collective-permute-start | bytes 737288 | tf_op jit(solution)/shard_map/ppermute | solution.py:922
  77.3 2.2 %collective-permute-start.20 = (bf16[160,768]{1,0:T(8,128)(2,1)S(1)}, bf16[160,768]{1,0:T(8,128)(2,1)S(1)}, u32[]{:S(2)}, u32[]{:S(2)}) collective-permute-start(bf16[160,768]{1,0:T(8,128)(2,1)S(1)} %get-tuple-element.147), channel_id=1, source_target_pairs={{0,12},{4,8},{8,4},{12,0},{1,13},{5,9},{9,5},{13,1},{2,14},{6,10},... | collective-permute-start | bytes 737288 | tf_op jit(solution)/shard_map/ppermute | solution.py:922
  79.6 2.0 %expert_grads.3 = bf16[2,2,192,768]{3,2,1,0:T(8,128)(2,1)S(1)} custom-call(s32[1]{0:T(128)} %constant.0.clone.1.refs_0_.pos_ref, bf16[608,768]{1,0:T(8,128)(2,1)S(1)} %get-tuple-element.149.refs_0_, bf16[608,768]{1,0:T(8,128)(2,1)S(1)} %lay_rows.1.x_ref.refs_1_, bf16[608,768]{1,0:T(8,128)(2,1)S(1)} %get-tuple-element.150.refs_2_, ...), custom_call_target="tpu_custom_call" | custom-call | tf_op jit(solution)/shard_map/expert_grads/pallas_call | solution.py:307
  82.2 2.0 %expert_grads.4 = bf16[2,2,192,768]{3,2,1,0:T(8,128)(2,1)S(1)} custom-call(s32[1]{0:T(128)} %constant.0.clone.1.refs_0_.pos_ref, bf16[608,768]{1,0:T(8,128)(2,1)S(1)} %get-tuple-element.149.refs_0_, bf16[608,768]{1,0:T(8,128)(2,1)S(1)} %lay_rows.1.x_ref.refs_1_, bf16[608,768]{1,0:T(8,128)(2,1)S(1)} %get-tuple-element.150.refs_2_, ...), custom_call_target="tpu_custom_call" | custom-call | tf_op jit(solution)/shard_map/expert_grads/pallas_call | solution.py:307
  84.9 2.6 %collective-permute-done.18.refs_1_ = bf16[160,768]{1,0:T(8,128)(2,1)S(1)} collective-permute-done((bf16[160,768]{1,0:T(8,128)(2,1)S(1)}, bf16[160,768]{1,0:T(8,128)(2,1)S(1)}, u32[]{:S(2)}, u32[]{:S(2)}) %collective-permute-start.18) | collective-permute-done | bytes 245792 | tf_op jit(solution)/shard_map/ppermute | solution.py:922
  87.5 8.0 %collective-permute-done.19.refs_2_ = bf16[160,768]{1,0:T(8,128)(2,1)S(1)} collective-permute-done((bf16[160,768]{1,0:T(8,128)(2,1)S(1)}, bf16[160,768]{1,0:T(8,128)(2,1)S(1)}, u32[]{:S(2)}, u32[]{:S(2)}) %collective-permute-start.19) | collective-permute-done | bytes 245792 | tf_op jit(solution)/shard_map/ppermute | solution.py:922
  96.3 3.9 %expert_grads.5 = (bf16[2,2,192,768]{3,2,1,0:T(8,128)(2,1)S(1)}, bf16[2,2,192,768]{3,2,1,0:T(8,128)(2,1)S(1)}) custom-call(s32[1]{0:T(128)} %constant.0.clone.1.refs_0_.pos_ref, bf16[608,768]{1,0:T(8,128)(2,1)S(1)} %get-tuple-element.157.refs_0_, bf16[608,768]{1,0:T(8,128)(2,1)S(1)} %lay_rows.1.x_ref.refs_1_, ...), custom_call_target="tpu_custom_call" | custom-call | tf_op jit(solution)/shard_map/expert_grads/pallas_call | solution.py:307
  100.2 4.9 %collective-permute-done.21.got_ref = bf16[2,152,768]{2,1,0:T(8,128)(2,1)S(1)} collective-permute-done((bf16[2,152,768]{2,1,0:T(8,128)(2,1)S(1)}, bf16[2,152,768]{2,1,0:T(8,128)(2,1)S(1)}, u32[]{:S(2)}, u32[]{:S(2)}) %collective-permute-start.21) | collective-permute-done | bytes 466976 | tf_op jit(solution)/shard_map/ppermute | solution.py:922
  105.7 13.9 %all_gather.6.up_ref = bf16[608,768]{1,0:T(8,128)(2,1)S(1)} all-gather(bf16[152,768]{1,0:T(8,128)(2,1)S(1)} %get-tuple-element.173), channel_id=1, replica_groups=mesh['dp'=2,'expert'=4,'tensor'=4] {'tensor'}, dimensions={0}, use_global_device_ids=true | all-gather | bytes 1167360 | tf_op jit(solution)/shard_map/all_gather | solution.py:1103
  119.7 5.9 %attention_back.1 = (f32[4,96,768]{2,1,0:T(8,128)S(1)}, bf16[4,96,768]{2,1,0:T(8,128)(2,1)S(1)}, bf16[168,768]{1,0:T(8,128)(2,1)S(1)}, bf16[168,768]{1,0:T(8,128...) custom-call(s32[1]{0:T(128)} %constant.0.clone.1.refs_0_.pos_ref, ...), custom_call_target="tpu_custom_call" | custom-call | flops 6000000000 | tf_op jit(solution)/shard_map/attention_back/pallas_call | solution.py:307
  129.5 2.0 %collective-permute-start.28 = (bf16[96,768]{1,0:T(8,128)(2,1)S(1)}, bf16[96,768]{1,0:T(8,128)(2,1)S(1)}, u32[]{:S(2)}, u32[]{:S(2)}) collective-permute-start(bf16[96,768]{1,0:T(8,128)(2,1)S(1)} %get-tuple-element.184), channel_id=1, source_target_pairs={{0,8},{4,12},{8,0},{12,4},{1,9},{5,13},{9,1},{13,5},{2,10},{6,14},... | collective-permute-start | bytes 442376 | tf_op jit(solution)/shard_map/ppermute | solution.py:922
  131.5 3.2 %collective-permute-done.23.refs_1_ = bf16[168,768]{1,0:T(8,128)(2,1)S(1)} collective-permute-done((bf16[168,768]{1,0:T(8,128)(2,1)S(1)}, bf16[168,768]{1,0:T(8,128)(2,1)S(1)}, u32[]{:S(2)}, u32[]{:S(2)}) %collective-permute-start.23) | collective-permute-done | bytes 258080 | tf_op jit(solution)/shard_map/ppermute | solution.py:927
  136.6 2.7 %collective-permute-done.24.refs_2_ = bf16[168,768]{1,0:T(8,128)(2,1)S(1)} collective-permute-done((bf16[168,768]{1,0:T(8,128)(2,1)S(1)}, bf16[168,768]{1,0:T(8,128)(2,1)S(1)}, u32[]{:S(2)}, u32[]{:S(2)}) %collective-permute-start.24) | collective-permute-done | bytes 258080 | tf_op jit(solution)/shard_map/ppermute | solution.py:927
  145.0 2.8 %collective-permute-start.31 = (bf16[112,768]{1,0:T(8,128)(2,1)S(1)}, bf16[112,768]{1,0:T(8,128)(2,1)S(1)}, u32[]{:S(2)}, u32[]{:S(2)}) collective-permute-start(bf16[112,768]{1,0:T(8,128)(2,1)S(1)} %get-tuple-element.187.refs_0_), channel_id=1, source_target_pairs={{0,8},{4,12},{8,0},{12,4},{1,9},{5,13},{9,1},{13,5},{2,10},{6,14},... | collective-permute-start | bytes 516104 | tf_op jit(solution)/shard_map/ppermute | solution.py:922
  148.2 15.5 %all_gather.7.refs_0_ = bf16[608,768]{1,0:T(8,128)(2,1)S(1)} all-gather(bf16[152,768]{1,0:T(8,128)(2,1)S(1)} %get-tuple-element.186), channel_id=1, replica_groups=mesh['dp'=2,'expert'=4,'tensor'=4] {'tensor'}, dimensions={0}, use_global_device_ids=true | all-gather | bytes 1167360 | tf_op jit(solution)/shard_map/all_gather | solution.py:1160
  166.3 1.8 %collective-permute-start.38 = (bf16[152,768]{1,0:T(8,128)(2,1)S(1)}, bf16[152,768]{1,0:T(8,128)(2,1)S(1)}, u32[]{:S(2)}, u32[]{:S(2)}) collective-permute-start(bf16[152,768]{1,0:T(8,128)(2,1)S(1)} %add_convert_fusion.refs_0_), channel_id=1, source_target_pairs={{0,2},{1,3},{2,0},{3,1},{4,6},{5,7},{6,4},{7,5},{8,10},{9,11},{10,... | collective-permute-start | bytes 700424 | tf_op jit(solution)/shard_map/ppermute | solution.py:927
  169.9 1.7 spread.1
  171.6 2.6 %weight_out.1 = (f32[1,768,768]{2,1,0:T(8,128)}, f32[1,768,768]{2,1,0:T(8,128)}) custom-call(s32[1]{0:T(128)} %constant.0.clone.1.refs_0_.pos_ref, bf16[2,384,768]{2,1,0:T(8,128)(2,1)S(1)} %weight_sum.1.mine_ref, bf16[2,384,768]{2,1,0:T(8,128)(2,1)S(1)} %collective-permute-done.35.other_ref), custom_call_target="tpu_custom_call" | custom-call | tf_op jit(solution)/shard_map/weight_out/pallas_call | solution.py:307
  174.5 4.0 %collective-permute-done.38.refs_2_ = bf16[152,768]{1,0:T(8,128)(2,1)S(1)} collective-permute-done((bf16[152,768]{1,0:T(8,128)(2,1)S(1)}, bf16[152,768]{1,0:T(8,128)(2,1)S(1)}, u32[]{:S(2)}, u32[]{:S(2)}) %collective-permute-start.38) | collective-permute-done | bytes 233504 | tf_op jit(solution)/shard_map/ppermute | solution.py:927
  (98 shorter events, 39.4 us)
Async XLA Ops:
  4.8 20.5 %collective-permute-start.2 = (bf16[168,768]{1,0:T(8,128)(2,1)}, bf16[168,768]{1,0:T(8,128)(2,1)S(1)}, u32[]{:S(2)}, u32[]{:S(2)}) collective-permute-start(bf16[168,768]{1,0:T(8,128)(2,1)} %get-tuple-element.117.refs_0_.refs_6_), channel_id=1, source_target_pairs={{0,8},{4,12},{8,0},{12,4},{1,9},{5,13},{9,1},{13,5},{2,10},{6,14},... | collective-permute-start | bytes 774152 | tf_op jit(solution)/shard_map/ppermute | solution.py:922
  8.9 15.0 %collective-permute-start = (bf16[2,192,768]{2,1,0:T(8,128)(2,1)}, bf16[2,192,768]{2,1,0:T(8,128)(2,1)S(1)}, u32[]{:S(2)}, u32[]{:S(2)}) collective-permute-start(bf16[2,192,768]{2,1,0:T(8,128)(2,1)} %get-tuple-element.113.refs_0_), channel_id=1, source_target_pairs={{0,1},{1,0},{2,3},{3,2},{4,5},{5,4},{6,7},{7,6},{8,9},{9,8},{10,11... | collective-permute-start | bytes 1769480 | tf_op jit(solution)/shard_map/ppermute | solution.py:927
  10.4 14.7 %collective-permute-start.1 = (bf16[2,192,768]{2,1,0:T(8,128)(2,1)}, bf16[2,192,768]{2,1,0:T(8,128)(2,1)S(1)}, u32[]{:S(2)}, u32[]{:S(2)}) collective-permute-start(bf16[2,192,768]{2,1,0:T(8,128)(2,1)} %get-tuple-element.114.refs_2_), channel_id=1, source_target_pairs={{0,2},{1,3},{2,0},{3,1},{4,6},{5,7},{6,4},{7,5},{8,10},{9,11},{10,... | collective-permute-start | bytes 1769480 | tf_op jit(solution)/shard_map/ppermute | solution.py:927
  25.3 18.4 %collective-permute-start.9 = (bf16[2,168,768]{2,1,0:T(8,128)(2,1)S(1)}, bf16[2,168,768]{2,1,0:T(8,128)(2,1)S(1)}, u32[]{:S(2)}, u32[]{:S(2)}) collective-permute-start(bf16[2,168,768]{2,1,0:T(8,128)(2,1)S(1)} %stack.3.near_ref), channel_id=1, source_target_pairs={{0,4},{4,0},{8,12},{12,8},{1,5},{5,1},{9,13},{13,9},{2,6},{6,2},{1... | collective-permute-start | bytes 1548296 | tf_op jit(solution)/shard_map/ppermute | solution.py:922
  27.5 9.5 %collective-permute-start.4 = (bf16[152,768]{1,0:T(8,128)(2,1)S(1)}, bf16[152,768]{1,0:T(8,128)(2,1)S(1)}, u32[]{:S(2)}, u32[]{:S(2)}) collective-permute-start(bf16[152,768]{1,0:T(8,128)(2,1)S(1)} %get-tuple-element.120), channel_id=1, source_target_pairs={{0,2},{1,3},{2,0},{3,1},{4,6},{5,7},{6,4},{7,5},{8,10},{9,11},{10,... | collective-permute-start | bytes 700424 | tf_op jit(solution)/shard_map/ppermute | solution.py:927
  29.0 9.6 %collective-permute-start.5 = (bf16[152,768]{1,0:T(8,128)(2,1)S(1)}, bf16[152,768]{1,0:T(8,128)(2,1)S(1)}, u32[]{:S(2)}, u32[]{:S(2)}) collective-permute-start(bf16[152,768]{1,0:T(8,128)(2,1)S(1)} %get-tuple-element.121), channel_id=1, source_target_pairs={{0,3},{1,2},{2,1},{3,0},{4,7},{5,6},{6,5},{7,4},{8,11},{9,10},{10,... | collective-permute-start | bytes 700424 | tf_op jit(solution)/shard_map/ppermute | solution.py:927
  39.3 10.5 %collective-permute-start.8 = (bf16[152,768]{1,0:T(8,128)(2,1)S(1)}, bf16[152,768]{1,0:T(8,128)(2,1)S(1)}, u32[]{:S(2)}, u32[]{:S(2)}) collective-permute-start(bf16[152,768]{1,0:T(8,128)(2,1)S(1)} %get-tuple-element.123.refs_0_), channel_id=1, source_target_pairs={{0,12},{4,8},{8,4},{12,0},{1,13},{5,9},{9,5},{13,1},{2,14},{6,10},... | collective-permute-start | bytes 700424 | tf_op jit(solution)/shard_map/ppermute | solution.py:922
  39.6 26.6 %collective-permute-start.12 = (bf16[2,2,192,768]{3,2,1,0:T(8,128)(2,1)S(1)}, bf16[2,2,192,768]{3,2,1,0:T(8,128)(2,1)S(1)}, u32[]{:S(2)}, u32[]{:S(2)}) collective-permute-start(bf16[2,2,192,768]{3,2,1,0:T(8,128)(2,1)S(1)} %get-tuple-element.133), channel_id=1, source_target_pairs={{0,2},{1,3},{2,0},{3,1},{4,6},{5,7},{6,4},{7,5},{8,10},{9,11},{10,... | collective-permute-start | bytes 3538952 | tf_op jit(solution)/shard_map/ppermute | solution.py:927
  40.6 25.6 %collective-permute-start.13 = (bf16[2,2,192,768]{3,2,1,0:T(8,128)(2,1)S(1)}, bf16[2,2,192,768]{3,2,1,0:T(8,128)(2,1)S(1)}, u32[]{:S(2)}, u32[]{:S(2)}) collective-permute-start(bf16[2,2,192,768]{3,2,1,0:T(8,128)(2,1)S(1)} %get-tuple-element.134), channel_id=1, source_target_pairs={{0,1},{1,0},{2,3},{3,2},{4,5},{5,4},{6,7},{7,6},{8,9},{9,8},{10,11... | collective-permute-start | bytes 3538952 | tf_op jit(solution)/shard_map/ppermute | solution.py:927
  42.2 16.5 %collective-permute-start.7 = (bf16[152,768]{1,0:T(8,128)(2,1)S(1)}, bf16[152,768]{1,0:T(8,128)(2,1)S(1)}, u32[]{:S(2)}, u32[]{:S(2)}) collective-permute-start(bf16[152,768]{1,0:T(8,128)(2,1)S(1)} %get-tuple-element.123.refs_0_), channel_id=1, source_target_pairs={{0,8},{4,12},{8,0},{12,4},{1,9},{5,13},{9,1},{13,5},{2,10},{6,14},... | collective-permute-start | bytes 700424 | tf_op jit(solution)/shard_map/ppermute | solution.py:922
  43.7 15.0 %collective-permute-start.6 = (bf16[152,768]{1,0:T(8,128)(2,1)S(1)}, bf16[152,768]{1,0:T(8,128)(2,1)S(1)}, u32[]{:S(2)}, u32[]{:S(2)}) collective-permute-start(bf16[152,768]{1,0:T(8,128)(2,1)S(1)} %get-tuple-element.123.refs_0_), channel_id=1, source_target_pairs={{0,4},{4,0},{8,12},{12,8},{1,5},{5,1},{9,13},{13,9},{2,6},{6,2},{1... | collective-permute-start | bytes 700424 | tf_op jit(solution)/shard_map/ppermute | solution.py:922
  49.8 12.8 %collective-permute-start.11 = (bf16[608,896]{1,0:T(8,128)(2,1)S(1)}, bf16[608,896]{1,0:T(8,128)(2,1)S(1)}, u32[]{:S(2)}, u32[]{:S(2)}) collective-permute-start(bf16[608,896]{1,0:T(8,128)(2,1)S(1)} %lay_payload.1.pay_ref), channel_id=1, source_target_pairs={{0,16},{16,0},{1,17},{17,1},{2,18},{18,2},{3,19},{19,3},{4,20},{20... | collective-permute-start | bytes 3268616 | tf_op jit(solution)/shard_map/ppermute | solution.py:917
  75.1 12.4 %collective-permute-start.18 = (bf16[160,768]{1,0:T(8,128)(2,1)S(1)}, bf16[160,768]{1,0:T(8,128)(2,1)S(1)}, u32[]{:S(2)}, u32[]{:S(2)}) collective-permute-start(bf16[160,768]{1,0:T(8,128)(2,1)S(1)} %get-tuple-element.145), channel_id=1, source_target_pairs={{0,4},{4,0},{8,12},{12,8},{1,5},{5,1},{9,13},{13,9},{2,6},{6,2},{1... | collective-permute-start | bytes 737288 | tf_op jit(solution)/shard_map/ppermute | solution.py:922
  75.2 20.3 %collective-permute-start.19 = (bf16[160,768]{1,0:T(8,128)(2,1)S(1)}, bf16[160,768]{1,0:T(8,128)(2,1)S(1)}, u32[]{:S(2)}, u32[]{:S(2)}) collective-permute-start(bf16[160,768]{1,0:T(8,128)(2,1)S(1)} %get-tuple-element.146), channel_id=1, source_target_pairs={{0,8},{4,12},{8,0},{12,4},{1,9},{5,13},{9,1},{13,5},{2,10},{6,14},... | collective-permute-start | bytes 737288 | tf_op jit(solution)/shard_map/ppermute | solution.py:922
  77.3 18.2 %collective-permute-start.20 = (bf16[160,768]{1,0:T(8,128)(2,1)S(1)}, bf16[160,768]{1,0:T(8,128)(2,1)S(1)}, u32[]{:S(2)}, u32[]{:S(2)}) collective-permute-start(bf16[160,768]{1,0:T(8,128)(2,1)S(1)} %get-tuple-element.147), channel_id=1, source_target_pairs={{0,12},{4,8},{8,4},{12,0},{1,13},{5,9},{9,5},{13,1},{2,14},{6,10},... | collective-permute-start | bytes 737288 | tf_op jit(solution)/shard_map/ppermute | solution.py:922
  81.6 38.0 %collective-permute-start.16 = (bf16[2,2,192,768]{3,2,1,0:T(8,128)(2,1)S(1)}, bf16[2,2,192,768]{3,2,1,0:T(8,128)(2,1)S(1)}, u32[]{:S(2)}, u32[]{:S(2)}) collective-permute-start(bf16[2,2,192,768]{3,2,1,0:T(8,128)(2,1)S(1)} %expert_grads.3), channel_id=1, source_target_pairs={{0,2},{1,3},{2,0},{3,1},{4,6},{5,7},{6,4},{7,5},{8,10},{9,11},{10,... | collective-permute-start | bytes 3538952 | tf_op jit(solution)/shard_map/ppermute | solution.py:927
  84.2 35.4 %collective-permute-start.17 = (bf16[2,2,192,768]{3,2,1,0:T(8,128)(2,1)S(1)}, bf16[2,2,192,768]{3,2,1,0:T(8,128)(2,1)S(1)}, u32[]{:S(2)}, u32[]{:S(2)}) collective-permute-start(bf16[2,2,192,768]{3,2,1,0:T(8,128)(2,1)S(1)} %expert_grads.4), channel_id=1, source_target_pairs={{0,1},{1,0},{2,3},{3,2},{4,5},{5,4},{6,7},{7,6},{8,9},{9,8},{10,11... | collective-permute-start | bytes 3538952 | tf_op jit(solution)/shard_map/ppermute | solution.py:927
  87.5 17.6 %collective-permute-start.21 = (bf16[2,152,768]{2,1,0:T(8,128)(2,1)S(1)}, bf16[2,152,768]{2,1,0:T(8,128)(2,1)S(1)}, u32[]{:S(2)}, u32[]{:S(2)}) collective-permute-start(bf16[2,152,768]{2,1,0:T(8,128)(2,1)S(1)} %get-tuple-element.166), channel_id=1, source_target_pairs={{0,4},{4,0},{8,12},{12,8},{1,5},{5,1},{9,13},{13,9},{2,6},{6,2},{1... | collective-permute-start | bytes 1400840 | tf_op jit(solution)/shard_map/ppermute | solution.py:922
  105.2 14.5 %collective-permute-start.22 = (bf16[152,768]{1,0:T(8,128)(2,1)S(1)}, bf16[152,768]{1,0:T(8,128)(2,1)S(1)}, u32[]{:S(2)}, u32[]{:S(2)}) collective-permute-start(bf16[152,768]{1,0:T(8,128)(2,1)S(1)} %get-tuple-element.168), channel_id=1, source_target_pairs={{0,8},{4,12},{8,0},{12,4},{1,9},{5,13},{9,1},{13,5},{2,10},{6,14},... | collective-permute-start | bytes 700424 | tf_op jit(solution)/shard_map/ppermute | solution.py:922
  125.6 9.1 %collective-permute-start.23 = (bf16[168,768]{1,0:T(8,128)(2,1)S(1)}, bf16[168,768]{1,0:T(8,128)(2,1)S(1)}, u32[]{:S(2)}, u32[]{:S(2)}) collective-permute-start(bf16[168,768]{1,0:T(8,128)(2,1)S(1)} %get-tuple-element.176), channel_id=1, source_target_pairs={{0,1},{1,0},{2,3},{3,2},{4,5},{5,4},{6,7},{7,6},{8,9},{9,8},{10,11... | collective-permute-start | bytes 774152 | tf_op jit(solution)/shard_map/ppermute | solution.py:927
  126.4 12.9 %collective-permute-start.24 = (bf16[168,768]{1,0:T(8,128)(2,1)S(1)}, bf16[168,768]{1,0:T(8,128)(2,1)S(1)}, u32[]{:S(2)}, u32[]{:S(2)}) collective-permute-start(bf16[168,768]{1,0:T(8,128)(2,1)S(1)} %get-tuple-element.177), channel_id=1, source_target_pairs={{0,2},{1,3},{2,0},{3,1},{4,6},{5,7},{6,4},{7,5},{8,10},{9,11},{10,... | collective-permute-start | bytes 774152 | tf_op jit(solution)/shard_map/ppermute | solution.py:927
  127.9 12.3 %collective-permute-start.25 = (bf16[168,768]{1,0:T(8,128)(2,1)S(1)}, bf16[168,768]{1,0:T(8,128)(2,1)S(1)}, u32[]{:S(2)}, u32[]{:S(2)}) collective-permute-start(bf16[168,768]{1,0:T(8,128)(2,1)S(1)} %get-tuple-element.178), channel_id=1, source_target_pairs={{0,3},{1,2},{2,1},{3,0},{4,7},{5,6},{6,5},{7,4},{8,11},{9,10},{10,... | collective-permute-start | bytes 774152 | tf_op jit(solution)/shard_map/ppermute | solution.py:927
  129.3 13.1 %collective-permute-start.27 = (bf16[96,768]{1,0:T(8,128)(2,1)S(1)}, bf16[96,768]{1,0:T(8,128)(2,1)S(1)}, u32[]{:S(2)}, u32[]{:S(2)}) collective-permute-start(bf16[96,768]{1,0:T(8,128)(2,1)S(1)} %get-tuple-element.183), channel_id=1, source_target_pairs={{0,4},{4,0},{8,12},{12,8},{1,5},{5,1},{9,13},{13,9},{2,6},{6,2},{1... | collective-permute-start | bytes 442376 | tf_op jit(solution)/shard_map/ppermute | solution.py:922
  129.5 13.7 %collective-permute-start.28 = (bf16[96,768]{1,0:T(8,128)(2,1)S(1)}, bf16[96,768]{1,0:T(8,128)(2,1)S(1)}, u32[]{:S(2)}, u32[]{:S(2)}) collective-permute-start(bf16[96,768]{1,0:T(8,128)(2,1)S(1)} %get-tuple-element.184), channel_id=1, source_target_pairs={{0,8},{4,12},{8,0},{12,4},{1,9},{5,13},{9,1},{13,5},{2,10},{6,14},... | collective-permute-start | bytes 442376 | tf_op jit(solution)/shard_map/ppermute | solution.py:922
  140.2 23.5 %collective-permute-start.33 = (bf16[2,192,768]{2,1,0:T(8,128)(2,1)S(1)}, bf16[2,192,768]{2,1,0:T(8,128)(2,1)S(1)}, u32[]{:S(2)}, u32[]{:S(2)}) collective-permute-start(bf16[2,192,768]{2,1,0:T(8,128)(2,1)S(1)} %get-tuple-element.193), channel_id=1, source_target_pairs={{0,1},{1,0},{2,3},{3,2},{4,5},{5,4},{6,7},{7,6},{8,9},{9,8},{10,11... | collective-permute-start | bytes 1769480 | tf_op jit(solution)/shard_map/ppermute | solution.py:927
  141.5 22.2 %collective-permute-start.34 = (bf16[2,192,768]{2,1,0:T(8,128)(2,1)S(1)}, bf16[2,192,768]{2,1,0:T(8,128)(2,1)S(1)}, u32[]{:S(2)}, u32[]{:S(2)}) collective-permute-start(bf16[2,192,768]{2,1,0:T(8,128)(2,1)S(1)} %get-tuple-element.194), channel_id=1, source_target_pairs={{0,2},{1,3},{2,0},{3,1},{4,6},{5,7},{6,4},{7,5},{8,10},{9,11},{10,... | collective-permute-start | bytes 1769480 | tf_op jit(solution)/shard_map/ppermute | solution.py:927
  143.7 20.0 %collective-permute-start.32 = (bf16[112,768]{1,0:T(8,128)(2,1)S(1)}, bf16[112,768]{1,0:T(8,128)(2,1)S(1)}, u32[]{:S(2)}, u32[]{:S(2)}) collective-permute-start(bf16[112,768]{1,0:T(8,128)(2,1)S(1)} %get-tuple-element.187.refs_0_), channel_id=1, source_target_pairs={{0,12},{4,8},{8,4},{12,0},{1,13},{5,9},{9,5},{13,1},{2,14},{6,10},... | collective-permute-start | bytes 516104 | tf_op jit(solution)/shard_map/ppermute | solution.py:922
  145.0 18.7 %collective-permute-start.31 = (bf16[112,768]{1,0:T(8,128)(2,1)S(1)}, bf16[112,768]{1,0:T(8,128)(2,1)S(1)}, u32[]{:S(2)}, u32[]{:S(2)}) collective-permute-start(bf16[112,768]{1,0:T(8,128)(2,1)S(1)} %get-tuple-element.187.refs_0_), channel_id=1, source_target_pairs={{0,8},{4,12},{8,0},{12,4},{1,9},{5,13},{9,1},{13,5},{2,10},{6,14},... | collective-permute-start | bytes 516104 | tf_op jit(solution)/shard_map/ppermute | solution.py:922
  147.9 15.8 %collective-permute-start.30 = (bf16[112,768]{1,0:T(8,128)(2,1)S(1)}, bf16[112,768]{1,0:T(8,128)(2,1)S(1)}, u32[]{:S(2)}, u32[]{:S(2)}) collective-permute-start(bf16[112,768]{1,0:T(8,128)(2,1)S(1)} %get-tuple-element.187.refs_0_), channel_id=1, source_target_pairs={{0,4},{4,0},{8,12},{12,8},{1,5},{5,1},{9,13},{13,9},{2,6},{6,2},{1... | collective-permute-start | bytes 516104 | tf_op jit(solution)/shard_map/ppermute | solution.py:922
  164.9 9.6 %collective-permute-start.39 = (bf16[152,768]{1,0:T(8,128)(2,1)S(1)}, bf16[152,768]{1,0:T(8,128)(2,1)S(1)}, u32[]{:S(2)}, u32[]{:S(2)}) collective-permute-start(bf16[152,768]{1,0:T(8,128)(2,1)S(1)} %add_convert_fusion.refs_0_), channel_id=1, source_target_pairs={{0,3},{1,2},{2,1},{3,0},{4,7},{5,6},{6,5},{7,4},{8,11},{9,10},{10,... | collective-permute-start | bytes 700424 | tf_op jit(solution)/shard_map/ppermute | solution.py:927
  166.3 12.2 %collective-permute-start.38 = (bf16[152,768]{1,0:T(8,128)(2,1)S(1)}, bf16[152,768]{1,0:T(8,128)(2,1)S(1)}, u32[]{:S(2)}, u32[]{:S(2)}) collective-permute-start(bf16[152,768]{1,0:T(8,128)(2,1)S(1)} %add_convert_fusion.refs_0_), channel_id=1, source_target_pairs={{0,2},{1,3},{2,0},{3,1},{4,6},{5,7},{6,4},{7,5},{8,10},{9,11},{10,... | collective-permute-start | bytes 700424 | tf_op jit(solution)/shard_map/ppermute | solution.py:927
  168.1 10.6 %collective-permute-start.37 = (bf16[152,768]{1,0:T(8,128)(2,1)S(1)}, bf16[152,768]{1,0:T(8,128)(2,1)S(1)}, u32[]{:S(2)}, u32[]{:S(2)}) collective-permute-start(bf16[152,768]{1,0:T(8,128)(2,1)S(1)} %add_convert_fusion.refs_0_), channel_id=1, source_target_pairs={{0,1},{1,0},{2,3},{3,2},{4,5},{5,4},{6,7},{7,6},{8,9},{9,8},{10,11... | collective-permute-start | bytes 700424 | tf_op jit(solution)/shard_map/ppermute | solution.py:927
  (18 other events, 149.5 us)

commit v5 on v4

--- a/solution.py
+++ b/solution.py
@@ -397,8 +397,8 @@
     kept = jnp.concatenate(
         [kept_ref[pl.ds(start, chunk), :], jnp.zeros((2 * LANES - chunk, LANES), jnp.float32)], axis=0
     ).T
-    pay_ref[chunk:, : 2 * LANES] = kept[0 : 2 * SMALL].astype(jnp.bfloat16)
-    pay_ref[chunk:, 2 * LANES :] = jnp.zeros((2 * SMALL, width - 2 * LANES), jnp.bfloat16)
+    pay_ref[chunk:, : 2 * LANES] = kept[0:SMALL].astype(jnp.bfloat16)
+    pay_ref[chunk:, 2 * LANES :] = jnp.zeros((SMALL, width - 2 * LANES), jnp.bfloat16)
     param_ref[...] = jnp.zeros_like(param_ref)
     param_ref[0:experts, :] = router_ref[...].astype(jnp.float32)
     param_ref[experts : experts + 1, :] = one_ref[...].reshape(1, width)
@@ -460,6 +460,25 @@
         [like((len(blocks) * chunk, width), blocks[0].dtype)],
         limit=4,
     )[0]
+
+
+def pack_small(small, experts):
+    high, low = split_high_low(small)
+    row = lax.broadcasted_iota(jnp.int32, (SMALL, LANES), 0)
+    loss_rows = (row == experts + 1) | (row == experts + 2)
+    low = jnp.where(loss_rows, low[:, :LANES].astype(jnp.float32), 0.0)
+    high = high.astype(jnp.float32)
+    packed = [high[:, :LANES], high[:, LANES : 2 * LANES] + low, high[:, 2 * LANES :]]
+    return jnp.concatenate(packed, axis=1).astype(jnp.bfloat16)
+
+
+def unpack_small(rows, experts):
+    rows = rows.astype(jnp.float32)
+    row = lax.broadcasted_iota(jnp.int32, (SMALL, LANES), 0)
+    loss_rows = (row == experts + 1) | (row == experts + 2)
+    low = rows[:, LANES : 2 * LANES]
+    first = rows[:, :LANES] + jnp.where(loss_rows, low, 0.0)
+    return jnp.concatenate([first, jnp.where(loss_rows, 0.0, low), rows[:, 2 * LANES :]], axis=1)
 
 
 def gain_row(param_ref, experts, which):
@@ -794,12 +813,12 @@
     for i in range(images):
         flat_ref[pl.ds(i * seq_len, seq_len), :] = sum_ref[i, 0:seq_len, :]
         gain_grad = gain_grad + gain_ref[i, 0:1, :]
-    high, low = split_high_low(
-        jnp.concatenate([small_ref[0 : SMALL - 1, :], gain_grad], axis=0)
+    small = pack_small(
+        jnp.concatenate([small_ref[0 : SMALL - 1, :], gain_grad], axis=0), experts
     )
     for j, part in enumerate(parts):
         part[0:chunk, :] = flat_ref[chunk_of(pos_ref, j, chunk), :].astype(jnp.bfloat16)
-        part[chunk:, :] = jnp.concatenate([high, low], axis=0)
+        part[chunk:, :] = small
     me, core = lax.axis_index("expert"), lax.axis_index("dp")
     piece = keep_ref.shape[1]
     for k in range(owners):
@@ -817,9 +836,9 @@
     upstream = jnp.zeros((chunk, width), jnp.float32)
     for j, part in enumerate(got):
         upstream = upstream + part[0:chunk, :].astype(jnp.float32)
-        small_ref[lax.bitwise_xor(lax.axis_index("tensor"), j)] = part[chunk : chunk + SMALL, :].astype(
-            jnp.float32
-        ) + part[chunk + SMALL :, :].astype(jnp.float32)
+        small_ref[lax.bitwise_xor(lax.axis_index("tensor"), j)] = unpack_small(
+            part[chunk:, :], experts
+        )
     small = small_ref[0]
     for j in range(1, tensors):
         small = small + small_ref[j]
@@ -832,7 +851,7 @@
     for part in parts:
         total = total + part[...].astype(jnp.float32)
     out_ref[0:piece, :] = total.astype(jnp.bfloat16)
-    out_ref[piece:, :] = jnp.concatenate(split_high_low(small), axis=0)
+    out_ref[piece:, :] = pack_small(small, experts)
 
 
 def second_step_kernel(pos_ref, near_ref, from_y, from_x, x_ref, y_ref):
@@ -860,7 +879,7 @@
     sides = refs[:2]
     qkv_ref, wo_ref, router_ref, one_ref, two_ref, loss_ref, big_ref, parts_ref = refs[2:]
     span = sides[0].shape[0] // owners
-    piece = span - 2 * SMALL
+    piece = span - SMALL
     core, me = lax.axis_index("dp"), lax.axis_index("expert")
     for c in range(2):
         side = core if c == 0 else 1 - core
@@ -869,9 +888,7 @@
             place = side * owners + lax.bitwise_xor(me, k)
             here = pl.ds(pl.multiple_of(place * piece, 8), piece)
             big_ref[here, :] = block[0:piece, :].astype(jnp.float32)
-            parts_ref[place] = block[piece : piece + SMALL, :].astype(jnp.float32) + block[
-                piece + SMALL :, :
-            ].astype(jnp.float32)
+            parts_ref[place] = unpack_small(block[piece:, :], experts)
     rows = qkv_ref.shape[0]
     qkv_ref[...] = big_ref[0:rows, :]
     wo_ref[...] = big_ref[rows:, :]
@@ -979,7 +996,7 @@
         ],
         [
             like((chunk, width), b16),
-            like((chunk + 2 * SMALL, width), b16),
+            like((chunk + SMALL, width), b16),
             like((SMALL, width), f32),
             like((2, half, width), b16),
             like((2, quarter, width), b16),
@@ -1111,7 +1128,7 @@
             like((owners, piece, width), f32),
             like((owners, piece, width), b16),
         ]
-        + [like((chunk + 2 * SMALL, width), b16)] * tensors,
+        + [like((chunk + SMALL, width), b16)] * tensors,
         [
             pltpu.VMEM((flat_rows, local), f32),
             pltpu.VMEM((flat_rows, width), f32),
@@ -1151,7 +1168,7 @@
         "norm_back",
         position,
         [*got, x_chunk, residual_grad, params, own_piece, *reduced],
-        [like((chunk, width), b16), like((piece + 2 * SMALL, width), b16)],
+        [like((chunk, width), b16), like((piece + SMALL, width), b16)],
         [pltpu.VMEM((tensors, SMALL, width), f32)],
         flops=40_000_000_000,
         limit=8,

time: 180 us -> 180 us (level)
  no operation moved by 1% of the time
where the time goes in v5:
time: 180 us; the launch traced here: 179 us
  waiting for transfers between devices  55.1 us (31%)
  Pallas kernels  48.6 us (27%)
  starting transfers between devices  44.8 us (25%)
  blocking collectives  28.9 us (16%)
    pallas_call x27, Pallas kernels, kernel_call(): pl.pallas_call(kernel, in_specs=[pl.BlockSpec(memory_space=pltpu.SMEM)] +...  48.6 us
    ppermute x16, waiting for transfers between devices, hop(): return lax.ppermute(value, 'expert', [(i, i ^ bit) for i in range(size)])  28.7 us
    ppermute x17, waiting for transfers between devices, cross(): return lax.ppermute(value, 'tensor', [(i, i ^ bit) for i in range(size)])  26.4 us
    ppermute x16, starting transfers between devices, hop(): return lax.ppermute(value, 'expert', [(i, i ^ bit) for i in range(size)])  23.6 us
    ppermute x17, starting transfers between devices, cross(): return lax.ppermute(value, 'tensor', [(i, i ^ bit) for i in range(size)])  19.7 us
    all_gather x1, blocking collectives, dense_body(): grad_rows = lax.all_gather(grad_chunk, 'tensor', axis=0, tiled=True)  15 us
    all_gather x1, blocking collectives, dense_body(): attn_grad = lax.all_gather(attn_grad, 'tensor', axis=0, tiled=True)  13.9 us
  transfers between devices with their start and end apart: 40, of which 17 were waited for; matrix products, arithmetic and copies ran while one was open for 0% of the time, Pallas kernels for 18%

profile of v5, /device:TPU:0, one launch (start us, length us, event | category | flops | bytes accessed | tf_op | source)
XLA Modules:
  0.0 179.3 jit_solution(6295963519403564759)
XLA Ops:
  0.7 4.1 %chunk.1 = (bf16[152,768]{1,0:T(8,128)(2,1)}, bf16[160,768]{1,0:T(8,128)(2,1)}, f32[8,768]{1,0:T(8,128)}, bf16[2,384,768]{2,1,0:T(8,128)(2,1)}, bf16[2,192,768]{...) custom-call(s32[1]{0:T(128)} %constant.0.clone.1.refs_0_.pos_ref, bf16[3,197,768]{2,1,0:T(8,128)(2,1)} %tok_ref.1, ...), custom_call_target="tpu_custom_call" | custom-call | tf_op jit(solution)/shard_map/chunk/pallas_call | solution.py:307
  4.8 4.1 %collective-permute-start.2 = (bf16[160,768]{1,0:T(8,128)(2,1)}, bf16[160,768]{1,0:T(8,128)(2,1)S(1)}, u32[]{:S(2)}, u32[]{:S(2)}) collective-permute-start(bf16[160,768]{1,0:T(8,128)(2,1)} %get-tuple-element.117.refs_0_.refs_6_), channel_id=1, source_target_pairs={{0,8},{4,12},{8,0},{12,4},{1,9},{5,13},{9,1},{13,5},{2,10},{6,14},... | collective-permute-start | bytes 737288 | tf_op jit(solution)/shard_map/ppermute | solution.py:939
  12.7 4.9 %attention.1 = (bf16[3,3,208,192]{3,2,1,0:T(8,128)(2,1)S(1)}, f32[3,208,128]{2,1,0:T(8,128)S(1)}, bf16[608,192]{1,0:T(8,128)(2,1)S(1)}, bf16[152,768]{1,0:T(8,12...) custom-call(s32[1]{0:T(128)} %constant.0.clone.1.refs_0_.pos_ref, ...), custom_call_target="tpu_custom_call" | custom-call | flops 40000000000 | tf_op jit(solution)/shard_map/attention/pallas_call | solution.py:307
  17.6 6.3 %collective-permute-done.refs_1_.xa_ref = bf16[2,192,768]{2,1,0:T(8,128)(2,1)S(1)} collective-permute-done((bf16[2,192,768]{2,1,0:T(8,128)(2,1)}, bf16[2,192,768]{2,1,0:T(8,128)(2,1)S(1)}, u32[]{:S(2)}, u32[]{:S(2)}) %collective-permute-start) | collective-permute-done | bytes 589856 | tf_op jit(solution)/shard_map/ppermute | solution.py:944
  30.5 4.7 %collective-permute-done.3.refs_1_ = bf16[152,768]{1,0:T(8,128)(2,1)S(1)} collective-permute-done((bf16[152,768]{1,0:T(8,128)(2,1)S(1)}, bf16[152,768]{1,0:T(8,128)(2,1)S(1)}, u32[]{:S(2)}, u32[]{:S(2)}) %collective-permute-start.3) | collective-permute-done | bytes 233504 | tf_op jit(solution)/shard_map/ppermute | solution.py:944
  35.1 1.9 %collective-permute-done.4.refs_2_ = bf16[152,768]{1,0:T(8,128)(2,1)S(1)} collective-permute-done((bf16[152,768]{1,0:T(8,128)(2,1)S(1)}, bf16[152,768]{1,0:T(8,128)(2,1)S(1)}, u32[]{:S(2)}, u32[]{:S(2)}) %collective-permute-start.4) | collective-permute-done | bytes 233504 | tf_op jit(solution)/shard_map/ppermute | solution.py:944
  42.2 2.1 %collective-permute-start.7 = (bf16[152,768]{1,0:T(8,128)(2,1)S(1)}, bf16[152,768]{1,0:T(8,128)(2,1)S(1)}, u32[]{:S(2)}, u32[]{:S(2)}) collective-permute-start(bf16[152,768]{1,0:T(8,128)(2,1)S(1)} %get-tuple-element.123.refs_0_), channel_id=1, source_target_pairs={{0,8},{4,12},{8,0},{12,4},{1,9},{5,13},{9,1},{13,5},{2,10},{6,14},... | collective-permute-start | bytes 700424 | tf_op jit(solution)/shard_map/ppermute | solution.py:939
  44.3 2.3 %collective-permute-start.6 = (bf16[152,768]{1,0:T(8,128)(2,1)S(1)}, bf16[152,768]{1,0:T(8,128)(2,1)S(1)}, u32[]{:S(2)}, u32[]{:S(2)}) collective-permute-start(bf16[152,768]{1,0:T(8,128)(2,1)S(1)} %get-tuple-element.123.refs_0_), channel_id=1, source_target_pairs={{0,4},{4,0},{8,12},{12,8},{1,5},{5,1},{9,13},{13,9},{2,6},{6,2},{1... | collective-permute-start | bytes 700424 | tf_op jit(solution)/shard_map/ppermute | solution.py:939
  46.7 3.1 %collective-permute-done.8.refs_3_ = bf16[152,768]{1,0:T(8,128)(2,1)S(1)} collective-permute-done((bf16[152,768]{1,0:T(8,128)(2,1)S(1)}, bf16[152,768]{1,0:T(8,128)(2,1)S(1)}, u32[]{:S(2)}, u32[]{:S(2)}) %collective-permute-start.8) | collective-permute-done | bytes 233504 | tf_op jit(solution)/shard_map/ppermute | solution.py:939
  49.8 8.9 %collective-permute-done.7.refs_2_ = bf16[152,768]{1,0:T(8,128)(2,1)S(1)} collective-permute-done((bf16[152,768]{1,0:T(8,128)(2,1)S(1)}, bf16[152,768]{1,0:T(8,128)(2,1)S(1)}, u32[]{:S(2)}, u32[]{:S(2)}) %collective-permute-start.7) | collective-permute-done | bytes 233504 | tf_op jit(solution)/shard_map/ppermute | solution.py:939
  58.8 3.7 %experts_first.2 = (bf16[608,768]{1,0:T(8,128)(2,1)S(1)}, bf16[608,768]{1,0:T(8,128)(2,1)S(1)}, bf16[608,768]{1,0:T(8,128)(2,1)S(1)}, f32[608,256]{1,0:T(8,128)S...) custom-call(s32[1]{0:T(128)} %constant.0.clone.1.refs_0_.pos_ref, bf16[608,768]{1,0:T(8,128)(2,1)S(1)} %lay_rows.1.x_ref.refs_1_, ...), custom_call_target="tpu_custom_call" | custom-call | tf_op jit(solution)/shard_map/experts_first/pallas_call | solution.py:307
  62.5 3.7 %experts_first.3 = (bf16[608,768]{1,0:T(8,128)(2,1)S(1)}, bf16[608,768]{1,0:T(8,128)(2,1)S(1)}, bf16[608,768]{1,0:T(8,128)(2,1)S(1)}, f32[608,256]{1,0:T(8,128)S...) custom-call(s32[1]{0:T(128)} %constant.0.clone.1.refs_0_.pos_ref, ...), custom_call_target="tpu_custom_call" | custom-call | tf_op jit(solution)/shard_map/experts_first/pallas_call | solution.py:307
  66.2 3.6 %experts_second.2 = (bf16[608,768]{1,0:T(8,128)(2,1)S(1)}, bf16[608,768]{1,0:T(8,128)(2,1)S(1)}, bf16[608,768]{1,0:T(8,128)(2,1)S(1)}, bf16[608,896]{1,0:T(8,128)(2,1)S(1)}) custom-call(s32[1]{0:T(128)} %constant.0.clone.1.refs_0_.pos_ref, bf16[608,768]{1,0:T(8,128)(2,1)S(1)} %collective-permute-done.10.x_ref.refs_3_, ...), custom_call_target="tpu_custom_call" | custom-call | tf_op jit(solution)/shard_map/experts_second/pallas_call | solution.py:307
  70.4 3.8 %experts_second.3 = (bf16[608,768]{1,0:T(8,128)(2,1)S(1)}, bf16[608,768]{1,0:T(8,128)(2,1)S(1)}, bf16[608,768]{1,0:T(8,128)(2,1)S(1)}, f32[608,896]{1,0:T(8,128)S(1)}) custom-call(s32[1]{0:T(128)} %constant.0.clone.1.refs_0_.pos_ref, bf16[608,768]{1,0:T(8,128)(2,1)S(1)} %lay_rows.1.x_ref.refs_1_, bf16[608,896]{1,0:T(8,128)(2,1)S(1)} %lay_payload.1.pay_ref, ...), custom_call_target="tpu_custom_call" | custom-call | tf_op jit(solution)/shard_map/experts_second/pallas_call | solution.py:307
  75.2 2.1 %collective-permute-start.19 = (bf16[160,768]{1,0:T(8,128)(2,1)S(1)}, bf16[160,768]{1,0:T(8,128)(2,1)S(1)}, u32[]{:S(2)}, u32[]{:S(2)}) collective-permute-start(bf16[160,768]{1,0:T(8,128)(2,1)S(1)} %get-tuple-element.146), channel_id=1, source_target_pairs={{0,8},{4,12},{8,0},{12,4},{1,9},{5,13},{9,1},{13,5},{2,10},{6,14},... | collective-permute-start | bytes 737288 | tf_op jit(solution)/shard_map/ppermute | solution.py:939
  77.3 2.3 %collective-permute-start.20 = (bf16[160,768]{1,0:T(8,128)(2,1)S(1)}, bf16[160,768]{1,0:T(8,128)(2,1)S(1)}, u32[]{:S(2)}, u32[]{:S(2)}) collective-permute-start(bf16[160,768]{1,0:T(8,128)(2,1)S(1)} %get-tuple-element.147), channel_id=1, source_target_pairs={{0,12},{4,8},{8,4},{12,0},{1,13},{5,9},{9,5},{13,1},{2,14},{6,10},... | collective-permute-start | bytes 737288 | tf_op jit(solution)/shard_map/ppermute | solution.py:939
  79.6 2.0 %expert_grads.3 = bf16[2,2,192,768]{3,2,1,0:T(8,128)(2,1)S(1)} custom-call(s32[1]{0:T(128)} %constant.0.clone.1.refs_0_.pos_ref, bf16[608,768]{1,0:T(8,128)(2,1)S(1)} %get-tuple-element.149.refs_0_, bf16[608,768]{1,0:T(8,128)(2,1)S(1)} %lay_rows.1.x_ref.refs_1_, bf16[608,768]{1,0:T(8,128)(2,1)S(1)} %get-tuple-element.150.refs_2_, ...), custom_call_target="tpu_custom_call" | custom-call | tf_op jit(solution)/shard_map/expert_grads/pallas_call | solution.py:307
  82.2 2.0 %expert_grads.4 = bf16[2,2,192,768]{3,2,1,0:T(8,128)(2,1)S(1)} custom-call(s32[1]{0:T(128)} %constant.0.clone.1.refs_0_.pos_ref, bf16[608,768]{1,0:T(8,128)(2,1)S(1)} %get-tuple-element.149.refs_0_, bf16[608,768]{1,0:T(8,128)(2,1)S(1)} %lay_rows.1.x_ref.refs_1_, bf16[608,768]{1,0:T(8,128)(2,1)S(1)} %get-tuple-element.150.refs_2_, ...), custom_call_target="tpu_custom_call" | custom-call | tf_op jit(solution)/shard_map/expert_grads/pallas_call | solution.py:307
  84.9 2.6 %collective-permute-done.18.refs_1_ = bf16[160,768]{1,0:T(8,128)(2,1)S(1)} collective-permute-done((bf16[160,768]{1,0:T(8,128)(2,1)S(1)}, bf16[160,768]{1,0:T(8,128)(2,1)S(1)}, u32[]{:S(2)}, u32[]{:S(2)}) %collective-permute-start.18) | collective-permute-done | bytes 245792 | tf_op jit(solution)/shard_map/ppermute | solution.py:939
  87.5 8.1 %collective-permute-done.19.refs_2_ = bf16[160,768]{1,0:T(8,128)(2,1)S(1)} collective-permute-done((bf16[160,768]{1,0:T(8,128)(2,1)S(1)}, bf16[160,768]{1,0:T(8,128)(2,1)S(1)}, u32[]{:S(2)}, u32[]{:S(2)}) %collective-permute-start.19) | collective-permute-done | bytes 245792 | tf_op jit(solution)/shard_map/ppermute | solution.py:939
  96.3 3.9 %expert_grads.5 = (bf16[2,2,192,768]{3,2,1,0:T(8,128)(2,1)S(1)}, bf16[2,2,192,768]{3,2,1,0:T(8,128)(2,1)S(1)}) custom-call(s32[1]{0:T(128)} %constant.0.clone.1.refs_0_.pos_ref, bf16[608,768]{1,0:T(8,128)(2,1)S(1)} %get-tuple-element.157.refs_0_, bf16[608,768]{1,0:T(8,128)(2,1)S(1)} %lay_rows.1.x_ref.refs_1_, ...), custom_call_target="tpu_custom_call" | custom-call | tf_op jit(solution)/shard_map/expert_grads/pallas_call | solution.py:307
  100.2 4.9 %collective-permute-done.21.got_ref = bf16[2,152,768]{2,1,0:T(8,128)(2,1)S(1)} collective-permute-done((bf16[2,152,768]{2,1,0:T(8,128)(2,1)S(1)}, bf16[2,152,768]{2,1,0:T(8,128)(2,1)S(1)}, u32[]{:S(2)}, u32[]{:S(2)}) %collective-permute-start.21) | collective-permute-done | bytes 466976 | tf_op jit(solution)/shard_map/ppermute | solution.py:939
  105.7 13.9 %all_gather.6.up_ref = bf16[608,768]{1,0:T(8,128)(2,1)S(1)} all-gather(bf16[152,768]{1,0:T(8,128)(2,1)S(1)} %get-tuple-element.173), channel_id=1, replica_groups=mesh['dp'=2,'expert'=4,'tensor'=4] {'tensor'}, dimensions={0}, use_global_device_ids=true | all-gather | bytes 1167360 | tf_op jit(solution)/shard_map/all_gather | solution.py:1120
  119.7 5.9 %attention_back.1 = (f32[4,96,768]{2,1,0:T(8,128)S(1)}, bf16[4,96,768]{2,1,0:T(8,128)(2,1)S(1)}, bf16[160,768]{1,0:T(8,128)(2,1)S(1)}, bf16[160,768]{1,0:T(8,128...) custom-call(s32[1]{0:T(128)} %constant.0.clone.1.refs_0_.pos_ref, ...), custom_call_target="tpu_custom_call" | custom-call | flops 6000000000 | tf_op jit(solution)/shard_map/attention_back/pallas_call | solution.py:307
  129.5 2.0 %collective-permute-start.28 = (bf16[96,768]{1,0:T(8,128)(2,1)S(1)}, bf16[96,768]{1,0:T(8,128)(2,1)S(1)}, u32[]{:S(2)}, u32[]{:S(2)}) collective-permute-start(bf16[96,768]{1,0:T(8,128)(2,1)S(1)} %get-tuple-element.184), channel_id=1, source_target_pairs={{0,8},{4,12},{8,0},{12,4},{1,9},{5,13},{9,1},{13,5},{2,10},{6,14},... | collective-permute-start | bytes 442376 | tf_op jit(solution)/shard_map/ppermute | solution.py:939
  131.5 2.9 %collective-permute-done.23.refs_1_ = bf16[160,768]{1,0:T(8,128)(2,1)S(1)} collective-permute-done((bf16[160,768]{1,0:T(8,128)(2,1)S(1)}, bf16[160,768]{1,0:T(8,128)(2,1)S(1)}, u32[]{:S(2)}, u32[]{:S(2)}) %collective-permute-start.23) | collective-permute-done | bytes 245792 | tf_op jit(solution)/shard_map/ppermute | solution.py:944
  136.3 2.4 %collective-permute-done.24.refs_2_ = bf16[160,768]{1,0:T(8,128)(2,1)S(1)} collective-permute-done((bf16[160,768]{1,0:T(8,128)(2,1)S(1)}, bf16[160,768]{1,0:T(8,128)(2,1)S(1)}, u32[]{:S(2)}, u32[]{:S(2)}) %collective-permute-start.24) | collective-permute-done | bytes 245792 | tf_op jit(solution)/shard_map/ppermute | solution.py:944
  145.0 2.8 %collective-permute-start.31 = (bf16[104,768]{1,0:T(8,128)(2,1)S(1)}, bf16[104,768]{1,0:T(8,128)(2,1)S(1)}, u32[]{:S(2)}, u32[]{:S(2)}) collective-permute-start(bf16[104,768]{1,0:T(8,128)(2,1)S(1)} %get-tuple-element.187.refs_0_), channel_id=1, source_target_pairs={{0,8},{4,12},{8,0},{12,4},{1,9},{5,13},{9,1},{13,5},{2,10},{6,14},... | collective-permute-start | bytes 479240 | tf_op jit(solution)/shard_map/ppermute | solution.py:939
  148.2 15.0 %all_gather.7.refs_0_ = bf16[608,768]{1,0:T(8,128)(2,1)S(1)} all-gather(bf16[152,768]{1,0:T(8,128)(2,1)S(1)} %get-tuple-element.186), channel_id=1, replica_groups=mesh['dp'=2,'expert'=4,'tensor'=4] {'tensor'}, dimensions={0}, use_global_device_ids=true | all-gather | bytes 1167360 | tf_op jit(solution)/shard_map/all_gather | solution.py:1177
  165.7 1.8 collective-permute-start.38
  171.1 2.6 %weight_out.1 = (f32[1,768,768]{2,1,0:T(8,128)}, f32[1,768,768]{2,1,0:T(8,128)}) custom-call(s32[1]{0:T(128)} %constant.0.clone.1.refs_0_.pos_ref, bf16[2,384,768]{2,1,0:T(8,128)(2,1)S(1)} %weight_sum.1.mine_ref, bf16[2,384,768]{2,1,0:T(8,128)(2,1)S(1)} %collective-permute-done.35.other_ref), custom_call_target="tpu_custom_call" | custom-call | tf_op jit(solution)/shard_map/weight_out/pallas_call | solution.py:307
  173.9 4.0 %collective-permute-done.38.refs_2_ = bf16[152,768]{1,0:T(8,128)(2,1)S(1)} collective-permute-done((bf16[152,768]{1,0:T(8,128)(2,1)S(1)}, bf16[152,768]{1,0:T(8,128)(2,1)S(1)}, u32[]{:S(2)}, u32[]{:S(2)}) %collective-permute-start.38) | collective-permute-done | bytes 233504 | tf_op jit(solution)/shard_map/ppermute | solution.py:944
  (98 shorter events, 40.1 us)
Async XLA Ops:
  4.8 20.5 %collective-permute-start.2 = (bf16[160,768]{1,0:T(8,128)(2,1)}, bf16[160,768]{1,0:T(8,128)(2,1)S(1)}, u32[]{:S(2)}, u32[]{:S(2)}) collective-permute-start(bf16[160,768]{1,0:T(8,128)(2,1)} %get-tuple-element.117.refs_0_.refs_6_), channel_id=1, source_target_pairs={{0,8},{4,12},{8,0},{12,4},{1,9},{5,13},{9,1},{13,5},{2,10},{6,14},... | collective-permute-start | bytes 737288 | tf_op jit(solution)/shard_map/ppermute | solution.py:939
  8.9 15.0 %collective-permute-start = (bf16[2,192,768]{2,1,0:T(8,128)(2,1)}, bf16[2,192,768]{2,1,0:T(8,128)(2,1)S(1)}, u32[]{:S(2)}, u32[]{:S(2)}) collective-permute-start(bf16[2,192,768]{2,1,0:T(8,128)(2,1)} %get-tuple-element.113.refs_0_), channel_id=1, source_target_pairs={{0,1},{1,0},{2,3},{3,2},{4,5},{5,4},{6,7},{7,6},{8,9},{9,8},{10,11... | collective-permute-start | bytes 1769480 | tf_op jit(solution)/shard_map/ppermute | solution.py:944
  10.4 14.7 %collective-permute-start.1 = (bf16[2,192,768]{2,1,0:T(8,128)(2,1)}, bf16[2,192,768]{2,1,0:T(8,128)(2,1)S(1)}, u32[]{:S(2)}, u32[]{:S(2)}) collective-permute-start(bf16[2,192,768]{2,1,0:T(8,128)(2,1)} %get-tuple-element.114.refs_2_), channel_id=1, source_target_pairs={{0,2},{1,3},{2,0},{3,1},{4,6},{5,7},{6,4},{7,5},{8,10},{9,11},{10,... | collective-permute-start | bytes 1769480 | tf_op jit(solution)/shard_map/ppermute | solution.py:944
  25.3 18.9 %collective-permute-start.9 = (bf16[2,160,768]{2,1,0:T(8,128)(2,1)S(1)}, bf16[2,160,768]{2,1,0:T(8,128)(2,1)S(1)}, u32[]{:S(2)}, u32[]{:S(2)}) collective-permute-start(bf16[2,160,768]{2,1,0:T(8,128)(2,1)S(1)} %stack.3.near_ref), channel_id=1, source_target_pairs={{0,4},{4,0},{8,12},{12,8},{1,5},{5,1},{9,13},{13,9},{2,6},{6,2},{1... | collective-permute-start | bytes 1474568 | tf_op jit(solution)/shard_map/ppermute | solution.py:939
  27.5 9.5 %collective-permute-start.4 = (bf16[152,768]{1,0:T(8,128)(2,1)S(1)}, bf16[152,768]{1,0:T(8,128)(2,1)S(1)}, u32[]{:S(2)}, u32[]{:S(2)}) collective-permute-start(bf16[152,768]{1,0:T(8,128)(2,1)S(1)} %get-tuple-element.120), channel_id=1, source_target_pairs={{0,2},{1,3},{2,0},{3,1},{4,6},{5,7},{6,4},{7,5},{8,10},{9,11},{10,... | collective-permute-start | bytes 700424 | tf_op jit(solution)/shard_map/ppermute | solution.py:944
  29.0 9.6 %collective-permute-start.5 = (bf16[152,768]{1,0:T(8,128)(2,1)S(1)}, bf16[152,768]{1,0:T(8,128)(2,1)S(1)}, u32[]{:S(2)}, u32[]{:S(2)}) collective-permute-start(bf16[152,768]{1,0:T(8,128)(2,1)S(1)} %get-tuple-element.121), channel_id=1, source_target_pairs={{0,3},{1,2},{2,1},{3,0},{4,7},{5,6},{6,5},{7,4},{8,11},{9,10},{10,... | collective-permute-start | bytes 700424 | tf_op jit(solution)/shard_map/ppermute | solution.py:944
  39.3 10.5 %collective-permute-start.8 = (bf16[152,768]{1,0:T(8,128)(2,1)S(1)}, bf16[152,768]{1,0:T(8,128)(2,1)S(1)}, u32[]{:S(2)}, u32[]{:S(2)}) collective-permute-start(bf16[152,768]{1,0:T(8,128)(2,1)S(1)} %get-tuple-element.123.refs_0_), channel_id=1, source_target_pairs={{0,12},{4,8},{8,4},{12,0},{1,13},{5,9},{9,5},{13,1},{2,14},{6,10},... | collective-permute-start | bytes 700424 | tf_op jit(solution)/shard_map/ppermute | solution.py:939
  39.6 26.6 %collective-permute-start.12 = (bf16[2,2,192,768]{3,2,1,0:T(8,128)(2,1)S(1)}, bf16[2,2,192,768]{3,2,1,0:T(8,128)(2,1)S(1)}, u32[]{:S(2)}, u32[]{:S(2)}) collective-permute-start(bf16[2,2,192,768]{3,2,1,0:T(8,128)(2,1)S(1)} %get-tuple-element.133), channel_id=1, source_target_pairs={{0,2},{1,3},{2,0},{3,1},{4,6},{5,7},{6,4},{7,5},{8,10},{9,11},{10,... | collective-permute-start | bytes 3538952 | tf_op jit(solution)/shard_map/ppermute | solution.py:944
  40.5 25.8 %collective-permute-start.13 = (bf16[2,2,192,768]{3,2,1,0:T(8,128)(2,1)S(1)}, bf16[2,2,192,768]{3,2,1,0:T(8,128)(2,1)S(1)}, u32[]{:S(2)}, u32[]{:S(2)}) collective-permute-start(bf16[2,2,192,768]{3,2,1,0:T(8,128)(2,1)S(1)} %get-tuple-element.134), channel_id=1, source_target_pairs={{0,1},{1,0},{2,3},{3,2},{4,5},{5,4},{6,7},{7,6},{8,9},{9,8},{10,11... | collective-permute-start | bytes 3538952 | tf_op jit(solution)/shard_map/ppermute | solution.py:944
  42.2 16.5 %collective-permute-start.7 = (bf16[152,768]{1,0:T(8,128)(2,1)S(1)}, bf16[152,768]{1,0:T(8,128)(2,1)S(1)}, u32[]{:S(2)}, u32[]{:S(2)}) collective-permute-start(bf16[152,768]{1,0:T(8,128)(2,1)S(1)} %get-tuple-element.123.refs_0_), channel_id=1, source_target_pairs={{0,8},{4,12},{8,0},{12,4},{1,9},{5,13},{9,1},{13,5},{2,10},{6,14},... | collective-permute-start | bytes 700424 | tf_op jit(solution)/shard_map/ppermute | solution.py:939
  44.3 14.4 %collective-permute-start.6 = (bf16[152,768]{1,0:T(8,128)(2,1)S(1)}, bf16[152,768]{1,0:T(8,128)(2,1)S(1)}, u32[]{:S(2)}, u32[]{:S(2)}) collective-permute-start(bf16[152,768]{1,0:T(8,128)(2,1)S(1)} %get-tuple-element.123.refs_0_), channel_id=1, source_target_pairs={{0,4},{4,0},{8,12},{12,8},{1,5},{5,1},{9,13},{13,9},{2,6},{6,2},{1... | collective-permute-start | bytes 700424 | tf_op jit(solution)/shard_map/ppermute | solution.py:939
  49.8 12.8 %collective-permute-start.11 = (bf16[608,896]{1,0:T(8,128)(2,1)S(1)}, bf16[608,896]{1,0:T(8,128)(2,1)S(1)}, u32[]{:S(2)}, u32[]{:S(2)}) collective-permute-start(bf16[608,896]{1,0:T(8,128)(2,1)S(1)} %lay_payload.1.pay_ref), channel_id=1, source_target_pairs={{0,16},{16,0},{1,17},{17,1},{2,18},{18,2},{3,19},{19,3},{4,20},{20... | collective-permute-start | bytes 3268616 | tf_op jit(solution)/shard_map/ppermute | solution.py:934
  75.1 12.4 %collective-permute-start.18 = (bf16[160,768]{1,0:T(8,128)(2,1)S(1)}, bf16[160,768]{1,0:T(8,128)(2,1)S(1)}, u32[]{:S(2)}, u32[]{:S(2)}) collective-permute-start(bf16[160,768]{1,0:T(8,128)(2,1)S(1)} %get-tuple-element.145), channel_id=1, source_target_pairs={{0,4},{4,0},{8,12},{12,8},{1,5},{5,1},{9,13},{13,9},{2,6},{6,2},{1... | collective-permute-start | bytes 737288 | tf_op jit(solution)/shard_map/ppermute | solution.py:939
  75.2 20.4 %collective-permute-start.19 = (bf16[160,768]{1,0:T(8,128)(2,1)S(1)}, bf16[160,768]{1,0:T(8,128)(2,1)S(1)}, u32[]{:S(2)}, u32[]{:S(2)}) collective-permute-start(bf16[160,768]{1,0:T(8,128)(2,1)S(1)} %get-tuple-element.146), channel_id=1, source_target_pairs={{0,8},{4,12},{8,0},{12,4},{1,9},{5,13},{9,1},{13,5},{2,10},{6,14},... | collective-permute-start | bytes 737288 | tf_op jit(solution)/shard_map/ppermute | solution.py:939
  77.3 18.2 %collective-permute-start.20 = (bf16[160,768]{1,0:T(8,128)(2,1)S(1)}, bf16[160,768]{1,0:T(8,128)(2,1)S(1)}, u32[]{:S(2)}, u32[]{:S(2)}) collective-permute-start(bf16[160,768]{1,0:T(8,128)(2,1)S(1)} %get-tuple-element.147), channel_id=1, source_target_pairs={{0,12},{4,8},{8,4},{12,0},{1,13},{5,9},{9,5},{13,1},{2,14},{6,10},... | collective-permute-start | bytes 737288 | tf_op jit(solution)/shard_map/ppermute | solution.py:939
  81.6 38.0 %collective-permute-start.16 = (bf16[2,2,192,768]{3,2,1,0:T(8,128)(2,1)S(1)}, bf16[2,2,192,768]{3,2,1,0:T(8,128)(2,1)S(1)}, u32[]{:S(2)}, u32[]{:S(2)}) collective-permute-start(bf16[2,2,192,768]{3,2,1,0:T(8,128)(2,1)S(1)} %expert_grads.3), channel_id=1, source_target_pairs={{0,2},{1,3},{2,0},{3,1},{4,6},{5,7},{6,4},{7,5},{8,10},{9,11},{10,... | collective-permute-start | bytes 3538952 | tf_op jit(solution)/shard_map/ppermute | solution.py:944
  84.3 35.4 %collective-permute-start.17 = (bf16[2,2,192,768]{3,2,1,0:T(8,128)(2,1)S(1)}, bf16[2,2,192,768]{3,2,1,0:T(8,128)(2,1)S(1)}, u32[]{:S(2)}, u32[]{:S(2)}) collective-permute-start(bf16[2,2,192,768]{3,2,1,0:T(8,128)(2,1)S(1)} %expert_grads.4), channel_id=1, source_target_pairs={{0,1},{1,0},{2,3},{3,2},{4,5},{5,4},{6,7},{7,6},{8,9},{9,8},{10,11... | collective-permute-start | bytes 3538952 | tf_op jit(solution)/shard_map/ppermute | solution.py:944
  87.5 17.6 %collective-permute-start.21 = (bf16[2,152,768]{2,1,0:T(8,128)(2,1)S(1)}, bf16[2,152,768]{2,1,0:T(8,128)(2,1)S(1)}, u32[]{:S(2)}, u32[]{:S(2)}) collective-permute-start(bf16[2,152,768]{2,1,0:T(8,128)(2,1)S(1)} %get-tuple-element.166), channel_id=1, source_target_pairs={{0,4},{4,0},{8,12},{12,8},{1,5},{5,1},{9,13},{13,9},{2,6},{6,2},{1... | collective-permute-start | bytes 1400840 | tf_op jit(solution)/shard_map/ppermute | solution.py:939
  105.2 14.4 %collective-permute-start.22 = (bf16[152,768]{1,0:T(8,128)(2,1)S(1)}, bf16[152,768]{1,0:T(8,128)(2,1)S(1)}, u32[]{:S(2)}, u32[]{:S(2)}) collective-permute-start(bf16[152,768]{1,0:T(8,128)(2,1)S(1)} %get-tuple-element.168), channel_id=1, source_target_pairs={{0,8},{4,12},{8,0},{12,4},{1,9},{5,13},{9,1},{13,5},{2,10},{6,14},... | collective-permute-start | bytes 700424 | tf_op jit(solution)/shard_map/ppermute | solution.py:939
  125.6 8.8 %collective-permute-start.23 = (bf16[160,768]{1,0:T(8,128)(2,1)S(1)}, bf16[160,768]{1,0:T(8,128)(2,1)S(1)}, u32[]{:S(2)}, u32[]{:S(2)}) collective-permute-start(bf16[160,768]{1,0:T(8,128)(2,1)S(1)} %get-tuple-element.176), channel_id=1, source_target_pairs={{0,1},{1,0},{2,3},{3,2},{4,5},{5,4},{6,7},{7,6},{8,9},{9,8},{10,11... | collective-permute-start | bytes 737288 | tf_op jit(solution)/shard_map/ppermute | solution.py:944
  126.4 12.3 %collective-permute-start.24 = (bf16[160,768]{1,0:T(8,128)(2,1)S(1)}, bf16[160,768]{1,0:T(8,128)(2,1)S(1)}, u32[]{:S(2)}, u32[]{:S(2)}) collective-permute-start(bf16[160,768]{1,0:T(8,128)(2,1)S(1)} %get-tuple-element.177), channel_id=1, source_target_pairs={{0,2},{1,3},{2,0},{3,1},{4,6},{5,7},{6,4},{7,5},{8,10},{9,11},{10,... | collective-permute-start | bytes 737288 | tf_op jit(solution)/shard_map/ppermute | solution.py:944
  127.9 11.8 %collective-permute-start.25 = (bf16[160,768]{1,0:T(8,128)(2,1)S(1)}, bf16[160,768]{1,0:T(8,128)(2,1)S(1)}, u32[]{:S(2)}, u32[]{:S(2)}) collective-permute-start(bf16[160,768]{1,0:T(8,128)(2,1)S(1)} %get-tuple-element.178), channel_id=1, source_target_pairs={{0,3},{1,2},{2,1},{3,0},{4,7},{5,6},{6,5},{7,4},{8,11},{9,10},{10,... | collective-permute-start | bytes 737288 | tf_op jit(solution)/shard_map/ppermute | solution.py:944
  129.3 12.6 %collective-permute-start.27 = (bf16[96,768]{1,0:T(8,128)(2,1)S(1)}, bf16[96,768]{1,0:T(8,128)(2,1)S(1)}, u32[]{:S(2)}, u32[]{:S(2)}) collective-permute-start(bf16[96,768]{1,0:T(8,128)(2,1)S(1)} %get-tuple-element.183), channel_id=1, source_target_pairs={{0,4},{4,0},{8,12},{12,8},{1,5},{5,1},{9,13},{13,9},{2,6},{6,2},{1... | collective-permute-start | bytes 442376 | tf_op jit(solution)/shard_map/ppermute | solution.py:939
  129.5 13.7 %collective-permute-start.28 = (bf16[96,768]{1,0:T(8,128)(2,1)S(1)}, bf16[96,768]{1,0:T(8,128)(2,1)S(1)}, u32[]{:S(2)}, u32[]{:S(2)}) collective-permute-start(bf16[96,768]{1,0:T(8,128)(2,1)S(1)} %get-tuple-element.184), channel_id=1, source_target_pairs={{0,8},{4,12},{8,0},{12,4},{1,9},{5,13},{9,1},{13,5},{2,10},{6,14},... | collective-permute-start | bytes 442376 | tf_op jit(solution)/shard_map/ppermute | solution.py:939
  139.7 23.5 %collective-permute-start.33 = (bf16[2,192,768]{2,1,0:T(8,128)(2,1)S(1)}, bf16[2,192,768]{2,1,0:T(8,128)(2,1)S(1)}, u32[]{:S(2)}, u32[]{:S(2)}) collective-permute-start(bf16[2,192,768]{2,1,0:T(8,128)(2,1)S(1)} %get-tuple-element.193), channel_id=1, source_target_pairs={{0,1},{1,0},{2,3},{3,2},{4,5},{5,4},{6,7},{7,6},{8,9},{9,8},{10,11... | collective-permute-start | bytes 1769480 | tf_op jit(solution)/shard_map/ppermute | solution.py:944
  141.0 22.2 %collective-permute-start.34 = (bf16[2,192,768]{2,1,0:T(8,128)(2,1)S(1)}, bf16[2,192,768]{2,1,0:T(8,128)(2,1)S(1)}, u32[]{:S(2)}, u32[]{:S(2)}) collective-permute-start(bf16[2,192,768]{2,1,0:T(8,128)(2,1)S(1)} %get-tuple-element.194), channel_id=1, source_target_pairs={{0,2},{1,3},{2,0},{3,1},{4,6},{5,7},{6,4},{7,5},{8,10},{9,11},{10,... | collective-permute-start | bytes 1769480 | tf_op jit(solution)/shard_map/ppermute | solution.py:944
  143.7 19.5 %collective-permute-start.32 = (bf16[104,768]{1,0:T(8,128)(2,1)S(1)}, bf16[104,768]{1,0:T(8,128)(2,1)S(1)}, u32[]{:S(2)}, u32[]{:S(2)}) collective-permute-start(bf16[104,768]{1,0:T(8,128)(2,1)S(1)} %get-tuple-element.187.refs_0_), channel_id=1, source_target_pairs={{0,12},{4,8},{8,4},{12,0},{1,13},{5,9},{9,5},{13,1},{2,14},{6,10},... | collective-permute-start | bytes 479240 | tf_op jit(solution)/shard_map/ppermute | solution.py:939
  145.0 18.2 %collective-permute-start.31 = (bf16[104,768]{1,0:T(8,128)(2,1)S(1)}, bf16[104,768]{1,0:T(8,128)(2,1)S(1)}, u32[]{:S(2)}, u32[]{:S(2)}) collective-permute-start(bf16[104,768]{1,0:T(8,128)(2,1)S(1)} %get-tuple-element.187.refs_0_), channel_id=1, source_target_pairs={{0,8},{4,12},{8,0},{12,4},{1,9},{5,13},{9,1},{13,5},{2,10},{6,14},... | collective-permute-start | bytes 479240 | tf_op jit(solution)/shard_map/ppermute | solution.py:939
  147.9 15.3 %collective-permute-start.30 = (bf16[104,768]{1,0:T(8,128)(2,1)S(1)}, bf16[104,768]{1,0:T(8,128)(2,1)S(1)}, u32[]{:S(2)}, u32[]{:S(2)}) collective-permute-start(bf16[104,768]{1,0:T(8,128)(2,1)S(1)} %get-tuple-element.187.refs_0_), channel_id=1, source_target_pairs={{0,4},{4,0},{8,12},{12,8},{1,5},{5,1},{9,13},{13,9},{2,6},{6,2},{1... | collective-permute-start | bytes 479240 | tf_op jit(solution)/shard_map/ppermute | solution.py:939
  164.4 9.6 %collective-permute-start.39 = (bf16[152,768]{1,0:T(8,128)(2,1)S(1)}, bf16[152,768]{1,0:T(8,128)(2,1)S(1)}, u32[]{:S(2)}, u32[]{:S(2)}) collective-permute-start(bf16[152,768]{1,0:T(8,128)(2,1)S(1)} %add_convert_fusion.refs_0_), channel_id=1, source_target_pairs={{0,3},{1,2},{2,1},{3,0},{4,7},{5,6},{6,5},{7,4},{8,11},{9,10},{10,... | collective-permute-start | bytes 700424 | tf_op jit(solution)/shard_map/ppermute | solution.py:944
  165.7 12.2 %collective-permute-start.38 = (bf16[152,768]{1,0:T(8,128)(2,1)S(1)}, bf16[152,768]{1,0:T(8,128)(2,1)S(1)}, u32[]{:S(2)}, u32[]{:S(2)}) collective-permute-start(bf16[152,768]{1,0:T(8,128)(2,1)S(1)} %add_convert_fusion.refs_0_), channel_id=1, source_target_pairs={{0,2},{1,3},{2,0},{3,1},{4,6},{5,7},{6,4},{7,5},{8,10},{9,11},{10,... | collective-permute-start | bytes 700424 | tf_op jit(solution)/shard_map/ppermute | solution.py:944
  167.5 10.6 %collective-permute-start.37 = (bf16[152,768]{1,0:T(8,128)(2,1)S(1)}, bf16[152,768]{1,0:T(8,128)(2,1)S(1)}, u32[]{:S(2)}, u32[]{:S(2)}) collective-permute-start(bf16[152,768]{1,0:T(8,128)(2,1)S(1)} %add_convert_fusion.refs_0_), channel_id=1, source_target_pairs={{0,1},{1,0},{2,3},{3,2},{4,5},{5,4},{6,7},{7,6},{8,9},{9,8},{10,11... | collective-permute-start | bytes 700424 | tf_op jit(solution)/shard_map/ppermute | solution.py:944
  (18 other events, 149.8 us)

commit v6 on v5

--- a/solution.py
+++ b/solution.py
@@ -359,7 +359,7 @@
 
 def chunk_kernel(
     tensors, arrive, pos_ref, tok_ref, cot_ref, ids_ref, rank_ref, router_ref, one_ref, two_ref, in_ref, out_ref,
-    x_ref, pay_ref, param_ref, mine_ref, first_ref, second_ref, flat_ref, kept_ref,
+    x_ref, pay_ref, param_ref, first_ref, second_ref, flat_ref, kept_ref,
 ):
     images, seq_len, width = tok_ref.shape
     chunk, experts = x_ref.shape[0], router_ref.shape[0]
@@ -405,10 +405,9 @@
     param_ref[experts + 1 : experts + 2, :] = two_ref[...].reshape(1, width)
     param_ref[SMALL - 1 : SMALL, :LANES] = counts * (1.0 / tensors)
     arrive(7, 8)
-    half = mine_ref.shape[1]
+    half = 2 * first_ref.shape[1]
     core = pl.multiple_of(lax.axis_index("dp") * half, LANES)
     for s, part in ((0, in_ref[0, :, pl.ds(core, half)].T), (1, out_ref[0, pl.ds(core, half), :])):
-        mine_ref[s] = part
         first_ref[s] = part[0 : half // 2]
         second_ref[s] = part[half // 2 :]
 
@@ -568,7 +567,8 @@
 
 
 def first_expert_kernel(
-    experts, pos_ref, x_ref, pay_ref, param_ref, w0_ref, xa_ref, yb_ref, hidden_ref, pre_ref, rg_ref,
+    experts, pos_ref, x_ref, pay_ref, param_ref, wa_ref, wb_ref, xa_ref, yb_ref, hidden_ref,
+    pre_ref, rg_ref,
     gate_ref, part_ref, back_ref,
 ):
     count, width = x_ref.shape
@@ -581,7 +581,8 @@
     gate_ref[:, LANES:] = jnp.broadcast_to(kept, (count, LANES))
     rg_ref[...] = (gate * pay_ref[:, :width].astype(jnp.float32)).astype(jnp.bfloat16)
     w_in, w_out = (
-        jnp.concatenate([w0_ref[s], xa_ref[s], yb_ref[s]], axis=0) for s in range(2)
+        jnp.concatenate([ref[s] for ref in (wa_ref, wb_ref, xa_ref, yb_ref)], axis=0)
+        for s in range(2)
     )
     part_ref[...], back_ref[...] = expert_halves(
         x_ref[...], rg_ref[...], w_in, w_out, hidden_ref, pre_ref
@@ -612,7 +613,7 @@
 
 def first_expert_pass(position, rows, payload, params, weights, experts):
     count, width = rows.shape
-    hidden = 2 * weights[0].shape[1]
+    hidden = 4 * weights[0].shape[1]
     return kernel_call(
         functools.partial(first_expert_kernel, experts),
         "experts_first",
@@ -979,7 +980,7 @@
     position = jnp.zeros((1,), jnp.int32)
     weight_rows = qkv_weight.transpose(0, 2, 1).reshape(3 * local, width)
 
-    x_chunk, payload, params, mine, first, second = kernel_call(
+    x_chunk, payload, params, first, second = kernel_call(
         functools.partial(chunk_kernel, tensors),
         "chunk",
         position,
@@ -998,7 +999,6 @@
             like((chunk, width), b16),
             like((chunk + SMALL, width), b16),
             like((SMALL, width), f32),
-            like((2, half, width), b16),
             like((2, quarter, width), b16),
             like((2, quarter, width), b16),
         ],
@@ -1016,7 +1016,7 @@
     qkv, lse, attended, *parts = kernel_call(
         functools.partial(attention_kernel, heads, experts),
         "attention",
-        after(position, mine),
+        after(position, first),
         [tokens, params, weight_rows, out_weight],
         [
             like((3, images, rows, local), b16),
@@ -1064,7 +1064,8 @@
     rows_mine = lay_rows(position, "lay_rows", blocks)
     rows_other = swap_core(rows_mine)
 
-    near_weights, far_weights = (mine, first_x, second_y), (pair_y, pair_x)
+    near_weights = (first, second, first_x, second_y)
+    far_weights = (pair_y, pair_x)
     first_a = first_expert_pass(position, rows_mine, payload_mine, params, near_weights, experts)
     first_b = first_expert_pass(
         after(position, first_a[2]), rows_other, payload_other, params, near_weights, experts

time: 180 us -> 179 us (level)
    ppermute x17, waiting for transfers between devices: 26.4 us -> 28.3 us  [cross(): return lax.ppermute(value, 'tensor', [(i, i ^ bit) for i in range(size)])]
  transfers between devices with their start and end apart: 40 -> 40, of which waited for: 17 -> 15; matrix products, arithmetic and copies ran while one was open for 0% -> 0% of each run, Pallas kernels for 18% -> 18%
where the time goes in v6:
time: 179 us
  waiting for transfers between devices  55.7 us (31%)
  Pallas kernels  47.9 us (27%)
  starting transfers between devices  44.4 us (25%)
  blocking collectives  28.7 us (16%)
    pallas_call x27, Pallas kernels, kernel_call(): pl.pallas_call(kernel, in_specs=[pl.BlockSpec(memory_space=pltpu.SMEM)] +...  47.9 us
    ppermute x17, waiting for transfers between devices, cross(): return lax.ppermute(value, 'tensor', [(i, i ^ bit) for i in range(size)])  28.3 us
    ppermute x16, waiting for transfers between devices, hop(): return lax.ppermute(value, 'expert', [(i, i ^ bit) for i in range(size)])  27.4 us
    ppermute x16, starting transfers between devices, hop(): return lax.ppermute(value, 'expert', [(i, i ^ bit) for i in range(size)])  23 us
    ppermute x17, starting transfers between devices, cross(): return lax.ppermute(value, 'tensor', [(i, i ^ bit) for i in range(size)])  20 us
    all_gather x1, blocking collectives, dense_body(): grad_rows = lax.all_gather(grad_chunk, 'tensor', axis=0, tiled=True)  14.5 us
    all_gather x1, blocking collectives, dense_body(): attn_grad = lax.all_gather(attn_grad, 'tensor', axis=0, tiled=True)  14.3 us
  transfers between devices with their start and end apart: 40, of which 15 were waited for; matrix products, arithmetic and copies ran while one was open for 0% of the time, Pallas kernels for 18%

profile of v6, /device:TPU:0, one launch (start us, length us, event | category | flops | bytes accessed | tf_op | source)
XLA Modules:
  0.0 178.7 jit_solution(8967213504837061320)
XLA Ops:
  0.7 3.7 %chunk.1 = (bf16[152,768]{1,0:T(8,128)(2,1)}, bf16[160,768]{1,0:T(8,128)(2,1)}, f32[8,768]{1,0:T(8,128)}, bf16[2,192,768]{2,1,0:T(8,128)(2,1)}, bf16[2,192,768]{2,1,0:T(8,128)(2,1)}) custom-call(s32[1]{0:T(128)} %constant.0.clone.1.refs_0_.pos_ref, bf16[3,197,768]{2,1,0:T(8,128)(2,1)} %tok_ref.1, bf16[3,197,768]{2,1,0:T(8,128)(2,1)} %refs_2_.1, ...), custom_call_target="tpu_custom_call" | custom-call | tf_op jit(solution)/shard_map/chunk/pallas_call | solution.py:307
  4.4 4.1 %collective-permute-start.2 = (bf16[160,768]{1,0:T(8,128)(2,1)}, bf16[160,768]{1,0:T(8,128)(2,1)S(1)}, u32[]{:S(2)}, u32[]{:S(2)}) collective-permute-start(bf16[160,768]{1,0:T(8,128)(2,1)} %get-tuple-element.115.refs_0_.refs_6_), channel_id=1, source_target_pairs={{0,8},{4,12},{8,0},{12,4},{1,9},{5,13},{9,1},{13,5},{2,10},{6,14},... | collective-permute-start | bytes 737288 | tf_op jit(solution)/shard_map/ppermute | solution.py:940
  12.2 4.7 %attention.1 = (bf16[3,3,208,192]{3,2,1,0:T(8,128)(2,1)S(1)}, f32[3,208,128]{2,1,0:T(8,128)S(1)}, bf16[608,192]{1,0:T(8,128)(2,1)S(1)}, bf16[152,768]{1,0:T(8,12...) custom-call(s32[1]{0:T(128)} %constant.0.clone.1.refs_0_.pos_ref, ...), custom_call_target="tpu_custom_call" | custom-call | flops 40000000000 | tf_op jit(solution)/shard_map/attention/pallas_call | solution.py:307
  17.0 6.5 %collective-permute-done.1.refs_3_.yb_ref = bf16[2,192,768]{2,1,0:T(8,128)(2,1)S(1)} collective-permute-done((bf16[2,192,768]{2,1,0:T(8,128)(2,1)}, bf16[2,192,768]{2,1,0:T(8,128)(2,1)S(1)}, u32[]{:S(2)}, u32[]{:S(2)}) %collective-permute-start.1) | collective-permute-done | bytes 589856 | tf_op jit(solution)/shard_map/ppermute | solution.py:945
  30.1 4.7 %collective-permute-done.3.refs_1_ = bf16[152,768]{1,0:T(8,128)(2,1)S(1)} collective-permute-done((bf16[152,768]{1,0:T(8,128)(2,1)S(1)}, bf16[152,768]{1,0:T(8,128)(2,1)S(1)}, u32[]{:S(2)}, u32[]{:S(2)}) %collective-permute-start.3) | collective-permute-done | bytes 233504 | tf_op jit(solution)/shard_map/ppermute | solution.py:945
  34.7 4.2 %collective-permute-done.4.refs_2_ = bf16[152,768]{1,0:T(8,128)(2,1)S(1)} collective-permute-done((bf16[152,768]{1,0:T(8,128)(2,1)S(1)}, bf16[152,768]{1,0:T(8,128)(2,1)S(1)}, u32[]{:S(2)}, u32[]{:S(2)}) %collective-permute-start.4) | collective-permute-done | bytes 233504 | tf_op jit(solution)/shard_map/ppermute | solution.py:945
  41.2 1.6 collective-permute-start.7
  42.8 2.5 %collective-permute-start.6 = (bf16[152,768]{1,0:T(8,128)(2,1)S(1)}, bf16[152,768]{1,0:T(8,128)(2,1)S(1)}, u32[]{:S(2)}, u32[]{:S(2)}) collective-permute-start(bf16[152,768]{1,0:T(8,128)(2,1)S(1)} %get-tuple-element.121.refs_0_), channel_id=1, source_target_pairs={{0,4},{4,0},{8,12},{12,8},{1,5},{5,1},{9,13},{13,9},{2,6},{6,2},{1... | collective-permute-start | bytes 700424 | tf_op jit(solution)/shard_map/ppermute | solution.py:940
  45.5 4.0 %collective-permute-done.8.refs_3_ = bf16[152,768]{1,0:T(8,128)(2,1)S(1)} collective-permute-done((bf16[152,768]{1,0:T(8,128)(2,1)S(1)}, bf16[152,768]{1,0:T(8,128)(2,1)S(1)}, u32[]{:S(2)}, u32[]{:S(2)}) %collective-permute-start.8) | collective-permute-done | bytes 233504 | tf_op jit(solution)/shard_map/ppermute | solution.py:940
  49.5 7.9 %collective-permute-done.7.refs_2_ = bf16[152,768]{1,0:T(8,128)(2,1)S(1)} collective-permute-done((bf16[152,768]{1,0:T(8,128)(2,1)S(1)}, bf16[152,768]{1,0:T(8,128)(2,1)S(1)}, u32[]{:S(2)}, u32[]{:S(2)}) %collective-permute-start.7) | collective-permute-done | bytes 233504 | tf_op jit(solution)/shard_map/ppermute | solution.py:940
  57.5 3.7 %experts_first.2 = (bf16[608,768]{1,0:T(8,128)(2,1)S(1)}, bf16[608,768]{1,0:T(8,128)(2,1)S(1)}, bf16[608,768]{1,0:T(8,128)(2,1)S(1)}, f32[608,256]{1,0:T(8,128)S...) custom-call(s32[1]{0:T(128)} %constant.0.clone.1.refs_0_.pos_ref, bf16[608,768]{1,0:T(8,128)(2,1)S(1)} %lay_rows.1.x_ref.refs_1_, ...), custom_call_target="tpu_custom_call" | custom-call | tf_op jit(solution)/shard_map/experts_first/pallas_call | solution.py:307
  61.2 3.6 %experts_first.3 = (bf16[608,768]{1,0:T(8,128)(2,1)S(1)}, bf16[608,768]{1,0:T(8,128)(2,1)S(1)}, bf16[608,768]{1,0:T(8,128)(2,1)S(1)}, f32[608,256]{1,0:T(8,128)S...) custom-call(s32[1]{0:T(128)} %constant.0.clone.1.refs_0_.pos_ref, ...), custom_call_target="tpu_custom_call" | custom-call | tf_op jit(solution)/shard_map/experts_first/pallas_call | solution.py:307
  64.9 3.6 %experts_second.2 = (bf16[608,768]{1,0:T(8,128)(2,1)S(1)}, bf16[608,768]{1,0:T(8,128)(2,1)S(1)}, bf16[608,768]{1,0:T(8,128)(2,1)S(1)}, bf16[608,896]{1,0:T(8,128)(2,1)S(1)}) custom-call(s32[1]{0:T(128)} %constant.0.clone.1.refs_0_.pos_ref, bf16[608,768]{1,0:T(8,128)(2,1)S(1)} %collective-permute-done.10.x_ref.refs_3_, ...), custom_call_target="tpu_custom_call" | custom-call | tf_op jit(solution)/shard_map/experts_second/pallas_call | solution.py:307
  69.1 3.8 %experts_second.3 = (bf16[608,768]{1,0:T(8,128)(2,1)S(1)}, bf16[608,768]{1,0:T(8,128)(2,1)S(1)}, bf16[608,768]{1,0:T(8,128)(2,1)S(1)}, f32[608,896]{1,0:T(8,128)S(1)}) custom-call(s32[1]{0:T(128)} %constant.0.clone.1.refs_0_.pos_ref, bf16[608,768]{1,0:T(8,128)(2,1)S(1)} %lay_rows.1.x_ref.refs_1_, bf16[608,896]{1,0:T(8,128)(2,1)S(1)} %lay_payload.1.pay_ref, ...), custom_call_target="tpu_custom_call" | custom-call | tf_op jit(solution)/shard_map/experts_second/pallas_call | solution.py:307
  73.9 3.0 %collective-permute-start.19 = (bf16[160,768]{1,0:T(8,128)(2,1)S(1)}, bf16[160,768]{1,0:T(8,128)(2,1)S(1)}, u32[]{:S(2)}, u32[]{:S(2)}) collective-permute-start(bf16[160,768]{1,0:T(8,128)(2,1)S(1)} %get-tuple-element.144), channel_id=1, source_target_pairs={{0,8},{4,12},{8,0},{12,4},{1,9},{5,13},{9,1},{13,5},{2,10},{6,14},... | collective-permute-start | bytes 737288 | tf_op jit(solution)/shard_map/ppermute | solution.py:940
  78.3 2.0 %expert_grads.3 = bf16[2,2,192,768]{3,2,1,0:T(8,128)(2,1)S(1)} custom-call(s32[1]{0:T(128)} %constant.0.clone.1.refs_0_.pos_ref, bf16[608,768]{1,0:T(8,128)(2,1)S(1)} %get-tuple-element.147.refs_0_, bf16[608,768]{1,0:T(8,128)(2,1)S(1)} %lay_rows.1.x_ref.refs_1_, bf16[608,768]{1,0:T(8,128)(2,1)S(1)} %get-tuple-element.148.refs_2_, ...), custom_call_target="tpu_custom_call" | custom-call | tf_op jit(solution)/shard_map/expert_grads/pallas_call | solution.py:307
  81.7 2.0 %expert_grads.4 = bf16[2,2,192,768]{3,2,1,0:T(8,128)(2,1)S(1)} custom-call(s32[1]{0:T(128)} %constant.0.clone.1.refs_0_.pos_ref, bf16[608,768]{1,0:T(8,128)(2,1)S(1)} %get-tuple-element.147.refs_0_, bf16[608,768]{1,0:T(8,128)(2,1)S(1)} %lay_rows.1.x_ref.refs_1_, bf16[608,768]{1,0:T(8,128)(2,1)S(1)} %get-tuple-element.148.refs_2_, ...), custom_call_target="tpu_custom_call" | custom-call | tf_op jit(solution)/shard_map/expert_grads/pallas_call | solution.py:307
  86.9 7.4 %collective-permute-done.19.refs_2_ = bf16[160,768]{1,0:T(8,128)(2,1)S(1)} collective-permute-done((bf16[160,768]{1,0:T(8,128)(2,1)S(1)}, bf16[160,768]{1,0:T(8,128)(2,1)S(1)}, u32[]{:S(2)}, u32[]{:S(2)}) %collective-permute-start.19) | collective-permute-done | bytes 245792 | tf_op jit(solution)/shard_map/ppermute | solution.py:940
  95.0 3.9 %expert_grads.5 = (bf16[2,2,192,768]{3,2,1,0:T(8,128)(2,1)S(1)}, bf16[2,2,192,768]{3,2,1,0:T(8,128)(2,1)S(1)}) custom-call(s32[1]{0:T(128)} %constant.0.clone.1.refs_0_.pos_ref, bf16[608,768]{1,0:T(8,128)(2,1)S(1)} %get-tuple-element.155.refs_0_, bf16[608,768]{1,0:T(8,128)(2,1)S(1)} %lay_rows.1.x_ref.refs_1_, ...), custom_call_target="tpu_custom_call" | custom-call | tf_op jit(solution)/shard_map/expert_grads/pallas_call | solution.py:307
  98.9 4.8 %collective-permute-done.21.got_ref = bf16[2,152,768]{2,1,0:T(8,128)(2,1)S(1)} collective-permute-done((bf16[2,152,768]{2,1,0:T(8,128)(2,1)S(1)}, bf16[2,152,768]{2,1,0:T(8,128)(2,1)S(1)}, u32[]{:S(2)}, u32[]{:S(2)}) %collective-permute-start.21) | collective-permute-done | bytes 466976 | tf_op jit(solution)/shard_map/ppermute | solution.py:940
  105.1 14.3 %all_gather.6.up_ref = bf16[608,768]{1,0:T(8,128)(2,1)S(1)} all-gather(bf16[152,768]{1,0:T(8,128)(2,1)S(1)} %get-tuple-element.171), channel_id=1, replica_groups=mesh['dp'=2,'expert'=4,'tensor'=4] {'tensor'}, dimensions={0}, use_global_device_ids=true | all-gather | bytes 1167360 | tf_op jit(solution)/shard_map/all_gather | solution.py:1121
  119.3 5.9 %attention_back.1 = (f32[4,96,768]{2,1,0:T(8,128)S(1)}, bf16[4,96,768]{2,1,0:T(8,128)(2,1)S(1)}, bf16[160,768]{1,0:T(8,128)(2,1)S(1)}, bf16[160,768]{1,0:T(8,128...) custom-call(s32[1]{0:T(128)} %constant.0.clone.1.refs_0_.pos_ref, ...), custom_call_target="tpu_custom_call" | custom-call | flops 6000000000 | tf_op jit(solution)/shard_map/attention_back/pallas_call | solution.py:307
  129.1 1.7 collective-permute-start.28
  130.8 3.3 %collective-permute-done.23.refs_1_ = bf16[160,768]{1,0:T(8,128)(2,1)S(1)} collective-permute-done((bf16[160,768]{1,0:T(8,128)(2,1)S(1)}, bf16[160,768]{1,0:T(8,128)(2,1)S(1)}, u32[]{:S(2)}, u32[]{:S(2)}) %collective-permute-start.23) | collective-permute-done | bytes 245792 | tf_op jit(solution)/shard_map/ppermute | solution.py:945
  135.5 3.9 %collective-permute-done.24.refs_2_ = bf16[160,768]{1,0:T(8,128)(2,1)S(1)} collective-permute-done((bf16[160,768]{1,0:T(8,128)(2,1)S(1)}, bf16[160,768]{1,0:T(8,128)(2,1)S(1)}, u32[]{:S(2)}, u32[]{:S(2)}) %collective-permute-start.24) | collective-permute-done | bytes 245792 | tf_op jit(solution)/shard_map/ppermute | solution.py:945
  141.3 1.7 collective-permute-done.28.refs_9_
  144.3 3.3 %collective-permute-start.31 = (bf16[104,768]{1,0:T(8,128)(2,1)S(1)}, bf16[104,768]{1,0:T(8,128)(2,1)S(1)}, u32[]{:S(2)}, u32[]{:S(2)}) collective-permute-start(bf16[104,768]{1,0:T(8,128)(2,1)S(1)} %get-tuple-element.185.refs_0_), channel_id=1, source_target_pairs={{0,8},{4,12},{8,0},{12,4},{1,9},{5,13},{9,1},{13,5},{2,10},{6,14},... | collective-permute-start | bytes 479240 | tf_op jit(solution)/shard_map/ppermute | solution.py:940
  148.0 14.5 %all_gather.7.refs_0_ = bf16[608,768]{1,0:T(8,128)(2,1)S(1)} all-gather(bf16[152,768]{1,0:T(8,128)(2,1)S(1)} %get-tuple-element.184), channel_id=1, replica_groups=mesh['dp'=2,'expert'=4,'tensor'=4] {'tensor'}, dimensions={0}, use_global_device_ids=true | all-gather | bytes 1167360 | tf_op jit(solution)/shard_map/all_gather | solution.py:1178
  163.7 1.7 collective-permute-start.39
  168.7 1.7 spread.1
  170.3 2.6 %weight_out.1 = (f32[1,768,768]{2,1,0:T(8,128)}, f32[1,768,768]{2,1,0:T(8,128)}) custom-call(s32[1]{0:T(128)} %constant.0.clone.1.refs_0_.pos_ref, bf16[2,384,768]{2,1,0:T(8,128)(2,1)S(1)} %weight_sum.1.mine_ref, bf16[2,384,768]{2,1,0:T(8,128)(2,1)S(1)} %collective-permute-done.35.other_ref), custom_call_target="tpu_custom_call" | custom-call | tf_op jit(solution)/shard_map/weight_out/pallas_call | solution.py:307
  173.2 4.0 %collective-permute-done.38.refs_2_ = bf16[152,768]{1,0:T(8,128)(2,1)S(1)} collective-permute-done((bf16[152,768]{1,0:T(8,128)(2,1)S(1)}, bf16[152,768]{1,0:T(8,128)(2,1)S(1)}, u32[]{:S(2)}, u32[]{:S(2)}) %collective-permute-start.38) | collective-permute-done | bytes 233504 | tf_op jit(solution)/shard_map/ppermute | solution.py:945
  (96 shorter events, 37.5 us)
Async XLA Ops:
  4.4 20.5 %collective-permute-start.2 = (bf16[160,768]{1,0:T(8,128)(2,1)}, bf16[160,768]{1,0:T(8,128)(2,1)S(1)}, u32[]{:S(2)}, u32[]{:S(2)}) collective-permute-start(bf16[160,768]{1,0:T(8,128)(2,1)} %get-tuple-element.115.refs_0_.refs_6_), channel_id=1, source_target_pairs={{0,8},{4,12},{8,0},{12,4},{1,9},{5,13},{9,1},{13,5},{2,10},{6,14},... | collective-permute-start | bytes 737288 | tf_op jit(solution)/shard_map/ppermute | solution.py:940
  8.5 15.0 %collective-permute-start.1 = (bf16[2,192,768]{2,1,0:T(8,128)(2,1)}, bf16[2,192,768]{2,1,0:T(8,128)(2,1)S(1)}, u32[]{:S(2)}, u32[]{:S(2)}) collective-permute-start(bf16[2,192,768]{2,1,0:T(8,128)(2,1)} %get-tuple-element.112.refs_2_.wb_ref), channel_id=1, source_target_pairs={{0,2},{1,3},{2,0},{3,1},{4,6},{5,7},{6,4},{7,5},{8,10},{9,11},{10,... | collective-permute-start | bytes 1769480 | tf_op jit(solution)/shard_map/ppermute | solution.py:945
  10.0 14.7 %collective-permute-start = (bf16[2,192,768]{2,1,0:T(8,128)(2,1)}, bf16[2,192,768]{2,1,0:T(8,128)(2,1)S(1)}, u32[]{:S(2)}, u32[]{:S(2)}) collective-permute-start(bf16[2,192,768]{2,1,0:T(8,128)(2,1)} %get-tuple-element.107.refs_0_.wa_ref), channel_id=1, source_target_pairs={{0,1},{1,0},{2,3},{3,2},{4,5},{5,4},{6,7},{7,6},{8,9},{9,8},{10,11... | collective-permute-start | bytes 1769480 | tf_op jit(solution)/shard_map/ppermute | solution.py:945
  24.9 17.9 %collective-permute-start.9 = (bf16[2,160,768]{2,1,0:T(8,128)(2,1)S(1)}, bf16[2,160,768]{2,1,0:T(8,128)(2,1)S(1)}, u32[]{:S(2)}, u32[]{:S(2)}) collective-permute-start(bf16[2,160,768]{2,1,0:T(8,128)(2,1)S(1)} %stack.3.near_ref), channel_id=1, source_target_pairs={{0,4},{4,0},{8,12},{12,8},{1,5},{5,1},{9,13},{13,9},{2,6},{6,2},{1... | collective-permute-start | bytes 1474568 | tf_op jit(solution)/shard_map/ppermute | solution.py:940
  28.1 10.9 %collective-permute-start.4 = (bf16[152,768]{1,0:T(8,128)(2,1)S(1)}, bf16[152,768]{1,0:T(8,128)(2,1)S(1)}, u32[]{:S(2)}, u32[]{:S(2)}) collective-permute-start(bf16[152,768]{1,0:T(8,128)(2,1)S(1)} %get-tuple-element.118), channel_id=1, source_target_pairs={{0,2},{1,3},{2,0},{3,1},{4,6},{5,7},{6,4},{7,5},{8,10},{9,11},{10,... | collective-permute-start | bytes 700424 | tf_op jit(solution)/shard_map/ppermute | solution.py:945
  28.6 10.4 %collective-permute-start.5 = (bf16[152,768]{1,0:T(8,128)(2,1)S(1)}, bf16[152,768]{1,0:T(8,128)(2,1)S(1)}, u32[]{:S(2)}, u32[]{:S(2)}) collective-permute-start(bf16[152,768]{1,0:T(8,128)(2,1)S(1)} %get-tuple-element.119), channel_id=1, source_target_pairs={{0,3},{1,2},{2,1},{3,0},{4,7},{5,6},{6,5},{7,4},{8,11},{9,10},{10,... | collective-permute-start | bytes 700424 | tf_op jit(solution)/shard_map/ppermute | solution.py:945
  39.6 9.9 %collective-permute-start.8 = (bf16[152,768]{1,0:T(8,128)(2,1)S(1)}, bf16[152,768]{1,0:T(8,128)(2,1)S(1)}, u32[]{:S(2)}, u32[]{:S(2)}) collective-permute-start(bf16[152,768]{1,0:T(8,128)(2,1)S(1)} %get-tuple-element.121.refs_0_), channel_id=1, source_target_pairs={{0,12},{4,8},{8,4},{12,0},{1,13},{5,9},{9,5},{13,1},{2,14},{6,10},... | collective-permute-start | bytes 700424 | tf_op jit(solution)/shard_map/ppermute | solution.py:940
  39.7 25.2 %collective-permute-start.12 = (bf16[2,2,192,768]{3,2,1,0:T(8,128)(2,1)S(1)}, bf16[2,2,192,768]{3,2,1,0:T(8,128)(2,1)S(1)}, u32[]{:S(2)}, u32[]{:S(2)}) collective-permute-start(bf16[2,2,192,768]{3,2,1,0:T(8,128)(2,1)S(1)} %get-tuple-element.131), channel_id=1, source_target_pairs={{0,2},{1,3},{2,0},{3,1},{4,6},{5,7},{6,4},{7,5},{8,10},{9,11},{10,... | collective-permute-start | bytes 3538952 | tf_op jit(solution)/shard_map/ppermute | solution.py:945
  40.0 24.9 %collective-permute-start.13 = (bf16[2,2,192,768]{3,2,1,0:T(8,128)(2,1)S(1)}, bf16[2,2,192,768]{3,2,1,0:T(8,128)(2,1)S(1)}, u32[]{:S(2)}, u32[]{:S(2)}) collective-permute-start(bf16[2,2,192,768]{3,2,1,0:T(8,128)(2,1)S(1)} %get-tuple-element.132), channel_id=1, source_target_pairs={{0,1},{1,0},{2,3},{3,2},{4,5},{5,4},{6,7},{7,6},{8,9},{9,8},{10,11... | collective-permute-start | bytes 3538952 | tf_op jit(solution)/shard_map/ppermute | solution.py:945
  41.2 16.2 %collective-permute-start.7 = (bf16[152,768]{1,0:T(8,128)(2,1)S(1)}, bf16[152,768]{1,0:T(8,128)(2,1)S(1)}, u32[]{:S(2)}, u32[]{:S(2)}) collective-permute-start(bf16[152,768]{1,0:T(8,128)(2,1)S(1)} %get-tuple-element.121.refs_0_), channel_id=1, source_target_pairs={{0,8},{4,12},{8,0},{12,4},{1,9},{5,13},{9,1},{13,5},{2,10},{6,14},... | collective-permute-start | bytes 700424 | tf_op jit(solution)/shard_map/ppermute | solution.py:940
  42.8 14.6 %collective-permute-start.6 = (bf16[152,768]{1,0:T(8,128)(2,1)S(1)}, bf16[152,768]{1,0:T(8,128)(2,1)S(1)}, u32[]{:S(2)}, u32[]{:S(2)}) collective-permute-start(bf16[152,768]{1,0:T(8,128)(2,1)S(1)} %get-tuple-element.121.refs_0_), channel_id=1, source_target_pairs={{0,4},{4,0},{8,12},{12,8},{1,5},{5,1},{9,13},{13,9},{2,6},{6,2},{1... | collective-permute-start | bytes 700424 | tf_op jit(solution)/shard_map/ppermute | solution.py:940
  49.5 11.7 %collective-permute-start.11 = (bf16[608,896]{1,0:T(8,128)(2,1)S(1)}, bf16[608,896]{1,0:T(8,128)(2,1)S(1)}, u32[]{:S(2)}, u32[]{:S(2)}) collective-permute-start(bf16[608,896]{1,0:T(8,128)(2,1)S(1)} %lay_payload.1.pay_ref), channel_id=1, source_target_pairs={{0,16},{16,0},{1,17},{17,1},{2,18},{18,2},{3,19},{19,3},{4,20},{20... | collective-permute-start | bytes 3268616 | tf_op jit(solution)/shard_map/ppermute | solution.py:935
  73.8 13.1 %collective-permute-start.18 = (bf16[160,768]{1,0:T(8,128)(2,1)S(1)}, bf16[160,768]{1,0:T(8,128)(2,1)S(1)}, u32[]{:S(2)}, u32[]{:S(2)}) collective-permute-start(bf16[160,768]{1,0:T(8,128)(2,1)S(1)} %get-tuple-element.143), channel_id=1, source_target_pairs={{0,4},{4,0},{8,12},{12,8},{1,5},{5,1},{9,13},{13,9},{2,6},{6,2},{1... | collective-permute-start | bytes 737288 | tf_op jit(solution)/shard_map/ppermute | solution.py:940
  73.9 20.4 %collective-permute-start.19 = (bf16[160,768]{1,0:T(8,128)(2,1)S(1)}, bf16[160,768]{1,0:T(8,128)(2,1)S(1)}, u32[]{:S(2)}, u32[]{:S(2)}) collective-permute-start(bf16[160,768]{1,0:T(8,128)(2,1)S(1)} %get-tuple-element.144), channel_id=1, source_target_pairs={{0,8},{4,12},{8,0},{12,4},{1,9},{5,13},{9,1},{13,5},{2,10},{6,14},... | collective-permute-start | bytes 737288 | tf_op jit(solution)/shard_map/ppermute | solution.py:940
  76.9 17.4 %collective-permute-start.20 = (bf16[160,768]{1,0:T(8,128)(2,1)S(1)}, bf16[160,768]{1,0:T(8,128)(2,1)S(1)}, u32[]{:S(2)}, u32[]{:S(2)}) collective-permute-start(bf16[160,768]{1,0:T(8,128)(2,1)S(1)} %get-tuple-element.145), channel_id=1, source_target_pairs={{0,12},{4,8},{8,4},{12,0},{1,13},{5,9},{9,5},{13,1},{2,14},{6,10},... | collective-permute-start | bytes 737288 | tf_op jit(solution)/shard_map/ppermute | solution.py:940
  80.3 39.1 %collective-permute-start.16 = (bf16[2,2,192,768]{3,2,1,0:T(8,128)(2,1)S(1)}, bf16[2,2,192,768]{3,2,1,0:T(8,128)(2,1)S(1)}, u32[]{:S(2)}, u32[]{:S(2)}) collective-permute-start(bf16[2,2,192,768]{3,2,1,0:T(8,128)(2,1)S(1)} %expert_grads.3), channel_id=1, source_target_pairs={{0,2},{1,3},{2,0},{3,1},{4,6},{5,7},{6,4},{7,5},{8,10},{9,11},{10,... | collective-permute-start | bytes 3538952 | tf_op jit(solution)/shard_map/ppermute | solution.py:945
  83.8 35.6 %collective-permute-start.17 = (bf16[2,2,192,768]{3,2,1,0:T(8,128)(2,1)S(1)}, bf16[2,2,192,768]{3,2,1,0:T(8,128)(2,1)S(1)}, u32[]{:S(2)}, u32[]{:S(2)}) collective-permute-start(bf16[2,2,192,768]{3,2,1,0:T(8,128)(2,1)S(1)} %expert_grads.4), channel_id=1, source_target_pairs={{0,1},{1,0},{2,3},{3,2},{4,5},{5,4},{6,7},{7,6},{8,9},{9,8},{10,11... | collective-permute-start | bytes 3538952 | tf_op jit(solution)/shard_map/ppermute | solution.py:945
  86.9 16.9 %collective-permute-start.21 = (bf16[2,152,768]{2,1,0:T(8,128)(2,1)S(1)}, bf16[2,152,768]{2,1,0:T(8,128)(2,1)S(1)}, u32[]{:S(2)}, u32[]{:S(2)}) collective-permute-start(bf16[2,152,768]{2,1,0:T(8,128)(2,1)S(1)} %get-tuple-element.164), channel_id=1, source_target_pairs={{0,4},{4,0},{8,12},{12,8},{1,5},{5,1},{9,13},{13,9},{2,6},{6,2},{1... | collective-permute-start | bytes 1400840 | tf_op jit(solution)/shard_map/ppermute | solution.py:940
  103.9 15.5 %collective-permute-start.22 = (bf16[152,768]{1,0:T(8,128)(2,1)S(1)}, bf16[152,768]{1,0:T(8,128)(2,1)S(1)}, u32[]{:S(2)}, u32[]{:S(2)}) collective-permute-start(bf16[152,768]{1,0:T(8,128)(2,1)S(1)} %get-tuple-element.166), channel_id=1, source_target_pairs={{0,8},{4,12},{8,0},{12,4},{1,9},{5,13},{9,1},{13,5},{2,10},{6,14},... | collective-permute-start | bytes 700424 | tf_op jit(solution)/shard_map/ppermute | solution.py:940
  126.1 13.3 %collective-permute-start.24 = (bf16[160,768]{1,0:T(8,128)(2,1)S(1)}, bf16[160,768]{1,0:T(8,128)(2,1)S(1)}, u32[]{:S(2)}, u32[]{:S(2)}) collective-permute-start(bf16[160,768]{1,0:T(8,128)(2,1)S(1)} %get-tuple-element.175), channel_id=1, source_target_pairs={{0,2},{1,3},{2,0},{3,1},{4,6},{5,7},{6,4},{7,5},{8,10},{9,11},{10,... | collective-permute-start | bytes 737288 | tf_op jit(solution)/shard_map/ppermute | solution.py:945
  127.2 12.2 %collective-permute-start.25 = (bf16[160,768]{1,0:T(8,128)(2,1)S(1)}, bf16[160,768]{1,0:T(8,128)(2,1)S(1)}, u32[]{:S(2)}, u32[]{:S(2)}) collective-permute-start(bf16[160,768]{1,0:T(8,128)(2,1)S(1)} %get-tuple-element.176), channel_id=1, source_target_pairs={{0,3},{1,2},{2,1},{3,0},{4,7},{5,6},{6,5},{7,4},{8,11},{9,10},{10,... | collective-permute-start | bytes 737288 | tf_op jit(solution)/shard_map/ppermute | solution.py:945
  129.0 12.4 %collective-permute-start.27 = (bf16[96,768]{1,0:T(8,128)(2,1)S(1)}, bf16[96,768]{1,0:T(8,128)(2,1)S(1)}, u32[]{:S(2)}, u32[]{:S(2)}) collective-permute-start(bf16[96,768]{1,0:T(8,128)(2,1)S(1)} %get-tuple-element.181), channel_id=1, source_target_pairs={{0,4},{4,0},{8,12},{12,8},{1,5},{5,1},{9,13},{13,9},{2,6},{6,2},{1... | collective-permute-start | bytes 442376 | tf_op jit(solution)/shard_map/ppermute | solution.py:940
  129.1 13.9 %collective-permute-start.28 = (bf16[96,768]{1,0:T(8,128)(2,1)S(1)}, bf16[96,768]{1,0:T(8,128)(2,1)S(1)}, u32[]{:S(2)}, u32[]{:S(2)}) collective-permute-start(bf16[96,768]{1,0:T(8,128)(2,1)S(1)} %get-tuple-element.182), channel_id=1, source_target_pairs={{0,8},{4,12},{8,0},{12,4},{1,9},{5,13},{9,1},{13,5},{2,10},{6,14},... | collective-permute-start | bytes 442376 | tf_op jit(solution)/shard_map/ppermute | solution.py:940
  134.1 8.9 %collective-permute-start.29 = (bf16[96,768]{1,0:T(8,128)(2,1)S(1)}, bf16[96,768]{1,0:T(8,128)(2,1)S(1)}, u32[]{:S(2)}, u32[]{:S(2)}) collective-permute-start(bf16[96,768]{1,0:T(8,128)(2,1)S(1)} %get-tuple-element.183), channel_id=1, source_target_pairs={{0,12},{4,8},{8,4},{12,0},{1,13},{5,9},{9,5},{13,1},{2,14},{6,10},... | collective-permute-start | bytes 442376 | tf_op jit(solution)/shard_map/ppermute | solution.py:940
  139.4 23.1 %collective-permute-start.33 = (bf16[2,192,768]{2,1,0:T(8,128)(2,1)S(1)}, bf16[2,192,768]{2,1,0:T(8,128)(2,1)S(1)}, u32[]{:S(2)}, u32[]{:S(2)}) collective-permute-start(bf16[2,192,768]{2,1,0:T(8,128)(2,1)S(1)} %get-tuple-element.191), channel_id=1, source_target_pairs={{0,1},{1,0},{2,3},{3,2},{4,5},{5,4},{6,7},{7,6},{8,9},{9,8},{10,11... | collective-permute-start | bytes 1769480 | tf_op jit(solution)/shard_map/ppermute | solution.py:945
  140.7 21.8 %collective-permute-start.34 = (bf16[2,192,768]{2,1,0:T(8,128)(2,1)S(1)}, bf16[2,192,768]{2,1,0:T(8,128)(2,1)S(1)}, u32[]{:S(2)}, u32[]{:S(2)}) collective-permute-start(bf16[2,192,768]{2,1,0:T(8,128)(2,1)S(1)} %get-tuple-element.192), channel_id=1, source_target_pairs={{0,2},{1,3},{2,0},{3,1},{4,6},{5,7},{6,4},{7,5},{8,10},{9,11},{10,... | collective-permute-start | bytes 1769480 | tf_op jit(solution)/shard_map/ppermute | solution.py:945
  143.5 18.9 %collective-permute-start.32 = (bf16[104,768]{1,0:T(8,128)(2,1)S(1)}, bf16[104,768]{1,0:T(8,128)(2,1)S(1)}, u32[]{:S(2)}, u32[]{:S(2)}) collective-permute-start(bf16[104,768]{1,0:T(8,128)(2,1)S(1)} %get-tuple-element.185.refs_0_), channel_id=1, source_target_pairs={{0,12},{4,8},{8,4},{12,0},{1,13},{5,9},{9,5},{13,1},{2,14},{6,10},... | collective-permute-start | bytes 479240 | tf_op jit(solution)/shard_map/ppermute | solution.py:940
  144.3 18.2 %collective-permute-start.31 = (bf16[104,768]{1,0:T(8,128)(2,1)S(1)}, bf16[104,768]{1,0:T(8,128)(2,1)S(1)}, u32[]{:S(2)}, u32[]{:S(2)}) collective-permute-start(bf16[104,768]{1,0:T(8,128)(2,1)S(1)} %get-tuple-element.185.refs_0_), channel_id=1, source_target_pairs={{0,8},{4,12},{8,0},{12,4},{1,9},{5,13},{9,1},{13,5},{2,10},{6,14},... | collective-permute-start | bytes 479240 | tf_op jit(solution)/shard_map/ppermute | solution.py:940
  147.5 14.9 %collective-permute-start.30 = (bf16[104,768]{1,0:T(8,128)(2,1)S(1)}, bf16[104,768]{1,0:T(8,128)(2,1)S(1)}, u32[]{:S(2)}, u32[]{:S(2)}) collective-permute-start(bf16[104,768]{1,0:T(8,128)(2,1)S(1)} %get-tuple-element.185.refs_0_), channel_id=1, source_target_pairs={{0,4},{4,0},{8,12},{12,8},{1,5},{5,1},{9,13},{13,9},{2,6},{6,2},{1... | collective-permute-start | bytes 479240 | tf_op jit(solution)/shard_map/ppermute | solution.py:940
  163.7 9.6 %collective-permute-start.39 = (bf16[152,768]{1,0:T(8,128)(2,1)S(1)}, bf16[152,768]{1,0:T(8,128)(2,1)S(1)}, u32[]{:S(2)}, u32[]{:S(2)}) collective-permute-start(bf16[152,768]{1,0:T(8,128)(2,1)S(1)} %add_convert_fusion.refs_0_), channel_id=1, source_target_pairs={{0,3},{1,2},{2,1},{3,0},{4,7},{5,6},{6,5},{7,4},{8,11},{9,10},{10,... | collective-permute-start | bytes 700424 | tf_op jit(solution)/shard_map/ppermute | solution.py:945
  165.4 11.9 %collective-permute-start.38 = (bf16[152,768]{1,0:T(8,128)(2,1)S(1)}, bf16[152,768]{1,0:T(8,128)(2,1)S(1)}, u32[]{:S(2)}, u32[]{:S(2)}) collective-permute-start(bf16[152,768]{1,0:T(8,128)(2,1)S(1)} %add_convert_fusion.refs_0_), channel_id=1, source_target_pairs={{0,2},{1,3},{2,0},{3,1},{4,6},{5,7},{6,4},{7,5},{8,10},{9,11},{10,... | collective-permute-start | bytes 700424 | tf_op jit(solution)/shard_map/ppermute | solution.py:945
  166.7 10.7 %collective-permute-start.37 = (bf16[152,768]{1,0:T(8,128)(2,1)S(1)}, bf16[152,768]{1,0:T(8,128)(2,1)S(1)}, u32[]{:S(2)}, u32[]{:S(2)}) collective-permute-start(bf16[152,768]{1,0:T(8,128)(2,1)S(1)} %add_convert_fusion.refs_0_), channel_id=1, source_target_pairs={{0,1},{1,0},{2,3},{3,2},{4,5},{5,4},{6,7},{7,6},{8,9},{9,8},{10,11... | collective-permute-start | bytes 700424 | tf_op jit(solution)/shard_map/ppermute | solution.py:945
  (17 other events, 155.8 us)

commit v7 on v6

--- a/solution.py
+++ b/solution.py
@@ -714,7 +714,7 @@
 def route_back_kernel(
     experts, token_rows, owners, pos_ref, *refs
 ):
-    backs = refs[:owners]
+    backs = refs[:owners][::-1]
     prob_ref, res_ref, pay_ref, param_ref = refs[owners : owners + 4]
     grad_ref, up_ref, small_ref = refs[owners + 4 :]
     chunk, width = res_ref.shape
@@ -1099,7 +1099,7 @@
         functools.partial(route_back_kernel, experts, token_rows, owners),
         "route_back",
         position,
-        [*backs, prob, residual, payload, params],
+        [*backs[::-1], prob, residual, payload, params],
         [like((chunk, width), f32), like((chunk, width), b16), like((SMALL, width), f32)],
         flops=40_000_000_000,
         limit=8,
@@ -1164,10 +1164,11 @@
     up_x, up_y = after((up_x, up_y), got[1:])
     last_x, last_y = cross(up_x, 1), cross(up_y, 2)
 
+    combined = (block_sum + gated_last.astype(f32)).astype(b16)
     grad_chunk, summed = kernel_call(
         functools.partial(norm_back_kernel, experts, tensors),
         "norm_back",
-        position,
+        after(position, combined),
         [*got, x_chunk, residual_grad, params, own_piece, *reduced],
         [like((chunk, width), b16), like((piece + SMALL, width), b16)],
         [pltpu.VMEM((tensors, SMALL, width), f32)],
@@ -1176,7 +1177,6 @@
     )
     around = [summed] + [hop(summed, k) for k in range(1, owners)]
     grad_rows = lax.all_gather(grad_chunk, "tensor", axis=0, tiled=True)
-    combined = (block_sum + gated_last.astype(f32)).astype(b16)
     combined = after(combined, grad_rows)
     block_parts = [combined] + [cross(combined, j) for j in range(1, tensors)]
 

time: 179 us -> 178 us (level)
  transfers between devices with their start and end apart: 40 -> 40, of which waited for: 15 -> 14; matrix products, arithmetic and copies ran while one was open for 0% -> 0% of each run, Pallas kernels for 18% -> 18%
where the time goes in v7:
time: 178 us
  waiting for transfers between devices  56.5 us (32%)
  Pallas kernels  48 us (27%)
  starting transfers between devices  43.4 us (24%)
  blocking collectives  27.9 us (16%)
    pallas_call x27, Pallas kernels, kernel_call(): pl.pallas_call(kernel, in_specs=[pl.BlockSpec(memory_space=pltpu.SMEM)] +...  48 us
    ppermute x16, waiting for transfers between devices, hop(): return lax.ppermute(value, 'expert', [(i, i ^ bit) for i in range(size)])  28.3 us
    ppermute x17, waiting for transfers between devices, cross(): return lax.ppermute(value, 'tensor', [(i, i ^ bit) for i in range(size)])  28.2 us
    ppermute x16, starting transfers between devices, hop(): return lax.ppermute(value, 'expert', [(i, i ^ bit) for i in range(size)])  22.1 us
    ppermute x17, starting transfers between devices, cross(): return lax.ppermute(value, 'tensor', [(i, i ^ bit) for i in range(size)])  20 us
    all_gather x1, blocking collectives, dense_body(): attn_grad = lax.all_gather(attn_grad, 'tensor', axis=0, tiled=True)  14.3 us
    all_gather x1, blocking collectives, dense_body(): grad_rows = lax.all_gather(grad_chunk, 'tensor', axis=0, tiled=True)  13.6 us
  transfers between devices with their start and end apart: 40, of which 14 were waited for; matrix products, arithmetic and copies ran while one was open for 0% of the time, Pallas kernels for 18%

profile of v7, /device:TPU:0, one launch (start us, length us, event | category | flops | bytes accessed | tf_op | source)
XLA Modules:
  0.0 177.7 jit_solution(10341836903588871335)
XLA Ops:
  0.7 3.7 %chunk.1 = (bf16[152,768]{1,0:T(8,128)(2,1)}, bf16[160,768]{1,0:T(8,128)(2,1)}, f32[8,768]{1,0:T(8,128)}, bf16[2,192,768]{2,1,0:T(8,128)(2,1)}, bf16[2,192,768]{2,1,0:T(8,128)(2,1)}) custom-call(s32[1]{0:T(128)} %constant.0.clone.1.refs_0_.pos_ref, bf16[3,197,768]{2,1,0:T(8,128)(2,1)} %tok_ref.1, bf16[3,197,768]{2,1,0:T(8,128)(2,1)} %refs_2_.1, ...), custom_call_target="tpu_custom_call" | custom-call | tf_op jit(solution)/shard_map/chunk/pallas_call | solution.py:307
  4.4 4.1 %collective-permute-start.2 = (bf16[160,768]{1,0:T(8,128)(2,1)}, bf16[160,768]{1,0:T(8,128)(2,1)S(1)}, u32[]{:S(2)}, u32[]{:S(2)}) collective-permute-start(bf16[160,768]{1,0:T(8,128)(2,1)} %get-tuple-element.116.refs_0_.refs_6_), channel_id=1, source_target_pairs={{0,8},{4,12},{8,0},{12,4},{1,9},{5,13},{9,1},{13,5},{2,10},{6,14},... | collective-permute-start | bytes 737288 | tf_op jit(solution)/shard_map/ppermute | solution.py:940
  12.2 4.7 %attention.1 = (bf16[3,3,208,192]{3,2,1,0:T(8,128)(2,1)S(1)}, f32[3,208,128]{2,1,0:T(8,128)S(1)}, bf16[608,192]{1,0:T(8,128)(2,1)S(1)}, bf16[152,768]{1,0:T(8,12...) custom-call(s32[1]{0:T(128)} %constant.0.clone.1.refs_0_.pos_ref, ...), custom_call_target="tpu_custom_call" | custom-call | flops 40000000000 | tf_op jit(solution)/shard_map/attention/pallas_call | solution.py:307
  17.0 6.5 %collective-permute-done.1.refs_3_.yb_ref = bf16[2,192,768]{2,1,0:T(8,128)(2,1)S(1)} collective-permute-done((bf16[2,192,768]{2,1,0:T(8,128)(2,1)}, bf16[2,192,768]{2,1,0:T(8,128)(2,1)S(1)}, u32[]{:S(2)}, u32[]{:S(2)}) %collective-permute-start.1) | collective-permute-done | bytes 589856 | tf_op jit(solution)/shard_map/ppermute | solution.py:945
  24.9 1.6 collective-permute-start.9
  30.1 4.7 %collective-permute-done.3.refs_1_ = bf16[152,768]{1,0:T(8,128)(2,1)S(1)} collective-permute-done((bf16[152,768]{1,0:T(8,128)(2,1)S(1)}, bf16[152,768]{1,0:T(8,128)(2,1)S(1)}, u32[]{:S(2)}, u32[]{:S(2)}) %collective-permute-start.3) | collective-permute-done | bytes 233504 | tf_op jit(solution)/shard_map/ppermute | solution.py:945
  34.7 4.2 %collective-permute-done.4.refs_2_ = bf16[152,768]{1,0:T(8,128)(2,1)S(1)} collective-permute-done((bf16[152,768]{1,0:T(8,128)(2,1)S(1)}, bf16[152,768]{1,0:T(8,128)(2,1)S(1)}, u32[]{:S(2)}, u32[]{:S(2)}) %collective-permute-start.4) | collective-permute-done | bytes 233504 | tf_op jit(solution)/shard_map/ppermute | solution.py:945
  41.2 1.6 collective-permute-start.7
  42.8 2.5 %collective-permute-start.6 = (bf16[152,768]{1,0:T(8,128)(2,1)S(1)}, bf16[152,768]{1,0:T(8,128)(2,1)S(1)}, u32[]{:S(2)}, u32[]{:S(2)}) collective-permute-start(bf16[152,768]{1,0:T(8,128)(2,1)S(1)} %get-tuple-element.122.refs_0_), channel_id=1, source_target_pairs={{0,4},{4,0},{8,12},{12,8},{1,5},{5,1},{9,13},{13,9},{2,6},{6,2},{1... | collective-permute-start | bytes 700424 | tf_op jit(solution)/shard_map/ppermute | solution.py:940
  45.5 4.0 %collective-permute-done.8.refs_3_ = bf16[152,768]{1,0:T(8,128)(2,1)S(1)} collective-permute-done((bf16[152,768]{1,0:T(8,128)(2,1)S(1)}, bf16[152,768]{1,0:T(8,128)(2,1)S(1)}, u32[]{:S(2)}, u32[]{:S(2)}) %collective-permute-start.8) | collective-permute-done | bytes 233504 | tf_op jit(solution)/shard_map/ppermute | solution.py:940
  49.5 7.9 %collective-permute-done.7.refs_2_ = bf16[152,768]{1,0:T(8,128)(2,1)S(1)} collective-permute-done((bf16[152,768]{1,0:T(8,128)(2,1)S(1)}, bf16[152,768]{1,0:T(8,128)(2,1)S(1)}, u32[]{:S(2)}, u32[]{:S(2)}) %collective-permute-start.7) | collective-permute-done | bytes 233504 | tf_op jit(solution)/shard_map/ppermute | solution.py:940
  57.5 3.7 %experts_first.2 = (bf16[608,768]{1,0:T(8,128)(2,1)S(1)}, bf16[608,768]{1,0:T(8,128)(2,1)S(1)}, bf16[608,768]{1,0:T(8,128)(2,1)S(1)}, f32[608,256]{1,0:T(8,128)S...) custom-call(s32[1]{0:T(128)} %constant.0.clone.1.refs_0_.pos_ref, bf16[608,768]{1,0:T(8,128)(2,1)S(1)} %lay_rows.1.x_ref.refs_1_, ...), custom_call_target="tpu_custom_call" | custom-call | tf_op jit(solution)/shard_map/experts_first/pallas_call | solution.py:307
  61.2 3.6 %experts_first.3 = (bf16[608,768]{1,0:T(8,128)(2,1)S(1)}, bf16[608,768]{1,0:T(8,128)(2,1)S(1)}, bf16[608,768]{1,0:T(8,128)(2,1)S(1)}, f32[608,256]{1,0:T(8,128)S...) custom-call(s32[1]{0:T(128)} %constant.0.clone.1.refs_0_.pos_ref, ...), custom_call_target="tpu_custom_call" | custom-call | tf_op jit(solution)/shard_map/experts_first/pallas_call | solution.py:307
  64.9 3.6 %experts_second.2 = (bf16[608,768]{1,0:T(8,128)(2,1)S(1)}, bf16[608,768]{1,0:T(8,128)(2,1)S(1)}, bf16[608,768]{1,0:T(8,128)(2,1)S(1)}, bf16[608,896]{1,0:T(8,128)(2,1)S(1)}) custom-call(s32[1]{0:T(128)} %constant.0.clone.1.refs_0_.pos_ref, bf16[608,768]{1,0:T(8,128)(2,1)S(1)} %collective-permute-done.10.x_ref.refs_3_, ...), custom_call_target="tpu_custom_call" | custom-call | tf_op jit(solution)/shard_map/experts_second/pallas_call | solution.py:307
  69.1 3.8 %experts_second.3 = (bf16[608,768]{1,0:T(8,128)(2,1)S(1)}, bf16[608,768]{1,0:T(8,128)(2,1)S(1)}, bf16[608,768]{1,0:T(8,128)(2,1)S(1)}, f32[608,896]{1,0:T(8,128)S(1)}) custom-call(s32[1]{0:T(128)} %constant.0.clone.1.refs_0_.pos_ref, bf16[608,768]{1,0:T(8,128)(2,1)S(1)} %lay_rows.1.x_ref.refs_1_, bf16[608,896]{1,0:T(8,128)(2,1)S(1)} %lay_payload.1.pay_ref, ...), custom_call_target="tpu_custom_call" | custom-call | tf_op jit(solution)/shard_map/experts_second/pallas_call | solution.py:307
  73.9 2.5 %collective-permute-start.16 = (bf16[160,768]{1,0:T(8,128)(2,1)S(1)}, bf16[160,768]{1,0:T(8,128)(2,1)S(1)}, u32[]{:S(2)}, u32[]{:S(2)}) collective-permute-start(bf16[160,768]{1,0:T(8,128)(2,1)S(1)} %get-tuple-element.143), channel_id=1, source_target_pairs={{0,12},{4,8},{8,4},{12,0},{1,13},{5,9},{9,5},{13,1},{2,14},{6,10},... | collective-permute-start | bytes 737288 | tf_op jit(solution)/shard_map/ppermute | solution.py:940
  77.4 2.0 %expert_grads.4 = bf16[2,2,192,768]{3,2,1,0:T(8,128)(2,1)S(1)} custom-call(s32[1]{0:T(128)} %constant.0.clone.1.refs_0_.pos_ref, bf16[608,768]{1,0:T(8,128)(2,1)S(1)} %get-tuple-element.166.refs_0_, bf16[608,768]{1,0:T(8,128)(2,1)S(1)} %lay_rows.1.x_ref.refs_1_, bf16[608,768]{1,0:T(8,128)(2,1)S(1)} %get-tuple-element.167.refs_2_, ...), custom_call_target="tpu_custom_call" | custom-call | tf_op jit(solution)/shard_map/expert_grads/pallas_call | solution.py:307
  80.8 2.0 %expert_grads.5 = bf16[2,2,192,768]{3,2,1,0:T(8,128)(2,1)S(1)} custom-call(s32[1]{0:T(128)} %constant.0.clone.1.refs_0_.pos_ref, bf16[608,768]{1,0:T(8,128)(2,1)S(1)} %get-tuple-element.166.refs_0_, bf16[608,768]{1,0:T(8,128)(2,1)S(1)} %lay_rows.1.x_ref.refs_1_, bf16[608,768]{1,0:T(8,128)(2,1)S(1)} %get-tuple-element.167.refs_2_, ...), custom_call_target="tpu_custom_call" | custom-call | tf_op jit(solution)/shard_map/expert_grads/pallas_call | solution.py:307
  85.4 3.0 %collective-permute-done.16.refs_0_ = bf16[160,768]{1,0:T(8,128)(2,1)S(1)} collective-permute-done((bf16[160,768]{1,0:T(8,128)(2,1)S(1)}, bf16[160,768]{1,0:T(8,128)(2,1)S(1)}, u32[]{:S(2)}, u32[]{:S(2)}) %collective-permute-start.16) | collective-permute-done | bytes 245792 | tf_op jit(solution)/shard_map/ppermute | solution.py:940
  88.4 10.8 %collective-permute-done.17.refs_1_ = bf16[160,768]{1,0:T(8,128)(2,1)S(1)} collective-permute-done((bf16[160,768]{1,0:T(8,128)(2,1)S(1)}, bf16[160,768]{1,0:T(8,128)(2,1)S(1)}, u32[]{:S(2)}, u32[]{:S(2)}) %collective-permute-start.17) | collective-permute-done | bytes 245792 | tf_op jit(solution)/shard_map/ppermute | solution.py:940
  100.0 3.9 %expert_grads.3 = (bf16[2,2,192,768]{3,2,1,0:T(8,128)(2,1)S(1)}, bf16[2,2,192,768]{3,2,1,0:T(8,128)(2,1)S(1)}) custom-call(s32[1]{0:T(128)} %constant.0.clone.1.refs_0_.pos_ref, bf16[608,768]{1,0:T(8,128)(2,1)S(1)} %get-tuple-element.151.refs_0_, bf16[608,768]{1,0:T(8,128)(2,1)S(1)} %lay_rows.1.x_ref.refs_1_, ...), custom_call_target="tpu_custom_call" | custom-call | tf_op jit(solution)/shard_map/expert_grads/pallas_call | solution.py:307
  104.1 14.3 %all_gather.6.up_ref = bf16[608,768]{1,0:T(8,128)(2,1)S(1)} all-gather(bf16[152,768]{1,0:T(8,128)(2,1)S(1)} %get-tuple-element.174), channel_id=1, replica_groups=mesh['dp'=2,'expert'=4,'tensor'=4] {'tensor'}, dimensions={0}, use_global_device_ids=true | all-gather | bytes 1167360 | tf_op jit(solution)/shard_map/all_gather | solution.py:1121
  118.5 5.9 %attention_back.1 = (f32[4,96,768]{2,1,0:T(8,128)S(1)}, bf16[4,96,768]{2,1,0:T(8,128)(2,1)S(1)}, bf16[160,768]{1,0:T(8,128)(2,1)S(1)}, bf16[160,768]{1,0:T(8,128...) custom-call(s32[1]{0:T(128)} %constant.0.clone.1.refs_0_.pos_ref, ...), custom_call_target="tpu_custom_call" | custom-call | flops 6000000000 | tf_op jit(solution)/shard_map/attention_back/pallas_call | solution.py:307
  130.1 3.2 %collective-permute-done.23.refs_1_ = bf16[160,768]{1,0:T(8,128)(2,1)S(1)} collective-permute-done((bf16[160,768]{1,0:T(8,128)(2,1)S(1)}, bf16[160,768]{1,0:T(8,128)(2,1)S(1)}, u32[]{:S(2)}, u32[]{:S(2)}) %collective-permute-start.23) | collective-permute-done | bytes 245792 | tf_op jit(solution)/shard_map/ppermute | solution.py:945
  134.7 3.8 %collective-permute-done.24.refs_2_ = bf16[160,768]{1,0:T(8,128)(2,1)S(1)} collective-permute-done((bf16[160,768]{1,0:T(8,128)(2,1)S(1)}, bf16[160,768]{1,0:T(8,128)(2,1)S(1)}, u32[]{:S(2)}, u32[]{:S(2)}) %collective-permute-start.24) | collective-permute-done | bytes 245792 | tf_op jit(solution)/shard_map/ppermute | solution.py:945
  140.4 2.5 %collective-permute-done.28.refs_9_ = bf16[96,768]{1,0:T(8,128)(2,1)S(1)} collective-permute-done((bf16[96,768]{1,0:T(8,128)(2,1)S(1)}, bf16[96,768]{1,0:T(8,128)(2,1)S(1)}, u32[]{:S(2)}, u32[]{:S(2)}) %collective-permute-start.28) | collective-permute-done | bytes 147488 | tf_op jit(solution)/shard_map/ppermute | solution.py:940
  143.5 1.7 collective-permute-start.32
  145.2 2.6 %collective-permute-start.31 = (bf16[104,768]{1,0:T(8,128)(2,1)S(1)}, bf16[104,768]{1,0:T(8,128)(2,1)S(1)}, u32[]{:S(2)}, u32[]{:S(2)}) collective-permute-start(bf16[104,768]{1,0:T(8,128)(2,1)S(1)} %get-tuple-element.188.refs_0_), channel_id=1, source_target_pairs={{0,8},{4,12},{8,0},{12,4},{1,9},{5,13},{9,1},{13,5},{2,10},{6,14},... | collective-permute-start | bytes 479240 | tf_op jit(solution)/shard_map/ppermute | solution.py:940
  147.9 13.6 %all_gather.7.refs_0_ = bf16[608,768]{1,0:T(8,128)(2,1)S(1)} all-gather(bf16[152,768]{1,0:T(8,128)(2,1)S(1)} %get-tuple-element.187), channel_id=1, replica_groups=mesh['dp'=2,'expert'=4,'tensor'=4] {'tensor'}, dimensions={0}, use_global_device_ids=true | all-gather | bytes 1167360 | tf_op jit(solution)/shard_map/all_gather | solution.py:1179
  167.7 1.7 spread.1
  169.3 2.6 %weight_out.1 = (f32[1,768,768]{2,1,0:T(8,128)}, f32[1,768,768]{2,1,0:T(8,128)}) custom-call(s32[1]{0:T(128)} %constant.0.clone.1.refs_0_.pos_ref, bf16[2,384,768]{2,1,0:T(8,128)(2,1)S(1)} %weight_sum.1.mine_ref, bf16[2,384,768]{2,1,0:T(8,128)(2,1)S(1)} %collective-permute-done.35.other_ref), custom_call_target="tpu_custom_call" | custom-call | tf_op jit(solution)/shard_map/weight_out/pallas_call | solution.py:307
  172.2 4.1 %collective-permute-done.38.refs_2_ = bf16[152,768]{1,0:T(8,128)(2,1)S(1)} collective-permute-done((bf16[152,768]{1,0:T(8,128)(2,1)S(1)}, bf16[152,768]{1,0:T(8,128)(2,1)S(1)}, u32[]{:S(2)}, u32[]{:S(2)}) %collective-permute-start.38) | collective-permute-done | bytes 233504 | tf_op jit(solution)/shard_map/ppermute | solution.py:945
  (96 shorter events, 36.2 us)
Async XLA Ops:
  4.4 20.5 %collective-permute-start.2 = (bf16[160,768]{1,0:T(8,128)(2,1)}, bf16[160,768]{1,0:T(8,128)(2,1)S(1)}, u32[]{:S(2)}, u32[]{:S(2)}) collective-permute-start(bf16[160,768]{1,0:T(8,128)(2,1)} %get-tuple-element.116.refs_0_.refs_6_), channel_id=1, source_target_pairs={{0,8},{4,12},{8,0},{12,4},{1,9},{5,13},{9,1},{13,5},{2,10},{6,14},... | collective-permute-start | bytes 737288 | tf_op jit(solution)/shard_map/ppermute | solution.py:940
  8.5 15.0 %collective-permute-start.1 = (bf16[2,192,768]{2,1,0:T(8,128)(2,1)}, bf16[2,192,768]{2,1,0:T(8,128)(2,1)S(1)}, u32[]{:S(2)}, u32[]{:S(2)}) collective-permute-start(bf16[2,192,768]{2,1,0:T(8,128)(2,1)} %get-tuple-element.113.refs_2_.wb_ref), channel_id=1, source_target_pairs={{0,2},{1,3},{2,0},{3,1},{4,6},{5,7},{6,4},{7,5},{8,10},{9,11},{10,... | collective-permute-start | bytes 1769480 | tf_op jit(solution)/shard_map/ppermute | solution.py:945
  10.0 14.7 %collective-permute-start = (bf16[2,192,768]{2,1,0:T(8,128)(2,1)}, bf16[2,192,768]{2,1,0:T(8,128)(2,1)S(1)}, u32[]{:S(2)}, u32[]{:S(2)}) collective-permute-start(bf16[2,192,768]{2,1,0:T(8,128)(2,1)} %get-tuple-element.108.refs_0_.wa_ref), channel_id=1, source_target_pairs={{0,1},{1,0},{2,3},{3,2},{4,5},{5,4},{6,7},{7,6},{8,9},{9,8},{10,11... | collective-permute-start | bytes 1769480 | tf_op jit(solution)/shard_map/ppermute | solution.py:945
  24.9 17.9 %collective-permute-start.9 = (bf16[2,160,768]{2,1,0:T(8,128)(2,1)S(1)}, bf16[2,160,768]{2,1,0:T(8,128)(2,1)S(1)}, u32[]{:S(2)}, u32[]{:S(2)}) collective-permute-start(bf16[2,160,768]{2,1,0:T(8,128)(2,1)S(1)} %stack.3.near_ref), channel_id=1, source_target_pairs={{0,4},{4,0},{8,12},{12,8},{1,5},{5,1},{9,13},{13,9},{2,6},{6,2},{1... | collective-permute-start | bytes 1474568 | tf_op jit(solution)/shard_map/ppermute | solution.py:940
  28.1 10.9 %collective-permute-start.4 = (bf16[152,768]{1,0:T(8,128)(2,1)S(1)}, bf16[152,768]{1,0:T(8,128)(2,1)S(1)}, u32[]{:S(2)}, u32[]{:S(2)}) collective-permute-start(bf16[152,768]{1,0:T(8,128)(2,1)S(1)} %get-tuple-element.119), channel_id=1, source_target_pairs={{0,2},{1,3},{2,0},{3,1},{4,6},{5,7},{6,4},{7,5},{8,10},{9,11},{10,... | collective-permute-start | bytes 700424 | tf_op jit(solution)/shard_map/ppermute | solution.py:945
  28.6 10.4 %collective-permute-start.5 = (bf16[152,768]{1,0:T(8,128)(2,1)S(1)}, bf16[152,768]{1,0:T(8,128)(2,1)S(1)}, u32[]{:S(2)}, u32[]{:S(2)}) collective-permute-start(bf16[152,768]{1,0:T(8,128)(2,1)S(1)} %get-tuple-element.120), channel_id=1, source_target_pairs={{0,3},{1,2},{2,1},{3,0},{4,7},{5,6},{6,5},{7,4},{8,11},{9,10},{10,... | collective-permute-start | bytes 700424 | tf_op jit(solution)/shard_map/ppermute | solution.py:945
  39.6 9.9 %collective-permute-start.8 = (bf16[152,768]{1,0:T(8,128)(2,1)S(1)}, bf16[152,768]{1,0:T(8,128)(2,1)S(1)}, u32[]{:S(2)}, u32[]{:S(2)}) collective-permute-start(bf16[152,768]{1,0:T(8,128)(2,1)S(1)} %get-tuple-element.122.refs_0_), channel_id=1, source_target_pairs={{0,12},{4,8},{8,4},{12,0},{1,13},{5,9},{9,5},{13,1},{2,14},{6,10},... | collective-permute-start | bytes 700424 | tf_op jit(solution)/shard_map/ppermute | solution.py:940
  39.7 25.2 %collective-permute-start.12 = (bf16[2,2,192,768]{3,2,1,0:T(8,128)(2,1)S(1)}, bf16[2,2,192,768]{3,2,1,0:T(8,128)(2,1)S(1)}, u32[]{:S(2)}, u32[]{:S(2)}) collective-permute-start(bf16[2,2,192,768]{3,2,1,0:T(8,128)(2,1)S(1)} %get-tuple-element.132), channel_id=1, source_target_pairs={{0,2},{1,3},{2,0},{3,1},{4,6},{5,7},{6,4},{7,5},{8,10},{9,11},{10,... | collective-permute-start | bytes 3538952 | tf_op jit(solution)/shard_map/ppermute | solution.py:945
  40.0 24.9 %collective-permute-start.13 = (bf16[2,2,192,768]{3,2,1,0:T(8,128)(2,1)S(1)}, bf16[2,2,192,768]{3,2,1,0:T(8,128)(2,1)S(1)}, u32[]{:S(2)}, u32[]{:S(2)}) collective-permute-start(bf16[2,2,192,768]{3,2,1,0:T(8,128)(2,1)S(1)} %get-tuple-element.133), channel_id=1, source_target_pairs={{0,1},{1,0},{2,3},{3,2},{4,5},{5,4},{6,7},{7,6},{8,9},{9,8},{10,11... | collective-permute-start | bytes 3538952 | tf_op jit(solution)/shard_map/ppermute | solution.py:945
  41.2 16.2 %collective-permute-start.7 = (bf16[152,768]{1,0:T(8,128)(2,1)S(1)}, bf16[152,768]{1,0:T(8,128)(2,1)S(1)}, u32[]{:S(2)}, u32[]{:S(2)}) collective-permute-start(bf16[152,768]{1,0:T(8,128)(2,1)S(1)} %get-tuple-element.122.refs_0_), channel_id=1, source_target_pairs={{0,8},{4,12},{8,0},{12,4},{1,9},{5,13},{9,1},{13,5},{2,10},{6,14},... | collective-permute-start | bytes 700424 | tf_op jit(solution)/shard_map/ppermute | solution.py:940
  42.8 14.6 %collective-permute-start.6 = (bf16[152,768]{1,0:T(8,128)(2,1)S(1)}, bf16[152,768]{1,0:T(8,128)(2,1)S(1)}, u32[]{:S(2)}, u32[]{:S(2)}) collective-permute-start(bf16[152,768]{1,0:T(8,128)(2,1)S(1)} %get-tuple-element.122.refs_0_), channel_id=1, source_target_pairs={{0,4},{4,0},{8,12},{12,8},{1,5},{5,1},{9,13},{13,9},{2,6},{6,2},{1... | collective-permute-start | bytes 700424 | tf_op jit(solution)/shard_map/ppermute | solution.py:940
  49.5 11.7 %collective-permute-start.11 = (bf16[608,896]{1,0:T(8,128)(2,1)S(1)}, bf16[608,896]{1,0:T(8,128)(2,1)S(1)}, u32[]{:S(2)}, u32[]{:S(2)}) collective-permute-start(bf16[608,896]{1,0:T(8,128)(2,1)S(1)} %lay_payload.1.pay_ref), channel_id=1, source_target_pairs={{0,16},{16,0},{1,17},{17,1},{2,18},{18,2},{3,19},{19,3},{4,20},{20... | collective-permute-start | bytes 3268616 | tf_op jit(solution)/shard_map/ppermute | solution.py:935
  73.8 10.6 %collective-permute-start.18 = (bf16[160,768]{1,0:T(8,128)(2,1)S(1)}, bf16[160,768]{1,0:T(8,128)(2,1)S(1)}, u32[]{:S(2)}, u32[]{:S(2)}) collective-permute-start(bf16[160,768]{1,0:T(8,128)(2,1)S(1)} %get-tuple-element.145), channel_id=1, source_target_pairs={{0,4},{4,0},{8,12},{12,8},{1,5},{5,1},{9,13},{13,9},{2,6},{6,2},{1... | collective-permute-start | bytes 737288 | tf_op jit(solution)/shard_map/ppermute | solution.py:940
  73.9 14.6 %collective-permute-start.16 = (bf16[160,768]{1,0:T(8,128)(2,1)S(1)}, bf16[160,768]{1,0:T(8,128)(2,1)S(1)}, u32[]{:S(2)}, u32[]{:S(2)}) collective-permute-start(bf16[160,768]{1,0:T(8,128)(2,1)S(1)} %get-tuple-element.143), channel_id=1, source_target_pairs={{0,12},{4,8},{8,4},{12,0},{1,13},{5,9},{9,5},{13,1},{2,14},{6,10},... | collective-permute-start | bytes 737288 | tf_op jit(solution)/shard_map/ppermute | solution.py:940
  76.4 22.9 %collective-permute-start.17 = (bf16[160,768]{1,0:T(8,128)(2,1)S(1)}, bf16[160,768]{1,0:T(8,128)(2,1)S(1)}, u32[]{:S(2)}, u32[]{:S(2)}) collective-permute-start(bf16[160,768]{1,0:T(8,128)(2,1)S(1)} %get-tuple-element.144), channel_id=1, source_target_pairs={{0,8},{4,12},{8,0},{12,4},{1,9},{5,13},{9,1},{13,5},{2,10},{6,14},... | collective-permute-start | bytes 737288 | tf_op jit(solution)/shard_map/ppermute | solution.py:940
  79.4 39.1 %collective-permute-start.21 = (bf16[2,2,192,768]{3,2,1,0:T(8,128)(2,1)S(1)}, bf16[2,2,192,768]{3,2,1,0:T(8,128)(2,1)S(1)}, u32[]{:S(2)}, u32[]{:S(2)}) collective-permute-start(bf16[2,2,192,768]{3,2,1,0:T(8,128)(2,1)S(1)} %expert_grads.4), channel_id=1, source_target_pairs={{0,2},{1,3},{2,0},{3,1},{4,6},{5,7},{6,4},{7,5},{8,10},{9,11},{10,... | collective-permute-start | bytes 3538952 | tf_op jit(solution)/shard_map/ppermute | solution.py:945
  82.9 35.6 %collective-permute-start.22 = (bf16[2,2,192,768]{3,2,1,0:T(8,128)(2,1)S(1)}, bf16[2,2,192,768]{3,2,1,0:T(8,128)(2,1)S(1)}, u32[]{:S(2)}, u32[]{:S(2)}) collective-permute-start(bf16[2,2,192,768]{3,2,1,0:T(8,128)(2,1)S(1)} %expert_grads.5), channel_id=1, source_target_pairs={{0,1},{1,0},{2,3},{3,2},{4,5},{5,4},{6,7},{7,6},{8,9},{9,8},{10,11... | collective-permute-start | bytes 3538952 | tf_op jit(solution)/shard_map/ppermute | solution.py:945
  84.4 19.5 %collective-permute-start.19 = (bf16[2,152,768]{2,1,0:T(8,128)(2,1)S(1)}, bf16[2,152,768]{2,1,0:T(8,128)(2,1)S(1)}, u32[]{:S(2)}, u32[]{:S(2)}) collective-permute-start(bf16[2,152,768]{2,1,0:T(8,128)(2,1)S(1)} %get-tuple-element.160), channel_id=1, source_target_pairs={{0,4},{4,0},{8,12},{12,8},{1,5},{5,1},{9,13},{13,9},{2,6},{6,2},{1... | collective-permute-start | bytes 1400840 | tf_op jit(solution)/shard_map/ppermute | solution.py:940
  104.0 14.4 %collective-permute-start.20 = (bf16[152,768]{1,0:T(8,128)(2,1)S(1)}, bf16[152,768]{1,0:T(8,128)(2,1)S(1)}, u32[]{:S(2)}, u32[]{:S(2)}) collective-permute-start(bf16[152,768]{1,0:T(8,128)(2,1)S(1)} %get-tuple-element.163), channel_id=1, source_target_pairs={{0,8},{4,12},{8,0},{12,4},{1,9},{5,13},{9,1},{13,5},{2,10},{6,14},... | collective-permute-start | bytes 700424 | tf_op jit(solution)/shard_map/ppermute | solution.py:940
  125.2 13.3 %collective-permute-start.24 = (bf16[160,768]{1,0:T(8,128)(2,1)S(1)}, bf16[160,768]{1,0:T(8,128)(2,1)S(1)}, u32[]{:S(2)}, u32[]{:S(2)}) collective-permute-start(bf16[160,768]{1,0:T(8,128)(2,1)S(1)} %get-tuple-element.178), channel_id=1, source_target_pairs={{0,2},{1,3},{2,0},{3,1},{4,6},{5,7},{6,4},{7,5},{8,10},{9,11},{10,... | collective-permute-start | bytes 737288 | tf_op jit(solution)/shard_map/ppermute | solution.py:945
  126.3 12.2 %collective-permute-start.25 = (bf16[160,768]{1,0:T(8,128)(2,1)S(1)}, bf16[160,768]{1,0:T(8,128)(2,1)S(1)}, u32[]{:S(2)}, u32[]{:S(2)}) collective-permute-start(bf16[160,768]{1,0:T(8,128)(2,1)S(1)} %get-tuple-element.179), channel_id=1, source_target_pairs={{0,3},{1,2},{2,1},{3,0},{4,7},{5,6},{6,5},{7,4},{8,11},{9,10},{10,... | collective-permute-start | bytes 737288 | tf_op jit(solution)/shard_map/ppermute | solution.py:945
  128.1 12.3 %collective-permute-start.27 = (bf16[96,768]{1,0:T(8,128)(2,1)S(1)}, bf16[96,768]{1,0:T(8,128)(2,1)S(1)}, u32[]{:S(2)}, u32[]{:S(2)}) collective-permute-start(bf16[96,768]{1,0:T(8,128)(2,1)S(1)} %get-tuple-element.184), channel_id=1, source_target_pairs={{0,4},{4,0},{8,12},{12,8},{1,5},{5,1},{9,13},{13,9},{2,6},{6,2},{1... | collective-permute-start | bytes 442376 | tf_op jit(solution)/shard_map/ppermute | solution.py:940
  129.7 13.2 %collective-permute-start.28 = (bf16[96,768]{1,0:T(8,128)(2,1)S(1)}, bf16[96,768]{1,0:T(8,128)(2,1)S(1)}, u32[]{:S(2)}, u32[]{:S(2)}) collective-permute-start(bf16[96,768]{1,0:T(8,128)(2,1)S(1)} %get-tuple-element.185), channel_id=1, source_target_pairs={{0,8},{4,12},{8,0},{12,4},{1,9},{5,13},{9,1},{13,5},{2,10},{6,14},... | collective-permute-start | bytes 442376 | tf_op jit(solution)/shard_map/ppermute | solution.py:940
  133.2 9.7 %collective-permute-start.29 = (bf16[96,768]{1,0:T(8,128)(2,1)S(1)}, bf16[96,768]{1,0:T(8,128)(2,1)S(1)}, u32[]{:S(2)}, u32[]{:S(2)}) collective-permute-start(bf16[96,768]{1,0:T(8,128)(2,1)S(1)} %get-tuple-element.186), channel_id=1, source_target_pairs={{0,12},{4,8},{8,4},{12,0},{1,13},{5,9},{9,5},{13,1},{2,14},{6,10},... | collective-permute-start | bytes 442376 | tf_op jit(solution)/shard_map/ppermute | solution.py:940
  138.5 23.1 %collective-permute-start.33 = (bf16[2,192,768]{2,1,0:T(8,128)(2,1)S(1)}, bf16[2,192,768]{2,1,0:T(8,128)(2,1)S(1)}, u32[]{:S(2)}, u32[]{:S(2)}) collective-permute-start(bf16[2,192,768]{2,1,0:T(8,128)(2,1)S(1)} %get-tuple-element.194), channel_id=1, source_target_pairs={{0,1},{1,0},{2,3},{3,2},{4,5},{5,4},{6,7},{7,6},{8,9},{9,8},{10,11... | collective-permute-start | bytes 1769480 | tf_op jit(solution)/shard_map/ppermute | solution.py:945
  139.8 21.8 %collective-permute-start.34 = (bf16[2,192,768]{2,1,0:T(8,128)(2,1)S(1)}, bf16[2,192,768]{2,1,0:T(8,128)(2,1)S(1)}, u32[]{:S(2)}, u32[]{:S(2)}) collective-permute-start(bf16[2,192,768]{2,1,0:T(8,128)(2,1)S(1)} %get-tuple-element.195), channel_id=1, source_target_pairs={{0,2},{1,3},{2,0},{3,1},{4,6},{5,7},{6,4},{7,5},{8,10},{9,11},{10,... | collective-permute-start | bytes 1769480 | tf_op jit(solution)/shard_map/ppermute | solution.py:945
  143.5 18.1 %collective-permute-start.32 = (bf16[104,768]{1,0:T(8,128)(2,1)S(1)}, bf16[104,768]{1,0:T(8,128)(2,1)S(1)}, u32[]{:S(2)}, u32[]{:S(2)}) collective-permute-start(bf16[104,768]{1,0:T(8,128)(2,1)S(1)} %get-tuple-element.188.refs_0_), channel_id=1, source_target_pairs={{0,12},{4,8},{8,4},{12,0},{1,13},{5,9},{9,5},{13,1},{2,14},{6,10},... | collective-permute-start | bytes 479240 | tf_op jit(solution)/shard_map/ppermute | solution.py:940
  145.2 16.4 %collective-permute-start.31 = (bf16[104,768]{1,0:T(8,128)(2,1)S(1)}, bf16[104,768]{1,0:T(8,128)(2,1)S(1)}, u32[]{:S(2)}, u32[]{:S(2)}) collective-permute-start(bf16[104,768]{1,0:T(8,128)(2,1)S(1)} %get-tuple-element.188.refs_0_), channel_id=1, source_target_pairs={{0,8},{4,12},{8,0},{12,4},{1,9},{5,13},{9,1},{13,5},{2,10},{6,14},... | collective-permute-start | bytes 479240 | tf_op jit(solution)/shard_map/ppermute | solution.py:940
  147.8 13.8 %collective-permute-start.30 = (bf16[104,768]{1,0:T(8,128)(2,1)S(1)}, bf16[104,768]{1,0:T(8,128)(2,1)S(1)}, u32[]{:S(2)}, u32[]{:S(2)}) collective-permute-start(bf16[104,768]{1,0:T(8,128)(2,1)S(1)} %get-tuple-element.188.refs_0_), channel_id=1, source_target_pairs={{0,4},{4,0},{8,12},{12,8},{1,5},{5,1},{9,13},{13,9},{2,6},{6,2},{1... | collective-permute-start | bytes 479240 | tf_op jit(solution)/shard_map/ppermute | solution.py:940
  162.7 9.5 %collective-permute-start.39 = (bf16[152,768]{1,0:T(8,128)(2,1)S(1)}, bf16[152,768]{1,0:T(8,128)(2,1)S(1)}, u32[]{:S(2)}, u32[]{:S(2)}) collective-permute-start(bf16[152,768]{1,0:T(8,128)(2,1)S(1)} %add_convert_fusion.refs_0_), channel_id=1, source_target_pairs={{0,3},{1,2},{2,1},{3,0},{4,7},{5,6},{6,5},{7,4},{8,11},{9,10},{10,... | collective-permute-start | bytes 700424 | tf_op jit(solution)/shard_map/ppermute | solution.py:945
  164.4 11.9 %collective-permute-start.38 = (bf16[152,768]{1,0:T(8,128)(2,1)S(1)}, bf16[152,768]{1,0:T(8,128)(2,1)S(1)}, u32[]{:S(2)}, u32[]{:S(2)}) collective-permute-start(bf16[152,768]{1,0:T(8,128)(2,1)S(1)} %add_convert_fusion.refs_0_), channel_id=1, source_target_pairs={{0,2},{1,3},{2,0},{3,1},{4,6},{5,7},{6,4},{7,5},{8,10},{9,11},{10,... | collective-permute-start | bytes 700424 | tf_op jit(solution)/shard_map/ppermute | solution.py:945
  165.7 10.8 %collective-permute-start.37 = (bf16[152,768]{1,0:T(8,128)(2,1)S(1)}, bf16[152,768]{1,0:T(8,128)(2,1)S(1)}, u32[]{:S(2)}, u32[]{:S(2)}) collective-permute-start(bf16[152,768]{1,0:T(8,128)(2,1)S(1)} %add_convert_fusion.refs_0_), channel_id=1, source_target_pairs={{0,1},{1,0},{2,3},{3,2},{4,5},{5,4},{6,7},{7,6},{8,9},{9,8},{10,11... | collective-permute-start | bytes 700424 | tf_op jit(solution)/shard_map/ppermute | solution.py:945
  (17 other events, 155.5 us)
